TPU v7x, 256 devices: a whole 4x4x8 slice. The times are simulated.
256 devices in a mesh: ctx: 8 (over y, x_hi), chan: 32 (over x_lo, z, core).
Axes of the slice: x: 4 (x_hi: 2, x_lo: 2; x = x_hi * 2 + x_lo), y: 4, z: 8, core: 2. Of those that a mesh axis runs over, the one named last changes fastest.
Arguments:
- token_ids: int32 [2048], P('ctx'), may hold values from 0 to 511
- embed_table: bfloat16 [512, 8192], P(None, 'chan'), may hold values from -6 to 6
- in_weight: bfloat16 [8192, 3, 8192], P(None, None, 'chan'), may hold values from -0.0625 to 0.0625
- feat_taps: float32 [3, 3, 8192], P(None, None, 'chan'), may hold values from -3.5 to 3.5
- modal_rates: float32 [16, 512], P(None, 'chan'), may hold values from 4.8828126e-05 to 0.03
- modal_residues: float32 [16, 512], P(None, 'chan'), may hold values from -1.5 to 1.5
- out_grad: bfloat16 [2048, 8192], P('ctx', 'chan'), may hold values from -6 to 6
Outputs:
- output: bfloat16 [2048, 8192], P('ctx', 'chan')
- grad_tokens: bfloat16 [2048, 8192], P('ctx', 'chan')
All inputs are finite; a program needn't handle non-finite values.
Results may differ from a plain program's by a relative error of at most 0.034.
Values may be sent and summed in bfloat16 or wider, within the bound.
No kernel may reach another device: no remote copies, remote signals or barrier semaphores. Data moves between devices by JAX's collectives and lax.ppermute only.
A program may use at most 128 MiB of HBM per device.

v0:
```python
import jax
import jax.numpy as jnp
from jax import lax
from jax.sharding import PartitionSpec as P

GROUP = 16
ORDER = 16
FEAT = 3


exact_mode = lax.Precision.HIGHEST


def passed_along(value, axis, by):
    count = lax.axis_size(axis)
    pairs = [(i, i + by) for i in range(count) if 0 <= i + by < count]
    return lax.ppermute(value, axis, pairs)


def neighbour_rows(pieces, offset):
    return passed_along(pieces, "ctx", offset)


def featurize_local(stream, taps):
    length = stream.shape[0]
    tail_rows = neighbour_rows(stream[length - (FEAT - 1) :], 1)
    widened = jnp.concatenate([tail_rows, stream], axis=0).astype(jnp.float32)
    summed = jnp.zeros(stream.shape, jnp.float32)
    for tap_index in range(FEAT):
        begin = FEAT - 1 - tap_index
        summed = summed + taps[:, tap_index, :][None] * widened[begin : begin + length]
    return summed


def featurize_back(stream, taps):
    length = stream.shape[0]
    head_rows = neighbour_rows(stream[: FEAT - 1], -1)
    widened = jnp.concatenate([stream, head_rows], axis=0).astype(jnp.float32)
    summed = jnp.zeros(stream.shape, jnp.float32)
    for tap_index in range(FEAT):
        summed = summed + taps[:, tap_index, :][None] * widened[tap_index : tap_index + length]
    return summed


def modal_tables(block_rates, block_gains, length):
    positions = jnp.arange(length, dtype=jnp.float32)
    powers = jnp.exp(-positions[:, None, None] * block_rates[None])
    growth = jnp.exp(positions[:, None, None] * block_rates[None])
    weighted = powers * block_gains[None]
    full_table = jnp.einsum("tog,sog->tsg", weighted, growth, precision=exact_mode)
    causal = (
        jnp.arange(length, dtype=jnp.int32)[:, None] >= jnp.arange(length, dtype=jnp.int32)[None, :]
    )
    toeplitz = jnp.where(causal[:, :, None], full_table, 0.0)
    start_weights = weighted * jnp.exp(-block_rates)[None]
    end_powers = jnp.exp(-(float(length - 1) - positions)[:, None, None] * block_rates[None])
    return (toeplitz, start_weights, end_powers)


def modal_block(sequence, tables):
    toeplitz, start_weights, end_powers = tables
    local_part = jnp.einsum("tsg,sgc->tgc", toeplitz, sequence, precision=exact_mode)
    end_state = jnp.einsum("sog,sgc->ogc", end_powers, sequence, precision=exact_mode)
    return (local_part, end_state)


def modal_apply(sequence, modal_rates, modal_residues, backward):
    length, channels = sequence.shape
    groups = channels // GROUP
    gain_terms = modal_residues * jnp.sqrt(-jnp.expm1(-2.0 * modal_rates))
    shaped = sequence.reshape(length, groups, GROUP)
    ctx_devices = lax.axis_size("ctx")
    share_groups = groups // ctx_devices
    exchanged = lax.all_to_all(
        shaped.astype(jnp.bfloat16), "ctx", split_axis=1, concat_axis=0, tiled=True
    ).astype(shaped.dtype)
    first_group = lax.axis_index("ctx") * share_groups
    own_rates = lax.dynamic_slice_in_dim(modal_rates, first_group, share_groups, 1)
    own_gains = lax.dynamic_slice_in_dim(gain_terms, first_group, share_groups, 1)
    if backward:
        exchanged = jnp.flip(exchanged, 0)
    pieces = exchanged.reshape(ctx_devices, length, share_groups, GROUP)
    tables = modal_tables(own_rates, own_gains, length)
    block_decay = jnp.exp(-own_rates * length)[:, :, None]

    def advance(carried, piece):
        local_part, end_state = modal_block(piece, tables)
        result = local_part + jnp.einsum("tog,ogc->tgc", tables[1], carried, precision=exact_mode)
        return (block_decay * carried + end_state, result)

    start_state = jnp.zeros((ORDER, share_groups, GROUP), jnp.float32)
    _, block_outs = lax.scan(advance, start_state, pieces)
    whole_out = block_outs.reshape(ctx_devices * length, share_groups, GROUP)
    if backward:
        whole_out = jnp.flip(whole_out, 0)
    returned = lax.all_to_all(
        whole_out.astype(jnp.bfloat16), "ctx", split_axis=0, concat_axis=1, tiled=True
    ).astype(whole_out.dtype)
    return returned.reshape(length, channels)


def body(token_ids, embed_table, in_weight, feat_taps, modal_rates, modal_residues, out_grad):
    length = token_ids.shape[0]
    vocab_size = embed_table.shape[0]
    model_width = in_weight.shape[0]
    channels = in_weight.shape[2]
    flat_weight = in_weight.reshape(model_width, 3 * channels)
    one_hot = (token_ids[:, None] == jnp.arange(vocab_size, dtype=jnp.int32)[None, :]).astype(
        jnp.bfloat16
    )
    own_features = jnp.dot(one_hot, embed_table, preferred_element_type=jnp.float32).astype(
        jnp.bfloat16
    )
    rows_used = flat_weight
    projected = jnp.dot(
        lax.all_gather(own_features, "chan", axis=1, tiled=True),
        rows_used,
        preferred_element_type=jnp.float32,
    )
    stream = projected.reshape(length, 3, channels).astype(jnp.bfloat16)
    stream = lax.optimization_barrier(stream)
    featured = featurize_local(stream, feat_taps)
    query_rows = featured[:, 0]
    key_rows = featured[:, 1]
    value_rows = featured[:, 2]
    mixed_rows = key_rows * value_rows
    long_conv = modal_apply(mixed_rows, modal_rates, modal_residues, False)
    output = (query_rows * long_conv).astype(jnp.bfloat16)
    grad_rows = out_grad.astype(jnp.float32)
    grad_query = grad_rows * long_conv
    grad_long = grad_rows * query_rows
    grad_mixed = modal_apply(grad_long, modal_rates, modal_residues, True)
    grad_feat = jnp.stack(
        [grad_query, grad_mixed * value_rows, grad_mixed * key_rows], axis=1
    ).astype(jnp.bfloat16)
    grad_feat = lax.optimization_barrier(grad_feat)
    grad_proj = (
        featurize_back(grad_feat, feat_taps).astype(jnp.bfloat16).reshape(length, 3 * channels)
    )
    rows_used = flat_weight
    summed_rows = lax.psum_scatter(
        lax.dot_general(
            rows_used, grad_proj, (((1,), (1,)), ((), ())), preferred_element_type=jnp.float32
        ).astype(jnp.bfloat16),
        "chan",
        scatter_dimension=0,
        tiled=True,
    ).astype(jnp.float32)
    return (output, summed_rows.T.astype(jnp.bfloat16))


def solution(mesh):
    in_specs = (
        P("ctx"),
        P(None, "chan"),
        P(None, None, "chan"),
        P(None, None, "chan"),
        P(None, "chan"),
        P(None, "chan"),
        P("ctx", "chan"),
    )
    out_specs = (P("ctx", "chan"), P("ctx", "chan"))
    return jax.shard_map(body, mesh=mesh, in_specs=in_specs, out_specs=out_specs, check_vma=False)
```

profile of v0, /device:TPU:24, one launch (start us, length us, event | category | flops | bytes accessed | tf_op | source)
XLA Modules:
  0.0 326.0 jit_solution(7893675662903279602)
XLA Ops:
  7.2 0.9 copy-done
  8.1 1.6 convolution_convert_fusion
  9.8 0.8 constant_dynamic-slice_fusion.1
  10.7 16.7 %copy.55 = bf16[8192,3,256]{0,2,1:T(8,128)(2,1)} copy(bf16[8192,3,256]{2,0,1:T(8,128)(2,1)} %param.13) | data formatting | bytes 25165824 | tf_op args[2]
  27.5 57.8 %all-gather.2.cloned.1.call-done = bf16[256,8192]{1,0:T(8,128)(2,1)} async-done(((bf16[256,256]{1,0:T(8,128)(2,1)}), bf16[256,8192]{1,0:T(8,128)(2,1)}) %all-gather.2.cloned.1.call-update) | async-done | bytes 4194320 | tf_op jit(solution)/shard_map/all_gather | solution.py:116
  85.3 9.3 %fusion.58 = bf16[256,3,256]{2,0,1:T(8,128)(2,1)S(1)} fusion(bf16[8192,3,256]{0,2,1:T(8,128)(2,1)} %copy.55, bf16[256,8192]{1,0:T(8,128)(2,1)} %all-gather.2.cloned.1.call-done), kind=kOutput, calls=%fused_computation.61 | convolution fusion | flops 3221422080 | bytes 17170432 | tf_op jit(solution)/shard_map/dot_general | solution.py:115
  94.7 4.9 %collective-permute-start = (bf16[2,3,256]{2,0,1:T(2,128)(2,1)S(1)}, bf16[2,3,256]{2,0,1:T(2,128)(2,1)S(1)}, u32[]{:S(2)}, u32[]{:S(2)}) collective-permute-start(bf16[2,3,256]{2,0,1:T(2,128)(2,1)S(1)} %slice.59), channel_id=1, source_target_pairs={{0,32},{32,64},{64,96},{96,128},{128,160},{160,192},{192,224},{1,3... | collective-permute-start | bytes 9224 | tf_op jit(solution)/shard_map/ppermute | solution.py:17
  99.6 3.0 collective-permute-done
  102.9 0.8 copy.67
  103.7 6.3 %all-to-all-start.2 = ((bf16[256,16,16]{0,2,1:T(8,128)(2,1)}), bf16[256,16,16]{0,2,1:T(8,128)(2,1)S(1)}, u32[]{:S(2)}, u32[]{:S(2)}) async-start(bf16[256,16,16]{0,2,1:T(8,128)(2,1)} %bitcast.14), calls=%async_computation.2 | async-start | bytes 262144 | tf_op jit(solution)/shard_map/all_to_all | solution.py:74
  110.0 0.7 fusion.63
  110.9 5.0 %all-to-all-done.2 = bf16[256,16,16]{0,2,1:T(8,128)(2,1)S(1)} async-done(((bf16[256,16,16]{0,2,1:T(8,128)(2,1)}), bf16[256,16,16]{0,2,1:T(8,128)(2,1)S(1)}, u32[]{:S(2)}, u32[]{:S(2)}) %all-to-all-start.2) | async-done | bytes 131104 | tf_op jit(solution)/shard_map/all_to_all | solution.py:74
  116.1 1.2 rev.7
  117.4 10.2 %while.31 = (s32[]{:T(128)}, f32[16,2,16]{0,2,1:T(8,128)S(1)}, bf16[8,256,2,16]{1,0,3,2:T(8,128)(2,1)S(1)}, f32[16,2,1]{0,1,2:T(2,128)S(1)}, f32[8,256,2,16]{1,0...) while((s32[]{:T(128)}, f32[16,2,16]{0,2,1:T(8,128)S(1)}, ...), condition=%wide.region_3.4_spmd.clone.clone.clone, body=%wide.region_2.3_spmd.clone.clone.clone.sunk | while | flops 28362756 | bytes 811800 | solution.py:92
  117.4 0.5 fusion.121
  118.7 0.5 fusion.121
  119.9 0.5 fusion.121
  121.2 0.5 fusion.121
  122.5 0.5 fusion.121
  123.8 0.5 fusion.121
  125.0 0.5 fusion.121
  126.3 0.5 fusion.121
  127.6 1.3 rev.8
  128.9 0.7 copy.72
  129.7 1.1 reshape.99
  130.7 10.6 %all_to_all.16 = bf16[8,2,4096]{2,1,0:T(2,128)(2,1)S(1)} all-to-all(bf16[8,2,4096]{2,1,0:T(2,128)(2,1)S(1)} %reshape.99), channel_id=1, replica_groups=mesh['ctx'=8,'chan'=32] {'ctx'}, dimensions={0} | all-to-all | bytes 262144 | tf_op jit(solution)/shard_map/all_to_all | solution.py:96
  141.4 0.7 reshape.100
  142.1 0.6 copy.73
  143.2 0.8 copy.57
  143.9 5.6 %all-to-all-start = ((bf16[256,16,16]{0,2,1:T(8,128)(2,1)}), bf16[256,16,16]{0,2,1:T(8,128)(2,1)S(1)}, u32[]{:S(2)}, u32[]{:S(2)}) async-start(bf16[256,16,16]{0,2,1:T(8,128)(2,1)} %bitcast.6), calls=%async_computation | async-start | bytes 262144 | tf_op jit(solution)/shard_map/all_to_all | solution.py:74
  149.5 5.9 %all-to-all-done = bf16[256,16,16]{0,2,1:T(8,128)(2,1)S(1)} async-done(((bf16[256,16,16]{0,2,1:T(8,128)(2,1)}), bf16[256,16,16]{0,2,1:T(8,128)(2,1)S(1)}, u32[]{:S(2)}, u32[]{:S(2)}) %all-to-all-start) | async-done | bytes 131104 | tf_op jit(solution)/shard_map/all_to_all | solution.py:74
  155.4 8.3 %while.30 = (s32[]{:T(128)}, f32[16,2,16]{0,2,1:T(8,128)S(1)}, bf16[8,256,2,16]{1,3,2,0:T(8,128)(2,1)S(1)}, f32[16,2,1]{0,1,2:T(2,128)S(1)}, f32[8,256,2,16]{1,3...) while((s32[]{:T(128)}, f32[16,2,16]{0,2,1:T(8,128)S(1)}, ...), condition=%wide.region_1.2_spmd.clone.clone.clone, body=%wide.region_0.1_spmd.clone.clone.clone.sunk | while | flops 28354564 | bytes 730268 | solution.py:92
  155.4 0.5 fusion.114
  156.5 0.5 fusion.114
  157.5 0.5 fusion.114
  158.6 0.5 fusion.114
  159.6 0.5 fusion.114
  160.7 0.5 fusion.114
  163.8 0.7 copy.77
  164.5 1.1 reshape.97
  165.6 10.6 %all_to_all.17 = bf16[8,2,4096]{2,1,0:T(2,128)(2,1)S(1)} all-to-all(bf16[8,2,4096]{2,1,0:T(2,128)(2,1)S(1)} %reshape.97), channel_id=1, replica_groups=mesh['ctx'=8,'chan'=32] {'ctx'}, dimensions={0} | all-to-all | bytes 262144 | tf_op jit(solution)/shard_map/all_to_all | solution.py:96
  176.2 0.7 reshape.98
  176.9 0.6 copy.63
  177.9 0.7 fusion.76
  178.7 2.5 collective-permute-start.1
  181.2 4.5 %collective-permute-done.1 = bf16[2,3,256]{2,0,1:T(2,128)(2,1)S(1)} collective-permute-done((bf16[2,3,256]{2,0,1:T(2,128)(2,1)S(1)}, bf16[2,3,256]{2,0,1:T(2,128)(2,1)S(1)}, u32[]{:S(2)}, u32[]{:S(2)}) %collective-permute-start.1) | collective-permute-done | bytes 3104 | tf_op jit(solution)/shard_map/ppermute | solution.py:17
  185.7 14.1 %fusion.56 = bf16[8192,256]{0,1:T(8,128)(2,1)} fusion(bf16[8192,3,256]{2,0,1:T(8,128)(2,1)} %param.13, f32[258,3,256]{2,0,1:T(8,128)S(1)} %maximum_convert_fusion.1, f32[3,256]{1,0:T(4,128)S(1)} %get-tuple-element.441, f32[3,256]{1,0:T(4,128)S(1)} %get-tuple-element.442, f32[3,256]{1,0:T(4,128)S(1)} %bitcast.160), kind=kOutput, calls=%fused_computation.59 | convolution fusion | flops 3224502272 | bytes 19148800 | tf_op jit(solution)/shard_map/dot_general | solution.py:142
  199.9 119.2 %reduce-scatter.2.cloned.1.call-done = bf16[256,256]{0,1:T(8,128)(2,1)} async-done(((bf16[8192,256]{0,1:T(8,128)(2,1)}), bf16[256,256]{0,1:T(8,128)(2,1)}) %reduce-scatter.2.cloned.1.call-update) | async-done | bytes 131088 | tf_op jit(solution)/shard_map/reduce_scatter | solution.py:141
  (101 shorter events, 12.6 us)
Async XLA Ops:
  7.2 1.0 copy-start
  7.2 78.2 %all-gather.2.cloned.1.call-start = ((), (), s32[]{:S(2)}) async-start(), calls=%async_computation.5 | async-start | bytes 4325376 | tf_op jit(solution)/shard_map/all_gather | solution.py:116
  10.7 16.8 %copy-start.2 = (f32[3,3,256]{2,1,0:T(4,128)S(1)}, f32[3,3,256]{2,1,0:T(4,128)}, u32[]{:S(2)}) copy-start(f32[3,3,256]{2,1,0:T(4,128)} %param.14) | copy-start | bytes 27652
  27.5 75.4 %copy-start.1 = (bf16[256,256]{1,0:T(8,128)(2,1)S(1)}, bf16[256,256]{1,0:T(8,128)(2,1)}, u32[]{:S(2)}) copy-start(bf16[256,256]{1,0:T(8,128)(2,1)} %param.17) | copy-start | bytes 393220
  94.7 7.9 %collective-permute-start = (bf16[2,3,256]{2,0,1:T(2,128)(2,1)S(1)}, bf16[2,3,256]{2,0,1:T(2,128)(2,1)S(1)}, u32[]{:S(2)}, u32[]{:S(2)}) collective-permute-start(bf16[2,3,256]{2,0,1:T(2,128)(2,1)S(1)} %slice.59), channel_id=1, source_target_pairs={{0,32},{32,64},{64,96},{96,128},{128,160},{160,192},{192,224},{1,3... | collective-permute-start | bytes 9224 | tf_op jit(solution)/shard_map/ppermute | solution.py:17
  103.7 12.2 %all-to-all-start.2 = ((bf16[256,16,16]{0,2,1:T(8,128)(2,1)}), bf16[256,16,16]{0,2,1:T(8,128)(2,1)S(1)}, u32[]{:S(2)}, u32[]{:S(2)}) async-start(bf16[256,16,16]{0,2,1:T(8,128)(2,1)} %bitcast.14), calls=%async_computation.2 | async-start | bytes 262144 | tf_op jit(solution)/shard_map/all_to_all | solution.py:74
  143.9 11.5 %all-to-all-start = ((bf16[256,16,16]{0,2,1:T(8,128)(2,1)}), bf16[256,16,16]{0,2,1:T(8,128)(2,1)S(1)}, u32[]{:S(2)}, u32[]{:S(2)}) async-start(bf16[256,16,16]{0,2,1:T(8,128)(2,1)} %bitcast.6), calls=%async_computation | async-start | bytes 262144 | tf_op jit(solution)/shard_map/all_to_all | solution.py:74
  149.5 169.7 %reduce-scatter.2.cloned.1.call-start = ((), (), s32[]{:S(2)}) async-start(), calls=%async_computation.6 | async-start | bytes 4325376 | tf_op jit(solution)/shard_map/reduce_scatter | solution.py:141
  178.7 7.0 %collective-permute-start.1 = (bf16[2,3,256]{2,0,1:T(2,128)(2,1)S(1)}, bf16[2,3,256]{2,0,1:T(2,128)(2,1)S(1)}, u32[]{:S(2)}, u32[]{:S(2)}) collective-permute-start(bf16[2,3,256]{2,0,1:T(2,128)(2,1)S(1)} %slice.66), channel_id=1, source_target_pairs={{32,0},{64,32},{96,64},{128,96},{160,128},{192,160},{224,192},{33,... | collective-permute-start | bytes 9224 | tf_op jit(solution)/shard_map/ppermute | solution.py:17
Sparse Core Ops, SparseCore 0:
  10.4 74.9 all-gather.1
  200.0 119.0 reduce-scatter.1
where the time goes:
time: 327 us; the launch traced here: 326 us
  waiting for transfers between devices  196 us (60%)
  matrix products  42 us (13%)
  local copies, waits for them, and re-layouts  31.7 us (10%)
  blocking collectives  21.2 us (6%)
  starting transfers between devices  19.2 us (6%)
  between operations  14.4 us (4%)
    reduce_scatter x1, waiting for transfers between devices, body(): lax.psum_scatter(lax.dot_general(rows_used, grad_proj, (((1,), (1,)), (()...  119 us
    all_gather x1, waiting for transfers between devices, body(): lax.all_gather(own_features, 'chan', axis=1, tiled=True)  57.8 us
    unnamed x19, local copies, waits for them, and re-layouts  21.8 us
    all_to_all x2, blocking collectives, modal_apply(): lax.all_to_all(whole_out.astype(jnp.bfloat16), 'ctx', split_axis=0, conca...  21.2 us
    dot_general x1, matrix products, body(): lax.dot_general(rows_used, grad_proj, (((1,), (1,)), ((), ())), preferred...  14.1 us
    all_to_all x2, starting transfers between devices, modal_apply(): lax.all_to_all(shaped.astype(jnp.bfloat16), 'ctx', split_axis=1, concat_a...  11.8 us
    all_to_all x2, waiting for transfers between devices, modal_apply(): lax.all_to_all(shaped.astype(jnp.bfloat16), 'ctx', split_axis=1, concat_a...  11 us
    dot_general x1, matrix products, body(): jnp.dot(lax.all_gather(own_features, 'chan', axis=1, tiled=True), rows_us...  9.3 us
  transfers between devices with their start and end apart: 6, of which 6 were waited for; matrix products, arithmetic and copies ran while one was open for 6% of the time, Pallas kernels for 0%

commit v1 on v0

v1 whole, which is shorter than its diff:
```python
import jax
import jax.numpy as jnp
from jax import lax
from jax.experimental import pallas as pl
from jax.experimental.pallas import tpu as pltpu
from jax.sharding import PartitionSpec as P

F32 = jnp.float32
BF16 = jnp.bfloat16
EXACT = lax.Precision.HIGHEST
N_CTX = 8
N_CHAN = 32
N_Z = 8
BLOCK = 256
GROUP = 16
ORDER = 16
GROUPS = BLOCK // GROUP
VOCAB = 512
SHARE = VOCAB // N_CTX
HALO = 128
EXTRA = 16
WINDOW = N_CTX * BLOCK

CORE_SWAP = [(i, i ^ 1) for i in range(N_CHAN)]
X_SWAP = [(i, i ^ 16) for i in range(N_CHAN)]
Z_GROUPS = [[x * 16 + z * 2 + c for z in range(N_Z)] for x in range(2) for c in range(2)]


def z_shift(by):
    return [(i, (i & 16) | ((i + 2 * by) & 15)) for i in range(N_CHAN)]


def nn(a, b):
    return lax.dot_general(a, b, (((1,), (0,)), ((), ())), preferred_element_type=F32)


def nt(a, b):
    return lax.dot_general(a, b, (((1,), (1,)), ((), ())), preferred_element_type=F32)


def lanes_of(shape):
    return lax.broadcasted_iota(jnp.int32, shape, 1)


def table_kernel(rate_ref, gain_ref, fwd_ref, bwd_ref, end_ref, begin_ref, enter_ref, leave_ref):
    rates = rate_ref[...]
    gains = gain_ref[...]
    position = lanes_of((BLOCK, BLOCK)).astype(F32)
    decay = jnp.exp(-position * rates)
    growth = jnp.exp(position * rates)
    weighted = decay * gains
    end_ref[...] = jnp.exp((position - (BLOCK - 1.0)) * rates).astype(BF16)
    begin_ref[...] = decay.astype(BF16)
    enter_ref[...] = (gains * jnp.exp(-(position + 1.0) * rates)).astype(BF16)
    wide = jnp.minimum(lanes_of((BLOCK, BLOCK + HALO)), BLOCK + 1).astype(F32)
    leave_ref[...] = (gains * jnp.exp((wide - float(BLOCK)) * rates)).astype(BF16)
    row = lax.broadcasted_iota(jnp.int32, (BLOCK, BLOCK), 0)
    col = lanes_of((BLOCK, BLOCK))
    for g in range(GROUPS):
        rows = slice(g * ORDER, (g + 1) * ORDER)
        grown, scaled = growth[rows], weighted[rows]
        dims = (((0,), (0,)), ((), ()))
        later = lax.dot_general(grown, scaled, dims, precision=EXACT, preferred_element_type=F32)
        fwd_ref[g] = jnp.where(col >= row, later, 0.0).astype(BF16)
        earlier = lax.dot_general(scaled, grown, dims, precision=EXACT, preferred_element_type=F32)
        bwd_ref[g] = jnp.where(row >= col, earlier, 0.0).astype(BF16)


def make_tables(rate_col, gain_col):
    square = jax.ShapeDtypeStruct((BLOCK, BLOCK), BF16)
    stack = jax.ShapeDtypeStruct((GROUPS, BLOCK, BLOCK), BF16)
    wide = jax.ShapeDtypeStruct((BLOCK, BLOCK + HALO), BF16)
    vmem = pl.BlockSpec(memory_space=pltpu.VMEM)
    return pl.pallas_call(
        table_kernel,
        out_shape=(stack, stack, square, square, square, wide),
        in_specs=[vmem] * 2,
        out_specs=(vmem,) * 6,
        compiler_params=pltpu.CompilerParams(vmem_limit_bytes=32 << 20),
        cost_estimate=pl.CostEstimate(flops=6 * 64 * 2**20, bytes_accessed=5 << 20, transcendentals=1 << 19),
        name="filter_tables",
    )(rate_col, gain_col)


def project_kernel(place_ref, rows_ref, weight_ref, out_ref, acc_ref):
    step = pl.program_id(0)

    @pl.when(step == 0)
    def _():
        acc_ref[...] = jnp.zeros_like(acc_ref)

    for z in range(4):
        rows = rows_ref[z]
        for s in range(3):
            cols = slice(s * BLOCK, (s + 1) * BLOCK)
            acc_ref[:, cols] += nn(rows, weight_ref[s, 0, z, 0])

    @pl.when(step == pl.num_programs(0) - 1)
    def _():
        out_ref[...] = acc_ref[...].astype(BF16)


def project(place, rows, weight):
    def weight_map(step, place):
        return (0, place[1] ^ ((step // 2) % 2), step % 2, place[3] ^ (step // 4), 0, 0)

    return pl.pallas_call(
        project_kernel,
        out_shape=jax.ShapeDtypeStruct((SHARE, 3 * BLOCK), BF16),
        grid_spec=pltpu.PrefetchScalarGridSpec(
            num_scalar_prefetch=1,
            grid=(8,),
            in_specs=[
                pl.BlockSpec((4, SHARE, BLOCK), lambda step, place: (step, 0, 0)),
                pl.BlockSpec((3, 1, 4, 1, BLOCK, BLOCK), weight_map),
            ],
            out_specs=pl.BlockSpec((SHARE, 3 * BLOCK), lambda step, place: (0, 0)),
            scratch_shapes=[pltpu.VMEM((SHARE, 3 * BLOCK), F32)],
        ),
        compiler_params=pltpu.CompilerParams(vmem_limit_bytes=32 << 20),
        cost_estimate=pl.CostEstimate(flops=2 * 64 * 768 * 8192, bytes_accessed=14 << 20, transcendentals=0),
        name="project",
    )(place, rows, weight)


def mixer_kernel(
    place_ref, table_ref, token_ref, grad_ref, tap_ref, rate_ref, gain_ref,
    fwd_ref, bwd_ref, end_ref, begin_ref, enter_ref, leave_ref,
    out_ref, grad_proj_ref, raw_ref,
):
    own = place_ref[0]
    table = table_ref[...].astype(F32).T.astype(BF16)
    vocab = lax.broadcasted_iota(jnp.int32, (VOCAB, BLOCK), 0)
    for tile in range((WINDOW + 2 * HALO) // BLOCK):
        lanes = slice(tile * BLOCK, (tile + 1) * BLOCK)
        one_hot = jnp.where(token_ref[:, lanes] == vocab, 1.0, 0.0).astype(BF16)
        raw_ref[:, lanes] = nn(table, one_hot)

    def featured(stream, block, width):
        rows = pl.ds(stream * BLOCK, BLOCK)
        begin = pl.multiple_of(block * BLOCK, BLOCK)
        raw = raw_ref[rows, pl.ds(begin, HALO + width)]
        total = tap_ref[rows, 0:1] * raw[:, HALO:]
        for tap in (1, 2):
            total += tap_ref[rows, tap : tap + 1] * raw[:, HALO - tap : HALO - tap + width]
        return total

    rate_row = rate_ref[...]
    gain_row = gain_ref[...]
    block_decay = jnp.exp(rate_row * -float(BLOCK))
    same_group = (
        lax.broadcasted_iota(jnp.int32, (BLOCK, BLOCK), 0) // GROUP == lanes_of((BLOCK, BLOCK)) // ORDER
    )

    def earlier(block, state):
        mixed = featured(1, block, BLOCK) * featured(2, block, BLOCK)
        return block_decay * state + nt(mixed.astype(BF16), end_ref[...])

    def later(step, state):
        block = N_CTX - 1 - step
        grad = grad_ref[block, 0:BLOCK, :].astype(F32) * featured(0, block, BLOCK)
        return block_decay * state + nt(grad.astype(BF16), begin_ref[...])

    zero = jnp.zeros((BLOCK, BLOCK), F32)
    before = lax.fori_loop(0, own, earlier, zero)
    after = lax.fori_loop(0, N_CTX - 1 - own, later, zero)

    wide = BLOCK + HALO
    query = featured(0, own, wide)
    key = featured(1, own, wide)
    value = featured(2, own, wide)
    mixed = key * value
    following = jnp.minimum(own + 1, N_CTX - 1)
    grad_rows = jnp.concatenate(
        [grad_ref[own, 0:BLOCK, :], grad_ref[following, 0:BLOCK, 0:HALO]], axis=1
    ).astype(F32)
    grad_long = grad_rows * query
    mixed_own = mixed[:, :BLOCK].astype(BF16)
    long_own = grad_long[:, :BLOCK].astype(BF16)

    through = block_decay * before + nt(mixed_own, end_ref[...])
    before = jnp.where(same_group, before, 0.0).astype(BF16)
    through = jnp.where(same_group, through, 0.0).astype(BF16)
    after = jnp.where(same_group, after, 0.0).astype(BF16)

    conv_rows, mixed_grads = [], []
    for g in range(GROUPS):
        rows = slice(g * GROUP, (g + 1) * GROUP)
        conv_rows.append(nn(mixed_own[rows], fwd_ref[g]))
        mixed_grads.append(nn(long_own[rows], bwd_ref[g]))
    conv = jnp.concatenate(conv_rows, axis=0) + nn(before, enter_ref[...])
    mixed_grad = jnp.concatenate(mixed_grads, axis=0) + nn(after, leave_ref[:, :BLOCK])

    def filter_at(lag):
        terms = jnp.where(same_group, gain_row * jnp.exp(rate_row * -float(lag)), 0.0)
        return jnp.sum(terms, axis=1, keepdims=True)

    second = lanes_of((BLOCK, HALO)) == 1
    conv_next = nn(through, enter_ref[:, :HALO]) + filter_at(0) * mixed[:, BLOCK:]
    conv_next += jnp.where(second, filter_at(1) * mixed[:, BLOCK - 1 : wide - 1], 0.0)
    grad_next = nn(after, leave_ref[:, BLOCK:])
    grad_next -= jnp.where(second, filter_at(-1) * grad_long[:, BLOCK - 1 : wide - 1], 0.0)

    out_ref[...] = (query[:, :BLOCK] * conv).T.astype(BF16)

    conv = jnp.concatenate([conv, conv_next], axis=1)
    mixed_grad = jnp.concatenate([mixed_grad, grad_next], axis=1)
    lane = lanes_of((BLOCK, wide))
    inside = (lane < BLOCK) | ((lane < BLOCK + 2) & (own < N_CTX - 1))
    streams = (grad_rows * conv, mixed_grad * value, mixed_grad * key)
    for s in range(3):
        rows = slice(s * BLOCK, (s + 1) * BLOCK)
        grads = jnp.where(inside, streams[s], 0.0).astype(BF16).astype(F32)
        total = tap_ref[rows, 0:1] * grads[:, :BLOCK]
        for tap in (1, 2):
            total += tap_ref[rows, tap : tap + 1] * grads[:, tap : tap + BLOCK]
        grad_proj_ref[rows, :] = total.astype(BF16)


def mix(place, table, tokens, grads, taps, rate_row, gain_row, tables):
    vmem = pl.BlockSpec(memory_space=pltpu.VMEM)
    return pl.pallas_call(
        mixer_kernel,
        out_shape=(
            jax.ShapeDtypeStruct((BLOCK, BLOCK), BF16),
            jax.ShapeDtypeStruct((3 * BLOCK, BLOCK), BF16),
        ),
        in_specs=[pl.BlockSpec(memory_space=pltpu.SMEM)] + [vmem] * 12,
        out_specs=(vmem, vmem),
        scratch_shapes=[pltpu.VMEM((3 * BLOCK, WINDOW + 2 * HALO), F32)],
        compiler_params=pltpu.CompilerParams(vmem_limit_bytes=48 << 20),
        cost_estimate=pl.CostEstimate(flops=3 << 30, bytes_accessed=8 << 20, transcendentals=1 << 16),
        name="mixer",
    )(place, table, tokens, grads, taps, rate_row, gain_row, *tables)


def back_kernel(place_ref, grad_ref, weight_ref, own_ref, other_ref):
    for core in range(2):
        target = own_ref if core == 0 else other_ref
        c = place_ref[3] ^ core
        for shift in range(2):
            x = place_ref[1] ^ shift
            total = nn(weight_ref[0, x, 0, c], grad_ref[0:BLOCK])
            total += nn(weight_ref[1, x, 0, c], grad_ref[BLOCK : 2 * BLOCK])
            total += nn(weight_ref[2, x, 0, c], grad_ref[2 * BLOCK :])
            target[0, shift] = total.astype(BF16)


def back_project(place, grad_proj, weight):
    part = jax.ShapeDtypeStruct((N_Z, 2, BLOCK, BLOCK), BF16)
    part_spec = pl.BlockSpec((1, 2, BLOCK, BLOCK), lambda step, place: (step, 0, 0, 0))
    return pl.pallas_call(
        back_kernel,
        out_shape=(part, part),
        grid_spec=pltpu.PrefetchScalarGridSpec(
            num_scalar_prefetch=1,
            grid=(N_Z,),
            in_specs=[
                pl.BlockSpec((3 * BLOCK, BLOCK), lambda step, place: (0, 0)),
                pl.BlockSpec(
                    (3, 2, 1, 2, BLOCK, BLOCK),
                    lambda step, place: (0, 0, (place[2] + step) % N_Z, 0, 0, 0),
                ),
            ],
            out_specs=(part_spec, part_spec),
        ),
        compiler_params=pltpu.CompilerParams(vmem_limit_bytes=32 << 20),
        cost_estimate=pl.CostEstimate(flops=2 * 256 * 768 * 8192, bytes_accessed=17 << 20, transcendentals=0),
        name="back_project",
    )(place, grad_proj, weight)


def added(a, *rest):
    total = a.astype(F32)
    for b in rest:
        total = total + b.astype(F32)
    return total.astype(BF16)


def gather_features(rows):
    held = lax.all_to_all(
        jnp.broadcast_to(rows[None], (N_Z,) + rows.shape), "chan", 0, 0, axis_index_groups=Z_GROUPS
    )
    held = jnp.concatenate([held, lax.ppermute(held, "chan", X_SWAP)], axis=0)
    return jnp.concatenate([held, lax.ppermute(held, "chan", CORE_SWAP)], axis=0)


def gather_ctx(value):
    return lax.all_to_all(jnp.broadcast_to(value[None], (N_CTX,) + value.shape), "ctx", 0, 0)


def reduce_chan(own, other):
    parts = added(own, lax.ppermute(other, "chan", CORE_SWAP))
    up, down = z_shift(1), z_shift(-1)
    ahead = added(lax.ppermute(parts[4], "chan", up), parts[3])
    ahead = added(lax.ppermute(ahead, "chan", up), parts[2])
    behind = added(lax.ppermute(parts[5], "chan", down), parts[6])
    ahead = added(lax.ppermute(ahead, "chan", up), parts[1])
    behind = added(lax.ppermute(behind, "chan", down), parts[7])
    total = added(parts[0], lax.ppermute(ahead, "chan", up), lax.ppermute(behind, "chan", down))
    return added(total[0], lax.ppermute(total[1], "chan", X_SWAP))


def body(token_ids, embed_table, in_weight, feat_taps, modal_rates, modal_residues, out_grad):
    ctx = lax.axis_index("ctx")
    chan = lax.axis_index("chan")
    place = jnp.stack([ctx, chan // 16, (chan // 2) % N_Z, chan % 2]).astype(jnp.int32)
    weight = in_weight.transpose(1, 0, 2).reshape(3, 2, N_Z, 2, BLOCK, BLOCK)

    own_vocab = lax.dynamic_slice_in_dim(embed_table, ctx * SHARE, SHARE, 0)
    features = gather_features(own_vocab)

    id_rows = jnp.stack([token_ids // 256, token_ids % 256]).astype(BF16)
    payload = jnp.concatenate(
        [out_grad.T, id_rows, jnp.zeros((EXTRA - 2, BLOCK), BF16)], axis=0
    )
    grads = gather_ctx(payload)
    ids = grads[:, BLOCK : BLOCK + 2, :].astype(jnp.int32)
    ids = (ids[:, 0] * 256 + ids[:, 1]).reshape(1, WINDOW)
    edge = jnp.full((1, HALO), -1, jnp.int32)
    tokens = jnp.concatenate([edge, ids, edge], axis=1)

    gains = modal_residues * jnp.sqrt(-jnp.expm1(-2.0 * modal_rates))
    rate_row = modal_rates.T.reshape(1, BLOCK)
    gain_row = gains.T.reshape(1, BLOCK)
    tables = make_tables(rate_row.reshape(BLOCK, 1), gain_row.reshape(BLOCK, 1))
    taps = feat_taps.transpose(0, 2, 1).reshape(3 * BLOCK, 3)

    table = gather_ctx(project(place, features, weight)).reshape(VOCAB, 3 * BLOCK)
    output, grad_proj = mix(place, table, tokens, grads, taps, rate_row, gain_row, tables)
    own, other = back_project(place, grad_proj, weight)
    return (output, reduce_chan(own, other).T)


def solution(mesh):
    in_specs = (
        P("ctx"),
        P(None, "chan"),
        P(None, None, "chan"),
        P(None, None, "chan"),
        P(None, "chan"),
        P(None, "chan"),
        P("ctx", "chan"),
    )
    out_specs = (P("ctx", "chan"), P("ctx", "chan"))
    return jax.shard_map(body, mesh=mesh, in_specs=in_specs, out_specs=out_specs, check_vma=False)
```

time: 327 us -> 148 us (0.45)
  waiting for transfers between devices: 196 us -> 56.4 us
  matrix products: 42 us -> 0 us
  Pallas kernels: 0 us -> 32.4 us
  blocking collectives: 21.2 us -> 0 us
  starting transfers between devices: 19.2 us -> 34.6 us
  local copies, waits for them, and re-layouts: 31.7 us -> 17.7 us
  between operations: 14.4 us -> 0.96 us
  other arithmetic: 1.37 us -> 5.27 us
    reduce_scatter x1 -> x0, waiting for transfers between devices: 119 us -> none  [body(): lax.psum_scatter(lax.dot_general(rows_used, grad_proj, (((1,), (1,)), (()...]
    all_gather x1 -> x0, waiting for transfers between devices: 57.8 us -> none  [body(): lax.all_gather(own_features, 'chan', axis=1, tiled=True)]
    dot_general x52 -> x0, matrix products: 42 us -> none  [the longest x1 14.1 us: body(): lax.dot_general(rows_used, grad_proj, (((1,), (1,)), ((), ())), preferred...]
    pallas_call x0 -> x4, Pallas kernels: none -> 32.4 us  [the longest x1 14.5 us: mix(): pl.pallas_call(mixer_kernel, out_shape=(jax.ShapeDtypeStruct((BLOCK, BLOC...]
    ppermute x2 -> x11, waiting for transfers between devices: 7.51 us -> 32.9 us  [the longest x1 8.71 us: reduce_chan(): ahead = added(lax.ppermute(ahead, 'chan', up), parts[2])]
    all_to_all x2 -> x0, blocking collectives: 21.2 us -> none  [modal_apply(): lax.all_to_all(whole_out.astype(jnp.bfloat16), 'ctx', split_axis=0, conca...]
    all_to_all x2 -> x3, waiting for transfers between devices: 11 us -> 23.5 us  [the longest x2 12.6 us: gather_ctx(): lax.all_to_all(jnp.broadcast_to(value[None], (N_CTX,) + value.shape), 'ct...]
    all_to_all x2 -> x3, starting transfers between devices: 11.8 us -> 22.7 us  [the longest x2 14.2 us: gather_ctx(): lax.all_to_all(jnp.broadcast_to(value[None], (N_CTX,) + value.shape), 'ct...]
  transfers between devices with their start and end apart: 6 -> 14, of which waited for: 6 -> 8; matrix products, arithmetic and copies ran while one was open for 6% -> 4% of each run, Pallas kernels for 0% -> 8%
where the time goes in v1:
time: 148 us; the launch traced here: 147 us
  waiting for transfers between devices  56.4 us (38%)
  starting transfers between devices  34.6 us (23%)
  Pallas kernels  32.4 us (22%)
  local copies, waits for them, and re-layouts  17.7 us (12%)
  other arithmetic  5.27 us (4%)
    pallas_call x1, Pallas kernels, mix(): pl.pallas_call(mixer_kernel, out_shape=(jax.ShapeDtypeStruct((BLOCK, BLOC...  14.5 us
    all_to_all x2, starting transfers between devices, gather_ctx(): lax.all_to_all(jnp.broadcast_to(value[None], (N_CTX,) + value.shape), 'ct...  14.2 us
    unnamed x19, local copies, waits for them, and re-layouts  13.8 us
    all_to_all x2, waiting for transfers between devices, gather_ctx(): lax.all_to_all(jnp.broadcast_to(value[None], (N_CTX,) + value.shape), 'ct...  12.6 us
    all_to_all x1, waiting for transfers between devices, gather_features(): lax.all_to_all(jnp.broadcast_to(rows[None], (N_Z,) + rows.shape), 'chan',...  10.9 us
    ppermute x1, waiting for transfers between devices, reduce_chan(): ahead = added(lax.ppermute(ahead, 'chan', up), parts[2])  8.71 us
    all_to_all x1, starting transfers between devices, gather_features(): lax.all_to_all(jnp.broadcast_to(rows[None], (N_Z,) + rows.shape), 'chan',...  8.47 us
    pallas_call x1, Pallas kernels, make_tables(): pl.pallas_call(table_kernel, out_shape=(stack, stack, square, square, squ...  6.82 us
  transfers between devices with their start and end apart: 14, of which 8 were waited for; matrix products, arithmetic and copies ran while one was open for 4% of the time, Pallas kernels for 8%

profile of v1, /device:TPU:24, one launch (start us, length us, event | category | flops | bytes accessed | tf_op | source)
XLA Modules:
  0.0 147.3 jit_solution(13362023624894860942)
XLA Ops:
  0.7 0.9 copy-done
  1.6 0.7 broadcast_in_dim.10
  2.3 8.5 %all-to-all-start = ((bf16[8,64,256]{2,1,0:T(8,128)(2,1)}), bf16[8,64,256]{2,1,0:T(8,128)(2,1)S(1)}, u32[]{:S(2)}, u32[]{:S(2)}) async-start(bf16[8,64,256]{2,1,0:T(8,128)(2,1)} %broadcast_in_dim.10), calls=%async_computation | async-start | bytes 524288 | tf_op jit(solution)/shard_map/all_to_all | solution.py:281
  10.8 0.7 fusion.10
  11.5 0.1 stack.32
  11.6 0.1 stack.33
  11.8 10.9 %all-to-all-done = bf16[8,64,256]{2,1,0:T(8,128)(2,1)S(1)} async-done(((bf16[8,64,256]{2,1,0:T(8,128)(2,1)}), bf16[8,64,256]{2,1,0:T(8,128)(2,1)S(1)}, u32[]{:S(2)}, u32[]{:S(2)}) %all-to-all-start) | async-done | bytes 262176 | tf_op jit(solution)/shard_map/all_to_all | solution.py:281
  22.6 1.5 %collective-permute-start = (bf16[8,64,256]{2,1,0:T(8,128)(2,1)S(1)}, bf16[8,64,256]{2,1,0:T(8,128)(2,1)S(1)}, u32[]{:S(2)}, u32[]{:S(2)}) collective-permute-start(bf16[8,64,256]{2,1,0:T(8,128)(2,1)S(1)} %all-to-all-done), channel_id=1, source_target_pairs={{0,16},{1,17},{2,18},{3,19},{4,20},{5,21},{6,22},{7,23},{8,24},{9,... | collective-permute-start | bytes 786440 | tf_op jit(solution)/shard_map/ppermute | solution.py:284
  24.1 1.0 maximum_maximum_fusion
  25.1 0.1 copy.18
  25.3 1.1 broadcast_in_dim.28
  26.4 7.0 %all-to-all-start.2 = ((bf16[8,272,256]{2,1,0:T(8,128)(2,1)}), bf16[8,272,256]{2,1,0:T(8,128)(2,1)S(1)}, u32[]{:S(2)}, u32[]{:S(2)}) async-start(bf16[8,272,256]{2,1,0:T(8,128)(2,1)} %broadcast_in_dim.28), calls=%async_computation.2 | async-start | bytes 2228224 | tf_op jit(solution)/shard_map/all_to_all | solution.py:289
  33.4 0.8 pad_maximum_fusion.1
  34.4 0.1 reshape_reshape.9.gain_ref
  34.7 0.1 reshape_reshape.8.rate_ref
  34.8 0.2 copy.19
  35.0 6.8 %filter_tables.1 = (bf16[16,256,256]{2,1,0:T(8,128)(2,1)S(1)}, bf16[16,256,256]{2,1,0:T(8,128)(2,1)S(1)}, bf16[256,256]{1,0:T(8,128)(2,1)S(1)}, bf16[256,256]{1,...) custom-call(f32[256,1]{1,0:T(8,128)S(1)} %reshape_reshape.8.rate_ref, ...), custom_call_target="tpu_custom_call" | custom-call | flops 402653184 | bytes 5242880 | tf_op jit(solution)/shard_map/filter_tables/pallas_call | solution.py:74
  41.9 1.4 copy-done.3
  43.3 1.5 %pad_maximum_fusion.rows_ref = bf16[32,64,256]{2,1,0:T(8,128)(2,1)S(1)} fusion(bf16[16,64,256]{2,1,0:T(8,128)(2,1)} %collective-permute-done.1, bf16[8,64,256]{2,1,0:T(8,128)(2,1)S(1)} %collective-permute-done, bf16[8,64,256]{2,1,0:T(8,128)(2,1)S(1)} %all-to-all-done), kind=kLoop, calls=%fused_computation.1 | loop fusion | flops 1048576 | bytes 2097152 | tf_op jit(solution)/shard_map/concatenate | solution.py:285
  44.9 4.6 %copy-done.1 = bf16[8192,3,256]{2,0,1:T(8,128)(2,1)S(1)} copy-done((bf16[8192,3,256]{2,0,1:T(8,128)(2,1)S(1)}, bf16[8192,3,256]{2,0,1:T(8,128)(2,1)}, u32[]{:S(2)}) %copy-start.1) | copy-done | bytes 12582936
  49.4 4.9 %project.1 = bf16[64,768]{1,0:T(8,128)(2,1)S(1)} custom-call(s32[4]{0:T(128)S(1)} %pad_add_fusion.1.place_ref, bf16[32,64,256]{2,1,0:T(8,128)(2,1)S(1)} %pad_maximum_fusion.rows_ref, bf16[3,2,8,2,256,256]{5,4,3,2,1,0:T(8,128)(2,1)S(1)} %bitcast.58), custom_call_target="tpu_custom_call" | custom-call | flops 805306368 | bytes 14680064 | tf_op jit(solution)/shard_map/project/pallas_call | solution.py:107
  54.4 1.0 broadcast_in_dim.11
  55.3 7.2 %all-to-all-start.1 = ((bf16[8,64,768]{2,1,0:T(8,128)(2,1)}), bf16[8,64,768]{2,1,0:T(8,128)(2,1)S(1)}, u32[]{:S(2)}, u32[]{:S(2)}) async-start(bf16[8,64,768]{2,1,0:T(8,128)(2,1)} %broadcast_in_dim.11), calls=%async_computation.1 | async-start | bytes 1572864 | tf_op jit(solution)/shard_map/all_to_all | solution.py:289
  62.6 12.6 %all-to-all-done.1 = bf16[8,64,768]{2,1,0:T(8,128)(2,1)S(1)} async-done(((bf16[8,64,768]{2,1,0:T(8,128)(2,1)}), bf16[8,64,768]{2,1,0:T(8,128)(2,1)S(1)}, u32[]{:S(2)}, u32[]{:S(2)}) %all-to-all-start.1) | async-done | bytes 786464 | tf_op jit(solution)/shard_map/all_to_all | solution.py:289
  75.2 1.6 %copy-done.4 = bf16[16,256,256]{2,1,0:T(8,128)(2,1)S(1)} copy-done((bf16[16,256,256]{2,1,0:T(8,128)(2,1)S(1)}, bf16[16,256,256]{2,1,0:T(8,128)(2,1)}, u32[]{:S(2)}) %copy-start.4) | copy-done | bytes 2097176
  76.8 14.5 %mixer.1 = (bf16[256,256]{1,0:T(8,128)(2,1)}, bf16[768,256]{1,0:T(8,128)(2,1)S(1)}) custom-call(s32[4]{0:T(128)S(1)} %pad_add_fusion.1.place_ref, bf16[512,768]{1,0:T(8,128)(2,1)S(1)} %bitcast.60, s32[1,2304]{1,0:T(1,128)S(1)} %pad_add_fusion.token_ref, bf16[8,272,256]{2,1,0:T(8,128)(2,1)S(1)} %all-to-all-done.2.grad_ref, f32[768,3]{1,0:T(8,128)S(1)} %bitcast.61, ...), custom_call_target="tpu_custom_call" | custom-call | flops 3221225472 | bytes 8388608 | tf_op jit(solution)/shard_map/mixer/pallas_call | solution.py:222
  91.3 4.6 %copy-done.2 = bf16[8192,3,256]{2,0,1:T(8,128)(2,1)S(1)} copy-done((bf16[8192,3,256]{2,0,1:T(8,128)(2,1)S(1)}, bf16[8192,3,256]{2,0,1:T(8,128)(2,1)}, u32[]{:S(2)}) %copy-start.2) | copy-done | bytes 12582936
  95.9 6.1 %back_project.1 = (bf16[8,2,256,256]{3,2,1,0:T(8,128)(2,1)S(1)}, bf16[8,2,256,256]{3,2,1,0:T(8,128)(2,1)S(1)}) custom-call(s32[4]{0:T(128)S(1)} %pad_add_fusion.1.place_ref, bf16[768,256]{1,0:T(8,128)(2,1)S(1)} %get-tuple-element.19.grad_ref, bf16[3,2,8,2,256,256]{5,4,3,2,1,0:T(8,128)(2,1)S(1)} %bitcast.59), custom_call_target="tpu_custom_call" | custom-call | flops 3221225472 | bytes 17825792 | tf_op jit(solution)/shard_map/back_project/pallas_call | solution.py:252
  102.1 0.1 collective-permute-start.2
  102.2 4.1 %collective-permute-done.2 = bf16[8,2,256,256]{3,2,1,0:T(8,128)(2,1)S(1)} collective-permute-done((bf16[8,2,256,256]{3,2,1,0:T(8,128)(2,1)S(1)}, bf16[8,2,256,256]{3,2,1,0:T(8,128)(2,1)S(1)}, u32[]{:S(2)}, u32[]{:S(2)}) %collective-permute-start.2) | collective-permute-done | bytes 2097184 | tf_op jit(solution)/shard_map/ppermute | solution.py:293
  106.3 0.6 add_convert_fusion
  107.0 0.6 collective-permute-start.3
  107.6 2.7 %collective-permute-start.7 = (bf16[2,256,256]{2,1,0:T(8,128)(2,1)S(1)}, bf16[2,256,256]{2,1,0:T(8,128)(2,1)S(1)}, u32[]{:S(2)}, u32[]{:S(2)}) collective-permute-start(bf16[2,256,256]{2,1,0:T(8,128)(2,1)S(1)} %get-tuple-element.31), channel_id=1, source_target_pairs={{0,14},{1,15},{2,0},{3,1},{4,2},{5,3},{6,4},{7,5},{8,6},{9,7},{10,... | collective-permute-start | bytes 786440 | tf_op jit(solution)/shard_map/ppermute | solution.py:297
  110.3 6.3 %collective-permute-done.3 = bf16[2,256,256]{2,1,0:T(8,128)(2,1)S(1)} collective-permute-done((bf16[2,256,256]{2,1,0:T(8,128)(2,1)S(1)}, bf16[2,256,256]{2,1,0:T(8,128)(2,1)S(1)}, u32[]{:S(2)}, u32[]{:S(2)}) %collective-permute-start.3) | collective-permute-done | bytes 262176 | tf_op jit(solution)/shard_map/ppermute | solution.py:295
  116.7 0.1 collective-permute-start.4
  116.8 8.7 %collective-permute-done.4 = bf16[2,256,256]{2,1,0:T(8,128)(2,1)S(1)} collective-permute-done((bf16[2,256,256]{2,1,0:T(8,128)(2,1)S(1)}, bf16[2,256,256]{2,1,0:T(8,128)(2,1)S(1)}, u32[]{:S(2)}, u32[]{:S(2)}) %collective-permute-start.4) | collective-permute-done | bytes 262176 | tf_op jit(solution)/shard_map/ppermute | solution.py:296
  125.5 0.1 fusion.3
  125.6 0.1 collective-permute-start.5
  125.7 3.2 %collective-permute-start.8 = (bf16[2,256,256]{2,1,0:T(8,128)(2,1)S(1)}, bf16[2,256,256]{2,1,0:T(8,128)(2,1)S(1)}, u32[]{:S(2)}, u32[]{:S(2)}) collective-permute-start(bf16[2,256,256]{2,1,0:T(8,128)(2,1)S(1)} %get-tuple-element.29), channel_id=1, source_target_pairs={{0,14},{1,15},{2,0},{3,1},{4,2},{5,3},{6,4},{7,5},{8,6},{9,7},{10,... | collective-permute-start | bytes 786440 | tf_op jit(solution)/shard_map/ppermute | solution.py:299
  128.9 4.6 %collective-permute-done.5 = bf16[2,256,256]{2,1,0:T(8,128)(2,1)S(1)} collective-permute-done((bf16[2,256,256]{2,1,0:T(8,128)(2,1)S(1)}, bf16[2,256,256]{2,1,0:T(8,128)(2,1)S(1)}, u32[]{:S(2)}, u32[]{:S(2)}) %collective-permute-start.5) | collective-permute-done | bytes 262176 | tf_op jit(solution)/shard_map/ppermute | solution.py:298
  133.5 0.1 fusion.2
  133.6 0.1 collective-permute-start.6
  133.7 3.2 %collective-permute-start.9 = (bf16[2,256,256]{2,1,0:T(8,128)(2,1)S(1)}, bf16[2,256,256]{2,1,0:T(8,128)(2,1)S(1)}, u32[]{:S(2)}, u32[]{:S(2)}) collective-permute-start(bf16[2,256,256]{2,1,0:T(8,128)(2,1)S(1)} %get-tuple-element.27), channel_id=1, source_target_pairs={{0,14},{1,15},{2,0},{3,1},{4,2},{5,3},{6,4},{7,5},{8,6},{9,7},{10,... | collective-permute-start | bytes 786440 | tf_op jit(solution)/shard_map/ppermute | solution.py:300
  137.0 4.3 %collective-permute-done.6 = bf16[2,256,256]{2,1,0:T(8,128)(2,1)S(1)} collective-permute-done((bf16[2,256,256]{2,1,0:T(8,128)(2,1)S(1)}, bf16[2,256,256]{2,1,0:T(8,128)(2,1)S(1)}, u32[]{:S(2)}, u32[]{:S(2)}) %collective-permute-start.6) | collective-permute-done | bytes 262176 | tf_op jit(solution)/shard_map/ppermute | solution.py:300
  141.3 0.1 fusion.6
  141.4 0.3 collective-permute-start.10
  141.7 4.8 %collective-permute-done.10 = bf16[256,256]{1,0:T(8,128)(2,1)S(1)} collective-permute-done((bf16[256,256]{1,0:T(8,128)(2,1)S(1)}, bf16[256,256]{1,0:T(8,128)(2,1)S(1)}, u32[]{:S(2)}, u32[]{:S(2)}) %collective-permute-start.10) | collective-permute-done | bytes 131104 | tf_op jit(solution)/shard_map/ppermute | solution.py:301
  146.5 0.8 copy.26
  (37 shorter events, 0.7 us)
Async XLA Ops:
  0.6 1.0 copy-start
  2.3 20.3 %all-to-all-start = ((bf16[8,64,256]{2,1,0:T(8,128)(2,1)}), bf16[8,64,256]{2,1,0:T(8,128)(2,1)S(1)}, u32[]{:S(2)}, u32[]{:S(2)}) async-start(bf16[8,64,256]{2,1,0:T(8,128)(2,1)} %broadcast_in_dim.10), calls=%async_computation | async-start | bytes 524288 | tf_op jit(solution)/shard_map/all_to_all | solution.py:281
  22.6 10.8 %collective-permute-start = (bf16[8,64,256]{2,1,0:T(8,128)(2,1)S(1)}, bf16[8,64,256]{2,1,0:T(8,128)(2,1)S(1)}, u32[]{:S(2)}, u32[]{:S(2)}) collective-permute-start(bf16[8,64,256]{2,1,0:T(8,128)(2,1)S(1)} %all-to-all-done), channel_id=1, source_target_pairs={{0,16},{1,17},{2,18},{3,19},{4,20},{5,21},{6,22},{7,23},{8,24},{9,... | collective-permute-start | bytes 786440 | tf_op jit(solution)/shard_map/ppermute | solution.py:284
  25.3 9.0 %copy-start.6 = (f32[16,16]{1,0:T(8,128)S(1)}, f32[16,16]{1,0:T(8,128)}, u32[]{:S(2)}) copy-start(f32[16,16]{1,0:T(8,128)} %param.11) | copy-start | bytes 3076
  25.3 9.0 %copy-start.8 = (f32[16,16]{1,0:T(8,128)S(1)}, f32[16,16]{1,0:T(8,128)}, u32[]{:S(2)}) copy-start(f32[16,16]{1,0:T(8,128)} %param.12) | copy-start | bytes 3076
  26.4 8.4 %copy-start.7 = (f32[3,3,256]{2,1,0:T(4,128)S(1)}, f32[3,3,256]{2,1,0:T(4,128)}, u32[]{:S(2)}) copy-start(f32[3,3,256]{2,1,0:T(4,128)} %param.10) | copy-start | bytes 27652
  26.4 27.9 %all-to-all-start.2 = ((bf16[8,272,256]{2,1,0:T(8,128)(2,1)}), bf16[8,272,256]{2,1,0:T(8,128)(2,1)S(1)}, u32[]{:S(2)}, u32[]{:S(2)}) async-start(bf16[8,272,256]{2,1,0:T(8,128)(2,1)} %broadcast_in_dim.28), calls=%async_computation.2 | async-start | bytes 2228224 | tf_op jit(solution)/shard_map/all_to_all | solution.py:289
  34.2 9.1 %collective-permute-start.1 = (bf16[16,64,256]{2,1,0:T(8,128)(2,1)}, bf16[16,64,256]{2,1,0:T(8,128)(2,1)}, u32[]{:S(2)}, u32[]{:S(2)}) collective-permute-start(bf16[16,64,256]{2,1,0:T(8,128)(2,1)} %pad_maximum_fusion.1), channel_id=1, source_target_pairs={{0,1},{1,0},{2,3},{3,2},{4,5},{5,4},{6,7},{7,6},{8,9},{9,8},{10,11... | collective-permute-start | bytes 1572872 | tf_op jit(solution)/shard_map/ppermute | solution.py:285
  41.9 1.4 copy-start.3
  43.2 1.6 %copy-start.5 = (bf16[16,256,256]{2,1,0:T(8,128)(2,1)}, bf16[16,256,256]{2,1,0:T(8,128)(2,1)S(1)}, u32[]{:S(2)}) copy-start(bf16[16,256,256]{2,1,0:T(8,128)(2,1)S(1)} %get-tuple-element.13.bwd_ref) | copy-start | bytes 6291460
  44.9 4.6 %copy-start.1 = (bf16[8192,3,256]{2,0,1:T(8,128)(2,1)S(1)}, bf16[8192,3,256]{2,0,1:T(8,128)(2,1)}, u32[]{:S(2)}) copy-start(bf16[8192,3,256]{2,0,1:T(8,128)(2,1)} %param.9) | copy-start | bytes 37748740
  55.3 19.9 %all-to-all-start.1 = ((bf16[8,64,768]{2,1,0:T(8,128)(2,1)}), bf16[8,64,768]{2,1,0:T(8,128)(2,1)S(1)}, u32[]{:S(2)}, u32[]{:S(2)}) async-start(bf16[8,64,768]{2,1,0:T(8,128)(2,1)} %broadcast_in_dim.11), calls=%async_computation.1 | async-start | bytes 1572864 | tf_op jit(solution)/shard_map/all_to_all | solution.py:289
  75.2 1.6 %copy-start.4 = (bf16[16,256,256]{2,1,0:T(8,128)(2,1)S(1)}, bf16[16,256,256]{2,1,0:T(8,128)(2,1)}, u32[]{:S(2)}) copy-start(bf16[16,256,256]{2,1,0:T(8,128)(2,1)} %copy-done.3) | copy-start | bytes 6291460
  91.3 4.6 %copy-start.2 = (bf16[8192,3,256]{2,0,1:T(8,128)(2,1)S(1)}, bf16[8192,3,256]{2,0,1:T(8,128)(2,1)}, u32[]{:S(2)}) copy-start(bf16[8192,3,256]{2,0,1:T(8,128)(2,1)} %param.9) | copy-start | bytes 37748740
  102.1 4.2 %collective-permute-start.2 = (bf16[8,2,256,256]{3,2,1,0:T(8,128)(2,1)S(1)}, bf16[8,2,256,256]{3,2,1,0:T(8,128)(2,1)S(1)}, u32[]{:S(2)}, u32[]{:S(2)}) collective-permute-start(bf16[8,2,256,256]{3,2,1,0:T(8,128)(2,1)S(1)} %get-tuple-element.21), channel_id=1, source_target_pairs={{0,1},{1,0},{2,3},{3,2},{4,5},{5,4},{6,7},{7,6},{8,9},{9,8},{10,11... | collective-permute-start | bytes 6291464 | tf_op jit(solution)/shard_map/ppermute | solution.py:293
  107.0 9.6 %collective-permute-start.3 = (bf16[2,256,256]{2,1,0:T(8,128)(2,1)S(1)}, bf16[2,256,256]{2,1,0:T(8,128)(2,1)S(1)}, u32[]{:S(2)}, u32[]{:S(2)}) collective-permute-start(bf16[2,256,256]{2,1,0:T(8,128)(2,1)S(1)} %get-tuple-element.30), channel_id=1, source_target_pairs={{0,2},{1,3},{2,4},{3,5},{4,6},{5,7},{6,8},{7,9},{8,10},{9,11},{10,... | collective-permute-start | bytes 786440 | tf_op jit(solution)/shard_map/ppermute | solution.py:295
  107.6 9.2 %collective-permute-start.7 = (bf16[2,256,256]{2,1,0:T(8,128)(2,1)S(1)}, bf16[2,256,256]{2,1,0:T(8,128)(2,1)S(1)}, u32[]{:S(2)}, u32[]{:S(2)}) collective-permute-start(bf16[2,256,256]{2,1,0:T(8,128)(2,1)S(1)} %get-tuple-element.31), channel_id=1, source_target_pairs={{0,14},{1,15},{2,0},{3,1},{4,2},{5,3},{6,4},{7,5},{8,6},{9,7},{10,... | collective-permute-start | bytes 786440 | tf_op jit(solution)/shard_map/ppermute | solution.py:297
  116.7 8.8 %collective-permute-start.4 = (bf16[2,256,256]{2,1,0:T(8,128)(2,1)S(1)}, bf16[2,256,256]{2,1,0:T(8,128)(2,1)S(1)}, u32[]{:S(2)}, u32[]{:S(2)}) collective-permute-start(bf16[2,256,256]{2,1,0:T(8,128)(2,1)S(1)} %fusion.4), channel_id=1, source_target_pairs={{0,2},{1,3},{2,4},{3,5},{4,6},{5,7},{6,8},{7,9},{8,10},{9,11},{10,... | collective-permute-start | bytes 786440 | tf_op jit(solution)/shard_map/ppermute | solution.py:296
  125.6 7.9 %collective-permute-start.5 = (bf16[2,256,256]{2,1,0:T(8,128)(2,1)S(1)}, bf16[2,256,256]{2,1,0:T(8,128)(2,1)S(1)}, u32[]{:S(2)}, u32[]{:S(2)}) collective-permute-start(bf16[2,256,256]{2,1,0:T(8,128)(2,1)S(1)} %get-tuple-element.28), channel_id=1, source_target_pairs={{0,2},{1,3},{2,4},{3,5},{4,6},{5,7},{6,8},{7,9},{8,10},{9,11},{10,... | collective-permute-start | bytes 786440 | tf_op jit(solution)/shard_map/ppermute | solution.py:298
  125.7 7.8 %collective-permute-start.8 = (bf16[2,256,256]{2,1,0:T(8,128)(2,1)S(1)}, bf16[2,256,256]{2,1,0:T(8,128)(2,1)S(1)}, u32[]{:S(2)}, u32[]{:S(2)}) collective-permute-start(bf16[2,256,256]{2,1,0:T(8,128)(2,1)S(1)} %get-tuple-element.29), channel_id=1, source_target_pairs={{0,14},{1,15},{2,0},{3,1},{4,2},{5,3},{6,4},{7,5},{8,6},{9,7},{10,... | collective-permute-start | bytes 786440 | tf_op jit(solution)/shard_map/ppermute | solution.py:299
  133.6 7.7 %collective-permute-start.6 = (bf16[2,256,256]{2,1,0:T(8,128)(2,1)S(1)}, bf16[2,256,256]{2,1,0:T(8,128)(2,1)S(1)}, u32[]{:S(2)}, u32[]{:S(2)}) collective-permute-start(bf16[2,256,256]{2,1,0:T(8,128)(2,1)S(1)} %get-tuple-element.26), channel_id=1, source_target_pairs={{0,2},{1,3},{2,4},{3,5},{4,6},{5,7},{6,8},{7,9},{8,10},{9,11},{10,... | collective-permute-start | bytes 786440 | tf_op jit(solution)/shard_map/ppermute | solution.py:300
  133.7 7.6 %collective-permute-start.9 = (bf16[2,256,256]{2,1,0:T(8,128)(2,1)S(1)}, bf16[2,256,256]{2,1,0:T(8,128)(2,1)S(1)}, u32[]{:S(2)}, u32[]{:S(2)}) collective-permute-start(bf16[2,256,256]{2,1,0:T(8,128)(2,1)S(1)} %get-tuple-element.27), channel_id=1, source_target_pairs={{0,14},{1,15},{2,0},{3,1},{4,2},{5,3},{6,4},{7,5},{8,6},{9,7},{10,... | collective-permute-start | bytes 786440 | tf_op jit(solution)/shard_map/ppermute | solution.py:300
  141.4 5.1 %collective-permute-start.10 = (bf16[256,256]{1,0:T(8,128)(2,1)S(1)}, bf16[256,256]{1,0:T(8,128)(2,1)S(1)}, u32[]{:S(2)}, u32[]{:S(2)}) collective-permute-start(bf16[256,256]{1,0:T(8,128)(2,1)S(1)} %slice_bitcast_fusion.8), channel_id=1, source_target_pairs={{0,16},{1,17},{2,18},{3,19},{4,20},{5,21},{6,22},{7,23},{8,24},{9,... | collective-permute-start | bytes 393224 | tf_op jit(solution)/shard_map/ppermute | solution.py:301

commit v2 on v1

v2 whole, which is shorter than its diff:
```python
import functools

import jax
import jax.numpy as jnp
from jax import lax
from jax.experimental import pallas as pl
from jax.experimental.pallas import tpu as pltpu
from jax.sharding import PartitionSpec as P

F32 = jnp.float32
BF16 = jnp.bfloat16
EXACT = lax.Precision.HIGHEST
N_CTX = 8
N_CHAN = 32
N_Z = 8
BLOCK = 256
GROUP = 16
ORDER = 16
GROUPS = BLOCK // GROUP
VOCAB = 512
SHARE = VOCAB // N_CTX
HALO = 128
EXTRA = 16
WINDOW = N_CTX * BLOCK

END = slice(0, BLOCK)
BEGIN = slice(BLOCK, 2 * BLOCK)
ENTER = slice(2 * BLOCK, 3 * BLOCK)
LEAVE = slice(3 * BLOCK, 4 * BLOCK + HALO)
SIDE = 4 * BLOCK + HALO

CORE_SWAP = [(i, i ^ 1) for i in range(N_CHAN)]
X_SWAP = [(i, i ^ 16) for i in range(N_CHAN)]
X_HALF_SWAP = [(i, i ^ 1) for i in range(N_CTX)]
Y_STEPS = (1, -1, 2)
Z_GROUPS = [[x * 16 + z * 2 + c for z in range(N_Z)] for x in range(2) for c in range(2)]


def z_shift(by):
    return [(i, (i & 16) | ((i + 2 * by) & 15)) for i in range(N_CHAN)]


def y_shift(by):
    return [(i, (i & 1) | ((i + 2 * by) & 7)) for i in range(N_CTX)]


def nn(a, b):
    return lax.dot_general(a, b, (((1,), (0,)), ((), ())), preferred_element_type=F32)


def nt(a, b):
    return lax.dot_general(a, b, (((1,), (1,)), ((), ())), preferred_element_type=F32)


def lanes_of(shape):
    return lax.broadcasted_iota(jnp.int32, shape, 1)


def place_of(axis):
    chan = lax.axis_index("chan")
    return {"x": chan // 16, "z": (chan // 2) & (N_Z - 1), "core": chan & 1}[axis]


def payload_kernel(grad_ref, token_ref, out_ref):
    out_ref[:BLOCK] = grad_ref[...].astype(F32).T.astype(BF16)
    tokens = token_ref[...]
    row = lax.broadcasted_iota(jnp.int32, (EXTRA, BLOCK), 0)
    ids = jnp.where(row == 0, tokens >> 8, jnp.where(row == 1, tokens & 255, 0))
    out_ref[BLOCK:] = ids.astype(F32).astype(BF16)


def make_payload(out_grad, token_ids):
    vmem = pl.BlockSpec(memory_space=pltpu.VMEM)
    return pl.pallas_call(
        payload_kernel,
        out_shape=jax.ShapeDtypeStruct((BLOCK + EXTRA, BLOCK), BF16),
        in_specs=[vmem] * 2,
        out_specs=vmem,
        compiler_params=pltpu.CompilerParams(vmem_limit_bytes=4 << 20),
        cost_estimate=pl.CostEstimate(flops=1 << 16, bytes_accessed=1 << 19, transcendentals=0),
        name="payload",
    )(out_grad, token_ids.reshape(1, BLOCK))


def table_kernel(
    rate_ref, gain_ref, tap_ref,
    fwd_ref, bwd_ref, side_ref, row_ref, tap_out_ref,
):
    shape = (BLOCK, ORDER)
    mode = lax.broadcasted_iota(jnp.int32, shape, 0)
    group_pick = jnp.where(mode // ORDER == lanes_of(shape), 1.0, 0.0)
    order_pick = mode % ORDER == lanes_of(shape)
    shape = (ORDER, BLOCK)
    group_row = jnp.where(lanes_of(shape) // ORDER == lax.broadcasted_iota(jnp.int32, shape, 0), 1.0, 0.0)
    order_row = lanes_of(shape) % ORDER == lax.broadcasted_iota(jnp.int32, shape, 0)

    def column(values):
        spread = lax.dot_general(
            group_pick, values, (((1,), (1,)), ((), ())), precision=EXACT, preferred_element_type=F32
        )
        return jnp.sum(jnp.where(order_pick, spread, 0.0), axis=1, keepdims=True)

    def as_row(values):
        spread = lax.dot_general(
            values, group_row, (((1,), (0,)), ((), ())), precision=EXACT, preferred_element_type=F32
        )
        return jnp.sum(jnp.where(order_row, spread, 0.0), axis=0, keepdims=True)

    row_ref[0:1] = as_row(rate_ref[...])
    row_ref[1:2] = as_row(gain_ref[...])
    for s in range(3):
        tap_out_ref[s * BLOCK : (s + 1) * BLOCK, :] = tap_ref[s].T
    rates = column(rate_ref[...])
    gains = column(gain_ref[...])
    position = lanes_of((BLOCK, BLOCK)).astype(F32)
    decay = jnp.exp(-position * rates)
    growth = jnp.exp(position * rates)
    weighted = decay * gains
    side_ref[:, END] = jnp.exp((position - (BLOCK - 1.0)) * rates).astype(BF16)
    side_ref[:, BEGIN] = decay.astype(BF16)
    side_ref[:, ENTER] = (gains * jnp.exp(-(position + 1.0) * rates)).astype(BF16)
    wide = jnp.minimum(lanes_of((BLOCK, BLOCK + HALO)), BLOCK + 1).astype(F32)
    side_ref[:, LEAVE] = (gains * jnp.exp((wide - float(BLOCK)) * rates)).astype(BF16)
    row = lax.broadcasted_iota(jnp.int32, (BLOCK, BLOCK), 0)
    col = lanes_of((BLOCK, BLOCK))
    for g in range(GROUPS):
        rows = slice(g * ORDER, (g + 1) * ORDER)
        grown, scaled = growth[rows], weighted[rows]
        dims = (((0,), (0,)), ((), ()))
        later = lax.dot_general(grown, scaled, dims, precision=EXACT, preferred_element_type=F32)
        fwd_ref[g] = jnp.where(col >= row, later, 0.0).astype(BF16)
        earlier = lax.dot_general(scaled, grown, dims, precision=EXACT, preferred_element_type=F32)
        bwd_ref[g] = jnp.where(row >= col, earlier, 0.0).astype(BF16)


def make_tables(rates, gains, taps):
    stack = jax.ShapeDtypeStruct((GROUPS, BLOCK, BLOCK), BF16)
    side = jax.ShapeDtypeStruct((BLOCK, SIDE), BF16)
    rows = jax.ShapeDtypeStruct((2, BLOCK), F32)
    columns = jax.ShapeDtypeStruct((3 * BLOCK, 3), F32)
    vmem = pl.BlockSpec(memory_space=pltpu.VMEM)
    return pl.pallas_call(
        table_kernel,
        out_shape=(stack, stack, side, rows, columns),
        in_specs=[vmem] * 3,
        out_specs=(vmem,) * 5,
        compiler_params=pltpu.CompilerParams(vmem_limit_bytes=8 << 20),
        cost_estimate=pl.CostEstimate(flops=6 * 64 * 2**20, bytes_accessed=5 << 20, transcendentals=1 << 19),
        name="filter_tables",
    )(rates, gains, taps)


def project_kernel(parts, first, last, *refs):
    row_refs, refs = refs[: len(parts)], refs[len(parts) :]
    weight_ref, refs = refs[0], refs[1:]
    out_ref, held_ref, sems = refs[-3:]
    copies = []
    for n, part in enumerate(parts):
        c, x = place_of("core") ^ (part // 2), place_of("x") ^ (part % 2)
        copies.append(pltpu.make_async_copy(weight_ref.at[:, x, :, c], held_ref.at[n], sems.at[n]))
        copies[n].start()
    total = tuple(
        jnp.zeros((SHARE, BLOCK), F32) if first else refs[0][:, s * BLOCK : (s + 1) * BLOCK] for s in range(3)
    )
    for n, row_ref in enumerate(row_refs):
        copies[n].wait()

        def add_block(z, total):
            rows = row_ref[z]
            return tuple(total[s] + nn(rows, held_ref[n, s, z]) for s in range(3))

        total = lax.fori_loop(0, N_Z, add_block, total, unroll=2)
    for s in range(3):
        out_ref[:, s * BLOCK : (s + 1) * BLOCK] = total[s].astype(BF16 if last else F32)


def project(parts, rows, weight, sums, last):
    vmem = pl.BlockSpec(memory_space=pltpu.VMEM)
    first = sums is None
    return pl.pallas_call(
        functools.partial(project_kernel, parts, first, last),
        out_shape=jax.ShapeDtypeStruct((SHARE, 3 * BLOCK), BF16 if last else F32),
        in_specs=[vmem] * len(parts) + [pl.BlockSpec(memory_space=pltpu.HBM)] + [vmem] * (not first),
        out_specs=vmem,
        scratch_shapes=[
            pltpu.VMEM((len(parts), 3, N_Z, BLOCK, BLOCK), BF16),
            pltpu.SemaphoreType.DMA((len(parts),)),
        ],
        compiler_params=pltpu.CompilerParams(vmem_limit_bytes=50 << 20),
        cost_estimate=pl.CostEstimate(
            flops=2 * 64 * 768 * 2048 * len(parts), bytes_accessed=len(parts) * (3 << 20), transcendentals=0
        ),
        name="project",
    )(*rows, weight, *([] if first else [sums]))


def mixer_kernel(*refs):
    table_refs, refs = refs[:N_CTX], refs[N_CTX:]
    sources, refs = refs[:4], refs[4:]
    row_ref, tap_ref, out_ref, grad_proj_ref, raw_ref = refs[:5]
    grad_ref, side_ref, fwd_ref, bwd_ref, sems = refs[5:]
    copies = [
        pltpu.make_async_copy(source, target, sems.at[n])
        for n, (source, target) in enumerate(zip(sources, (grad_ref, side_ref, fwd_ref, bwd_ref)))
    ]
    for copy in copies:
        copy.start()
    own = lax.axis_index("ctx")
    table = jnp.concatenate([ref[...].astype(F32) for ref in table_refs], axis=0).T.astype(BF16)
    share_row = lax.broadcasted_iota(jnp.int32, (SHARE, BLOCK), 0)
    vocab = []
    for step in (0,) + Y_STEPS:
        for half in range(2):
            source = ((own - 2 * step) & 6) | ((own & 1) ^ half)
            vocab.append(share_row + source * SHARE)
    vocab = jnp.concatenate(vocab, axis=0)

    edge = jnp.zeros((3 * BLOCK, HALO), F32)
    raw_ref[:, :HALO] = edge
    raw_ref[:, HALO + WINDOW :] = edge

    def look_up(block, carried):
        ids = grad_ref[block, BLOCK : BLOCK + EXTRA, :].astype(F32)
        ids = (ids[0:1] * 256.0 + ids[1:2]).astype(jnp.int32)
        one_hot = jnp.where(ids == vocab, 1.0, 0.0).astype(BF16)
        raw_ref[:, pl.ds(pl.multiple_of(HALO + block * BLOCK, HALO), BLOCK)] = nn(table, one_hot)
        return carried

    copies[0].wait()
    lax.fori_loop(0, N_CTX, look_up, 0)
    copies[1].wait()

    def featured(stream, block, width):
        rows = pl.ds(stream * BLOCK, BLOCK)
        begin = pl.multiple_of(block * BLOCK, BLOCK)
        raw = raw_ref[rows, pl.ds(begin, HALO + width)]
        total = tap_ref[rows, 0:1] * raw[:, HALO:]
        for tap in (1, 2):
            total += tap_ref[rows, tap : tap + 1] * raw[:, HALO - tap : HALO - tap + width]
        return total

    rate_row = row_ref[0:1]
    gain_row = row_ref[1:2]
    block_decay = jnp.exp(rate_row * -float(BLOCK))
    same_group = (
        lax.broadcasted_iota(jnp.int32, (BLOCK, BLOCK), 0) // GROUP == lanes_of((BLOCK, BLOCK)) // ORDER
    )

    def earlier(block, state):
        mixed = featured(1, block, BLOCK) * featured(2, block, BLOCK)
        return block_decay * state + nt(mixed.astype(BF16), side_ref[:, END])

    def later(step, state):
        block = N_CTX - 1 - step
        grad = grad_ref[block, 0:BLOCK, :].astype(F32) * featured(0, block, BLOCK)
        return block_decay * state + nt(grad.astype(BF16), side_ref[:, BEGIN])

    zero = jnp.zeros((BLOCK, BLOCK), F32)
    before = lax.fori_loop(0, own, earlier, zero)
    after = lax.fori_loop(0, N_CTX - 1 - own, later, zero)

    wide = BLOCK + HALO
    query = featured(0, own, wide)
    key = featured(1, own, wide)
    value = featured(2, own, wide)
    mixed = key * value
    following = jnp.minimum(own + 1, N_CTX - 1)
    grad_rows = jnp.concatenate(
        [grad_ref[own, 0:BLOCK, :], grad_ref[following, 0:BLOCK, 0:HALO]], axis=1
    ).astype(F32)
    grad_long = grad_rows * query
    mixed_own = mixed[:, :BLOCK].astype(BF16)
    long_own = grad_long[:, :BLOCK].astype(BF16)

    through = block_decay * before + nt(mixed_own, side_ref[:, END])
    before = jnp.where(same_group, before, 0.0).astype(BF16)
    through = jnp.where(same_group, through, 0.0).astype(BF16)
    after = jnp.where(same_group, after, 0.0).astype(BF16)

    copies[2].wait()
    copies[3].wait()
    conv_rows, mixed_grads = [], []
    for g in range(GROUPS):
        rows = slice(g * GROUP, (g + 1) * GROUP)
        conv_rows.append(nn(mixed_own[rows], fwd_ref[g]))
        mixed_grads.append(nn(long_own[rows], bwd_ref[g]))
    conv = jnp.concatenate(conv_rows, axis=0) + nn(before, side_ref[:, ENTER])
    mixed_grad = jnp.concatenate(mixed_grads, axis=0) + nn(after, side_ref[:, LEAVE.start : LEAVE.start + BLOCK])

    def filter_at(lag):
        terms = jnp.where(same_group, gain_row * jnp.exp(rate_row * -float(lag)), 0.0)
        return jnp.sum(terms, axis=1, keepdims=True)

    second = lanes_of((BLOCK, HALO)) == 1
    conv_next = nn(through, side_ref[:, ENTER.start : ENTER.start + HALO]) + filter_at(0) * mixed[:, BLOCK:]
    conv_next += jnp.where(second, filter_at(1) * mixed[:, BLOCK - 1 : wide - 1], 0.0)
    grad_next = nn(after, side_ref[:, LEAVE.start + BLOCK :])
    grad_next -= jnp.where(second, filter_at(-1) * grad_long[:, BLOCK - 1 : wide - 1], 0.0)

    out_ref[...] = (query[:, :BLOCK] * conv).T.astype(BF16)

    conv = jnp.concatenate([conv, conv_next], axis=1)
    mixed_grad = jnp.concatenate([mixed_grad, grad_next], axis=1)
    lane = lanes_of((BLOCK, wide))
    inside = (lane < BLOCK) | ((lane < BLOCK + 2) & (own < N_CTX - 1))
    streams = (grad_rows * conv, mixed_grad * value, mixed_grad * key)
    for s in range(3):
        rows = slice(s * BLOCK, (s + 1) * BLOCK)
        grads = jnp.where(inside, streams[s], 0.0).astype(BF16).astype(F32)
        total = tap_ref[rows, 0:1] * grads[:, :BLOCK]
        for tap in (1, 2):
            total += tap_ref[rows, tap : tap + 1] * grads[:, tap : tap + BLOCK]
        grad_proj_ref[rows, :] = total.astype(BF16)


def mix(pieces, grads, tables):
    fwd, bwd, side, row, taps = tables
    vmem = pl.BlockSpec(memory_space=pltpu.VMEM)
    return pl.pallas_call(
        mixer_kernel,
        out_shape=(
            jax.ShapeDtypeStruct((BLOCK, BLOCK), BF16),
            jax.ShapeDtypeStruct((3 * BLOCK, BLOCK), BF16),
        ),
        in_specs=[vmem] * N_CTX + [pl.BlockSpec(memory_space=pl.ANY)] * 4 + [vmem] * 2,
        out_specs=(vmem, vmem),
        scratch_shapes=[
            pltpu.VMEM((3 * BLOCK, WINDOW + 2 * HALO), F32),
            pltpu.VMEM((N_CTX, BLOCK + EXTRA, BLOCK), BF16),
            pltpu.VMEM((BLOCK, SIDE), BF16),
            pltpu.VMEM((GROUPS, BLOCK, BLOCK), BF16),
            pltpu.VMEM((GROUPS, BLOCK, BLOCK), BF16),
            pltpu.SemaphoreType.DMA((4,)),
        ],
        compiler_params=pltpu.CompilerParams(vmem_limit_bytes=50 << 20),
        cost_estimate=pl.CostEstimate(flops=3 << 30, bytes_accessed=8 << 20, transcendentals=1 << 16),
        name="mixer",
    )(*pieces, grads, side, fwd, bwd, row, taps)


def back_kernel(step_ref, grad_ref, weight_ref, own_ref, other_ref, held_ref, sems):
    count = own_ref.shape[0]

    def copy(n):
        z = (place_of("z") + step_ref[n]) & (N_Z - 1)
        return pltpu.make_async_copy(weight_ref.at[:, :, z], held_ref.at[n], sems.at[n])

    for n in range(count):
        copy(n).start()

    def one_step(n, carried):
        copy(n).wait()
        for core in (1, 0):
            target = other_ref if core else own_ref
            c = place_of("core") ^ core
            for shift in range(2):
                x = place_of("x") ^ shift
                total = nn(held_ref[n, 0, x, c], grad_ref[0:BLOCK])
                total += nn(held_ref[n, 1, x, c], grad_ref[BLOCK : 2 * BLOCK])
                total += nn(held_ref[n, 2, x, c], grad_ref[2 * BLOCK :])
                target[n, shift] = total.astype(BF16)
        return carried

    lax.fori_loop(0, count, one_step, 0)


def back_project(grad_proj, weight, steps):
    vmem = pl.BlockSpec(memory_space=pltpu.VMEM)
    count = len(steps)
    part = jax.ShapeDtypeStruct((count, 2, BLOCK, BLOCK), BF16)
    return pl.pallas_call(
        back_kernel,
        out_shape=(part, part),
        in_specs=[pl.BlockSpec(memory_space=pltpu.SMEM), vmem, pl.BlockSpec(memory_space=pltpu.HBM)],
        out_specs=(vmem, vmem),
        scratch_shapes=[
            pltpu.VMEM((count, 3, 2, 2, BLOCK, BLOCK), BF16),
            pltpu.SemaphoreType.DMA((count,)),
        ],
        compiler_params=pltpu.CompilerParams(vmem_limit_bytes=50 << 20),
        cost_estimate=pl.CostEstimate(
            flops=2 * 256 * 768 * 1024 * count, bytes_accessed=count << 21, transcendentals=0
        ),
        name="back_project",
    )(jnp.asarray(steps, jnp.int32), grad_proj, weight)


def project_features(rows, weight):
    held = lax.all_to_all(
        jnp.broadcast_to(rows[None], (N_Z,) + rows.shape), "chan", 0, 0, axis_index_groups=Z_GROUPS
    )
    beside = lax.ppermute(held, "chan", X_SWAP)
    across = lax.ppermute(held, "chan", CORE_SWAP)
    both = lax.ppermute(beside, "chan", CORE_SWAP)
    sums = project((0,), (held,), weight, None, False)
    sums = project((2, 1), (across, beside), weight, sums, False)
    return project((3,), (both,), weight, sums, True)


def gather_ctx(value):
    across = lax.ppermute(value, "ctx", X_HALF_SWAP)
    found = [value, across]
    for piece in (value, across):
        found += [lax.ppermute(piece, "ctx", y_shift(by)) for by in Y_STEPS]
    return [found[n] for n in (0, 1, 2, 5, 3, 6, 4, 7)]


def reduce_chan(grad_proj, weight):
    up, down = z_shift(1), z_shift(-1)
    terms = {}
    for steps in ((4,), (3, 5), (2, 6, 1, 7, 0)):
        own, other = back_project(grad_proj, weight, steps)
        swapped = lax.ppermute(other, "chan", CORE_SWAP)
        for n, step in enumerate(steps):
            terms[step] = own[n].astype(F32) + swapped[n].astype(F32)
    far = terms[4].astype(BF16)
    ahead = lax.ppermute(far[0], "chan", up).astype(F32)
    behind = lax.ppermute(far[1], "chan", down).astype(F32)
    ahead = jnp.stack([terms[3][0] + ahead, terms[3][1]])
    behind = jnp.stack([terms[5][0], terms[5][1] + behind])
    for near, other in ((2, 6), (1, 7)):
        ahead = terms[near] + lax.ppermute(ahead.astype(BF16), "chan", up).astype(F32)
        behind = terms[other] + lax.ppermute(behind.astype(BF16), "chan", down).astype(F32)
    total = terms[0] + lax.ppermute(ahead.astype(BF16), "chan", up).astype(F32)
    total = total + lax.ppermute(behind.astype(BF16), "chan", down).astype(F32)
    total = total[0] + lax.ppermute(total[1].astype(BF16), "chan", X_SWAP).astype(F32)
    return total.astype(BF16)


def body(token_ids, embed_table, in_weight, feat_taps, modal_rates, modal_residues, out_grad):
    weight = in_weight.transpose(1, 0, 2).reshape(3, 2, N_Z, 2, BLOCK, BLOCK)
    own_vocab = lax.dynamic_slice_in_dim(embed_table, lax.axis_index("ctx") * SHARE, SHARE, 0)
    payload = make_payload(out_grad, token_ids)
    grads = lax.all_gather(payload, "ctx", axis=0)

    part = project_features(own_vocab, weight)
    modal_rates, part = lax.optimization_barrier((modal_rates, part))
    pieces = gather_ctx(part)

    gains = modal_residues * jnp.sqrt(-jnp.expm1(-2.0 * modal_rates))
    tables = make_tables(modal_rates, gains, feat_taps)

    output, grad_proj = mix(pieces, grads, tables)
    return (output, reduce_chan(grad_proj, weight).T)


def solution(mesh):
    in_specs = (
        P("ctx"),
        P(None, "chan"),
        P(None, None, "chan"),
        P(None, None, "chan"),
        P(None, "chan"),
        P(None, "chan"),
        P("ctx", "chan"),
    )
    out_specs = (P("ctx", "chan"), P("ctx", "chan"))
    return jax.shard_map(body, mesh=mesh, in_specs=in_specs, out_specs=out_specs, check_vma=False)
```

time: 148 us -> 148 us (level)
  blocking collectives: 0 us -> 20.1 us
  waiting for transfers between devices: 56.4 us -> 39 us
  between operations: 0.96 us -> 14.4 us
  local copies, waits for them, and re-layouts: 17.7 us -> 6.43 us
  starting transfers between devices: 34.6 us -> 23.7 us
  Pallas kernels: 32.4 us -> 41.7 us
  other arithmetic: 5.27 us -> 0.87 us
    all_to_all x3 -> x0, waiting for transfers between devices: 23.5 us -> none  [the longest x2 12.6 us: gather_ctx(): lax.all_to_all(jnp.broadcast_to(value[None], (N_CTX,) + value.shape), 'ct...]
    all_to_all x3 -> x0, starting transfers between devices: 22.7 us -> none  [the longest x2 14.2 us: gather_ctx(): lax.all_to_all(jnp.broadcast_to(value[None], (N_CTX,) + value.shape), 'ct...]
    all_to_all x0 -> x1, blocking collectives: none -> 20.1 us  [project_features(): lax.all_to_all(jnp.broadcast_to(rows[None], (N_Z,) + rows.shape), 'chan',...]
    ppermute x11 -> x22, starting transfers between devices: 11.9 us -> 23.7 us  [the longest x6 7.74 us: gather_ctx(): found += [lax.ppermute(piece, 'ctx', y_shift(by)) for by in Y_STEPS]]
    pallas_call x3 -> x8, Pallas kernels: 17.9 us -> 28.1 us  [the longest x3 10.1 us: project(): pl.pallas_call(functools.partial(project_kernel, parts, first, last), out...]
    unnamed x19 -> x23, local copies, waits for them, and re-layouts: 13.8 us -> 6.33 us
    ppermute x11 -> x22, waiting for transfers between devices: 32.9 us -> 39 us  [the longest x2 13.9 us: reduce_chan(): lax.ppermute(ahead.astype(BF16), 'chan', up).astype(F32)]
    concatenate x4 -> x0, other arithmetic: 3.38 us -> none  [the longest x1 1.53 us: gather_features(): jnp.concatenate([held, lax.ppermute(held, 'chan', CORE_SWAP)], axis=0)]
  transfers between devices with their start and end apart: 14 -> 23, of which waited for: 8 -> 9; matrix products, arithmetic and copies ran while one was open for 4% -> 0% of each run, Pallas kernels for 8% -> 17%
where the time goes in v2:
time: 148 us; the launch traced here: 146 us
  Pallas kernels  41.7 us (28%)
  waiting for transfers between devices  39 us (26%)
  starting transfers between devices  23.7 us (16%)
  blocking collectives  20.1 us (14%)
  between operations  14.4 us (10%)
  local copies, waits for them, and re-layouts  6.43 us (4%)
    all_to_all x1, blocking collectives, project_features(): lax.all_to_all(jnp.broadcast_to(rows[None], (N_Z,) + rows.shape), 'chan',...  20.1 us
    ppermute x2, waiting for transfers between devices, reduce_chan(): lax.ppermute(ahead.astype(BF16), 'chan', up).astype(F32)  13.9 us
    pallas_call x1, Pallas kernels, mix(): pl.pallas_call(mixer_kernel, out_shape=(jax.ShapeDtypeStruct((BLOCK, BLOC...  13.6 us
    pallas_call x3, Pallas kernels, project(): pl.pallas_call(functools.partial(project_kernel, parts, first, last), out...  10.1 us
    pallas_call x3, Pallas kernels, back_project(): pl.pallas_call(back_kernel, out_shape=(part, part), in_specs=[pl.BlockSpe...  10.1 us
    ppermute x6, starting transfers between devices, gather_ctx(): found += [lax.ppermute(piece, 'ctx', y_shift(by)) for by in Y_STEPS]  7.74 us
    pallas_call x1, Pallas kernels, make_tables(): pl.pallas_call(table_kernel, out_shape=(stack, stack, side, rows, columns...  7.17 us
    unnamed x23, local copies, waits for them, and re-layouts  6.33 us
  transfers between devices with their start and end apart: 23, of which 9 were waited for; matrix products, arithmetic and copies ran while one was open for 0% of the time, Pallas kernels for 17%

profile of v2, /device:TPU:24, one launch (start us, length us, event | category | flops | bytes accessed | tf_op | source)
XLA Modules:
  0.0 146.2 jit_solution(17555146256460240852)
XLA Ops:
  7.2 0.9 copy-done.1
  8.2 0.7 copy-done.3
  8.8 0.8 payload.1
  9.7 20.1 %all_to_all.5.refs_0_ = bf16[8,64,256]{2,1,0:T(8,128)(2,1)S(1)} all-to-all(bf16[8,64,256]{2,1,0:T(8,128)(2,1)S(1)} %broadcast_in_dim.2), channel_id=1, replica_groups={{0,2,4,6,8,10,12,14},{1,3,5,7,9,11,13,15},{16,18,20,22,24,26,28,30},{17..., dimensions={0} | all-to-all | bytes 524288 | tf_op jit(solution)/shard_map/all_to_all | solution.py:389
  29.8 1.5 %collective-permute-start = (bf16[8,64,256]{2,1,0:T(8,128)(2,1)S(1)}, bf16[8,64,256]{2,1,0:T(8,128)(2,1)S(1)}, u32[]{:S(2)}, u32[]{:S(2)}) collective-permute-start(bf16[8,64,256]{2,1,0:T(8,128)(2,1)S(1)} %all_to_all.5.refs_0_), channel_id=1, source_target_pairs={{0,16},{1,17},{2,18},{3,19},{4,20},{5,21},{6,22},{7,23},{8,24},{9,... | collective-permute-start | bytes 786440 | tf_op jit(solution)/shard_map/ppermute | solution.py:392
  31.3 4.9 %collective-permute-done.refs_1_ = bf16[8,64,256]{2,1,0:T(8,128)(2,1)S(1)} collective-permute-done((bf16[8,64,256]{2,1,0:T(8,128)(2,1)S(1)}, bf16[8,64,256]{2,1,0:T(8,128)(2,1)S(1)}, u32[]{:S(2)}, u32[]{:S(2)}) %collective-permute-start) | collective-permute-done | bytes 262176 | tf_op jit(solution)/shard_map/ppermute | solution.py:392
  36.2 3.0 %project.3.refs_3_ = f32[64,768]{1,0:T(8,128)S(1)} custom-call(bf16[8,64,256]{2,1,0:T(8,128)(2,1)S(1)} %all_to_all.5.refs_0_, bf16[3,2,8,2,256,256]{5,4,3,2,1,0:T(8,128)(2,1)} %bitcast.67), custom_call_target="tpu_custom_call" | custom-call | flops 201326592 | bytes 3145728 | tf_op jit(solution)/shard_map/project/pallas_call | solution.py:180
  39.2 4.1 %project.4.refs_2_ = f32[64,768]{1,0:T(8,128)S(1)} custom-call(bf16[8,64,256]{2,1,0:T(8,128)(2,1)S(1)} %collective-permute-done.2.refs_0_, bf16[8,64,256]{2,1,0:T(8,128)(2,1)S(1)} %collective-permute-done.refs_1_, bf16[3,2,8,2,256,256]{5,4,3,2,1,0:T(8,128)(2,1)} %bitcast.68, f32[64,768]{1,0:T(8,128)S(1)} %project.3.refs_3_), custom_call_target="tpu_custom_call" | custom-call | flops 402653184 | bytes 6291456 | tf_op jit(solution)/shard_map/project/pallas_call | solution.py:180
  43.4 3.0 %project.5.refs_0_ = bf16[64,768]{1,0:T(8,128)(2,1)S(1)} custom-call(bf16[8,64,256]{2,1,0:T(8,128)(2,1)S(1)} %collective-permute-done.1.refs_0_, bf16[3,2,8,2,256,256]{5,4,3,2,1,0:T(8,128)(2,1)} %bitcast.69, f32[64,768]{1,0:T(8,128)S(1)} %project.4.refs_2_), custom_call_target="tpu_custom_call" | custom-call | flops 201326592 | bytes 3145728 | tf_op jit(solution)/shard_map/project/pallas_call | solution.py:180
  46.4 3.1 %collective-permute-start.3 = (bf16[64,768]{1,0:T(8,128)(2,1)S(1)}, bf16[64,768]{1,0:T(8,128)(2,1)S(1)}, u32[]{:S(2)}, u32[]{:S(2)}) collective-permute-start(bf16[64,768]{1,0:T(8,128)(2,1)S(1)} %project.5.refs_0_), channel_id=1, source_target_pairs={{0,32},{32,0},{64,96},{96,64},{128,160},{160,128},{192,224},{224,1... | collective-permute-start | bytes 294920 | tf_op jit(solution)/shard_map/ppermute | solution.py:401
  49.5 1.2 collective-permute-start.8
  50.7 3.2 %collective-permute-start.4 = (bf16[64,768]{1,0:T(8,128)(2,1)S(1)}, bf16[64,768]{1,0:T(8,128)(2,1)S(1)}, u32[]{:S(2)}, u32[]{:S(2)}) collective-permute-start(bf16[64,768]{1,0:T(8,128)(2,1)S(1)} %project.5.refs_0_), channel_id=1, source_target_pairs={{0,64},{32,96},{64,128},{96,160},{128,192},{160,224},{192,0},{224,... | collective-permute-start | bytes 294920 | tf_op jit(solution)/shard_map/ppermute | solution.py:404
  54.0 0.3 collective-permute-done.3.refs_1_
  54.3 1.2 collective-permute-start.9
  55.5 0.2 collective-permute-start.7
  55.8 1.2 collective-permute-done.8.refs_6_
  57.0 1.8 %collective-permute-start.5 = (bf16[64,768]{1,0:T(8,128)(2,1)S(1)}, bf16[64,768]{1,0:T(8,128)(2,1)S(1)}, u32[]{:S(2)}, u32[]{:S(2)}) collective-permute-start(bf16[64,768]{1,0:T(8,128)(2,1)S(1)} %collective-permute-done.3.refs_1_), channel_id=1, source_target_pairs={{0,64},{32,96},{64,128},{96,160},{128,192},{160,224},{192,0},{224,... | collective-permute-start | bytes 294920 | tf_op jit(solution)/shard_map/ppermute | solution.py:404
  58.8 7.2 %filter_tables.1 = (bf16[16,256,256]{2,1,0:T(8,128)(2,1)S(1)}, bf16[16,256,256]{2,1,0:T(8,128)(2,1)S(1)}, bf16[256,1152]{1,0:T(8,128)(2,1)S(1)}, f32[2,256]{1,0:T(2,128)S(1)}, f32[768,3]{1,0:T(8,128)S(1)}) custom-call(f32[16,16]{1,0:T(8,128)S(1)} %copy-done.2, f32[16,16]{1,0:T(8,128)S(1)} %sqrt_multiply_fusion.gain_ref, f32[3,3,256]{2,1,0:T(4,128)S(1)} %copy-done.7), custom_call_target="tpu_custom_call" | custom-call | flops 402653184 | bytes 5242880 | tf_op jit(solution)/shard_map/filter_tables/pallas_call | solution.py:142
  66.0 1.4 copy-done.8
  67.4 1.3 copy-done.9
  68.7 1.2 copy-done.6
  70.0 13.6 %mixer.1 = (bf16[256,256]{1,0:T(8,128)(2,1)}, bf16[768,256]{1,0:T(8,128)(2,1)S(1)}) custom-call(bf16[64,768]{1,0:T(8,128)(2,1)S(1)} %project.5.refs_0_, bf16[64,768]{1,0:T(8,128)(2,1)S(1)} %collective-permute-done.3.refs_1_, bf16[64,768]{1,0:T(8,128)(2,1)S(1)} %collective-permute-done.4.refs_2_, bf16[64,768]{1,0:T(8,128)(2,1)S(1)} %collective-permute-done.5.refs_3_, ...), custom_call_target="tpu_custom_call" | custom-call | flops 3221225472 | bytes 8388608 | tf_op jit(solution)/shard_map/mixer/pallas_call | solution.py:319
  83.6 2.0 %back_project.5 = (bf16[1,2,256,256]{3,2,1,0:T(8,128)(2,1)S(1)}, bf16[1,2,256,256]{3,2,1,0:T(8,128)(2,1)S(1)}) custom-call(s32[1]{0:T(128)} %constant.20.clone.step_ref, bf16[768,256]{1,0:T(8,128)(2,1)S(1)} %get-tuple-element.25.grad_ref, bf16[3,2,8,2,256,256]{5,4,3,2,1,0:T(8,128)(2,1)} %bitcast.70), custom_call_target="tpu_custom_call" | custom-call | flops 402653184 | bytes 2097152 | tf_op jit(solution)/shard_map/back_project/pallas_call | solution.py:371
  85.6 0.3 collective-permute-start.12
  86.0 3.1 %back_project.4 = (bf16[2,2,256,256]{3,2,1,0:T(8,128)(2,1)S(1)}, bf16[2,2,256,256]{3,2,1,0:T(8,128)(2,1)S(1)}) custom-call(s32[2]{0:T(128)S(1)} %copy-done.5, bf16[768,256]{1,0:T(8,128)(2,1)S(1)} %get-tuple-element.25.grad_ref, bf16[3,2,8,2,256,256]{5,4,3,2,1,0:T(8,128)(2,1)} %bitcast.71), custom_call_target="tpu_custom_call" | custom-call | flops 805306368 | bytes 4194304 | tf_op jit(solution)/shard_map/back_project/pallas_call | solution.py:371
  89.1 0.6 collective-permute-start.11
  89.7 4.9 %back_project.3 = (bf16[5,2,256,256]{3,2,1,0:T(8,128)(2,1)S(1)}, bf16[5,2,256,256]{3,2,1,0:T(8,128)(2,1)S(1)}) custom-call(s32[5]{0:T(128)S(1)} %copy-done.4, bf16[768,256]{1,0:T(8,128)(2,1)S(1)} %get-tuple-element.25.grad_ref, bf16[3,2,8,2,256,256]{5,4,3,2,1,0:T(8,128)(2,1)} %bitcast.72), custom_call_target="tpu_custom_call" | custom-call | flops 2013265920 | bytes 10485760 | tf_op jit(solution)/shard_map/back_project/pallas_call | solution.py:371
  94.6 0.1 collective-permute-start.10
  94.8 0.9 collective-permute-start.13
  95.8 2.4 %collective-permute-start.17 = (bf16[256,256]{1,0:T(8,128)(2,1)S(1)}, bf16[256,256]{1,0:T(8,128)(2,1)S(1)}, u32[]{:S(2)}, u32[]{:S(2)}) collective-permute-start(bf16[256,256]{1,0:T(8,128)(2,1)S(1)} %get-tuple-element.39), channel_id=1, source_target_pairs={{0,14},{1,15},{2,0},{3,1},{4,2},{5,3},{6,4},{7,5},{8,6},{9,7},{10,... | collective-permute-start | bytes 393224 | tf_op jit(solution)/shard_map/ppermute | solution.py:418
  98.1 0.1 convert_add_fusion.1
  98.3 3.7 %collective-permute-done.13 = bf16[256,256]{1,0:T(8,128)(2,1)S(1)} collective-permute-done((bf16[256,256]{1,0:T(8,128)(2,1)S(1)}, bf16[256,256]{1,0:T(8,128)(2,1)S(1)}, u32[]{:S(2)}, u32[]{:S(2)}) %collective-permute-start.13) | collective-permute-done | bytes 131104 | tf_op jit(solution)/shard_map/ppermute | solution.py:417
  102.1 0.1 collective-permute-start.14
  102.3 3.3 %collective-permute-start.18 = (bf16[2,256,256]{2,1,0:T(8,128)(2,1)S(1)}, bf16[2,256,256]{2,1,0:T(8,128)(2,1)S(1)}, u32[]{:S(2)}, u32[]{:S(2)}) collective-permute-start(bf16[2,256,256]{2,1,0:T(8,128)(2,1)S(1)} %pad_maximum_fusion.1), channel_id=1, source_target_pairs={{0,14},{1,15},{2,0},{3,1},{4,2},{5,3},{6,4},{7,5},{8,6},{9,7},{10,... | collective-permute-start | bytes 786440 | tf_op jit(solution)/shard_map/ppermute | solution.py:423
  105.6 5.7 %collective-permute-done.14 = bf16[2,256,256]{2,1,0:T(8,128)(2,1)S(1)} collective-permute-done((bf16[2,256,256]{2,1,0:T(8,128)(2,1)S(1)}, bf16[2,256,256]{2,1,0:T(8,128)(2,1)S(1)}, u32[]{:S(2)}, u32[]{:S(2)}) %collective-permute-start.14) | collective-permute-done | bytes 262176 | tf_op jit(solution)/shard_map/ppermute | solution.py:422
  111.3 0.1 fusion.2
  111.4 0.1 collective-permute-start.15
  111.5 8.2 %collective-permute-done.15 = bf16[2,256,256]{2,1,0:T(8,128)(2,1)S(1)} collective-permute-done((bf16[2,256,256]{2,1,0:T(8,128)(2,1)S(1)}, bf16[2,256,256]{2,1,0:T(8,128)(2,1)S(1)}, u32[]{:S(2)}, u32[]{:S(2)}) %collective-permute-start.15) | collective-permute-done | bytes 262176 | tf_op jit(solution)/shard_map/ppermute | solution.py:422
  119.7 0.2 fusion.3
  120.0 2.0 %collective-permute-start.16 = (bf16[2,256,256]{2,1,0:T(8,128)(2,1)S(1)}, bf16[2,256,256]{2,1,0:T(8,128)(2,1)S(1)}, u32[]{:S(2)}, u32[]{:S(2)}) collective-permute-start(bf16[2,256,256]{2,1,0:T(8,128)(2,1)S(1)} %get-tuple-element.34), channel_id=1, source_target_pairs={{0,2},{1,3},{2,4},{3,5},{4,6},{5,7},{6,8},{7,9},{8,10},{9,11},{10,... | collective-permute-start | bytes 786440 | tf_op jit(solution)/shard_map/ppermute | solution.py:424
  122.0 4.8 %collective-permute-done.19 = bf16[2,256,256]{2,1,0:T(8,128)(2,1)S(1)} collective-permute-done((bf16[2,256,256]{2,1,0:T(8,128)(2,1)S(1)}, bf16[2,256,256]{2,1,0:T(8,128)(2,1)S(1)}, u32[]{:S(2)}, u32[]{:S(2)}) %collective-permute-start.19) | collective-permute-done | bytes 262176 | tf_op jit(solution)/shard_map/ppermute | solution.py:423
  126.8 0.1 fusion.1
  126.9 0.9 collective-permute-start.20
  127.8 5.5 %collective-permute-done.20 = bf16[2,256,256]{2,1,0:T(8,128)(2,1)S(1)} collective-permute-done((bf16[2,256,256]{2,1,0:T(8,128)(2,1)S(1)}, bf16[2,256,256]{2,1,0:T(8,128)(2,1)S(1)}, u32[]{:S(2)}, u32[]{:S(2)}) %collective-permute-start.20) | collective-permute-done | bytes 262176 | tf_op jit(solution)/shard_map/ppermute | solution.py:425
  133.3 0.1 fusion.4
  133.5 0.5 collective-permute-start.21
  134.0 4.5 %collective-permute-done.21 = bf16[256,256]{1,0:T(8,128)(2,1)S(1)} collective-permute-done((bf16[256,256]{1,0:T(8,128)(2,1)S(1)}, bf16[256,256]{1,0:T(8,128)(2,1)S(1)}, u32[]{:S(2)}, u32[]{:S(2)}) %collective-permute-start.21) | collective-permute-done | bytes 131104 | tf_op jit(solution)/shard_map/ppermute | solution.py:426
  138.6 0.8 copy.12
  (50 shorter events, 0.6 us)
Async XLA Ops:
  7.2 2.5 %copy-start = (bf16[512,256]{1,0:T(8,128)(2,1)S(1)}, bf16[512,256]{1,0:T(8,128)(2,1)}, u32[]{:S(2)}) copy-start(bf16[512,256]{1,0:T(8,128)(2,1)} %param.11) | copy-start | bytes 786436
  7.2 61.5 %all-gather.3.cloned.1.call-start = ((), (), s32[]{:S(2)}) async-start(), calls=%async_computation.1 | async-start | bytes 1253376 | tf_op jit(solution)/shard_map/all_gather | solution.py:434
  7.2 0.9 copy-start.1
  8.2 0.7 copy-start.3
  29.8 6.4 %collective-permute-start = (bf16[8,64,256]{2,1,0:T(8,128)(2,1)S(1)}, bf16[8,64,256]{2,1,0:T(8,128)(2,1)S(1)}, u32[]{:S(2)}, u32[]{:S(2)}) collective-permute-start(bf16[8,64,256]{2,1,0:T(8,128)(2,1)S(1)} %all_to_all.5.refs_0_), channel_id=1, source_target_pairs={{0,16},{1,17},{2,18},{3,19},{4,20},{5,21},{6,22},{7,23},{8,24},{9,... | collective-permute-start | bytes 786440 | tf_op jit(solution)/shard_map/ppermute | solution.py:392
  31.3 7.9 %collective-permute-start.2 = (bf16[8,64,256]{2,1,0:T(8,128)(2,1)S(1)}, bf16[8,64,256]{2,1,0:T(8,128)(2,1)S(1)}, u32[]{:S(2)}, u32[]{:S(2)}) collective-permute-start(bf16[8,64,256]{2,1,0:T(8,128)(2,1)S(1)} %all_to_all.5.refs_0_), channel_id=1, source_target_pairs={{0,1},{1,0},{2,3},{3,2},{4,5},{5,4},{6,7},{7,6},{8,9},{9,8},{10,11... | collective-permute-start | bytes 786440 | tf_op jit(solution)/shard_map/ppermute | solution.py:393
  36.2 7.1 %collective-permute-start.1 = (bf16[8,64,256]{2,1,0:T(8,128)(2,1)S(1)}, bf16[8,64,256]{2,1,0:T(8,128)(2,1)S(1)}, u32[]{:S(2)}, u32[]{:S(2)}) collective-permute-start(bf16[8,64,256]{2,1,0:T(8,128)(2,1)S(1)} %collective-permute-done.refs_1_), channel_id=1, source_target_pairs={{0,1},{1,0},{2,3},{3,2},{4,5},{5,4},{6,7},{7,6},{8,9},{9,8},{10,11... | collective-permute-start | bytes 786440 | tf_op jit(solution)/shard_map/ppermute | solution.py:394
  43.3 15.5 %copy-start.2 = (f32[16,16]{1,0:T(8,128)S(1)}, f32[16,16]{1,0:T(8,128)}, u32[]{:S(2)}) copy-start(f32[16,16]{1,0:T(8,128)} %rate_ref) | copy-start | bytes 3076
  43.3 15.5 %copy-start.10 = (f32[16,16]{1,0:T(8,128)S(1)}, f32[16,16]{1,0:T(8,128)}, u32[]{:S(2)}) copy-start(f32[16,16]{1,0:T(8,128)} %param.15) | copy-start | bytes 3076
  43.3 15.5 %copy-start.7 = (f32[3,3,256]{2,1,0:T(4,128)S(1)}, f32[3,3,256]{2,1,0:T(4,128)}, u32[]{:S(2)}) copy-start(f32[3,3,256]{2,1,0:T(4,128)} %tap_ref.1) | copy-start | bytes 27652
  46.4 7.9 %collective-permute-start.3 = (bf16[64,768]{1,0:T(8,128)(2,1)S(1)}, bf16[64,768]{1,0:T(8,128)(2,1)S(1)}, u32[]{:S(2)}, u32[]{:S(2)}) collective-permute-start(bf16[64,768]{1,0:T(8,128)(2,1)S(1)} %project.5.refs_0_), channel_id=1, source_target_pairs={{0,32},{32,0},{64,96},{96,64},{128,160},{160,128},{192,224},{224,1... | collective-permute-start | bytes 294920 | tf_op jit(solution)/shard_map/ppermute | solution.py:401
  49.5 7.5 %collective-permute-start.8 = (bf16[64,768]{1,0:T(8,128)(2,1)S(1)}, bf16[64,768]{1,0:T(8,128)(2,1)S(1)}, u32[]{:S(2)}, u32[]{:S(2)}) collective-permute-start(bf16[64,768]{1,0:T(8,128)(2,1)S(1)} %project.5.refs_0_), channel_id=1, source_target_pairs={{0,128},{32,160},{64,192},{96,224},{128,0},{160,32},{192,64},{224,... | collective-permute-start | bytes 294920 | tf_op jit(solution)/shard_map/ppermute | solution.py:404
  50.7 18.0 %collective-permute-start.6 = (bf16[64,768]{1,0:T(8,128)(2,1)S(1)}, bf16[64,768]{1,0:T(8,128)(2,1)S(1)}, u32[]{:S(2)}, u32[]{:S(2)}) collective-permute-start(bf16[64,768]{1,0:T(8,128)(2,1)S(1)} %project.5.refs_0_), channel_id=1, source_target_pairs={{0,192},{32,224},{64,0},{96,32},{128,64},{160,96},{192,128},{224,1... | collective-permute-start | bytes 294920 | tf_op jit(solution)/shard_map/ppermute | solution.py:404
  50.7 18.0 %collective-permute-start.4 = (bf16[64,768]{1,0:T(8,128)(2,1)S(1)}, bf16[64,768]{1,0:T(8,128)(2,1)S(1)}, u32[]{:S(2)}, u32[]{:S(2)}) collective-permute-start(bf16[64,768]{1,0:T(8,128)(2,1)S(1)} %project.5.refs_0_), channel_id=1, source_target_pairs={{0,64},{32,96},{64,128},{96,160},{128,192},{160,224},{192,0},{224,... | collective-permute-start | bytes 294920 | tf_op jit(solution)/shard_map/ppermute | solution.py:404
  54.3 14.4 %collective-permute-start.9 = (bf16[64,768]{1,0:T(8,128)(2,1)S(1)}, bf16[64,768]{1,0:T(8,128)(2,1)S(1)}, u32[]{:S(2)}, u32[]{:S(2)}) collective-permute-start(bf16[64,768]{1,0:T(8,128)(2,1)S(1)} %collective-permute-done.3.refs_1_), channel_id=1, source_target_pairs={{0,128},{32,160},{64,192},{96,224},{128,0},{160,32},{192,64},{224,... | collective-permute-start | bytes 294920 | tf_op jit(solution)/shard_map/ppermute | solution.py:404
  55.5 13.2 %collective-permute-start.7 = (bf16[64,768]{1,0:T(8,128)(2,1)S(1)}, bf16[64,768]{1,0:T(8,128)(2,1)S(1)}, u32[]{:S(2)}, u32[]{:S(2)}) collective-permute-start(bf16[64,768]{1,0:T(8,128)(2,1)S(1)} %collective-permute-done.3.refs_1_), channel_id=1, source_target_pairs={{0,192},{32,224},{64,0},{96,32},{128,64},{160,96},{192,128},{224,1... | collective-permute-start | bytes 294920 | tf_op jit(solution)/shard_map/ppermute | solution.py:404
  57.0 11.7 %collective-permute-start.5 = (bf16[64,768]{1,0:T(8,128)(2,1)S(1)}, bf16[64,768]{1,0:T(8,128)(2,1)S(1)}, u32[]{:S(2)}, u32[]{:S(2)}) collective-permute-start(bf16[64,768]{1,0:T(8,128)(2,1)S(1)} %collective-permute-done.3.refs_1_), channel_id=1, source_target_pairs={{0,64},{32,96},{64,128},{96,160},{128,192},{160,224},{192,0},{224,... | collective-permute-start | bytes 294920 | tf_op jit(solution)/shard_map/ppermute | solution.py:404
  66.0 1.4 copy-start.8
  67.3 1.3 copy-start.9
  68.7 1.2 copy-start.6
  83.6 2.4 %copy-start.5 = (s32[2]{0:T(128)S(1)}, s32[2]{0:T(128)}, u32[]{:S(2)}) copy-start(s32[2]{0:T(128)} %constant.21.clone.step_ref) | copy-start | bytes 28
  85.6 4.1 %copy-start.4 = (s32[5]{0:T(128)S(1)}, s32[5]{0:T(128)}, u32[]{:S(2)}) copy-start(s32[5]{0:T(128)} %constant.22.clone.step_ref) | copy-start | bytes 64
  85.6 9.1 %collective-permute-start.12 = (bf16[1,2,256,256]{3,2,1,0:T(8,128)(2,1)S(1)}, bf16[1,2,256,256]{3,2,1,0:T(8,128)(2,1)S(1)}, u32[]{:S(2)}, u32[]{:S(2)}) collective-permute-start(bf16[1,2,256,256]{3,2,1,0:T(8,128)(2,1)S(1)} %get-tuple-element.31), channel_id=1, source_target_pairs={{0,1},{1,0},{2,3},{3,2},{4,5},{5,4},{6,7},{7,6},{8,9},{9,8},{10,11... | collective-permute-start | bytes 786440 | tf_op jit(solution)/shard_map/ppermute | solution.py:413
  89.1 9.0 %collective-permute-start.11 = (bf16[2,2,256,256]{3,2,1,0:T(8,128)(2,1)S(1)}, bf16[2,2,256,256]{3,2,1,0:T(8,128)(2,1)S(1)}, u32[]{:S(2)}, u32[]{:S(2)}) collective-permute-start(bf16[2,2,256,256]{3,2,1,0:T(8,128)(2,1)S(1)} %get-tuple-element.29), channel_id=1, source_target_pairs={{0,1},{1,0},{2,3},{3,2},{4,5},{5,4},{6,7},{7,6},{8,9},{9,8},{10,11... | collective-permute-start | bytes 1572872 | tf_op jit(solution)/shard_map/ppermute | solution.py:413
  94.6 16.7 %collective-permute-start.10 = (bf16[5,2,256,256]{3,2,1,0:T(8,128)(2,1)S(1)}, bf16[5,2,256,256]{3,2,1,0:T(8,128)(2,1)S(1)}, u32[]{:S(2)}, u32[]{:S(2)}) collective-permute-start(bf16[5,2,256,256]{3,2,1,0:T(8,128)(2,1)S(1)} %get-tuple-element.27), channel_id=1, source_target_pairs={{0,1},{1,0},{2,3},{3,2},{4,5},{5,4},{6,7},{7,6},{8,9},{9,8},{10,11... | collective-permute-start | bytes 3932168 | tf_op jit(solution)/shard_map/ppermute | solution.py:413
  94.8 7.2 %collective-permute-start.13 = (bf16[256,256]{1,0:T(8,128)(2,1)S(1)}, bf16[256,256]{1,0:T(8,128)(2,1)S(1)}, u32[]{:S(2)}, u32[]{:S(2)}) collective-permute-start(bf16[256,256]{1,0:T(8,128)(2,1)S(1)} %get-tuple-element.38), channel_id=1, source_target_pairs={{0,2},{1,3},{2,4},{3,5},{4,6},{5,7},{6,8},{7,9},{8,10},{9,11},{10,... | collective-permute-start | bytes 393224 | tf_op jit(solution)/shard_map/ppermute | solution.py:417
  95.8 6.4 %collective-permute-start.17 = (bf16[256,256]{1,0:T(8,128)(2,1)S(1)}, bf16[256,256]{1,0:T(8,128)(2,1)S(1)}, u32[]{:S(2)}, u32[]{:S(2)}) collective-permute-start(bf16[256,256]{1,0:T(8,128)(2,1)S(1)} %get-tuple-element.39), channel_id=1, source_target_pairs={{0,14},{1,15},{2,0},{3,1},{4,2},{5,3},{6,4},{7,5},{8,6},{9,7},{10,... | collective-permute-start | bytes 393224 | tf_op jit(solution)/shard_map/ppermute | solution.py:418
  102.1 9.2 %collective-permute-start.14 = (bf16[2,256,256]{2,1,0:T(8,128)(2,1)S(1)}, bf16[2,256,256]{2,1,0:T(8,128)(2,1)S(1)}, u32[]{:S(2)}, u32[]{:S(2)}) collective-permute-start(bf16[2,256,256]{2,1,0:T(8,128)(2,1)S(1)} %pad_maximum_fusion), channel_id=1, source_target_pairs={{0,2},{1,3},{2,4},{3,5},{4,6},{5,7},{6,8},{7,9},{8,10},{9,11},{10,... | collective-permute-start | bytes 786440 | tf_op jit(solution)/shard_map/ppermute | solution.py:422
  102.3 9.2 %collective-permute-start.18 = (bf16[2,256,256]{2,1,0:T(8,128)(2,1)S(1)}, bf16[2,256,256]{2,1,0:T(8,128)(2,1)S(1)}, u32[]{:S(2)}, u32[]{:S(2)}) collective-permute-start(bf16[2,256,256]{2,1,0:T(8,128)(2,1)S(1)} %pad_maximum_fusion.1), channel_id=1, source_target_pairs={{0,14},{1,15},{2,0},{3,1},{4,2},{5,3},{6,4},{7,5},{8,6},{9,7},{10,... | collective-permute-start | bytes 786440 | tf_op jit(solution)/shard_map/ppermute | solution.py:423
  111.4 8.3 %collective-permute-start.15 = (bf16[2,256,256]{2,1,0:T(8,128)(2,1)S(1)}, bf16[2,256,256]{2,1,0:T(8,128)(2,1)S(1)}, u32[]{:S(2)}, u32[]{:S(2)}) collective-permute-start(bf16[2,256,256]{2,1,0:T(8,128)(2,1)S(1)} %fusion.2), channel_id=1, source_target_pairs={{0,2},{1,3},{2,4},{3,5},{4,6},{5,7},{6,8},{7,9},{8,10},{9,11},{10,... | collective-permute-start | bytes 786440 | tf_op jit(solution)/shard_map/ppermute | solution.py:422
  119.9 6.9 %collective-permute-start.19 = (bf16[2,256,256]{2,1,0:T(8,128)(2,1)S(1)}, bf16[2,256,256]{2,1,0:T(8,128)(2,1)S(1)}, u32[]{:S(2)}, u32[]{:S(2)}) collective-permute-start(bf16[2,256,256]{2,1,0:T(8,128)(2,1)S(1)} %get-tuple-element.35), channel_id=1, source_target_pairs={{0,14},{1,15},{2,0},{3,1},{4,2},{5,3},{6,4},{7,5},{8,6},{9,7},{10,... | collective-permute-start | bytes 786440 | tf_op jit(solution)/shard_map/ppermute | solution.py:423
  120.0 7.8 %collective-permute-start.16 = (bf16[2,256,256]{2,1,0:T(8,128)(2,1)S(1)}, bf16[2,256,256]{2,1,0:T(8,128)(2,1)S(1)}, u32[]{:S(2)}, u32[]{:S(2)}) collective-permute-start(bf16[2,256,256]{2,1,0:T(8,128)(2,1)S(1)} %get-tuple-element.34), channel_id=1, source_target_pairs={{0,2},{1,3},{2,4},{3,5},{4,6},{5,7},{6,8},{7,9},{8,10},{9,11},{10,... | collective-permute-start | bytes 786440 | tf_op jit(solution)/shard_map/ppermute | solution.py:424
  126.9 6.4 %collective-permute-start.20 = (bf16[2,256,256]{2,1,0:T(8,128)(2,1)S(1)}, bf16[2,256,256]{2,1,0:T(8,128)(2,1)S(1)}, u32[]{:S(2)}, u32[]{:S(2)}) collective-permute-start(bf16[2,256,256]{2,1,0:T(8,128)(2,1)S(1)} %fusion.1), channel_id=1, source_target_pairs={{0,14},{1,15},{2,0},{3,1},{4,2},{5,3},{6,4},{7,5},{8,6},{9,7},{10,... | collective-permute-start | bytes 786440 | tf_op jit(solution)/shard_map/ppermute | solution.py:425
  133.5 5.1 %collective-permute-start.21 = (bf16[256,256]{1,0:T(8,128)(2,1)S(1)}, bf16[256,256]{1,0:T(8,128)(2,1)S(1)}, u32[]{:S(2)}, u32[]{:S(2)}) collective-permute-start(bf16[256,256]{1,0:T(8,128)(2,1)S(1)} %fusion.16), channel_id=1, source_target_pairs={{0,16},{1,17},{2,18},{3,19},{4,20},{5,21},{6,22},{7,23},{8,24},{9,... | collective-permute-start | bytes 393224 | tf_op jit(solution)/shard_map/ppermute | solution.py:426
Sparse Core Ops, SparseCore 0:
  10.6 56.2 all-gather.2

commit v3 on v2

--- a/solution.py
+++ b/solution.py
@@ -84,7 +84,7 @@
 
 def table_kernel(
     rate_ref, gain_ref, tap_ref,
-    fwd_ref, bwd_ref, side_ref, row_ref, tap_out_ref,
+    fwd_ref, side_ref, row_ref, tap_out_ref,
 ):
     shape = (BLOCK, ORDER)
     mode = lax.broadcasted_iota(jnp.int32, shape, 0)
@@ -129,8 +129,6 @@
         dims = (((0,), (0,)), ((), ()))
         later = lax.dot_general(grown, scaled, dims, precision=EXACT, preferred_element_type=F32)
         fwd_ref[g] = jnp.where(col >= row, later, 0.0).astype(BF16)
-        earlier = lax.dot_general(scaled, grown, dims, precision=EXACT, preferred_element_type=F32)
-        bwd_ref[g] = jnp.where(row >= col, earlier, 0.0).astype(BF16)
 
 
 def make_tables(rates, gains, taps):
@@ -141,9 +139,9 @@
     vmem = pl.BlockSpec(memory_space=pltpu.VMEM)
     return pl.pallas_call(
         table_kernel,
-        out_shape=(stack, stack, side, rows, columns),
+        out_shape=(stack, side, rows, columns),
         in_specs=[vmem] * 3,
-        out_specs=(vmem,) * 5,
+        out_specs=(vmem,) * 4,
         compiler_params=pltpu.CompilerParams(vmem_limit_bytes=8 << 20),
         cost_estimate=pl.CostEstimate(flops=6 * 64 * 2**20, bytes_accessed=5 << 20, transcendentals=1 << 19),
         name="filter_tables",
@@ -194,26 +192,27 @@
     )(*rows, weight, *([] if first else [sums]))
 
 
+def source_of(own, n):
+    return ((own - 2 * ((0,) + Y_STEPS)[n // 2]) & 6) | ((own & 1) ^ (n % 2))
+
+
 def mixer_kernel(*refs):
+    own = lax.axis_index("ctx")
     table_refs, refs = refs[:N_CTX], refs[N_CTX:]
-    sources, refs = refs[:4], refs[4:]
+    sources, refs = refs[:6], refs[6:]
     row_ref, tap_ref, out_ref, grad_proj_ref, raw_ref = refs[:5]
-    grad_ref, side_ref, fwd_ref, bwd_ref, sems = refs[5:]
-    copies = [
-        pltpu.make_async_copy(source, target, sems.at[n])
-        for n, (source, target) in enumerate(zip(sources, (grad_ref, side_ref, fwd_ref, bwd_ref)))
-    ]
+    grad_ref, side_ref, fwd_ref, sems = refs[5:]
+    copies = []
+    for n in range(N_CTX):
+        target = grad_ref.at[source_of(own, n)]
+        copies.append(pltpu.make_async_copy(sources[n // 2].at[n % 2], target, sems.at[n]))
+    copies.append(pltpu.make_async_copy(sources[4], side_ref, sems.at[N_CTX]))
+    copies.append(pltpu.make_async_copy(sources[5], fwd_ref, sems.at[N_CTX + 1]))
     for copy in copies:
         copy.start()
-    own = lax.axis_index("ctx")
     table = jnp.concatenate([ref[...].astype(F32) for ref in table_refs], axis=0).T.astype(BF16)
     share_row = lax.broadcasted_iota(jnp.int32, (SHARE, BLOCK), 0)
-    vocab = []
-    for step in (0,) + Y_STEPS:
-        for half in range(2):
-            source = ((own - 2 * step) & 6) | ((own & 1) ^ half)
-            vocab.append(share_row + source * SHARE)
-    vocab = jnp.concatenate(vocab, axis=0)
+    vocab = jnp.concatenate([share_row + source_of(own, n) * SHARE for n in range(N_CTX)], axis=0)
 
     edge = jnp.zeros((3 * BLOCK, HALO), F32)
     raw_ref[:, :HALO] = edge
@@ -226,9 +225,10 @@
         raw_ref[:, pl.ds(pl.multiple_of(HALO + block * BLOCK, HALO), BLOCK)] = nn(table, one_hot)
         return carried
 
-    copies[0].wait()
+    for copy in copies[:N_CTX]:
+        copy.wait()
     lax.fori_loop(0, N_CTX, look_up, 0)
-    copies[1].wait()
+    copies[N_CTX].wait()
 
     def featured(stream, block, width):
         rows = pl.ds(stream * BLOCK, BLOCK)
@@ -277,13 +277,12 @@
     through = jnp.where(same_group, through, 0.0).astype(BF16)
     after = jnp.where(same_group, after, 0.0).astype(BF16)
 
-    copies[2].wait()
-    copies[3].wait()
+    copies[N_CTX + 1].wait()
     conv_rows, mixed_grads = [], []
     for g in range(GROUPS):
         rows = slice(g * GROUP, (g + 1) * GROUP)
         conv_rows.append(nn(mixed_own[rows], fwd_ref[g]))
-        mixed_grads.append(nn(long_own[rows], bwd_ref[g]))
+        mixed_grads.append(nt(long_own[rows], fwd_ref[g]))
     conv = jnp.concatenate(conv_rows, axis=0) + nn(before, side_ref[:, ENTER])
     mixed_grad = jnp.concatenate(mixed_grads, axis=0) + nn(after, side_ref[:, LEAVE.start : LEAVE.start + BLOCK])
 
@@ -314,7 +313,7 @@
 
 
 def mix(pieces, grads, tables):
-    fwd, bwd, side, row, taps = tables
+    fwd, side, row, taps = tables
     vmem = pl.BlockSpec(memory_space=pltpu.VMEM)
     return pl.pallas_call(
         mixer_kernel,
@@ -322,20 +321,19 @@
             jax.ShapeDtypeStruct((BLOCK, BLOCK), BF16),
             jax.ShapeDtypeStruct((3 * BLOCK, BLOCK), BF16),
         ),
-        in_specs=[vmem] * N_CTX + [pl.BlockSpec(memory_space=pl.ANY)] * 4 + [vmem] * 2,
+        in_specs=[vmem] * N_CTX + [pl.BlockSpec(memory_space=pl.ANY)] * 6 + [vmem] * 2,
         out_specs=(vmem, vmem),
         scratch_shapes=[
             pltpu.VMEM((3 * BLOCK, WINDOW + 2 * HALO), F32),
             pltpu.VMEM((N_CTX, BLOCK + EXTRA, BLOCK), BF16),
             pltpu.VMEM((BLOCK, SIDE), BF16),
             pltpu.VMEM((GROUPS, BLOCK, BLOCK), BF16),
-            pltpu.VMEM((GROUPS, BLOCK, BLOCK), BF16),
-            pltpu.SemaphoreType.DMA((4,)),
+            pltpu.SemaphoreType.DMA((N_CTX + 2,)),
         ],
         compiler_params=pltpu.CompilerParams(vmem_limit_bytes=50 << 20),
         cost_estimate=pl.CostEstimate(flops=3 << 30, bytes_accessed=8 << 20, transcendentals=1 << 16),
         name="mixer",
-    )(*pieces, grads, side, fwd, bwd, row, taps)
+    )(*pieces, *grads, side, fwd, row, taps)
 
 
 def back_kernel(step_ref, grad_ref, weight_ref, own_ref, other_ref, held_ref, sems):
@@ -385,16 +383,18 @@
     )(jnp.asarray(steps, jnp.int32), grad_proj, weight)
 
 
-def project_features(rows, weight):
+def project_features(rows, weight, tables):
     held = lax.all_to_all(
         jnp.broadcast_to(rows[None], (N_Z,) + rows.shape), "chan", 0, 0, axis_index_groups=Z_GROUPS
     )
+    held, tables = lax.optimization_barrier((held, tables))
     beside = lax.ppermute(held, "chan", X_SWAP)
     across = lax.ppermute(held, "chan", CORE_SWAP)
+    sums = project((0,), (held,), weight, None, False)
+    beside, sums = lax.optimization_barrier((beside, sums))
     both = lax.ppermute(beside, "chan", CORE_SWAP)
-    sums = project((0,), (held,), weight, None, False)
     sums = project((2, 1), (across, beside), weight, sums, False)
-    return project((3,), (both,), weight, sums, True)
+    return project((3,), (both,), weight, sums, True), tables
 
 
 def gather_ctx(value):
@@ -405,42 +405,50 @@
     return [found[n] for n in (0, 1, 2, 5, 3, 6, 4, 7)]
 
 
+def gather_ctx_staged(value):
+    pair = jnp.stack([value, lax.ppermute(value, "ctx", X_HALF_SWAP)])
+    return [pair] + [lax.ppermute(pair, "ctx", y_shift(by)) for by in Y_STEPS]
+
+
+def moved(value, by):
+    return lax.ppermute(value.astype(BF16), "chan", z_shift(by)).astype(F32)
+
+
 def reduce_chan(grad_proj, weight):
-    up, down = z_shift(1), z_shift(-1)
     terms = {}
-    for steps in ((4,), (3, 5), (2, 6, 1, 7, 0)):
+
+    def add_terms(grad_proj, steps):
         own, other = back_project(grad_proj, weight, steps)
         swapped = lax.ppermute(other, "chan", CORE_SWAP)
         for n, step in enumerate(steps):
-            terms[step] = own[n].astype(F32) + swapped[n].astype(F32)
-    far = terms[4].astype(BF16)
-    ahead = lax.ppermute(far[0], "chan", up).astype(F32)
-    behind = lax.ppermute(far[1], "chan", down).astype(F32)
-    ahead = jnp.stack([terms[3][0] + ahead, terms[3][1]])
-    behind = jnp.stack([terms[5][0], terms[5][1] + behind])
-    for near, other in ((2, 6), (1, 7)):
-        ahead = terms[near] + lax.ppermute(ahead.astype(BF16), "chan", up).astype(F32)
-        behind = terms[other] + lax.ppermute(behind.astype(BF16), "chan", down).astype(F32)
-    total = terms[0] + lax.ppermute(ahead.astype(BF16), "chan", up).astype(F32)
-    total = total + lax.ppermute(behind.astype(BF16), "chan", down).astype(F32)
-    total = total[0] + lax.ppermute(total[1].astype(BF16), "chan", X_SWAP).astype(F32)
+            for half in range(2):
+                terms[step, half] = own[n, half].astype(F32) + swapped[n, half].astype(F32)
+
+    add_terms(grad_proj, (4,))
+    add_terms(grad_proj, (3, 5))
+    far = [terms[4, half].astype(BF16) for half in range(2)]
+    far, grad_proj = lax.optimization_barrier((far, grad_proj))
+    add_terms(grad_proj, (2, 6, 1, 7, 0))
+    totals = []
+    for half, long, short in ((1, 1, -1), (0, -1, 1)):
+        chain = {long: moved(far[half], long) + terms[(4 - long) % 8, half], short: terms[(4 - short) % 8, half]}
+        for hop in (2, 1):
+            for by in (long, short):
+                chain[by] = moved(chain[by], by) + terms[(by * hop) % 8, half]
+        totals.append(terms[0, half] + moved(chain[long], long) + moved(chain[short], short))
+    far_half, near_half = totals
+    total = near_half + lax.ppermute(far_half.astype(BF16), "chan", X_SWAP).astype(F32)
     return total.astype(BF16)
 
 
 def body(token_ids, embed_table, in_weight, feat_taps, modal_rates, modal_residues, out_grad):
     weight = in_weight.transpose(1, 0, 2).reshape(3, 2, N_Z, 2, BLOCK, BLOCK)
     own_vocab = lax.dynamic_slice_in_dim(embed_table, lax.axis_index("ctx") * SHARE, SHARE, 0)
-    payload = make_payload(out_grad, token_ids)
-    grads = lax.all_gather(payload, "ctx", axis=0)
-
-    part = project_features(own_vocab, weight)
-    modal_rates, part = lax.optimization_barrier((modal_rates, part))
-    pieces = gather_ctx(part)
-
+    grads = gather_ctx_staged(make_payload(out_grad, token_ids))
     gains = modal_residues * jnp.sqrt(-jnp.expm1(-2.0 * modal_rates))
     tables = make_tables(modal_rates, gains, feat_taps)
-
-    output, grad_proj = mix(pieces, grads, tables)
+    part, tables = project_features(own_vocab, weight, tables)
+    output, grad_proj = mix(gather_ctx(part), grads, tables)
     return (output, reduce_chan(grad_proj, weight).T)
 
 

time: 148 us -> 127 us (0.86); the launches traced: 146 us -> 127 us
  starting transfers between devices: 23.7 us -> 44.7 us
  blocking collectives: 20.1 us -> 0 us
  between operations: 14.4 us -> 0.86 us
  waiting for transfers between devices: 39 us -> 35.4 us
  Pallas kernels: 41.7 us -> 39.2 us
    all_to_all x1 -> x0, blocking collectives: 20.1 us -> none  [project_features(): lax.all_to_all(jnp.broadcast_to(rows[None], (N_Z,) + rows.shape), 'chan',...]
    ppermute x12 -> x22, starting transfers between devices: 11.3 us -> 25 us  [the longest x14 16.5 us: moved(): return lax.ppermute(value.astype(BF16), 'chan', z_shift(by)).astype(F32)]
    all_to_all x0 -> x1, starting transfers between devices: none -> 8.47 us  [project_features(): lax.all_to_all(jnp.broadcast_to(rows[None], (N_Z,) + rows.shape), 'chan',...]
    ppermute x12 -> x22, waiting for transfers between devices: 32.5 us -> 26.7 us  [the longest x14 19.9 us: moved(): return lax.ppermute(value.astype(BF16), 'chan', z_shift(by)).astype(F32)]
    ppermute x1, waiting for transfers between devices: 4.88 us -> 0.34 us  [project_features(): beside = lax.ppermute(held, 'chan', X_SWAP)]
    all_to_all x0 -> x1, waiting for transfers between devices: none -> 4.48 us  [project_features(): lax.all_to_all(jnp.broadcast_to(rows[None], (N_Z,) + rows.shape), 'chan',...]
    pallas_call x1, Pallas kernels: 7.17 us -> 3.91 us  [make_tables(): pl.pallas_call(table_kernel, out_shape=(stack, side, rows, columns), in_s...]
    ppermute x1, starting transfers between devices: 3.11 us -> 0.88 us  [gather_ctx(): across = lax.ppermute(value, 'ctx', X_HALF_SWAP)]
  transfers between devices with their start and end apart: 23 -> 33, of which waited for: 9 -> 21; matrix products, arithmetic and copies ran while one was open for 0% -> 1% of each run, Pallas kernels for 17% -> 14%
where the time goes in v3:
time: 127 us
  starting transfers between devices  44.7 us (35%)
  Pallas kernels  39.2 us (31%)
  waiting for transfers between devices  35.4 us (28%)
  local copies, waits for them, and re-layouts  5.19 us (4%)
  other arithmetic  1.57 us (1%)
    ppermute x14, waiting for transfers between devices, moved(): return lax.ppermute(value.astype(BF16), 'chan', z_shift(by)).astype(F32)  19.9 us
    ppermute x14, starting transfers between devices, moved(): return lax.ppermute(value.astype(BF16), 'chan', z_shift(by)).astype(F32)  16.5 us
    pallas_call x1, Pallas kernels, mix(): pl.pallas_call(mixer_kernel, out_shape=(jax.ShapeDtypeStruct((BLOCK, BLOC...  15.1 us
    pallas_call x3, Pallas kernels, project(): pl.pallas_call(functools.partial(project_kernel, parts, first, last), out...  10.1 us
    pallas_call x3, Pallas kernels, back_project(): pl.pallas_call(back_kernel, out_shape=(part, part), in_specs=[pl.BlockSpe...  10.1 us
    ppermute x6, starting transfers between devices, gather_ctx(): found += [lax.ppermute(piece, 'ctx', y_shift(by)) for by in Y_STEPS]  8.64 us
    all_to_all x1, starting transfers between devices, project_features(): lax.all_to_all(jnp.broadcast_to(rows[None], (N_Z,) + rows.shape), 'chan',...  8.47 us
    ppermute x3, starting transfers between devices, gather_ctx_staged(): return [pair] + [lax.ppermute(pair, 'ctx', y_shift(by)) for by in Y_STEPS]  4.56 us
  transfers between devices with their start and end apart: 33, of which 21 were waited for; matrix products, arithmetic and copies ran while one was open for 1% of the time, Pallas kernels for 14%

profile of v3, /device:TPU:24, one launch (start us, length us, event | category | flops | bytes accessed | tf_op | source)
XLA Modules:
  0.0 126.9 jit_solution(9718991585601702412)
XLA Ops:
  0.7 0.9 copy-done
  2.3 8.5 %all-to-all-start = ((bf16[8,64,256]{2,1,0:T(8,128)(2,1)}), bf16[8,64,256]{2,1,0:T(8,128)(2,1)S(1)}, u32[]{:S(2)}, u32[]{:S(2)}) async-start(bf16[8,64,256]{2,1,0:T(8,128)(2,1)} %broadcast_in_dim.2), calls=%async_computation | async-start | bytes 524288 | tf_op jit(solution)/shard_map/all_to_all | solution.py:387
  12.9 3.9 %filter_tables.1 = (bf16[16,256,256]{2,1,0:T(8,128)(2,1)S(1)}, bf16[256,1152]{1,0:T(8,128)(2,1)S(1)}, f32[2,256]{1,0:T(2,128)S(1)}, f32[768,3]{1,0:T(8,128)S(1)}) custom-call(f32[16,16]{1,0:T(8,128)S(1)} %copy-done.2, f32[16,16]{1,0:T(8,128)S(1)} %sqrt_multiply_fusion.gain_ref, f32[3,3,256]{2,1,0:T(4,128)S(1)} %copy-done.6), custom_call_target="tpu_custom_call" | custom-call | flops 402653184 | bytes 5242880 | tf_op jit(solution)/shard_map/filter_tables/pallas_call | solution.py:140
  16.9 1.3 %copy-done.7 = bf16[16,256,256]{2,1,0:T(8,128)(2,1)} copy-done((bf16[16,256,256]{2,1,0:T(8,128)(2,1)}, bf16[16,256,256]{2,1,0:T(8,128)(2,1)S(1)}, u32[]{:S(2)}) %copy-start.7) | copy-done | bytes 2097176
  18.2 4.5 %all-to-all-done.refs_0_ = bf16[8,64,256]{2,1,0:T(8,128)(2,1)S(1)} async-done(((bf16[8,64,256]{2,1,0:T(8,128)(2,1)}), bf16[8,64,256]{2,1,0:T(8,128)(2,1)S(1)}, u32[]{:S(2)}, u32[]{:S(2)}) %all-to-all-start) | async-done | bytes 262176 | tf_op jit(solution)/shard_map/all_to_all | solution.py:387
  22.7 1.5 %collective-permute-start = (bf16[8,64,256]{2,1,0:T(8,128)(2,1)S(1)}, bf16[8,64,256]{2,1,0:T(8,128)(2,1)S(1)}, u32[]{:S(2)}, u32[]{:S(2)}) collective-permute-start(bf16[8,64,256]{2,1,0:T(8,128)(2,1)S(1)} %all-to-all-done.refs_0_), channel_id=1, source_target_pairs={{0,16},{1,17},{2,18},{3,19},{4,20},{5,21},{6,22},{7,23},{8,24},{9,... | collective-permute-start | bytes 786440 | tf_op jit(solution)/shard_map/ppermute | solution.py:391
  24.3 2.8 %collective-permute-start.10 = (bf16[272,256]{1,0:T(8,128)(2,1)S(1)}, bf16[272,256]{1,0:T(8,128)(2,1)S(1)}, u32[]{:S(2)}, u32[]{:S(2)}) collective-permute-start(bf16[272,256]{1,0:T(8,128)(2,1)S(1)} %payload.1), channel_id=1, source_target_pairs={{0,32},{32,0},{64,96},{96,64},{128,160},{160,128},{192,224},{224,1... | collective-permute-start | bytes 417800 | tf_op jit(solution)/shard_map/ppermute | solution.py:409
  27.1 3.0 %project.3.refs_3_ = f32[64,768]{1,0:T(8,128)S(1)} custom-call(bf16[8,64,256]{2,1,0:T(8,128)(2,1)S(1)} %all-to-all-done.refs_0_, bf16[3,2,8,2,256,256]{5,4,3,2,1,0:T(8,128)(2,1)} %bitcast.74), custom_call_target="tpu_custom_call" | custom-call | flops 201326592 | bytes 3145728 | tf_op jit(solution)/shard_map/project/pallas_call | solution.py:178
  30.7 3.4 %collective-permute-done.10 = bf16[272,256]{1,0:T(8,128)(2,1)S(1)} collective-permute-done((bf16[272,256]{1,0:T(8,128)(2,1)S(1)}, bf16[272,256]{1,0:T(8,128)(2,1)S(1)}, u32[]{:S(2)}, u32[]{:S(2)}) %collective-permute-start.10) | collective-permute-done | bytes 139296 | tf_op jit(solution)/shard_map/ppermute | solution.py:409
  34.1 1.3 %collective-permute-start.13 = (bf16[2,272,256]{2,1,0:T(8,128)(2,1)S(1)}, bf16[2,272,256]{2,1,0:T(8,128)(2,1)S(1)}, u32[]{:S(2)}, u32[]{:S(2)}) collective-permute-start(bf16[2,272,256]{2,1,0:T(8,128)(2,1)S(1)} %pad_maximum_fusion.refs_8_), channel_id=1, source_target_pairs={{0,128},{32,160},{64,192},{96,224},{128,0},{160,32},{192,64},{224,... | collective-permute-start | bytes 835592 | tf_op jit(solution)/shard_map/ppermute | solution.py:410
  35.5 3.2 %collective-permute-start.11 = (bf16[2,272,256]{2,1,0:T(8,128)(2,1)S(1)}, bf16[2,272,256]{2,1,0:T(8,128)(2,1)S(1)}, u32[]{:S(2)}, u32[]{:S(2)}) collective-permute-start(bf16[2,272,256]{2,1,0:T(8,128)(2,1)S(1)} %pad_maximum_fusion.refs_8_), channel_id=1, source_target_pairs={{0,64},{32,96},{64,128},{96,160},{128,192},{160,224},{192,0},{224,... | collective-permute-start | bytes 835592 | tf_op jit(solution)/shard_map/ppermute | solution.py:410
  38.7 4.1 %project.4.refs_2_ = f32[64,768]{1,0:T(8,128)S(1)} custom-call(bf16[8,64,256]{2,1,0:T(8,128)(2,1)S(1)} %collective-permute-done.2.refs_0_, bf16[8,64,256]{2,1,0:T(8,128)(2,1)S(1)} %collective-permute-done.refs_1_, bf16[3,2,8,2,256,256]{5,4,3,2,1,0:T(8,128)(2,1)} %bitcast.75, f32[64,768]{1,0:T(8,128)S(1)} %project.3.refs_3_), custom_call_target="tpu_custom_call" | custom-call | flops 402653184 | bytes 6291456 | tf_op jit(solution)/shard_map/project/pallas_call | solution.py:178
  42.8 3.0 %project.5.refs_0_ = bf16[64,768]{1,0:T(8,128)(2,1)S(1)} custom-call(bf16[8,64,256]{2,1,0:T(8,128)(2,1)S(1)} %collective-permute-done.1.refs_0_, bf16[3,2,8,2,256,256]{5,4,3,2,1,0:T(8,128)(2,1)} %bitcast.76, f32[64,768]{1,0:T(8,128)S(1)} %project.4.refs_2_), custom_call_target="tpu_custom_call" | custom-call | flops 201326592 | bytes 3145728 | tf_op jit(solution)/shard_map/project/pallas_call | solution.py:178
  45.8 0.9 collective-permute-start.3
  46.7 1.1 collective-permute-start.8
  47.8 0.7 collective-permute-start.6
  48.5 2.5 %collective-permute-start.4 = (bf16[64,768]{1,0:T(8,128)(2,1)S(1)}, bf16[64,768]{1,0:T(8,128)(2,1)S(1)}, u32[]{:S(2)}, u32[]{:S(2)}) collective-permute-start(bf16[64,768]{1,0:T(8,128)(2,1)S(1)} %project.5.refs_0_), channel_id=1, source_target_pairs={{0,64},{32,96},{64,128},{96,160},{128,192},{160,224},{192,0},{224,... | collective-permute-start | bytes 294920 | tf_op jit(solution)/shard_map/ppermute | solution.py:404
  51.0 1.0 collective-permute-done.3.refs_1_
  52.0 1.1 collective-permute-start.9
  53.9 2.5 %collective-permute-start.5 = (bf16[64,768]{1,0:T(8,128)(2,1)S(1)}, bf16[64,768]{1,0:T(8,128)(2,1)S(1)}, u32[]{:S(2)}, u32[]{:S(2)}) collective-permute-start(bf16[64,768]{1,0:T(8,128)(2,1)S(1)} %collective-permute-done.3.refs_1_), channel_id=1, source_target_pairs={{0,64},{32,96},{64,128},{96,160},{128,192},{160,224},{192,0},{224,... | collective-permute-start | bytes 294920 | tf_op jit(solution)/shard_map/ppermute | solution.py:404
  56.4 1.8 %collective-permute-done.9.refs_7_ = bf16[64,768]{1,0:T(8,128)(2,1)S(1)} collective-permute-done((bf16[64,768]{1,0:T(8,128)(2,1)S(1)}, bf16[64,768]{1,0:T(8,128)(2,1)S(1)}, u32[]{:S(2)}, u32[]{:S(2)}) %collective-permute-start.9) | collective-permute-done | bytes 98336 | tf_op jit(solution)/shard_map/ppermute | solution.py:404
  58.2 1.0 collective-permute-done.7.refs_5_
  59.2 15.1 %mixer.1 = (bf16[256,256]{1,0:T(8,128)(2,1)}, bf16[768,256]{1,0:T(8,128)(2,1)S(1)}) custom-call(bf16[64,768]{1,0:T(8,128)(2,1)S(1)} %project.5.refs_0_, bf16[64,768]{1,0:T(8,128)(2,1)S(1)} %collective-permute-done.3.refs_1_, bf16[64,768]{1,0:T(8,128)(2,1)S(1)} %collective-permute-done.4.refs_2_, bf16[64,768]{1,0:T(8,128)(2,1)S(1)} %collective-permute-done.5.refs_3_, ...), custom_call_target="tpu_custom_call" | custom-call | flops 3221225472 | bytes 8388608 | tf_op jit(solution)/shard_map/mixer/pallas_call | solution.py:318
  74.3 2.0 %back_project.3 = (bf16[1,2,256,256]{3,2,1,0:T(8,128)(2,1)S(1)}, bf16[1,2,256,256]{3,2,1,0:T(8,128)(2,1)S(1)}) custom-call(s32[1]{0:T(128)} %constant.20.clone.step_ref, bf16[768,256]{1,0:T(8,128)(2,1)S(1)} %get-tuple-element.39.grad_ref, bf16[3,2,8,2,256,256]{5,4,3,2,1,0:T(8,128)(2,1)} %bitcast.77), custom_call_target="tpu_custom_call" | custom-call | flops 402653184 | bytes 2097152 | tf_op jit(solution)/shard_map/back_project/pallas_call | solution.py:369
  76.4 1.5 %collective-permute-done.14 = bf16[1,2,256,256]{3,2,1,0:T(8,128)(2,1)S(1)} collective-permute-done((bf16[1,2,256,256]{3,2,1,0:T(8,128)(2,1)S(1)}, bf16[1,2,256,256]{3,2,1,0:T(8,128)(2,1)S(1)}, u32[]{:S(2)}, u32[]{:S(2)}) %collective-permute-start.14) | collective-permute-done | bytes 262176 | tf_op jit(solution)/shard_map/ppermute | solution.py:422
  78.0 4.9 %back_project.4 = (bf16[5,2,256,256]{3,2,1,0:T(8,128)(2,1)S(1)}, bf16[5,2,256,256]{3,2,1,0:T(8,128)(2,1)S(1)}) custom-call(s32[5]{0:T(128)S(1)} %copy-done.5, bf16[768,256]{1,0:T(8,128)(2,1)S(1)} %get-tuple-element.39.grad_ref, bf16[3,2,8,2,256,256]{5,4,3,2,1,0:T(8,128)(2,1)} %bitcast.78), custom_call_target="tpu_custom_call" | custom-call | flops 2013265920 | bytes 10485760 | tf_op jit(solution)/shard_map/back_project/pallas_call | solution.py:369
  83.2 3.1 %back_project.5 = (bf16[2,2,256,256]{3,2,1,0:T(8,128)(2,1)S(1)}, bf16[2,2,256,256]{3,2,1,0:T(8,128)(2,1)S(1)}) custom-call(s32[2]{0:T(128)S(1)} %copy-done.4, bf16[768,256]{1,0:T(8,128)(2,1)S(1)} %get-tuple-element.39.grad_ref, bf16[3,2,8,2,256,256]{5,4,3,2,1,0:T(8,128)(2,1)} %bitcast.79), custom_call_target="tpu_custom_call" | custom-call | flops 805306368 | bytes 4194304 | tf_op jit(solution)/shard_map/back_project/pallas_call | solution.py:369
  86.8 2.0 %collective-permute-start.24 = (bf16[256,256]{1,0:T(8,128)(2,1)S(1)}, bf16[256,256]{1,0:T(8,128)(2,1)S(1)}, u32[]{:S(2)}, u32[]{:S(2)}) collective-permute-start(bf16[256,256]{1,0:T(8,128)(2,1)S(1)} %get-tuple-element.45), channel_id=1, source_target_pairs={{0,2},{1,3},{2,4},{3,5},{4,6},{5,7},{6,8},{7,9},{8,10},{9,11},{10,... | collective-permute-start | bytes 393224 | tf_op jit(solution)/shard_map/ppermute | solution.py:414
  88.8 3.5 %collective-permute-done.16 = bf16[256,256]{1,0:T(8,128)(2,1)S(1)} collective-permute-done((bf16[256,256]{1,0:T(8,128)(2,1)S(1)}, bf16[256,256]{1,0:T(8,128)(2,1)S(1)}, u32[]{:S(2)}, u32[]{:S(2)}) %collective-permute-start.16) | collective-permute-done | bytes 131104 | tf_op jit(solution)/shard_map/ppermute | solution.py:414
  92.3 1.3 collective-permute-done.24
  93.7 0.8 collective-permute-start.18
  94.5 1.3 %collective-permute-start.25 = (bf16[256,256]{1,0:T(8,128)(2,1)S(1)}, bf16[256,256]{1,0:T(8,128)(2,1)S(1)}, u32[]{:S(2)}, u32[]{:S(2)}) collective-permute-start(bf16[256,256]{1,0:T(8,128)(2,1)S(1)} %get-tuple-element.57), channel_id=1, source_target_pairs={{0,2},{1,3},{2,4},{3,5},{4,6},{5,7},{6,8},{7,9},{8,10},{9,11},{10,... | collective-permute-start | bytes 393224 | tf_op jit(solution)/shard_map/ppermute | solution.py:414
  95.9 0.8 collective-permute-start.21
  96.7 2.7 %collective-permute-start.28 = (bf16[256,256]{1,0:T(8,128)(2,1)S(1)}, bf16[256,256]{1,0:T(8,128)(2,1)S(1)}, u32[]{:S(2)}, u32[]{:S(2)}) collective-permute-start(bf16[256,256]{1,0:T(8,128)(2,1)S(1)} %get-tuple-element.59), channel_id=1, source_target_pairs={{0,14},{1,15},{2,0},{3,1},{4,2},{5,3},{6,4},{7,5},{8,6},{9,7},{10,... | collective-permute-start | bytes 393224 | tf_op jit(solution)/shard_map/ppermute | solution.py:414
  99.8 1.7 %collective-permute-done.25 = bf16[256,256]{1,0:T(8,128)(2,1)S(1)} collective-permute-done((bf16[256,256]{1,0:T(8,128)(2,1)S(1)}, bf16[256,256]{1,0:T(8,128)(2,1)S(1)}, u32[]{:S(2)}, u32[]{:S(2)}) %collective-permute-start.25) | collective-permute-done | bytes 131104 | tf_op jit(solution)/shard_map/ppermute | solution.py:414
  101.6 1.4 %collective-permute-done.21 = bf16[256,256]{1,0:T(8,128)(2,1)S(1)} collective-permute-done((bf16[256,256]{1,0:T(8,128)(2,1)S(1)}, bf16[256,256]{1,0:T(8,128)(2,1)S(1)}, u32[]{:S(2)}, u32[]{:S(2)}) %collective-permute-start.21) | collective-permute-done | bytes 131104 | tf_op jit(solution)/shard_map/ppermute | solution.py:414
  103.2 2.7 %collective-permute-start.19 = (bf16[256,256]{1,0:T(8,128)(2,1)S(1)}, bf16[256,256]{1,0:T(8,128)(2,1)S(1)}, u32[]{:S(2)}, u32[]{:S(2)}) collective-permute-start(bf16[256,256]{1,0:T(8,128)(2,1)S(1)} %get-tuple-element.52), channel_id=1, source_target_pairs={{0,14},{1,15},{2,0},{3,1},{4,2},{5,3},{6,4},{7,5},{8,6},{9,7},{10,... | collective-permute-start | bytes 393224 | tf_op jit(solution)/shard_map/ppermute | solution.py:414
  106.0 1.9 %collective-permute-start.26 = (bf16[256,256]{1,0:T(8,128)(2,1)S(1)}, bf16[256,256]{1,0:T(8,128)(2,1)S(1)}, u32[]{:S(2)}, u32[]{:S(2)}) collective-permute-start(bf16[256,256]{1,0:T(8,128)(2,1)S(1)} %get-tuple-element.54), channel_id=1, source_target_pairs={{0,2},{1,3},{2,4},{3,5},{4,6},{5,7},{6,8},{7,9},{8,10},{9,11},{10,... | collective-permute-start | bytes 393224 | tf_op jit(solution)/shard_map/ppermute | solution.py:414
  108.4 2.4 %collective-permute-done.29 = bf16[256,256]{1,0:T(8,128)(2,1)S(1)} collective-permute-done((bf16[256,256]{1,0:T(8,128)(2,1)S(1)}, bf16[256,256]{1,0:T(8,128)(2,1)S(1)}, u32[]{:S(2)}, u32[]{:S(2)}) %collective-permute-start.29) | collective-permute-done | bytes 131104 | tf_op jit(solution)/shard_map/ppermute | solution.py:414
  110.9 1.3 %collective-permute-done.26 = bf16[256,256]{1,0:T(8,128)(2,1)S(1)} collective-permute-done((bf16[256,256]{1,0:T(8,128)(2,1)S(1)}, bf16[256,256]{1,0:T(8,128)(2,1)S(1)}, u32[]{:S(2)}, u32[]{:S(2)}) %collective-permute-start.26) | collective-permute-done | bytes 131104 | tf_op jit(solution)/shard_map/ppermute | solution.py:414
  112.2 1.9 %collective-permute-done.22 = bf16[256,256]{1,0:T(8,128)(2,1)S(1)} collective-permute-done((bf16[256,256]{1,0:T(8,128)(2,1)S(1)}, bf16[256,256]{1,0:T(8,128)(2,1)S(1)}, u32[]{:S(2)}, u32[]{:S(2)}) %collective-permute-start.22) | collective-permute-done | bytes 131104 | tf_op jit(solution)/shard_map/ppermute | solution.py:414
  114.7 1.7 %collective-permute-start.27 = (bf16[256,256]{1,0:T(8,128)(2,1)S(1)}, bf16[256,256]{1,0:T(8,128)(2,1)S(1)}, u32[]{:S(2)}, u32[]{:S(2)}) collective-permute-start(bf16[256,256]{1,0:T(8,128)(2,1)S(1)} %get-tuple-element.50), channel_id=1, source_target_pairs={{0,2},{1,3},{2,4},{3,5},{4,6},{5,7},{6,8},{7,9},{8,10},{9,11},{10,... | collective-permute-start | bytes 393224 | tf_op jit(solution)/shard_map/ppermute | solution.py:414
  116.4 1.6 %collective-permute-start.20 = (bf16[256,256]{1,0:T(8,128)(2,1)S(1)}, bf16[256,256]{1,0:T(8,128)(2,1)S(1)}, u32[]{:S(2)}, u32[]{:S(2)}) collective-permute-start(bf16[256,256]{1,0:T(8,128)(2,1)S(1)} %get-tuple-element.48), channel_id=1, source_target_pairs={{0,14},{1,15},{2,0},{3,1},{4,2},{5,3},{6,4},{7,5},{8,6},{9,7},{10,... | collective-permute-start | bytes 393224 | tf_op jit(solution)/shard_map/ppermute | solution.py:414
  118.4 0.9 collective-permute-done.30
  119.3 1.6 %collective-permute-done.27 = bf16[256,256]{1,0:T(8,128)(2,1)S(1)} collective-permute-done((bf16[256,256]{1,0:T(8,128)(2,1)S(1)}, bf16[256,256]{1,0:T(8,128)(2,1)S(1)}, u32[]{:S(2)}, u32[]{:S(2)}) %collective-permute-start.27) | collective-permute-done | bytes 131104 | tf_op jit(solution)/shard_map/ppermute | solution.py:414
  121.4 2.8 %collective-permute-done.23 = bf16[256,256]{1,0:T(8,128)(2,1)S(1)} collective-permute-done((bf16[256,256]{1,0:T(8,128)(2,1)S(1)}, bf16[256,256]{1,0:T(8,128)(2,1)S(1)}, u32[]{:S(2)}, u32[]{:S(2)}) %collective-permute-start.23) | collective-permute-done | bytes 131104 | tf_op jit(solution)/shard_map/ppermute | solution.py:414
  124.2 1.9 %collective-permute-done.31 = bf16[256,256]{1,0:T(8,128)(2,1)S(1)} collective-permute-done((bf16[256,256]{1,0:T(8,128)(2,1)S(1)}, bf16[256,256]{1,0:T(8,128)(2,1)S(1)}, u32[]{:S(2)}, u32[]{:S(2)}) %collective-permute-start.31) | collective-permute-done | bytes 131104 | tf_op jit(solution)/shard_map/ppermute | solution.py:440
  126.1 0.8 copy.12
  (55 shorter events, 8.3 us)
Async XLA Ops:
  0.6 1.0 copy-start
  0.6 23.5 %copy-start.1 = (bf16[256,256]{1,0:T(8,128)(2,1)S(1)}, bf16[256,256]{1,0:T(8,128)(2,1)}, u32[]{:S(2)}) copy-start(bf16[256,256]{1,0:T(8,128)(2,1)} %grad_ref.1) | copy-start | bytes 393220
  0.7 23.5 %copy-start.3 = (s32[256]{0:T(256)S(1)}, s32[256]{0:T(256)}, u32[]{:S(2)}) copy-start(s32[256]{0:T(256)} %param.10) | copy-start | bytes 3076
  2.3 20.3 %all-to-all-start = ((bf16[8,64,256]{2,1,0:T(8,128)(2,1)}), bf16[8,64,256]{2,1,0:T(8,128)(2,1)S(1)}, u32[]{:S(2)}, u32[]{:S(2)}) async-start(bf16[8,64,256]{2,1,0:T(8,128)(2,1)} %broadcast_in_dim.2), calls=%async_computation | async-start | bytes 524288 | tf_op jit(solution)/shard_map/all_to_all | solution.py:387
  11.5 0.7 copy-start.2
  12.2 0.7 copy-start.6
  16.9 1.3 %copy-start.7 = (bf16[16,256,256]{2,1,0:T(8,128)(2,1)}, bf16[16,256,256]{2,1,0:T(8,128)(2,1)S(1)}, u32[]{:S(2)}) copy-start(bf16[16,256,256]{2,1,0:T(8,128)(2,1)S(1)} %get-tuple-element.32.refs_13_) | copy-start | bytes 6291460
  22.7 7.8 %collective-permute-start = (bf16[8,64,256]{2,1,0:T(8,128)(2,1)S(1)}, bf16[8,64,256]{2,1,0:T(8,128)(2,1)S(1)}, u32[]{:S(2)}, u32[]{:S(2)}) collective-permute-start(bf16[8,64,256]{2,1,0:T(8,128)(2,1)S(1)} %all-to-all-done.refs_0_), channel_id=1, source_target_pairs={{0,16},{1,17},{2,18},{3,19},{4,20},{5,21},{6,22},{7,23},{8,24},{9,... | collective-permute-start | bytes 786440 | tf_op jit(solution)/shard_map/ppermute | solution.py:391
  24.3 9.8 %collective-permute-start.10 = (bf16[272,256]{1,0:T(8,128)(2,1)S(1)}, bf16[272,256]{1,0:T(8,128)(2,1)S(1)}, u32[]{:S(2)}, u32[]{:S(2)}) collective-permute-start(bf16[272,256]{1,0:T(8,128)(2,1)S(1)} %payload.1), channel_id=1, source_target_pairs={{0,32},{32,0},{64,96},{96,64},{128,160},{160,128},{192,224},{224,1... | collective-permute-start | bytes 417800 | tf_op jit(solution)/shard_map/ppermute | solution.py:409
  27.1 11.6 %collective-permute-start.2 = (bf16[8,64,256]{2,1,0:T(8,128)(2,1)S(1)}, bf16[8,64,256]{2,1,0:T(8,128)(2,1)S(1)}, u32[]{:S(2)}, u32[]{:S(2)}) collective-permute-start(bf16[8,64,256]{2,1,0:T(8,128)(2,1)S(1)} %all-to-all-done.refs_0_), channel_id=1, source_target_pairs={{0,1},{1,0},{2,3},{3,2},{4,5},{5,4},{6,7},{7,6},{8,9},{9,8},{10,11... | collective-permute-start | bytes 786440 | tf_op jit(solution)/shard_map/ppermute | solution.py:392
  30.4 12.4 %collective-permute-start.1 = (bf16[8,64,256]{2,1,0:T(8,128)(2,1)S(1)}, bf16[8,64,256]{2,1,0:T(8,128)(2,1)S(1)}, u32[]{:S(2)}, u32[]{:S(2)}) collective-permute-start(bf16[8,64,256]{2,1,0:T(8,128)(2,1)S(1)} %collective-permute-done.refs_1_), channel_id=1, source_target_pairs={{0,1},{1,0},{2,3},{3,2},{4,5},{5,4},{6,7},{7,6},{8,9},{9,8},{10,11... | collective-permute-start | bytes 786440 | tf_op jit(solution)/shard_map/ppermute | solution.py:395
  34.1 13.6 %collective-permute-start.13 = (bf16[2,272,256]{2,1,0:T(8,128)(2,1)S(1)}, bf16[2,272,256]{2,1,0:T(8,128)(2,1)S(1)}, u32[]{:S(2)}, u32[]{:S(2)}) collective-permute-start(bf16[2,272,256]{2,1,0:T(8,128)(2,1)S(1)} %pad_maximum_fusion.refs_8_), channel_id=1, source_target_pairs={{0,128},{32,160},{64,192},{96,224},{128,0},{160,32},{192,64},{224,... | collective-permute-start | bytes 835592 | tf_op jit(solution)/shard_map/ppermute | solution.py:410
  35.5 13.1 %collective-permute-start.12 = (bf16[2,272,256]{2,1,0:T(8,128)(2,1)S(1)}, bf16[2,272,256]{2,1,0:T(8,128)(2,1)S(1)}, u32[]{:S(2)}, u32[]{:S(2)}) collective-permute-start(bf16[2,272,256]{2,1,0:T(8,128)(2,1)S(1)} %pad_maximum_fusion.refs_8_), channel_id=1, source_target_pairs={{0,192},{32,224},{64,0},{96,32},{128,64},{160,96},{192,128},{224,1... | collective-permute-start | bytes 835592 | tf_op jit(solution)/shard_map/ppermute | solution.py:410
  35.5 17.6 %collective-permute-start.11 = (bf16[2,272,256]{2,1,0:T(8,128)(2,1)S(1)}, bf16[2,272,256]{2,1,0:T(8,128)(2,1)S(1)}, u32[]{:S(2)}, u32[]{:S(2)}) collective-permute-start(bf16[2,272,256]{2,1,0:T(8,128)(2,1)S(1)} %pad_maximum_fusion.refs_8_), channel_id=1, source_target_pairs={{0,64},{32,96},{64,128},{96,160},{128,192},{160,224},{192,0},{224,... | collective-permute-start | bytes 835592 | tf_op jit(solution)/shard_map/ppermute | solution.py:410
  45.8 6.2 %collective-permute-start.3 = (bf16[64,768]{1,0:T(8,128)(2,1)S(1)}, bf16[64,768]{1,0:T(8,128)(2,1)S(1)}, u32[]{:S(2)}, u32[]{:S(2)}) collective-permute-start(bf16[64,768]{1,0:T(8,128)(2,1)S(1)} %project.5.refs_0_), channel_id=1, source_target_pairs={{0,32},{32,0},{64,96},{96,64},{128,160},{160,128},{192,224},{224,1... | collective-permute-start | bytes 294920 | tf_op jit(solution)/shard_map/ppermute | solution.py:401
  46.7 7.2 %collective-permute-start.8 = (bf16[64,768]{1,0:T(8,128)(2,1)S(1)}, bf16[64,768]{1,0:T(8,128)(2,1)S(1)}, u32[]{:S(2)}, u32[]{:S(2)}) collective-permute-start(bf16[64,768]{1,0:T(8,128)(2,1)S(1)} %project.5.refs_0_), channel_id=1, source_target_pairs={{0,128},{32,160},{64,192},{96,224},{128,0},{160,32},{192,64},{224,... | collective-permute-start | bytes 294920 | tf_op jit(solution)/shard_map/ppermute | solution.py:404
  47.8 8.6 %collective-permute-start.6 = (bf16[64,768]{1,0:T(8,128)(2,1)S(1)}, bf16[64,768]{1,0:T(8,128)(2,1)S(1)}, u32[]{:S(2)}, u32[]{:S(2)}) collective-permute-start(bf16[64,768]{1,0:T(8,128)(2,1)S(1)} %project.5.refs_0_), channel_id=1, source_target_pairs={{0,192},{32,224},{64,0},{96,32},{128,64},{160,96},{192,128},{224,1... | collective-permute-start | bytes 294920 | tf_op jit(solution)/shard_map/ppermute | solution.py:404
  48.5 7.8 %collective-permute-start.4 = (bf16[64,768]{1,0:T(8,128)(2,1)S(1)}, bf16[64,768]{1,0:T(8,128)(2,1)S(1)}, u32[]{:S(2)}, u32[]{:S(2)}) collective-permute-start(bf16[64,768]{1,0:T(8,128)(2,1)S(1)} %project.5.refs_0_), channel_id=1, source_target_pairs={{0,64},{32,96},{64,128},{96,160},{128,192},{160,224},{192,0},{224,... | collective-permute-start | bytes 294920 | tf_op jit(solution)/shard_map/ppermute | solution.py:404
  52.0 6.1 %collective-permute-start.9 = (bf16[64,768]{1,0:T(8,128)(2,1)S(1)}, bf16[64,768]{1,0:T(8,128)(2,1)S(1)}, u32[]{:S(2)}, u32[]{:S(2)}) collective-permute-start(bf16[64,768]{1,0:T(8,128)(2,1)S(1)} %collective-permute-done.3.refs_1_), channel_id=1, source_target_pairs={{0,128},{32,160},{64,192},{96,224},{128,0},{160,32},{192,64},{224,... | collective-permute-start | bytes 294920 | tf_op jit(solution)/shard_map/ppermute | solution.py:404
  53.1 6.1 %collective-permute-start.7 = (bf16[64,768]{1,0:T(8,128)(2,1)S(1)}, bf16[64,768]{1,0:T(8,128)(2,1)S(1)}, u32[]{:S(2)}, u32[]{:S(2)}) collective-permute-start(bf16[64,768]{1,0:T(8,128)(2,1)S(1)} %collective-permute-done.3.refs_1_), channel_id=1, source_target_pairs={{0,192},{32,224},{64,0},{96,32},{128,64},{160,96},{192,128},{224,1... | collective-permute-start | bytes 294920 | tf_op jit(solution)/shard_map/ppermute | solution.py:404
  53.9 5.3 %collective-permute-start.5 = (bf16[64,768]{1,0:T(8,128)(2,1)S(1)}, bf16[64,768]{1,0:T(8,128)(2,1)S(1)}, u32[]{:S(2)}, u32[]{:S(2)}) collective-permute-start(bf16[64,768]{1,0:T(8,128)(2,1)S(1)} %collective-permute-done.3.refs_1_), channel_id=1, source_target_pairs={{0,64},{32,96},{64,128},{96,160},{128,192},{160,224},{192,0},{224,... | collective-permute-start | bytes 294920 | tf_op jit(solution)/shard_map/ppermute | solution.py:404
  74.3 3.7 %copy-start.5 = (s32[5]{0:T(128)S(1)}, s32[5]{0:T(128)}, u32[]{:S(2)}) copy-start(s32[5]{0:T(128)} %constant.22.clone.step_ref) | copy-start | bytes 64
  76.3 1.6 %collective-permute-start.14 = (bf16[1,2,256,256]{3,2,1,0:T(8,128)(2,1)S(1)}, bf16[1,2,256,256]{3,2,1,0:T(8,128)(2,1)S(1)}, u32[]{:S(2)}, u32[]{:S(2)}) collective-permute-start(bf16[1,2,256,256]{3,2,1,0:T(8,128)(2,1)S(1)} %get-tuple-element.38), channel_id=1, source_target_pairs={{0,1},{1,0},{2,3},{3,2},{4,5},{5,4},{6,7},{7,6},{8,9},{9,8},{10,11... | collective-permute-start | bytes 786440 | tf_op jit(solution)/shard_map/ppermute | solution.py:422
  78.0 5.2 %copy-start.4 = (s32[2]{0:T(128)S(1)}, s32[2]{0:T(128)}, u32[]{:S(2)}) copy-start(s32[2]{0:T(128)} %constant.21.clone.step_ref) | copy-start | bytes 28
  83.0 20.0 %collective-permute-start.15 = (bf16[5,2,256,256]{3,2,1,0:T(8,128)(2,1)S(1)}, bf16[5,2,256,256]{3,2,1,0:T(8,128)(2,1)S(1)}, u32[]{:S(2)}, u32[]{:S(2)}) collective-permute-start(bf16[5,2,256,256]{3,2,1,0:T(8,128)(2,1)S(1)} %get-tuple-element.41), channel_id=1, source_target_pairs={{0,1},{1,0},{2,3},{3,2},{4,5},{5,4},{6,7},{7,6},{8,9},{9,8},{10,11... | collective-permute-start | bytes 3932168 | tf_op jit(solution)/shard_map/ppermute | solution.py:422
  86.3 7.3 %collective-permute-start.17 = (bf16[2,2,256,256]{3,2,1,0:T(8,128)(2,1)S(1)}, bf16[2,2,256,256]{3,2,1,0:T(8,128)(2,1)S(1)}, u32[]{:S(2)}, u32[]{:S(2)}) collective-permute-start(bf16[2,2,256,256]{3,2,1,0:T(8,128)(2,1)S(1)} %get-tuple-element.44), channel_id=1, source_target_pairs={{0,1},{1,0},{2,3},{3,2},{4,5},{5,4},{6,7},{7,6},{8,9},{9,8},{10,11... | collective-permute-start | bytes 1572872 | tf_op jit(solution)/shard_map/ppermute | solution.py:422
  86.8 5.5 %collective-permute-start.16 = (bf16[256,256]{1,0:T(8,128)(2,1)S(1)}, bf16[256,256]{1,0:T(8,128)(2,1)S(1)}, u32[]{:S(2)}, u32[]{:S(2)}) collective-permute-start(bf16[256,256]{1,0:T(8,128)(2,1)S(1)} %get-tuple-element.42), channel_id=1, source_target_pairs={{0,14},{1,15},{2,0},{3,1},{4,2},{5,3},{6,4},{7,5},{8,6},{9,7},{10,... | collective-permute-start | bytes 393224 | tf_op jit(solution)/shard_map/ppermute | solution.py:414
  86.8 6.8 %collective-permute-start.24 = (bf16[256,256]{1,0:T(8,128)(2,1)S(1)}, bf16[256,256]{1,0:T(8,128)(2,1)S(1)}, u32[]{:S(2)}, u32[]{:S(2)}) collective-permute-start(bf16[256,256]{1,0:T(8,128)(2,1)S(1)} %get-tuple-element.45), channel_id=1, source_target_pairs={{0,2},{1,3},{2,4},{3,5},{4,6},{5,7},{6,8},{7,9},{8,10},{9,11},{10,... | collective-permute-start | bytes 393224 | tf_op jit(solution)/shard_map/ppermute | solution.py:414
  93.7 6.1 %collective-permute-start.18 = (bf16[256,256]{1,0:T(8,128)(2,1)S(1)}, bf16[256,256]{1,0:T(8,128)(2,1)S(1)}, u32[]{:S(2)}, u32[]{:S(2)}) collective-permute-start(bf16[256,256]{1,0:T(8,128)(2,1)S(1)} %get-tuple-element.56), channel_id=1, source_target_pairs={{0,14},{1,15},{2,0},{3,1},{4,2},{5,3},{6,4},{7,5},{8,6},{9,7},{10,... | collective-permute-start | bytes 393224 | tf_op jit(solution)/shard_map/ppermute | solution.py:414
  94.5 7.1 %collective-permute-start.25 = (bf16[256,256]{1,0:T(8,128)(2,1)S(1)}, bf16[256,256]{1,0:T(8,128)(2,1)S(1)}, u32[]{:S(2)}, u32[]{:S(2)}) collective-permute-start(bf16[256,256]{1,0:T(8,128)(2,1)S(1)} %get-tuple-element.57), channel_id=1, source_target_pairs={{0,2},{1,3},{2,4},{3,5},{4,6},{5,7},{6,8},{7,9},{8,10},{9,11},{10,... | collective-permute-start | bytes 393224 | tf_op jit(solution)/shard_map/ppermute | solution.py:414
  95.9 7.1 %collective-permute-start.21 = (bf16[256,256]{1,0:T(8,128)(2,1)S(1)}, bf16[256,256]{1,0:T(8,128)(2,1)S(1)}, u32[]{:S(2)}, u32[]{:S(2)}) collective-permute-start(bf16[256,256]{1,0:T(8,128)(2,1)S(1)} %get-tuple-element.58), channel_id=1, source_target_pairs={{0,2},{1,3},{2,4},{3,5},{4,6},{5,7},{6,8},{7,9},{8,10},{9,11},{10,... | collective-permute-start | bytes 393224 | tf_op jit(solution)/shard_map/ppermute | solution.py:414
  96.7 6.3 %collective-permute-start.28 = (bf16[256,256]{1,0:T(8,128)(2,1)S(1)}, bf16[256,256]{1,0:T(8,128)(2,1)S(1)}, u32[]{:S(2)}, u32[]{:S(2)}) collective-permute-start(bf16[256,256]{1,0:T(8,128)(2,1)S(1)} %get-tuple-element.59), channel_id=1, source_target_pairs={{0,14},{1,15},{2,0},{3,1},{4,2},{5,3},{6,4},{7,5},{8,6},{9,7},{10,... | collective-permute-start | bytes 393224 | tf_op jit(solution)/shard_map/ppermute | solution.py:414
  103.2 5.2 %collective-permute-start.19 = (bf16[256,256]{1,0:T(8,128)(2,1)S(1)}, bf16[256,256]{1,0:T(8,128)(2,1)S(1)}, u32[]{:S(2)}, u32[]{:S(2)}) collective-permute-start(bf16[256,256]{1,0:T(8,128)(2,1)S(1)} %get-tuple-element.52), channel_id=1, source_target_pairs={{0,14},{1,15},{2,0},{3,1},{4,2},{5,3},{6,4},{7,5},{8,6},{9,7},{10,... | collective-permute-start | bytes 393224 | tf_op jit(solution)/shard_map/ppermute | solution.py:414
  105.9 5.0 %collective-permute-start.29 = (bf16[256,256]{1,0:T(8,128)(2,1)S(1)}, bf16[256,256]{1,0:T(8,128)(2,1)S(1)}, u32[]{:S(2)}, u32[]{:S(2)}) collective-permute-start(bf16[256,256]{1,0:T(8,128)(2,1)S(1)} %get-tuple-element.53), channel_id=1, source_target_pairs={{0,14},{1,15},{2,0},{3,1},{4,2},{5,3},{6,4},{7,5},{8,6},{9,7},{10,... | collective-permute-start | bytes 393224 | tf_op jit(solution)/shard_map/ppermute | solution.py:414
  106.0 6.2 %collective-permute-start.26 = (bf16[256,256]{1,0:T(8,128)(2,1)S(1)}, bf16[256,256]{1,0:T(8,128)(2,1)S(1)}, u32[]{:S(2)}, u32[]{:S(2)}) collective-permute-start(bf16[256,256]{1,0:T(8,128)(2,1)S(1)} %get-tuple-element.54), channel_id=1, source_target_pairs={{0,2},{1,3},{2,4},{3,5},{4,6},{5,7},{6,8},{7,9},{8,10},{9,11},{10,... | collective-permute-start | bytes 393224 | tf_op jit(solution)/shard_map/ppermute | solution.py:414
  107.9 6.2 %collective-permute-start.22 = (bf16[256,256]{1,0:T(8,128)(2,1)S(1)}, bf16[256,256]{1,0:T(8,128)(2,1)S(1)}, u32[]{:S(2)}, u32[]{:S(2)}) collective-permute-start(bf16[256,256]{1,0:T(8,128)(2,1)S(1)} %get-tuple-element.55), channel_id=1, source_target_pairs={{0,2},{1,3},{2,4},{3,5},{4,6},{5,7},{6,8},{7,9},{8,10},{9,11},{10,... | collective-permute-start | bytes 393224 | tf_op jit(solution)/shard_map/ppermute | solution.py:414
  114.3 5.0 %collective-permute-start.30 = (bf16[256,256]{1,0:T(8,128)(2,1)S(1)}, bf16[256,256]{1,0:T(8,128)(2,1)S(1)}, u32[]{:S(2)}, u32[]{:S(2)}) collective-permute-start(bf16[256,256]{1,0:T(8,128)(2,1)S(1)} %get-tuple-element.49), channel_id=1, source_target_pairs={{0,14},{1,15},{2,0},{3,1},{4,2},{5,3},{6,4},{7,5},{8,6},{9,7},{10,... | collective-permute-start | bytes 393224 | tf_op jit(solution)/shard_map/ppermute | solution.py:414
  114.7 6.2 %collective-permute-start.27 = (bf16[256,256]{1,0:T(8,128)(2,1)S(1)}, bf16[256,256]{1,0:T(8,128)(2,1)S(1)}, u32[]{:S(2)}, u32[]{:S(2)}) collective-permute-start(bf16[256,256]{1,0:T(8,128)(2,1)S(1)} %get-tuple-element.50), channel_id=1, source_target_pairs={{0,2},{1,3},{2,4},{3,5},{4,6},{5,7},{6,8},{7,9},{8,10},{9,11},{10,... | collective-permute-start | bytes 393224 | tf_op jit(solution)/shard_map/ppermute | solution.py:414
  116.4 5.0 %collective-permute-start.20 = (bf16[256,256]{1,0:T(8,128)(2,1)S(1)}, bf16[256,256]{1,0:T(8,128)(2,1)S(1)}, u32[]{:S(2)}, u32[]{:S(2)}) collective-permute-start(bf16[256,256]{1,0:T(8,128)(2,1)S(1)} %get-tuple-element.48), channel_id=1, source_target_pairs={{0,14},{1,15},{2,0},{3,1},{4,2},{5,3},{6,4},{7,5},{8,6},{9,7},{10,... | collective-permute-start | bytes 393224 | tf_op jit(solution)/shard_map/ppermute | solution.py:414
  118.0 6.2 %collective-permute-start.23 = (bf16[256,256]{1,0:T(8,128)(2,1)S(1)}, bf16[256,256]{1,0:T(8,128)(2,1)S(1)}, u32[]{:S(2)}, u32[]{:S(2)}) collective-permute-start(bf16[256,256]{1,0:T(8,128)(2,1)S(1)} %get-tuple-element.51), channel_id=1, source_target_pairs={{0,2},{1,3},{2,4},{3,5},{4,6},{5,7},{6,8},{7,9},{8,10},{9,11},{10,... | collective-permute-start | bytes 393224 | tf_op jit(solution)/shard_map/ppermute | solution.py:414
  121.0 5.1 %collective-permute-start.31 = (bf16[256,256]{1,0:T(8,128)(2,1)S(1)}, bf16[256,256]{1,0:T(8,128)(2,1)S(1)}, u32[]{:S(2)}, u32[]{:S(2)}) collective-permute-start(bf16[256,256]{1,0:T(8,128)(2,1)S(1)} %fusion.6), channel_id=1, source_target_pairs={{0,16},{1,17},{2,18},{3,19},{4,20},{5,21},{6,22},{7,23},{8,24},{9,... | collective-permute-start | bytes 393224 | tf_op jit(solution)/shard_map/ppermute | solution.py:440

commit v4 on v3

--- a/solution.py
+++ b/solution.py
@@ -148,48 +148,69 @@
     )(rates, gains, taps)
 
 
-def project_kernel(parts, first, last, *refs):
-    row_refs, refs = refs[: len(parts)], refs[len(parts) :]
-    weight_ref, refs = refs[0], refs[1:]
-    out_ref, held_ref, sems = refs[-3:]
+def project_kernel(part, first, ready, ahead, *refs):
+    row_ref, weight_ref, refs = refs[0], refs[1], refs[2:]
+    sum_ref, refs = (None, refs) if first else (refs[0], refs[1:])
+    out_ref, refs = refs[0], refs[1:]
+
+    def fetch(part, target, sem):
+        c, x = place_of("core") ^ (part // 2), place_of("x") ^ (part % 2)
+        copy = pltpu.make_async_copy(weight_ref.at[:, x, :, c], target, sem)
+        copy.start()
+        return copy
+
     copies = []
-    for n, part in enumerate(parts):
-        c, x = place_of("core") ^ (part // 2), place_of("x") ^ (part % 2)
-        copies.append(pltpu.make_async_copy(weight_ref.at[:, x, :, c], held_ref.at[n], sems.at[n]))
-        copies[n].start()
+    held = weight_ref
+    if not ready:
+        held, sems = refs[-2:]
+        copies = [fetch(part, held, sems.at[0])]
+        copies += [fetch(later, refs[n], sems.at[n + 1]) for n, later in enumerate(ahead)]
+        copies[0].wait()
     total = tuple(
-        jnp.zeros((SHARE, BLOCK), F32) if first else refs[0][:, s * BLOCK : (s + 1) * BLOCK] for s in range(3)
+        jnp.zeros((SHARE, BLOCK), F32) if first else sum_ref[:, s * BLOCK : (s + 1) * BLOCK] for s in range(3)
     )
-    for n, row_ref in enumerate(row_refs):
-        copies[n].wait()
-
-        def add_block(z, total):
-            rows = row_ref[z]
-            return tuple(total[s] + nn(rows, held_ref[n, s, z]) for s in range(3))
-
-        total = lax.fori_loop(0, N_Z, add_block, total, unroll=2)
+
+    def add_block(z, total):
+        rows = row_ref[z]
+        return tuple(total[s] + nn(rows, held[s, z]) for s in range(3))
+
+    total = lax.fori_loop(0, N_Z, add_block, total, unroll=2)
     for s in range(3):
-        out_ref[:, s * BLOCK : (s + 1) * BLOCK] = total[s].astype(BF16 if last else F32)
-
-
-def project(parts, rows, weight, sums, last):
+        out_ref[:, s * BLOCK : (s + 1) * BLOCK] = total[s].astype(out_ref.dtype)
+    for copy in copies[1:]:
+        copy.wait()
+
+
+def project(part, rows, weight, sums=None, ready=False, ahead=(), last=False):
     vmem = pl.BlockSpec(memory_space=pltpu.VMEM)
-    first = sums is None
+    result = jax.ShapeDtypeStruct((SHARE, 3 * BLOCK), BF16 if last else F32)
+    block = (3, N_Z, BLOCK, BLOCK)
+    scratch = [pltpu.VMEM(block, BF16), pltpu.SemaphoreType.DMA((1 + len(ahead),))]
+    earlier = [] if sums is None else [sums]
     return pl.pallas_call(
-        functools.partial(project_kernel, parts, first, last),
-        out_shape=jax.ShapeDtypeStruct((SHARE, 3 * BLOCK), BF16 if last else F32),
-        in_specs=[vmem] * len(parts) + [pl.BlockSpec(memory_space=pltpu.HBM)] + [vmem] * (not first),
-        out_specs=vmem,
-        scratch_shapes=[
-            pltpu.VMEM((len(parts), 3, N_Z, BLOCK, BLOCK), BF16),
-            pltpu.SemaphoreType.DMA((len(parts),)),
-        ],
-        compiler_params=pltpu.CompilerParams(vmem_limit_bytes=50 << 20),
+        functools.partial(project_kernel, part, sums is None, ready, ahead),
+        out_shape=(result,) + (jax.ShapeDtypeStruct(block, BF16),) * len(ahead),
+        in_specs=[vmem, vmem if ready else pl.BlockSpec(memory_space=pltpu.HBM)] + [vmem] * len(earlier),
+        out_specs=(vmem,) * (1 + len(ahead)),
+        scratch_shapes=[] if ready else scratch,
+        compiler_params=pltpu.CompilerParams(vmem_limit_bytes=(4 if ready else 46) << 20),
         cost_estimate=pl.CostEstimate(
-            flops=2 * 64 * 768 * 2048 * len(parts), bytes_accessed=len(parts) * (3 << 20), transcendentals=0
+            flops=2 * 64 * 768 * 2048, bytes_accessed=(1 + len(ahead)) * (3 << 20), transcendentals=0
         ),
         name="project",
-    )(*rows, weight, *([] if first else [sums]))
+    )(rows, weight, *earlier)
+
+
+def back_step(n, held_ref, grad_ref, own_ref, other_ref):
+    for core in (1, 0):
+        target = other_ref if core else own_ref
+        c = place_of("core") ^ core
+        for shift in range(2):
+            x = place_of("x") ^ shift
+            total = nn(held_ref[n, 0, x, c], grad_ref[0:BLOCK])
+            total += nn(held_ref[n, 1, x, c], grad_ref[BLOCK : 2 * BLOCK])
+            total += nn(held_ref[n, 2, x, c], grad_ref[2 * BLOCK :])
+            target[n, shift] = total.astype(BF16)
 
 
 def source_of(own, n):
@@ -199,44 +220,58 @@
 def mixer_kernel(*refs):
     own = lax.axis_index("ctx")
     table_refs, refs = refs[:N_CTX], refs[N_CTX:]
-    sources, refs = refs[:6], refs[6:]
-    row_ref, tap_ref, out_ref, grad_proj_ref, raw_ref = refs[:5]
-    grad_ref, side_ref, fwd_ref, sems = refs[5:]
+    sources, refs = refs[:7], refs[7:]
+    row_ref, tap_ref, out_ref, grad_proj_ref, own_ref, other_ref = refs[:6]
+    raw_ref, tapped_ref, id_ref, grad_ref, side_ref, fwd_ref, weight_ref, sems = refs[6:]
     copies = []
     for n in range(N_CTX):
         target = grad_ref.at[source_of(own, n)]
         copies.append(pltpu.make_async_copy(sources[n // 2].at[n % 2], target, sems.at[n]))
     copies.append(pltpu.make_async_copy(sources[4], side_ref, sems.at[N_CTX]))
     copies.append(pltpu.make_async_copy(sources[5], fwd_ref, sems.at[N_CTX + 1]))
+    far_z = (place_of("z") + N_Z // 2) & (N_Z - 1)
+    copies.append(pltpu.make_async_copy(sources[6].at[:, :, far_z], weight_ref.at[0], sems.at[N_CTX + 2]))
     for copy in copies:
         copy.start()
     table = jnp.concatenate([ref[...].astype(F32) for ref in table_refs], axis=0).T.astype(BF16)
     share_row = lax.broadcasted_iota(jnp.int32, (SHARE, BLOCK), 0)
     vocab = jnp.concatenate([share_row + source_of(own, n) * SHARE for n in range(N_CTX)], axis=0)
-
-    edge = jnp.zeros((3 * BLOCK, HALO), F32)
-    raw_ref[:, :HALO] = edge
-    raw_ref[:, HALO + WINDOW :] = edge
-
-    def look_up(block, carried):
+    table = jnp.concatenate([ref[...].astype(F32) for ref in table_refs], axis=0).T
+    for tap in range(3):
+        tapped_ref[:, tap * VOCAB : (tap + 1) * VOCAB] = (tap_ref[:, tap : tap + 1] * table).astype(BF16)
+    table = table.astype(BF16)
+
+    for copy in copies[:N_CTX]:
+        copy.wait()
+    edge = jnp.full((1, HALO), -1, jnp.int32)
+    id_ref[:, :HALO] = edge
+    id_ref[:, HALO + WINDOW :] = edge
+    for block in range(N_CTX):
         ids = grad_ref[block, BLOCK : BLOCK + EXTRA, :].astype(F32)
         ids = (ids[0:1] * 256.0 + ids[1:2]).astype(jnp.int32)
-        one_hot = jnp.where(ids == vocab, 1.0, 0.0).astype(BF16)
-        raw_ref[:, pl.ds(pl.multiple_of(HALO + block * BLOCK, HALO), BLOCK)] = nn(table, one_hot)
-        return carried
-
-    for copy in copies[:N_CTX]:
-        copy.wait()
-    lax.fori_loop(0, N_CTX, look_up, 0)
+        id_ref[:, HALO + block * BLOCK : HALO + (block + 1) * BLOCK] = ids
     copies[N_CTX].wait()
 
-    def featured(stream, block, width):
-        rows = pl.ds(stream * BLOCK, BLOCK)
-        begin = pl.multiple_of(block * BLOCK, BLOCK)
-        raw = raw_ref[rows, pl.ds(begin, HALO + width)]
+    def one_hot(ids):
+        return jnp.where(ids == vocab, 1.0, 0.0).astype(BF16)
+
+    def far_lookup(block):
+        ids = id_ref[:, pl.ds(pl.multiple_of(block * BLOCK, BLOCK), HALO + BLOCK)]
+        return jnp.concatenate([one_hot(ids[:, HALO - tap : HALO - tap + BLOCK]) for tap in range(3)], axis=0)
+
+    def far_features(stream, picks):
+        return nn(tapped_ref[stream * BLOCK : (stream + 1) * BLOCK, :], picks)
+
+    for half in range(2):
+        begin = pl.multiple_of(own * BLOCK + half * BLOCK, BLOCK)
+        raw_ref[:, half * BLOCK : (half + 1) * BLOCK] = nn(table, one_hot(id_ref[:, pl.ds(begin, BLOCK)]))
+
+    def featured(stream):
+        rows = slice(stream * BLOCK, (stream + 1) * BLOCK)
+        raw = raw_ref[rows, :]
         total = tap_ref[rows, 0:1] * raw[:, HALO:]
         for tap in (1, 2):
-            total += tap_ref[rows, tap : tap + 1] * raw[:, HALO - tap : HALO - tap + width]
+            total += tap_ref[rows, tap : tap + 1] * raw[:, HALO - tap : 2 * BLOCK - tap]
         return total
 
     rate_row = row_ref[0:1]
@@ -247,12 +282,13 @@
     )
 
     def earlier(block, state):
-        mixed = featured(1, block, BLOCK) * featured(2, block, BLOCK)
+        picks = far_lookup(block)
+        mixed = far_features(1, picks) * far_features(2, picks)
         return block_decay * state + nt(mixed.astype(BF16), side_ref[:, END])
 
     def later(step, state):
         block = N_CTX - 1 - step
-        grad = grad_ref[block, 0:BLOCK, :].astype(F32) * featured(0, block, BLOCK)
+        grad = grad_ref[block, 0:BLOCK, :].astype(F32) * far_features(0, far_lookup(block))
         return block_decay * state + nt(grad.astype(BF16), side_ref[:, BEGIN])
 
     zero = jnp.zeros((BLOCK, BLOCK), F32)
@@ -260,9 +296,7 @@
     after = lax.fori_loop(0, N_CTX - 1 - own, later, zero)
 
     wide = BLOCK + HALO
-    query = featured(0, own, wide)
-    key = featured(1, own, wide)
-    value = featured(2, own, wide)
+    query, key, value = featured(0), featured(1), featured(2)
     mixed = key * value
     following = jnp.minimum(own + 1, N_CTX - 1)
     grad_rows = jnp.concatenate(
@@ -310,9 +344,11 @@
         for tap in (1, 2):
             total += tap_ref[rows, tap : tap + 1] * grads[:, tap : tap + BLOCK]
         grad_proj_ref[rows, :] = total.astype(BF16)
-
-
-def mix(pieces, grads, tables):
+    copies[N_CTX + 2].wait()
+    back_step(0, weight_ref, grad_proj_ref, own_ref, other_ref)
+
+
+def mix(pieces, grads, tables, weight):
     fwd, side, row, taps = tables
     vmem = pl.BlockSpec(memory_space=pltpu.VMEM)
     return pl.pallas_call(
@@ -320,20 +356,25 @@
         out_shape=(
             jax.ShapeDtypeStruct((BLOCK, BLOCK), BF16),
             jax.ShapeDtypeStruct((3 * BLOCK, BLOCK), BF16),
+            jax.ShapeDtypeStruct((1, 2, BLOCK, BLOCK), BF16),
+            jax.ShapeDtypeStruct((1, 2, BLOCK, BLOCK), BF16),
         ),
-        in_specs=[vmem] * N_CTX + [pl.BlockSpec(memory_space=pl.ANY)] * 6 + [vmem] * 2,
-        out_specs=(vmem, vmem),
+        in_specs=[vmem] * N_CTX + [pl.BlockSpec(memory_space=pl.ANY)] * 7 + [vmem] * 2,
+        out_specs=(vmem,) * 4,
         scratch_shapes=[
-            pltpu.VMEM((3 * BLOCK, WINDOW + 2 * HALO), F32),
+            pltpu.VMEM((3 * BLOCK, 2 * BLOCK), F32),
+            pltpu.VMEM((3 * BLOCK, 3 * VOCAB), BF16),
+            pltpu.VMEM((1, WINDOW + 2 * HALO), jnp.int32),
             pltpu.VMEM((N_CTX, BLOCK + EXTRA, BLOCK), BF16),
             pltpu.VMEM((BLOCK, SIDE), BF16),
             pltpu.VMEM((GROUPS, BLOCK, BLOCK), BF16),
-            pltpu.SemaphoreType.DMA((N_CTX + 2,)),
+            pltpu.VMEM((1, 3, 2, 2, BLOCK, BLOCK), BF16),
+            pltpu.SemaphoreType.DMA((N_CTX + 3,)),
         ],
-        compiler_params=pltpu.CompilerParams(vmem_limit_bytes=50 << 20),
+        compiler_params=pltpu.CompilerParams(vmem_limit_bytes=47 << 20),
         cost_estimate=pl.CostEstimate(flops=3 << 30, bytes_accessed=8 << 20, transcendentals=1 << 16),
         name="mixer",
-    )(*pieces, *grads, side, fwd, row, taps)
+    )(*pieces, *grads, side, fwd, weight, row, taps)
 
 
 def back_kernel(step_ref, grad_ref, weight_ref, own_ref, other_ref, held_ref, sems):
@@ -348,15 +389,7 @@
 
     def one_step(n, carried):
         copy(n).wait()
-        for core in (1, 0):
-            target = other_ref if core else own_ref
-            c = place_of("core") ^ core
-            for shift in range(2):
-                x = place_of("x") ^ shift
-                total = nn(held_ref[n, 0, x, c], grad_ref[0:BLOCK])
-                total += nn(held_ref[n, 1, x, c], grad_ref[BLOCK : 2 * BLOCK])
-                total += nn(held_ref[n, 2, x, c], grad_ref[2 * BLOCK :])
-                target[n, shift] = total.astype(BF16)
+        back_step(n, held_ref, grad_ref, own_ref, other_ref)
         return carried
 
     lax.fori_loop(0, count, one_step, 0)
@@ -383,18 +416,21 @@
     )(jnp.asarray(steps, jnp.int32), grad_proj, weight)
 
 
-def project_features(rows, weight, tables):
+def project_features(rows, weight, pair):
     held = lax.all_to_all(
         jnp.broadcast_to(rows[None], (N_Z,) + rows.shape), "chan", 0, 0, axis_index_groups=Z_GROUPS
     )
-    held, tables = lax.optimization_barrier((held, tables))
+    held, pair = lax.optimization_barrier((held, pair))
     beside = lax.ppermute(held, "chan", X_SWAP)
     across = lax.ppermute(held, "chan", CORE_SWAP)
-    sums = project((0,), (held,), weight, None, False)
+    sums, weight_beside, weight_both = project(0, held, weight, ahead=(1, 3))
+    (sums,) = project(2, across, weight, sums)
     beside, sums = lax.optimization_barrier((beside, sums))
     both = lax.ppermute(beside, "chan", CORE_SWAP)
-    sums = project((2, 1), (across, beside), weight, sums, False)
-    return project((3,), (both,), weight, sums, True), tables
+    (sums,) = project(1, beside, weight_beside, sums, ready=True)
+    both, sums = lax.optimization_barrier((both, sums))
+    (part,) = project(3, both, weight_both, sums, ready=True, last=True)
+    return part, pair
 
 
 def gather_ctx(value):
@@ -405,38 +441,65 @@
     return [found[n] for n in (0, 1, 2, 5, 3, 6, 4, 7)]
 
 
-def gather_ctx_staged(value):
-    pair = jnp.stack([value, lax.ppermute(value, "ctx", X_HALF_SWAP)])
+def pair_ctx(value):
+    return jnp.stack([value, lax.ppermute(value, "ctx", X_HALF_SWAP)])
+
+
+def gather_pairs(pair):
     return [pair] + [lax.ppermute(pair, "ctx", y_shift(by)) for by in Y_STEPS]
 
 
 def moved(value, by):
-    return lax.ppermute(value.astype(BF16), "chan", z_shift(by)).astype(F32)
-
-
-def reduce_chan(grad_proj, weight):
+    return lax.ppermute(value.astype(BF16), "chan", z_shift(by))
+
+
+def reduce_chan(far_parts, grad_proj, weight):
     terms = {}
 
-    def add_terms(grad_proj, steps):
-        own, other = back_project(grad_proj, weight, steps)
-        swapped = lax.ppermute(other, "chan", CORE_SWAP)
+    def swap(parts):
+        return parts[0], lax.ppermute(parts[1], "chan", CORE_SWAP)
+
+    def add_terms(steps, own, swapped):
         for n, step in enumerate(steps):
             for half in range(2):
                 terms[step, half] = own[n, half].astype(F32) + swapped[n, half].astype(F32)
 
-    add_terms(grad_proj, (4,))
-    add_terms(grad_proj, (3, 5))
-    far = [terms[4, half].astype(BF16) for half in range(2)]
-    far, grad_proj = lax.optimization_barrier((far, grad_proj))
-    add_terms(grad_proj, (2, 6, 1, 7, 0))
-    totals = []
-    for half, long, short in ((1, 1, -1), (0, -1, 1)):
-        chain = {long: moved(far[half], long) + terms[(4 - long) % 8, half], short: terms[(4 - short) % 8, half]}
-        for hop in (2, 1):
-            for by in (long, short):
-                chain[by] = moved(chain[by], by) + terms[(by * hop) % 8, half]
-        totals.append(terms[0, half] + moved(chain[long], long) + moved(chain[short], short))
-    far_half, near_half = totals
+    def arrive(values, tied):
+        values, tied = lax.optimization_barrier((values, tied))
+        return values, tied
+
+    def send(values):
+        return {(half, by): moved(value, by) for (half, by), value in values.items()}
+
+    own, swapped = swap(far_parts)
+    near = back_project(grad_proj, weight, (3, 5))
+    (swapped, near) = lax.optimization_barrier((swapped, near))
+    add_terms((4,), own, swapped)
+    ways = {1: (1, -1), 0: (-1, 1)}
+    chain = send({(half, ways[half][0]): terms[4, half] for half in (1, 0)})
+    grad_proj, near = lax.optimization_barrier((grad_proj, near))
+    near_own, near_swapped = swap(near)
+    middle = back_project(grad_proj, weight, (2, 6))
+    arrived, middle = arrive(chain, middle)
+    add_terms((3, 5), near_own, near_swapped)
+    middle_own, middle_swapped = swap(middle)
+    chain = {}
+    for half in (1, 0):
+        long, short = ways[half]
+        chain[half, long] = terms[(3 * long) % 8, half] + arrived[half, long].astype(F32)
+        chain[half, short] = terms[(3 * short) % 8, half]
+    chain = send(chain)
+    grad_proj, middle_own = lax.optimization_barrier((grad_proj, middle_own))
+    last = back_project(grad_proj, weight, (1, 7, 0))
+    arrived, last = arrive(chain, last)
+    add_terms((2, 6), middle_own, middle_swapped)
+    last_own, last_swapped = swap(last)
+    chain = send({(half, by): value.astype(F32) + terms[(2 * by) % 8, half] for (half, by), value in arrived.items()})
+    add_terms((1, 7, 0), last_own, last_swapped)
+    chain = send({(half, by): value.astype(F32) + terms[by % 8, half] for (half, by), value in chain.items()})
+    far_half, near_half = (
+        terms[0, half] + chain[half, 1].astype(F32) + chain[half, -1].astype(F32) for half in (1, 0)
+    )
     total = near_half + lax.ppermute(far_half.astype(BF16), "chan", X_SWAP).astype(F32)
     return total.astype(BF16)
 
@@ -444,12 +507,15 @@
 def body(token_ids, embed_table, in_weight, feat_taps, modal_rates, modal_residues, out_grad):
     weight = in_weight.transpose(1, 0, 2).reshape(3, 2, N_Z, 2, BLOCK, BLOCK)
     own_vocab = lax.dynamic_slice_in_dim(embed_table, lax.axis_index("ctx") * SHARE, SHARE, 0)
-    grads = gather_ctx_staged(make_payload(out_grad, token_ids))
+    pair = pair_ctx(make_payload(out_grad, token_ids))
+    part, pair = project_features(own_vocab, weight, pair)
+    grads = gather_pairs(pair)
+    modal_rates, part = lax.optimization_barrier((modal_rates, part))
+    pieces = gather_ctx(part)
     gains = modal_residues * jnp.sqrt(-jnp.expm1(-2.0 * modal_rates))
     tables = make_tables(modal_rates, gains, feat_taps)
-    part, tables = project_features(own_vocab, weight, tables)
-    output, grad_proj = mix(gather_ctx(part), grads, tables)
-    return (output, reduce_chan(grad_proj, weight).T)
+    output, grad_proj, *far_parts = mix(pieces, grads, tables, weight)
+    return (output, reduce_chan(far_parts, grad_proj, weight).T)
 
 
 def solution(mesh):

time: 127 us -> 117 us (0.921); the launches traced: 127 us -> 115 us
  waiting for transfers between devices: 35.4 us -> 17.5 us
  starting transfers between devices: 44.7 us -> 54.8 us
  Pallas kernels: 39.2 us -> 37.1 us
    ppermute x21 -> x22, waiting for transfers between devices: 24.8 us -> 11 us  [the longest x14 6.87 us: moved(): return lax.ppermute(value.astype(BF16), 'chan', z_shift(by))]
    ppermute x6, starting transfers between devices: 8.64 us -> 12.4 us  [gather_ctx(): found += [lax.ppermute(piece, 'ctx', y_shift(by)) for by in Y_STEPS]]
    ppermute x21 -> x22, starting transfers between devices: 24.7 us -> 27.8 us  [the longest x14 20.6 us: moved(): return lax.ppermute(value.astype(BF16), 'chan', z_shift(by))]
    ppermute x6, waiting for transfers between devices: 2.85 us -> 0.08 us  [gather_ctx(): found += [lax.ppermute(piece, 'ctx', y_shift(by)) for by in Y_STEPS]]
    ppermute x1, starting transfers between devices: 0.88 us -> 3.11 us  [gather_ctx(): across = lax.ppermute(value, 'ctx', X_HALF_SWAP)]
    ppermute x1, starting transfers between devices: 0.29 us -> 1.58 us  [reduce_chan(): lax.ppermute(far_half.astype(BF16), 'chan', X_SWAP).astype(F32)]
    unnamed x17 -> x19, local copies, waits for them, and re-layouts: 4.44 us -> 3.31 us
    pallas_call x3 -> x4, Pallas kernels: 10.1 us -> 8.97 us  [project(): pl.pallas_call(functools.partial(project_kernel, part, sums is None, read...]
  transfers between devices with their start and end apart: 33 -> 34, of which waited for: 21 -> 13; matrix products, arithmetic and copies ran while one was open for 1% -> 0% of each run, Pallas kernels for 14% -> 20%
where the time goes in v4:
time: 117 us; the launch traced here: 115 us
  starting transfers between devices  54.8 us (47%)
  Pallas kernels  37.1 us (32%)
  waiting for transfers between devices  17.5 us (15%)
  local copies, waits for them, and re-layouts  4.03 us (3%)
    ppermute x14, starting transfers between devices, moved(): return lax.ppermute(value.astype(BF16), 'chan', z_shift(by))  20.6 us
    pallas_call x1, Pallas kernels, mix(): pl.pallas_call(mixer_kernel, out_shape=(jax.ShapeDtypeStruct((BLOCK, BLOC...  14.1 us
    ppermute x6, starting transfers between devices, gather_ctx(): found += [lax.ppermute(piece, 'ctx', y_shift(by)) for by in Y_STEPS]  12.4 us
    pallas_call x3, Pallas kernels, back_project(): pl.pallas_call(back_kernel, out_shape=(part, part), in_specs=[pl.BlockSpe...  10 us
    pallas_call x4, Pallas kernels, project(): pl.pallas_call(functools.partial(project_kernel, part, sums is None, read...  8.97 us
    all_to_all x1, starting transfers between devices, project_features(): lax.all_to_all(jnp.broadcast_to(rows[None], (N_Z,) + rows.shape), 'chan',...  8.47 us
    ppermute x14, waiting for transfers between devices, moved(): return lax.ppermute(value.astype(BF16), 'chan', z_shift(by))  6.87 us
    pallas_call x1, Pallas kernels, make_tables(): pl.pallas_call(table_kernel, out_shape=(stack, side, rows, columns), in_s...  3.91 us
  transfers between devices with their start and end apart: 34, of which 13 were waited for; matrix products, arithmetic and copies ran while one was open for 0% of the time, Pallas kernels for 20%

profile of v4, /device:TPU:24, one launch (start us, length us, event | category | flops | bytes accessed | tf_op | source)
XLA Modules:
  0.0 115.3 jit_solution(16671184581875135582)
XLA Ops:
  0.6 0.9 copy-done
  1.6 0.7 broadcast_in_dim.2
  2.3 8.5 %all-to-all-start = ((bf16[8,64,256]{2,1,0:T(8,128)(2,1)}), bf16[8,64,256]{2,1,0:T(8,128)(2,1)S(1)}, u32[]{:S(2)}, u32[]{:S(2)}) async-start(bf16[8,64,256]{2,1,0:T(8,128)(2,1)} %broadcast_in_dim.2), calls=%async_computation | async-start | bytes 524288 | tf_op jit(solution)/shard_map/all_to_all | solution.py:420
  10.8 0.9 copy-done.1
  11.7 0.7 copy-done.3
  12.5 3.1 %collective-permute-start = (bf16[272,256]{1,0:T(8,128)(2,1)S(1)}, bf16[272,256]{1,0:T(8,128)(2,1)S(1)}, u32[]{:S(2)}, u32[]{:S(2)}) collective-permute-start(bf16[272,256]{1,0:T(8,128)(2,1)S(1)} %payload.1), channel_id=1, source_target_pairs={{0,32},{32,0},{64,96},{96,64},{128,160},{160,128},{192,224},{224,1... | collective-permute-start | bytes 417800 | tf_op jit(solution)/shard_map/ppermute | solution.py:445
  15.6 3.6 %collective-permute-done = bf16[272,256]{1,0:T(8,128)(2,1)S(1)} collective-permute-done((bf16[272,256]{1,0:T(8,128)(2,1)S(1)}, bf16[272,256]{1,0:T(8,128)(2,1)S(1)}, u32[]{:S(2)}, u32[]{:S(2)}) %collective-permute-start) | collective-permute-done | bytes 139296 | tf_op jit(solution)/shard_map/ppermute | solution.py:445
  19.2 3.4 %all-to-all-done.refs_0_ = bf16[8,64,256]{2,1,0:T(8,128)(2,1)S(1)} async-done(((bf16[8,64,256]{2,1,0:T(8,128)(2,1)}), bf16[8,64,256]{2,1,0:T(8,128)(2,1)S(1)}, u32[]{:S(2)}, u32[]{:S(2)}) %all-to-all-start) | async-done | bytes 262176 | tf_op jit(solution)/shard_map/all_to_all | solution.py:420
  22.7 1.5 %collective-permute-start.1 = (bf16[8,64,256]{2,1,0:T(8,128)(2,1)S(1)}, bf16[8,64,256]{2,1,0:T(8,128)(2,1)S(1)}, u32[]{:S(2)}, u32[]{:S(2)}) collective-permute-start(bf16[8,64,256]{2,1,0:T(8,128)(2,1)S(1)} %all-to-all-done.refs_0_), channel_id=1, source_target_pairs={{0,16},{1,17},{2,18},{3,19},{4,20},{5,21},{6,22},{7,23},{8,24},{9,... | collective-permute-start | bytes 786440 | tf_op jit(solution)/shard_map/ppermute | solution.py:424
  24.1 3.8 %project.4 = (f32[64,768]{1,0:T(8,128)S(1)}, bf16[3,8,256,256]{3,2,1,0:T(8,128)(2,1)S(1)}, bf16[3,8,256,256]{3,2,1,0:T(8,128)(2,1)S(1)}) custom-call(bf16[8,64,256]{2,1,0:T(8,128)(2,1)S(1)} %all-to-all-done.refs_0_, bf16[3,2,8,2,256,256]{5,4,3,2,1,0:T(8,128)(2,1)} %bitcast.74), custom_call_target="tpu_custom_call" | custom-call | flops 201326592 | bytes 9437184 | tf_op jit(solution)/shard_map/project/pallas_call | solution.py:190
  27.9 3.0 %project.5.refs_2_ = f32[64,768]{1,0:T(8,128)S(1)} custom-call(bf16[8,64,256]{2,1,0:T(8,128)(2,1)S(1)} %collective-permute-done.2.refs_0_, bf16[3,2,8,2,256,256]{5,4,3,2,1,0:T(8,128)(2,1)} %bitcast.75, f32[64,768]{1,0:T(8,128)S(1)} %get-tuple-element.46.refs_2_), custom_call_target="tpu_custom_call" | custom-call | flops 201326592 | bytes 3145728 | tf_op jit(solution)/shard_map/project/pallas_call | solution.py:190
  31.0 0.4 collective-permute-done.1.refs_0_
  31.4 0.2 collective-permute-start.11
  31.6 1.8 %collective-permute-start.12 = (bf16[2,272,256]{2,1,0:T(8,128)(2,1)S(1)}, bf16[2,272,256]{2,1,0:T(8,128)(2,1)S(1)}, u32[]{:S(2)}, u32[]{:S(2)}) collective-permute-start(bf16[2,272,256]{2,1,0:T(8,128)(2,1)S(1)} %pad_maximum_fusion.refs_8_), channel_id=1, source_target_pairs={{0,192},{32,224},{64,0},{96,32},{128,64},{160,96},{192,128},{224,1... | collective-permute-start | bytes 835592 | tf_op jit(solution)/shard_map/ppermute | solution.py:449
  33.4 1.2 %collective-permute-start.13 = (bf16[2,272,256]{2,1,0:T(8,128)(2,1)S(1)}, bf16[2,272,256]{2,1,0:T(8,128)(2,1)S(1)}, u32[]{:S(2)}, u32[]{:S(2)}) collective-permute-start(bf16[2,272,256]{2,1,0:T(8,128)(2,1)S(1)} %pad_maximum_fusion.refs_8_), channel_id=1, source_target_pairs={{0,128},{32,160},{64,192},{96,224},{128,0},{160,32},{192,64},{224,... | collective-permute-start | bytes 835592 | tf_op jit(solution)/shard_map/ppermute | solution.py:449
  34.6 1.1 project.6.refs_2_
  35.7 1.1 project.7.refs_0_
  36.8 3.1 %collective-permute-start.4 = (bf16[64,768]{1,0:T(8,128)(2,1)S(1)}, bf16[64,768]{1,0:T(8,128)(2,1)S(1)}, u32[]{:S(2)}, u32[]{:S(2)}) collective-permute-start(bf16[64,768]{1,0:T(8,128)(2,1)S(1)} %project.7.refs_0_), channel_id=1, source_target_pairs={{0,32},{32,0},{64,96},{96,64},{128,160},{160,128},{192,224},{224,1... | collective-permute-start | bytes 294920 | tf_op jit(solution)/shard_map/ppermute | solution.py:437
  40.0 2.2 %collective-permute-start.5 = (bf16[64,768]{1,0:T(8,128)(2,1)S(1)}, bf16[64,768]{1,0:T(8,128)(2,1)S(1)}, u32[]{:S(2)}, u32[]{:S(2)}) collective-permute-start(bf16[64,768]{1,0:T(8,128)(2,1)S(1)} %project.7.refs_0_), channel_id=1, source_target_pairs={{0,64},{32,96},{64,128},{96,160},{128,192},{160,224},{192,0},{224,... | collective-permute-start | bytes 294920 | tf_op jit(solution)/shard_map/ppermute | solution.py:440
  42.1 4.7 %collective-permute-start.7 = (bf16[64,768]{1,0:T(8,128)(2,1)S(1)}, bf16[64,768]{1,0:T(8,128)(2,1)S(1)}, u32[]{:S(2)}, u32[]{:S(2)}) collective-permute-start(bf16[64,768]{1,0:T(8,128)(2,1)S(1)} %project.7.refs_0_), channel_id=1, source_target_pairs={{0,192},{32,224},{64,0},{96,32},{128,64},{160,96},{192,128},{224,1... | collective-permute-start | bytes 294920 | tf_op jit(solution)/shard_map/ppermute | solution.py:440
  46.8 0.5 collective-permute-done.12.refs_10_
  47.3 3.5 %collective-permute-start.10 = (bf16[64,768]{1,0:T(8,128)(2,1)S(1)}, bf16[64,768]{1,0:T(8,128)(2,1)S(1)}, u32[]{:S(2)}, u32[]{:S(2)}) collective-permute-start(bf16[64,768]{1,0:T(8,128)(2,1)S(1)} %collective-permute-done.4.refs_1_), channel_id=1, source_target_pairs={{0,128},{32,160},{64,192},{96,224},{128,0},{160,32},{192,64},{224,... | collective-permute-start | bytes 294920 | tf_op jit(solution)/shard_map/ppermute | solution.py:440
  50.9 2.0 %collective-permute-start.8 = (bf16[64,768]{1,0:T(8,128)(2,1)S(1)}, bf16[64,768]{1,0:T(8,128)(2,1)S(1)}, u32[]{:S(2)}, u32[]{:S(2)}) collective-permute-start(bf16[64,768]{1,0:T(8,128)(2,1)S(1)} %collective-permute-done.4.refs_1_), channel_id=1, source_target_pairs={{0,192},{32,224},{64,0},{96,32},{128,64},{160,96},{192,128},{224,1... | collective-permute-start | bytes 294920 | tf_op jit(solution)/shard_map/ppermute | solution.py:440
  52.9 3.9 %filter_tables.1 = (bf16[16,256,256]{2,1,0:T(8,128)(2,1)S(1)}, bf16[256,1152]{1,0:T(8,128)(2,1)S(1)}, f32[2,256]{1,0:T(2,128)S(1)}, f32[768,3]{1,0:T(8,128)S(1)}) custom-call(f32[16,16]{1,0:T(8,128)S(1)} %copy-done.2, f32[16,16]{1,0:T(8,128)S(1)} %sqrt_multiply_fusion.gain_ref, f32[3,3,256]{2,1,0:T(4,128)S(1)} %copy-done.7), custom_call_target="tpu_custom_call" | custom-call | flops 402653184 | bytes 5242880 | tf_op jit(solution)/shard_map/filter_tables/pallas_call | solution.py:140
  57.0 14.1 %mixer.1 = (bf16[256,256]{1,0:T(8,128)(2,1)}, bf16[768,256]{1,0:T(8,128)(2,1)S(1)}, bf16[1,2,256,256]{3,2,1,0:T(8,128)(2,1)S(1)}, bf16[1,2,256,256]{3,2,1,0:T(8,128)(2,1)S(1)}) custom-call(bf16[64,768]{1,0:T(8,128)(2,1)S(1)} %project.7.refs_0_, bf16[64,768]{1,0:T(8,128)(2,1)S(1)} %collective-permute-done.4.refs_1_, ...), custom_call_target="tpu_custom_call" | custom-call | flops 3221225472 | bytes 8388608 | tf_op jit(solution)/shard_map/mixer/pallas_call | solution.py:354
  71.2 3.1 %back_project.3 = (bf16[2,2,256,256]{3,2,1,0:T(8,128)(2,1)S(1)}, bf16[2,2,256,256]{3,2,1,0:T(8,128)(2,1)S(1)}) custom-call(s32[2]{0:T(128)S(1)} %copy-done.6, bf16[768,256]{1,0:T(8,128)(2,1)S(1)} %get-tuple-element.77.grad_ref, bf16[3,2,8,2,256,256]{5,4,3,2,1,0:T(8,128)(2,1)} %bitcast.77), custom_call_target="tpu_custom_call" | custom-call | flops 805306368 | bytes 4194304 | tf_op jit(solution)/shard_map/back_project/pallas_call | solution.py:402
  74.4 0.6 collective-permute-start.15
  75.1 2.0 %collective-permute-start.17 = (bf16[256,256]{1,0:T(8,128)(2,1)S(1)}, bf16[256,256]{1,0:T(8,128)(2,1)S(1)}, u32[]{:S(2)}, u32[]{:S(2)}) collective-permute-start(bf16[256,256]{1,0:T(8,128)(2,1)S(1)} %get-tuple-element.102), channel_id=1, source_target_pairs={{0,2},{1,3},{2,4},{3,5},{4,6},{5,7},{6,8},{7,9},{8,10},{9,11},{10,... | collective-permute-start | bytes 393224 | tf_op jit(solution)/shard_map/ppermute | solution.py:453
  77.1 3.1 %back_project.4 = (bf16[2,2,256,256]{3,2,1,0:T(8,128)(2,1)S(1)}, bf16[2,2,256,256]{3,2,1,0:T(8,128)(2,1)S(1)}) custom-call(s32[2]{0:T(128)S(1)} %copy-done.5, bf16[768,256]{1,0:T(8,128)(2,1)S(1)} %get-tuple-element.77.grad_ref, bf16[3,2,8,2,256,256]{5,4,3,2,1,0:T(8,128)(2,1)} %bitcast.78), custom_call_target="tpu_custom_call" | custom-call | flops 805306368 | bytes 4194304 | tf_op jit(solution)/shard_map/back_project/pallas_call | solution.py:402
  80.3 0.3 collective-permute-done.16
  80.5 1.5 %collective-permute-done.17 = bf16[256,256]{1,0:T(8,128)(2,1)S(1)} collective-permute-done((bf16[256,256]{1,0:T(8,128)(2,1)S(1)}, bf16[256,256]{1,0:T(8,128)(2,1)S(1)}, u32[]{:S(2)}, u32[]{:S(2)}) %collective-permute-start.17) | collective-permute-done | bytes 131104 | tf_op jit(solution)/shard_map/ppermute | solution.py:453
  82.1 0.3 collective-permute-start.19
  82.4 3.0 %collective-permute-start.20 = (bf16[256,256]{1,0:T(8,128)(2,1)S(1)}, bf16[256,256]{1,0:T(8,128)(2,1)S(1)}, u32[]{:S(2)}, u32[]{:S(2)}) collective-permute-start(bf16[256,256]{1,0:T(8,128)(2,1)S(1)} %get-tuple-element.100), channel_id=1, source_target_pairs={{0,14},{1,15},{2,0},{3,1},{4,2},{5,3},{6,4},{7,5},{8,6},{9,7},{10,... | collective-permute-start | bytes 393224 | tf_op jit(solution)/shard_map/ppermute | solution.py:453
  85.7 2.0 %collective-permute-start.21 = (bf16[256,256]{1,0:T(8,128)(2,1)S(1)}, bf16[256,256]{1,0:T(8,128)(2,1)S(1)}, u32[]{:S(2)}, u32[]{:S(2)}) collective-permute-start(bf16[256,256]{1,0:T(8,128)(2,1)S(1)} %get-tuple-element.98), channel_id=1, source_target_pairs={{0,2},{1,3},{2,4},{3,5},{4,6},{5,7},{6,8},{7,9},{8,10},{9,11},{10,... | collective-permute-start | bytes 393224 | tf_op jit(solution)/shard_map/ppermute | solution.py:453
  87.7 3.7 %back_project.5 = (bf16[3,2,256,256]{3,2,1,0:T(8,128)(2,1)S(1)}, bf16[3,2,256,256]{3,2,1,0:T(8,128)(2,1)S(1)}) custom-call(s32[3]{0:T(128)S(1)} %copy-done.4, bf16[768,256]{1,0:T(8,128)(2,1)S(1)} %get-tuple-element.77.grad_ref, bf16[3,2,8,2,256,256]{5,4,3,2,1,0:T(8,128)(2,1)} %bitcast.79), custom_call_target="tpu_custom_call" | custom-call | flops 1207959552 | bytes 6291456 | tf_op jit(solution)/shard_map/back_project/pallas_call | solution.py:402
  91.4 0.5 collective-permute-done.21
  92.3 0.7 collective-permute-start.24
  92.9 2.7 %collective-permute-start.26 = (bf16[256,256]{1,0:T(8,128)(2,1)S(1)}, bf16[256,256]{1,0:T(8,128)(2,1)S(1)}, u32[]{:S(2)}, u32[]{:S(2)}) collective-permute-start(bf16[256,256]{1,0:T(8,128)(2,1)S(1)} %get-tuple-element.97), channel_id=1, source_target_pairs={{0,14},{1,15},{2,0},{3,1},{4,2},{5,3},{6,4},{7,5},{8,6},{9,7},{10,... | collective-permute-start | bytes 393224 | tf_op jit(solution)/shard_map/ppermute | solution.py:453
  95.6 3.2 %collective-permute-start.30 = (bf16[256,256]{1,0:T(8,128)(2,1)S(1)}, bf16[256,256]{1,0:T(8,128)(2,1)S(1)}, u32[]{:S(2)}, u32[]{:S(2)}) collective-permute-start(bf16[256,256]{1,0:T(8,128)(2,1)S(1)} %get-tuple-element.95), channel_id=1, source_target_pairs={{0,14},{1,15},{2,0},{3,1},{4,2},{5,3},{6,4},{7,5},{8,6},{9,7},{10,... | collective-permute-start | bytes 393224 | tf_op jit(solution)/shard_map/ppermute | solution.py:453
  98.8 0.6 collective-permute-done.24
  99.4 2.7 %collective-permute-done.28 = bf16[256,256]{1,0:T(8,128)(2,1)S(1)} collective-permute-done((bf16[256,256]{1,0:T(8,128)(2,1)S(1)}, bf16[256,256]{1,0:T(8,128)(2,1)S(1)}, u32[]{:S(2)}, u32[]{:S(2)}) %collective-permute-start.28) | collective-permute-done | bytes 131104 | tf_op jit(solution)/shard_map/ppermute | solution.py:453
  102.4 3.2 %collective-permute-start.31 = (bf16[256,256]{1,0:T(8,128)(2,1)S(1)}, bf16[256,256]{1,0:T(8,128)(2,1)S(1)}, u32[]{:S(2)}, u32[]{:S(2)}) collective-permute-start(bf16[256,256]{1,0:T(8,128)(2,1)S(1)} %get-tuple-element.91), channel_id=1, source_target_pairs={{0,14},{1,15},{2,0},{3,1},{4,2},{5,3},{6,4},{7,5},{8,6},{9,7},{10,... | collective-permute-start | bytes 393224 | tf_op jit(solution)/shard_map/ppermute | solution.py:453
  105.7 3.2 %collective-permute-start.27 = (bf16[256,256]{1,0:T(8,128)(2,1)S(1)}, bf16[256,256]{1,0:T(8,128)(2,1)S(1)}, u32[]{:S(2)}, u32[]{:S(2)}) collective-permute-start(bf16[256,256]{1,0:T(8,128)(2,1)S(1)} %get-tuple-element.93), channel_id=1, source_target_pairs={{0,14},{1,15},{2,0},{3,1},{4,2},{5,3},{6,4},{7,5},{8,6},{9,7},{10,... | collective-permute-start | bytes 393224 | tf_op jit(solution)/shard_map/ppermute | solution.py:453
  108.9 0.4 collective-permute-done.29
  109.4 1.6 %collective-permute-start.32 = (bf16[256,256]{1,0:T(8,128)(2,1)S(1)}, bf16[256,256]{1,0:T(8,128)(2,1)S(1)}, u32[]{:S(2)}, u32[]{:S(2)}) collective-permute-start(bf16[256,256]{1,0:T(8,128)(2,1)S(1)} %fusion.5), channel_id=1, source_target_pairs={{0,16},{1,17},{2,18},{3,19},{4,20},{5,21},{6,22},{7,23},{8,24},{9,... | collective-permute-start | bytes 393224 | tf_op jit(solution)/shard_map/ppermute | solution.py:503
  110.9 0.9 collective-permute-done.25
  111.9 2.6 %collective-permute-done.32 = bf16[256,256]{1,0:T(8,128)(2,1)S(1)} collective-permute-done((bf16[256,256]{1,0:T(8,128)(2,1)S(1)}, bf16[256,256]{1,0:T(8,128)(2,1)S(1)}, u32[]{:S(2)}, u32[]{:S(2)}) %collective-permute-start.32) | collective-permute-done | bytes 131104 | tf_op jit(solution)/shard_map/ppermute | solution.py:503
  114.5 0.8 copy.12
  (60 shorter events, 1.6 us)
Async XLA Ops:
  0.6 1.0 copy-start
  2.3 20.3 %all-to-all-start = ((bf16[8,64,256]{2,1,0:T(8,128)(2,1)}), bf16[8,64,256]{2,1,0:T(8,128)(2,1)S(1)}, u32[]{:S(2)}, u32[]{:S(2)}) async-start(bf16[8,64,256]{2,1,0:T(8,128)(2,1)} %broadcast_in_dim.2), calls=%async_computation | async-start | bytes 524288 | tf_op jit(solution)/shard_map/all_to_all | solution.py:420
  10.8 0.9 copy-start.1
  11.7 0.7 copy-start.3
  12.5 6.7 %collective-permute-start = (bf16[272,256]{1,0:T(8,128)(2,1)S(1)}, bf16[272,256]{1,0:T(8,128)(2,1)S(1)}, u32[]{:S(2)}, u32[]{:S(2)}) collective-permute-start(bf16[272,256]{1,0:T(8,128)(2,1)S(1)} %payload.1), channel_id=1, source_target_pairs={{0,32},{32,0},{64,96},{96,64},{128,160},{160,128},{192,224},{224,1... | collective-permute-start | bytes 417800 | tf_op jit(solution)/shard_map/ppermute | solution.py:445
  22.6 5.3 %collective-permute-start.2 = (bf16[8,64,256]{2,1,0:T(8,128)(2,1)S(1)}, bf16[8,64,256]{2,1,0:T(8,128)(2,1)S(1)}, u32[]{:S(2)}, u32[]{:S(2)}) collective-permute-start(bf16[8,64,256]{2,1,0:T(8,128)(2,1)S(1)} %all-to-all-done.refs_0_), channel_id=1, source_target_pairs={{0,1},{1,0},{2,3},{3,2},{4,5},{5,4},{6,7},{7,6},{8,9},{9,8},{10,11... | collective-permute-start | bytes 786440 | tf_op jit(solution)/shard_map/ppermute | solution.py:425
  22.7 8.7 %collective-permute-start.1 = (bf16[8,64,256]{2,1,0:T(8,128)(2,1)S(1)}, bf16[8,64,256]{2,1,0:T(8,128)(2,1)S(1)}, u32[]{:S(2)}, u32[]{:S(2)}) collective-permute-start(bf16[8,64,256]{2,1,0:T(8,128)(2,1)S(1)} %all-to-all-done.refs_0_), channel_id=1, source_target_pairs={{0,16},{1,17},{2,18},{3,19},{4,20},{5,21},{6,22},{7,23},{8,24},{9,... | collective-permute-start | bytes 786440 | tf_op jit(solution)/shard_map/ppermute | solution.py:424
  31.4 4.4 %collective-permute-start.3 = (bf16[8,64,256]{2,1,0:T(8,128)(2,1)S(1)}, bf16[8,64,256]{2,1,0:T(8,128)(2,1)S(1)}, u32[]{:S(2)}, u32[]{:S(2)}) collective-permute-start(bf16[8,64,256]{2,1,0:T(8,128)(2,1)S(1)} %collective-permute-done.1.refs_0_), channel_id=1, source_target_pairs={{0,1},{1,0},{2,3},{3,2},{4,5},{5,4},{6,7},{7,6},{8,9},{9,8},{10,11... | collective-permute-start | bytes 786440 | tf_op jit(solution)/shard_map/ppermute | solution.py:429
  31.4 10.8 %collective-permute-start.11 = (bf16[2,272,256]{2,1,0:T(8,128)(2,1)S(1)}, bf16[2,272,256]{2,1,0:T(8,128)(2,1)S(1)}, u32[]{:S(2)}, u32[]{:S(2)}) collective-permute-start(bf16[2,272,256]{2,1,0:T(8,128)(2,1)S(1)} %pad_maximum_fusion.refs_8_), channel_id=1, source_target_pairs={{0,64},{32,96},{64,128},{96,160},{128,192},{160,224},{192,0},{224,... | collective-permute-start | bytes 835592 | tf_op jit(solution)/shard_map/ppermute | solution.py:449
  31.6 15.7 %collective-permute-start.12 = (bf16[2,272,256]{2,1,0:T(8,128)(2,1)S(1)}, bf16[2,272,256]{2,1,0:T(8,128)(2,1)S(1)}, u32[]{:S(2)}, u32[]{:S(2)}) collective-permute-start(bf16[2,272,256]{2,1,0:T(8,128)(2,1)S(1)} %pad_maximum_fusion.refs_8_), channel_id=1, source_target_pairs={{0,192},{32,224},{64,0},{96,32},{128,64},{160,96},{192,128},{224,1... | collective-permute-start | bytes 835592 | tf_op jit(solution)/shard_map/ppermute | solution.py:449
  33.4 17.5 %collective-permute-start.13 = (bf16[2,272,256]{2,1,0:T(8,128)(2,1)S(1)}, bf16[2,272,256]{2,1,0:T(8,128)(2,1)S(1)}, u32[]{:S(2)}, u32[]{:S(2)}) collective-permute-start(bf16[2,272,256]{2,1,0:T(8,128)(2,1)S(1)} %pad_maximum_fusion.refs_8_), channel_id=1, source_target_pairs={{0,128},{32,160},{64,192},{96,224},{128,0},{160,32},{192,64},{224,... | collective-permute-start | bytes 835592 | tf_op jit(solution)/shard_map/ppermute | solution.py:449
  34.6 18.3 %copy-start.2 = (f32[16,16]{1,0:T(8,128)S(1)}, f32[16,16]{1,0:T(8,128)}, u32[]{:S(2)}) copy-start(f32[16,16]{1,0:T(8,128)} %rate_ref) | copy-start | bytes 3076
  34.6 18.3 %copy-start.8 = (f32[16,16]{1,0:T(8,128)S(1)}, f32[16,16]{1,0:T(8,128)}, u32[]{:S(2)}) copy-start(f32[16,16]{1,0:T(8,128)} %param.15) | copy-start | bytes 3076
  34.6 18.3 %copy-start.7 = (f32[3,3,256]{2,1,0:T(4,128)S(1)}, f32[3,3,256]{2,1,0:T(4,128)}, u32[]{:S(2)}) copy-start(f32[3,3,256]{2,1,0:T(4,128)} %tap_ref.1) | copy-start | bytes 27652
  36.8 10.5 %collective-permute-start.4 = (bf16[64,768]{1,0:T(8,128)(2,1)S(1)}, bf16[64,768]{1,0:T(8,128)(2,1)S(1)}, u32[]{:S(2)}, u32[]{:S(2)}) collective-permute-start(bf16[64,768]{1,0:T(8,128)(2,1)S(1)} %project.7.refs_0_), channel_id=1, source_target_pairs={{0,32},{32,0},{64,96},{96,64},{128,160},{160,128},{192,224},{224,1... | collective-permute-start | bytes 294920 | tf_op jit(solution)/shard_map/ppermute | solution.py:437
  40.0 10.9 %collective-permute-start.5 = (bf16[64,768]{1,0:T(8,128)(2,1)S(1)}, bf16[64,768]{1,0:T(8,128)(2,1)S(1)}, u32[]{:S(2)}, u32[]{:S(2)}) collective-permute-start(bf16[64,768]{1,0:T(8,128)(2,1)S(1)} %project.7.refs_0_), channel_id=1, source_target_pairs={{0,64},{32,96},{64,128},{96,160},{128,192},{160,224},{192,0},{224,... | collective-permute-start | bytes 294920 | tf_op jit(solution)/shard_map/ppermute | solution.py:440
  42.1 14.7 %collective-permute-start.7 = (bf16[64,768]{1,0:T(8,128)(2,1)S(1)}, bf16[64,768]{1,0:T(8,128)(2,1)S(1)}, u32[]{:S(2)}, u32[]{:S(2)}) collective-permute-start(bf16[64,768]{1,0:T(8,128)(2,1)S(1)} %project.7.refs_0_), channel_id=1, source_target_pairs={{0,192},{32,224},{64,0},{96,32},{128,64},{160,96},{192,128},{224,1... | collective-permute-start | bytes 294920 | tf_op jit(solution)/shard_map/ppermute | solution.py:440
  47.3 9.5 %collective-permute-start.9 = (bf16[64,768]{1,0:T(8,128)(2,1)S(1)}, bf16[64,768]{1,0:T(8,128)(2,1)S(1)}, u32[]{:S(2)}, u32[]{:S(2)}) collective-permute-start(bf16[64,768]{1,0:T(8,128)(2,1)S(1)} %project.7.refs_0_), channel_id=1, source_target_pairs={{0,128},{32,160},{64,192},{96,224},{128,0},{160,32},{192,64},{224,... | collective-permute-start | bytes 294920 | tf_op jit(solution)/shard_map/ppermute | solution.py:440
  47.3 9.5 %collective-permute-start.10 = (bf16[64,768]{1,0:T(8,128)(2,1)S(1)}, bf16[64,768]{1,0:T(8,128)(2,1)S(1)}, u32[]{:S(2)}, u32[]{:S(2)}) collective-permute-start(bf16[64,768]{1,0:T(8,128)(2,1)S(1)} %collective-permute-done.4.refs_1_), channel_id=1, source_target_pairs={{0,128},{32,160},{64,192},{96,224},{128,0},{160,32},{192,64},{224,... | collective-permute-start | bytes 294920 | tf_op jit(solution)/shard_map/ppermute | solution.py:440
  50.9 6.0 %collective-permute-start.6 = (bf16[64,768]{1,0:T(8,128)(2,1)S(1)}, bf16[64,768]{1,0:T(8,128)(2,1)S(1)}, u32[]{:S(2)}, u32[]{:S(2)}) collective-permute-start(bf16[64,768]{1,0:T(8,128)(2,1)S(1)} %collective-permute-done.4.refs_1_), channel_id=1, source_target_pairs={{0,64},{32,96},{64,128},{96,160},{128,192},{160,224},{192,0},{224,... | collective-permute-start | bytes 294920 | tf_op jit(solution)/shard_map/ppermute | solution.py:440
  50.9 6.1 %collective-permute-start.8 = (bf16[64,768]{1,0:T(8,128)(2,1)S(1)}, bf16[64,768]{1,0:T(8,128)(2,1)S(1)}, u32[]{:S(2)}, u32[]{:S(2)}) collective-permute-start(bf16[64,768]{1,0:T(8,128)(2,1)S(1)} %collective-permute-done.4.refs_1_), channel_id=1, source_target_pairs={{0,192},{32,224},{64,0},{96,32},{128,64},{160,96},{192,128},{224,1... | collective-permute-start | bytes 294920 | tf_op jit(solution)/shard_map/ppermute | solution.py:440
  57.0 14.3 %copy-start.6 = (s32[2]{0:T(128)S(1)}, s32[2]{0:T(128)}, u32[]{:S(2)}) copy-start(s32[2]{0:T(128)} %constant.20.clone.step_ref) | copy-start | bytes 28
  71.1 3.3 %collective-permute-start.14 = (bf16[1,2,256,256]{3,2,1,0:T(8,128)(2,1)S(1)}, bf16[1,2,256,256]{3,2,1,0:T(8,128)(2,1)S(1)}, u32[]{:S(2)}, u32[]{:S(2)}) collective-permute-start(bf16[1,2,256,256]{3,2,1,0:T(8,128)(2,1)S(1)} %get-tuple-element.62), channel_id=1, source_target_pairs={{0,1},{1,0},{2,3},{3,2},{4,5},{5,4},{6,7},{7,6},{8,9},{9,8},{10,11... | collective-permute-start | bytes 786440 | tf_op jit(solution)/shard_map/ppermute | solution.py:460
  71.2 5.9 %copy-start.5 = (s32[2]{0:T(128)S(1)}, s32[2]{0:T(128)}, u32[]{:S(2)}) copy-start(s32[2]{0:T(128)} %constant.21.clone.step_ref) | copy-start | bytes 28
  74.4 7.7 %collective-permute-start.15 = (bf16[2,2,256,256]{3,2,1,0:T(8,128)(2,1)S(1)}, bf16[2,2,256,256]{3,2,1,0:T(8,128)(2,1)S(1)}, u32[]{:S(2)}, u32[]{:S(2)}) collective-permute-start(bf16[2,2,256,256]{3,2,1,0:T(8,128)(2,1)S(1)} %get-tuple-element.68), channel_id=1, source_target_pairs={{0,1},{1,0},{2,3},{3,2},{4,5},{5,4},{6,7},{7,6},{8,9},{9,8},{10,11... | collective-permute-start | bytes 1572872 | tf_op jit(solution)/shard_map/ppermute | solution.py:460
  75.0 5.5 %collective-permute-start.16 = (bf16[256,256]{1,0:T(8,128)(2,1)S(1)}, bf16[256,256]{1,0:T(8,128)(2,1)S(1)}, u32[]{:S(2)}, u32[]{:S(2)}) collective-permute-start(bf16[256,256]{1,0:T(8,128)(2,1)S(1)} %get-tuple-element.103), channel_id=1, source_target_pairs={{0,14},{1,15},{2,0},{3,1},{4,2},{5,3},{6,4},{7,5},{8,6},{9,7},{10,... | collective-permute-start | bytes 393224 | tf_op jit(solution)/shard_map/ppermute | solution.py:453
  75.1 12.6 %copy-start.4 = (s32[3]{0:T(128)S(1)}, s32[3]{0:T(128)}, u32[]{:S(2)}) copy-start(s32[3]{0:T(128)} %constant.22.clone.step_ref) | copy-start | bytes 40
  75.1 6.9 %collective-permute-start.17 = (bf16[256,256]{1,0:T(8,128)(2,1)S(1)}, bf16[256,256]{1,0:T(8,128)(2,1)S(1)}, u32[]{:S(2)}, u32[]{:S(2)}) collective-permute-start(bf16[256,256]{1,0:T(8,128)(2,1)S(1)} %get-tuple-element.102), channel_id=1, source_target_pairs={{0,2},{1,3},{2,4},{3,5},{4,6},{5,7},{6,8},{7,9},{8,10},{9,11},{10,... | collective-permute-start | bytes 393224 | tf_op jit(solution)/shard_map/ppermute | solution.py:453
  82.1 9.3 %collective-permute-start.19 = (bf16[256,256]{1,0:T(8,128)(2,1)S(1)}, bf16[256,256]{1,0:T(8,128)(2,1)S(1)}, u32[]{:S(2)}, u32[]{:S(2)}) collective-permute-start(bf16[256,256]{1,0:T(8,128)(2,1)S(1)} %get-tuple-element.101), channel_id=1, source_target_pairs={{0,2},{1,3},{2,4},{3,5},{4,6},{5,7},{6,8},{7,9},{8,10},{9,11},{10,... | collective-permute-start | bytes 393224 | tf_op jit(solution)/shard_map/ppermute | solution.py:453
  82.4 9.0 %collective-permute-start.20 = (bf16[256,256]{1,0:T(8,128)(2,1)S(1)}, bf16[256,256]{1,0:T(8,128)(2,1)S(1)}, u32[]{:S(2)}, u32[]{:S(2)}) collective-permute-start(bf16[256,256]{1,0:T(8,128)(2,1)S(1)} %get-tuple-element.100), channel_id=1, source_target_pairs={{0,14},{1,15},{2,0},{3,1},{4,2},{5,3},{6,4},{7,5},{8,6},{9,7},{10,... | collective-permute-start | bytes 393224 | tf_op jit(solution)/shard_map/ppermute | solution.py:453
  85.6 5.9 %collective-permute-start.18 = (bf16[256,256]{1,0:T(8,128)(2,1)S(1)}, bf16[256,256]{1,0:T(8,128)(2,1)S(1)}, u32[]{:S(2)}, u32[]{:S(2)}) collective-permute-start(bf16[256,256]{1,0:T(8,128)(2,1)S(1)} %get-tuple-element.99), channel_id=1, source_target_pairs={{0,14},{1,15},{2,0},{3,1},{4,2},{5,3},{6,4},{7,5},{8,6},{9,7},{10,... | collective-permute-start | bytes 393224 | tf_op jit(solution)/shard_map/ppermute | solution.py:453
  85.7 6.3 %collective-permute-start.21 = (bf16[256,256]{1,0:T(8,128)(2,1)S(1)}, bf16[256,256]{1,0:T(8,128)(2,1)S(1)}, u32[]{:S(2)}, u32[]{:S(2)}) collective-permute-start(bf16[256,256]{1,0:T(8,128)(2,1)S(1)} %get-tuple-element.98), channel_id=1, source_target_pairs={{0,2},{1,3},{2,4},{3,5},{4,6},{5,7},{6,8},{7,9},{8,10},{9,11},{10,... | collective-permute-start | bytes 393224 | tf_op jit(solution)/shard_map/ppermute | solution.py:453
  87.7 4.4 %collective-permute-start.23 = (bf16[2,2,256,256]{3,2,1,0:T(8,128)(2,1)S(1)}, bf16[2,2,256,256]{3,2,1,0:T(8,128)(2,1)S(1)}, u32[]{:S(2)}, u32[]{:S(2)}) collective-permute-start(bf16[2,2,256,256]{3,2,1,0:T(8,128)(2,1)S(1)} %get-tuple-element.84), channel_id=1, source_target_pairs={{0,1},{1,0},{2,3},{3,2},{4,5},{5,4},{6,7},{7,6},{8,9},{9,8},{10,11... | collective-permute-start | bytes 1572872 | tf_op jit(solution)/shard_map/ppermute | solution.py:460
  91.9 10.2 %collective-permute-start.22 = (bf16[3,2,256,256]{3,2,1,0:T(8,128)(2,1)S(1)}, bf16[3,2,256,256]{3,2,1,0:T(8,128)(2,1)S(1)}, u32[]{:S(2)}, u32[]{:S(2)}) collective-permute-start(bf16[3,2,256,256]{3,2,1,0:T(8,128)(2,1)S(1)} %get-tuple-element.81), channel_id=1, source_target_pairs={{0,1},{1,0},{2,3},{3,2},{4,5},{5,4},{6,7},{7,6},{8,9},{9,8},{10,11... | collective-permute-start | bytes 2359304 | tf_op jit(solution)/shard_map/ppermute | solution.py:460
  92.3 7.1 %collective-permute-start.24 = (bf16[256,256]{1,0:T(8,128)(2,1)S(1)}, bf16[256,256]{1,0:T(8,128)(2,1)S(1)}, u32[]{:S(2)}, u32[]{:S(2)}) collective-permute-start(bf16[256,256]{1,0:T(8,128)(2,1)S(1)} %get-tuple-element.94), channel_id=1, source_target_pairs={{0,2},{1,3},{2,4},{3,5},{4,6},{5,7},{6,8},{7,9},{8,10},{9,11},{10,... | collective-permute-start | bytes 393224 | tf_op jit(solution)/shard_map/ppermute | solution.py:453
  92.9 6.5 %collective-permute-start.26 = (bf16[256,256]{1,0:T(8,128)(2,1)S(1)}, bf16[256,256]{1,0:T(8,128)(2,1)S(1)}, u32[]{:S(2)}, u32[]{:S(2)}) collective-permute-start(bf16[256,256]{1,0:T(8,128)(2,1)S(1)} %get-tuple-element.97), channel_id=1, source_target_pairs={{0,14},{1,15},{2,0},{3,1},{4,2},{5,3},{6,4},{7,5},{8,6},{9,7},{10,... | collective-permute-start | bytes 393224 | tf_op jit(solution)/shard_map/ppermute | solution.py:453
  95.6 6.5 %collective-permute-start.28 = (bf16[256,256]{1,0:T(8,128)(2,1)S(1)}, bf16[256,256]{1,0:T(8,128)(2,1)S(1)}, u32[]{:S(2)}, u32[]{:S(2)}) collective-permute-start(bf16[256,256]{1,0:T(8,128)(2,1)S(1)} %get-tuple-element.96), channel_id=1, source_target_pairs={{0,2},{1,3},{2,4},{3,5},{4,6},{5,7},{6,8},{7,9},{8,10},{9,11},{10,... | collective-permute-start | bytes 393224 | tf_op jit(solution)/shard_map/ppermute | solution.py:453
  95.6 6.5 %collective-permute-start.30 = (bf16[256,256]{1,0:T(8,128)(2,1)S(1)}, bf16[256,256]{1,0:T(8,128)(2,1)S(1)}, u32[]{:S(2)}, u32[]{:S(2)}) collective-permute-start(bf16[256,256]{1,0:T(8,128)(2,1)S(1)} %get-tuple-element.95), channel_id=1, source_target_pairs={{0,14},{1,15},{2,0},{3,1},{4,2},{5,3},{6,4},{7,5},{8,6},{9,7},{10,... | collective-permute-start | bytes 393224 | tf_op jit(solution)/shard_map/ppermute | solution.py:453
  102.4 6.9 %collective-permute-start.29 = (bf16[256,256]{1,0:T(8,128)(2,1)S(1)}, bf16[256,256]{1,0:T(8,128)(2,1)S(1)}, u32[]{:S(2)}, u32[]{:S(2)}) collective-permute-start(bf16[256,256]{1,0:T(8,128)(2,1)S(1)} %get-tuple-element.92), channel_id=1, source_target_pairs={{0,2},{1,3},{2,4},{3,5},{4,6},{5,7},{6,8},{7,9},{8,10},{9,11},{10,... | collective-permute-start | bytes 393224 | tf_op jit(solution)/shard_map/ppermute | solution.py:453
  102.4 6.8 %collective-permute-start.31 = (bf16[256,256]{1,0:T(8,128)(2,1)S(1)}, bf16[256,256]{1,0:T(8,128)(2,1)S(1)}, u32[]{:S(2)}, u32[]{:S(2)}) collective-permute-start(bf16[256,256]{1,0:T(8,128)(2,1)S(1)} %get-tuple-element.91), channel_id=1, source_target_pairs={{0,14},{1,15},{2,0},{3,1},{4,2},{5,3},{6,4},{7,5},{8,6},{9,7},{10,... | collective-permute-start | bytes 393224 | tf_op jit(solution)/shard_map/ppermute | solution.py:453
  105.7 6.2 %collective-permute-start.25 = (bf16[256,256]{1,0:T(8,128)(2,1)S(1)}, bf16[256,256]{1,0:T(8,128)(2,1)S(1)}, u32[]{:S(2)}, u32[]{:S(2)}) collective-permute-start(bf16[256,256]{1,0:T(8,128)(2,1)S(1)} %get-tuple-element.90), channel_id=1, source_target_pairs={{0,2},{1,3},{2,4},{3,5},{4,6},{5,7},{6,8},{7,9},{8,10},{9,11},{10,... | collective-permute-start | bytes 393224 | tf_op jit(solution)/shard_map/ppermute | solution.py:453
  105.7 6.2 %collective-permute-start.27 = (bf16[256,256]{1,0:T(8,128)(2,1)S(1)}, bf16[256,256]{1,0:T(8,128)(2,1)S(1)}, u32[]{:S(2)}, u32[]{:S(2)}) collective-permute-start(bf16[256,256]{1,0:T(8,128)(2,1)S(1)} %get-tuple-element.93), channel_id=1, source_target_pairs={{0,14},{1,15},{2,0},{3,1},{4,2},{5,3},{6,4},{7,5},{8,6},{9,7},{10,... | collective-permute-start | bytes 393224 | tf_op jit(solution)/shard_map/ppermute | solution.py:453
  109.4 5.1 %collective-permute-start.32 = (bf16[256,256]{1,0:T(8,128)(2,1)S(1)}, bf16[256,256]{1,0:T(8,128)(2,1)S(1)}, u32[]{:S(2)}, u32[]{:S(2)}) collective-permute-start(bf16[256,256]{1,0:T(8,128)(2,1)S(1)} %fusion.5), channel_id=1, source_target_pairs={{0,16},{1,17},{2,18},{3,19},{4,20},{5,21},{6,22},{7,23},{8,24},{9,... | collective-permute-start | bytes 393224 | tf_op jit(solution)/shard_map/ppermute | solution.py:503

commit v5 on v4

--- a/solution.py
+++ b/solution.py
@@ -234,8 +234,6 @@
     for copy in copies:
         copy.start()
     table = jnp.concatenate([ref[...].astype(F32) for ref in table_refs], axis=0).T.astype(BF16)
-    share_row = lax.broadcasted_iota(jnp.int32, (SHARE, BLOCK), 0)
-    vocab = jnp.concatenate([share_row + source_of(own, n) * SHARE for n in range(N_CTX)], axis=0)
     table = jnp.concatenate([ref[...].astype(F32) for ref in table_refs], axis=0).T
     for tap in range(3):
         tapped_ref[:, tap * VOCAB : (tap + 1) * VOCAB] = (tap_ref[:, tap : tap + 1] * table).astype(BF16)
@@ -252,8 +250,17 @@
         id_ref[:, HALO + block * BLOCK : HALO + (block + 1) * BLOCK] = ids
     copies[N_CTX].wait()
 
+    tile_rows = [(lax.broadcasted_iota(jnp.int32, (16, BLOCK), 0) + 16 * n).astype(F32).astype(BF16) for n in range(SHARE // 16)]
+    one, none = jnp.ones((16, BLOCK), BF16), jnp.zeros((16, BLOCK), BF16)
+
     def one_hot(ids):
-        return jnp.where(ids == vocab, 1.0, 0.0).astype(BF16)
+        share, row = ids >> 6, (ids & (SHARE - 1)).astype(F32)
+        tiles = []
+        for n in range(N_CTX):
+            rows = jnp.where(share == source_of(own, n), row, -1.0)
+            rows = jnp.broadcast_to(rows, (16, BLOCK)).astype(BF16)
+            tiles += [jnp.where(rows == tile, one, none) for tile in tile_rows]
+        return jnp.concatenate(tiles, axis=0)
 
     def far_lookup(block):
         ids = id_ref[:, pl.ds(pl.multiple_of(block * BLOCK, BLOCK), HALO + BLOCK)]
@@ -420,17 +427,18 @@
     held = lax.all_to_all(
         jnp.broadcast_to(rows[None], (N_Z,) + rows.shape), "chan", 0, 0, axis_index_groups=Z_GROUPS
     )
-    held, pair = lax.optimization_barrier((held, pair))
     beside = lax.ppermute(held, "chan", X_SWAP)
     across = lax.ppermute(held, "chan", CORE_SWAP)
+    held, pair = lax.optimization_barrier((held, pair))
+    grads = gather_pairs(pair)
     sums, weight_beside, weight_both = project(0, held, weight, ahead=(1, 3))
     (sums,) = project(2, across, weight, sums)
     beside, sums = lax.optimization_barrier((beside, sums))
     both = lax.ppermute(beside, "chan", CORE_SWAP)
     (sums,) = project(1, beside, weight_beside, sums, ready=True)
-    both, sums = lax.optimization_barrier((both, sums))
+    both, sums, grads = lax.optimization_barrier((both, sums, grads))
     (part,) = project(3, both, weight_both, sums, ready=True, last=True)
-    return part, pair
+    return part, grads
 
 
 def gather_ctx(value):
@@ -508,8 +516,7 @@
     weight = in_weight.transpose(1, 0, 2).reshape(3, 2, N_Z, 2, BLOCK, BLOCK)
     own_vocab = lax.dynamic_slice_in_dim(embed_table, lax.axis_index("ctx") * SHARE, SHARE, 0)
     pair = pair_ctx(make_payload(out_grad, token_ids))
-    part, pair = project_features(own_vocab, weight, pair)
-    grads = gather_pairs(pair)
+    part, grads = project_features(own_vocab, weight, pair)
     modal_rates, part = lax.optimization_barrier((modal_rates, part))
     pieces = gather_ctx(part)
     gains = modal_residues * jnp.sqrt(-jnp.expm1(-2.0 * modal_rates))

time: 117 us -> 115 us (0.983)
  starting transfers between devices: 54.8 us -> 49.8 us
  waiting for transfers between devices: 17.5 us -> 22.5 us
  Pallas kernels: 37.1 us -> 35.6 us
    ppermute x3, waiting for transfers between devices: 0.5 us -> 4.74 us  [gather_pairs(): return [pair] + [lax.ppermute(pair, 'ctx', y_shift(by)) for by in Y_STEPS]]
    all_to_all x1, waiting for transfers between devices: 3.43 us -> 7.08 us  [project_features(): lax.all_to_all(jnp.broadcast_to(rows[None], (N_Z,) + rows.shape), 'chan',...]
    ppermute x6, starting transfers between devices: 12.4 us -> 8.79 us  [gather_ctx(): found += [lax.ppermute(piece, 'ctx', y_shift(by)) for by in Y_STEPS]]
    ppermute x1, waiting for transfers between devices: 3.61 us -> 0.01 us  [pair_ctx(): return jnp.stack([value, lax.ppermute(value, 'ctx', X_HALF_SWAP)])]
    pallas_call x1, Pallas kernels: 14.1 us -> 12.6 us  [mix(): pl.pallas_call(mixer_kernel, out_shape=(jax.ShapeDtypeStruct((BLOCK, BLOC...]
    ppermute x1, starting transfers between devices: 1.58 us -> 0.34 us  [reduce_chan(): lax.ppermute(far_half.astype(BF16), 'chan', X_SWAP).astype(F32)]
    ppermute x14, waiting for transfers between devices: 6.87 us -> 8.11 us  [moved(): return lax.ppermute(value.astype(BF16), 'chan', z_shift(by))]
  transfers between devices with their start and end apart: 34 -> 34, of which waited for: 13 -> 10; matrix products, arithmetic and copies ran while one was open for 0% -> 0% of each run, Pallas kernels for 20% -> 19%
where the time goes in v5:
time: 115 us; the launch traced here: 114 us
  starting transfers between devices  49.8 us (43%)
  Pallas kernels  35.6 us (31%)
  waiting for transfers between devices  22.5 us (20%)
  local copies, waits for them, and re-layouts  4.04 us (4%)
    ppermute x14, starting transfers between devices, moved(): return lax.ppermute(value.astype(BF16), 'chan', z_shift(by))  20.6 us
    pallas_call x1, Pallas kernels, mix(): pl.pallas_call(mixer_kernel, out_shape=(jax.ShapeDtypeStruct((BLOCK, BLOC...  12.6 us
    pallas_call x3, Pallas kernels, back_project(): pl.pallas_call(back_kernel, out_shape=(part, part), in_specs=[pl.BlockSpe...  10 us
    pallas_call x4, Pallas kernels, project(): pl.pallas_call(functools.partial(project_kernel, part, sums is None, read...  8.97 us
    ppermute x6, starting transfers between devices, gather_ctx(): found += [lax.ppermute(piece, 'ctx', y_shift(by)) for by in Y_STEPS]  8.79 us
    all_to_all x1, starting transfers between devices, project_features(): lax.all_to_all(jnp.broadcast_to(rows[None], (N_Z,) + rows.shape), 'chan',...  8.47 us
    ppermute x14, waiting for transfers between devices, moved(): return lax.ppermute(value.astype(BF16), 'chan', z_shift(by))  8.11 us
    all_to_all x1, waiting for transfers between devices, project_features(): lax.all_to_all(jnp.broadcast_to(rows[None], (N_Z,) + rows.shape), 'chan',...  7.08 us
  transfers between devices with their start and end apart: 34, of which 10 were waited for; matrix products, arithmetic and copies ran while one was open for 0% of the time, Pallas kernels for 19%

profile of v5, /device:TPU:24, one launch (start us, length us, event | category | flops | bytes accessed | tf_op | source)
XLA Modules:
  0.0 113.8 jit_solution(6508387466565149448)
XLA Ops:
  0.6 0.9 copy-done
  1.6 0.7 broadcast_in_dim.2
  2.3 8.5 %all-to-all-start = ((bf16[8,64,256]{2,1,0:T(8,128)(2,1)}), bf16[8,64,256]{2,1,0:T(8,128)(2,1)S(1)}, u32[]{:S(2)}, u32[]{:S(2)}) async-start(bf16[8,64,256]{2,1,0:T(8,128)(2,1)} %broadcast_in_dim.2), calls=%async_computation | async-start | bytes 524288 | tf_op jit(solution)/shard_map/all_to_all | solution.py:427
  10.8 0.9 copy-done.1
  11.7 0.7 copy-done.3
  12.5 3.1 %collective-permute-start.2 = (bf16[272,256]{1,0:T(8,128)(2,1)S(1)}, bf16[272,256]{1,0:T(8,128)(2,1)S(1)}, u32[]{:S(2)}, u32[]{:S(2)}) collective-permute-start(bf16[272,256]{1,0:T(8,128)(2,1)S(1)} %payload.1), channel_id=1, source_target_pairs={{0,32},{32,0},{64,96},{96,64},{128,160},{160,128},{192,224},{224,1... | collective-permute-start | bytes 417800 | tf_op jit(solution)/shard_map/ppermute | solution.py:453
  15.6 7.1 %all-to-all-done.refs_0_ = bf16[8,64,256]{2,1,0:T(8,128)(2,1)S(1)} async-done(((bf16[8,64,256]{2,1,0:T(8,128)(2,1)}), bf16[8,64,256]{2,1,0:T(8,128)(2,1)S(1)}, u32[]{:S(2)}, u32[]{:S(2)}) %all-to-all-start) | async-done | bytes 262176 | tf_op jit(solution)/shard_map/all_to_all | solution.py:427
  22.7 1.5 %collective-permute-start = (bf16[8,64,256]{2,1,0:T(8,128)(2,1)S(1)}, bf16[8,64,256]{2,1,0:T(8,128)(2,1)S(1)}, u32[]{:S(2)}, u32[]{:S(2)}) collective-permute-start(bf16[8,64,256]{2,1,0:T(8,128)(2,1)S(1)} %all-to-all-done.refs_0_), channel_id=1, source_target_pairs={{0,16},{1,17},{2,18},{3,19},{4,20},{5,21},{6,22},{7,23},{8,24},{9,... | collective-permute-start | bytes 786440 | tf_op jit(solution)/shard_map/ppermute | solution.py:430
  24.2 0.3 collective-permute-start.4
  24.5 1.8 %collective-permute-start.5 = (bf16[2,272,256]{2,1,0:T(8,128)(2,1)S(1)}, bf16[2,272,256]{2,1,0:T(8,128)(2,1)S(1)}, u32[]{:S(2)}, u32[]{:S(2)}) collective-permute-start(bf16[2,272,256]{2,1,0:T(8,128)(2,1)S(1)} %pad_maximum_fusion.refs_8_), channel_id=1, source_target_pairs={{0,192},{32,224},{64,0},{96,32},{128,64},{160,96},{192,128},{224,1... | collective-permute-start | bytes 835592 | tf_op jit(solution)/shard_map/ppermute | solution.py:457
  26.3 1.2 %collective-permute-start.6 = (bf16[2,272,256]{2,1,0:T(8,128)(2,1)S(1)}, bf16[2,272,256]{2,1,0:T(8,128)(2,1)S(1)}, u32[]{:S(2)}, u32[]{:S(2)}) collective-permute-start(bf16[2,272,256]{2,1,0:T(8,128)(2,1)S(1)} %pad_maximum_fusion.refs_8_), channel_id=1, source_target_pairs={{0,128},{32,160},{64,192},{96,224},{128,0},{160,32},{192,64},{224,... | collective-permute-start | bytes 835592 | tf_op jit(solution)/shard_map/ppermute | solution.py:457
  27.5 3.8 %project.4 = (f32[64,768]{1,0:T(8,128)S(1)}, bf16[3,8,256,256]{3,2,1,0:T(8,128)(2,1)S(1)}, bf16[3,8,256,256]{3,2,1,0:T(8,128)(2,1)S(1)}) custom-call(bf16[8,64,256]{2,1,0:T(8,128)(2,1)S(1)} %all-to-all-done.refs_0_, bf16[3,2,8,2,256,256]{5,4,3,2,1,0:T(8,128)(2,1)} %bitcast.74), custom_call_target="tpu_custom_call" | custom-call | flops 201326592 | bytes 9437184 | tf_op jit(solution)/shard_map/project/pallas_call | solution.py:190
  31.3 3.0 %project.5.refs_2_ = f32[64,768]{1,0:T(8,128)S(1)} custom-call(bf16[8,64,256]{2,1,0:T(8,128)(2,1)S(1)} %collective-permute-done.1.refs_0_, bf16[3,2,8,2,256,256]{5,4,3,2,1,0:T(8,128)(2,1)} %bitcast.75, f32[64,768]{1,0:T(8,128)S(1)} %get-tuple-element.50.refs_2_), custom_call_target="tpu_custom_call" | custom-call | flops 201326592 | bytes 3145728 | tf_op jit(solution)/shard_map/project/pallas_call | solution.py:190
  34.5 1.1 project.6.refs_2_
  35.6 4.7 %collective-permute-done.5.refs_10_ = bf16[2,272,256]{2,1,0:T(8,128)(2,1)S(1)} collective-permute-done((bf16[2,272,256]{2,1,0:T(8,128)(2,1)S(1)}, bf16[2,272,256]{2,1,0:T(8,128)(2,1)S(1)}, u32[]{:S(2)}, u32[]{:S(2)}) %collective-permute-start.5) | collective-permute-done | bytes 278560 | tf_op jit(solution)/shard_map/ppermute | solution.py:457
  40.3 1.1 project.7.refs_0_
  41.4 2.8 %collective-permute-start.7 = (bf16[64,768]{1,0:T(8,128)(2,1)S(1)}, bf16[64,768]{1,0:T(8,128)(2,1)S(1)}, u32[]{:S(2)}, u32[]{:S(2)}) collective-permute-start(bf16[64,768]{1,0:T(8,128)(2,1)S(1)} %project.7.refs_0_), channel_id=1, source_target_pairs={{0,32},{32,0},{64,96},{96,64},{128,160},{160,128},{192,224},{224,1... | collective-permute-start | bytes 294920 | tf_op jit(solution)/shard_map/ppermute | solution.py:445
  44.2 2.8 %collective-permute-start.12 = (bf16[64,768]{1,0:T(8,128)(2,1)S(1)}, bf16[64,768]{1,0:T(8,128)(2,1)S(1)}, u32[]{:S(2)}, u32[]{:S(2)}) collective-permute-start(bf16[64,768]{1,0:T(8,128)(2,1)S(1)} %project.7.refs_0_), channel_id=1, source_target_pairs={{0,128},{32,160},{64,192},{96,224},{128,0},{160,32},{192,64},{224,... | collective-permute-start | bytes 294920 | tf_op jit(solution)/shard_map/ppermute | solution.py:448
  47.1 1.8 %collective-permute-start.8 = (bf16[64,768]{1,0:T(8,128)(2,1)S(1)}, bf16[64,768]{1,0:T(8,128)(2,1)S(1)}, u32[]{:S(2)}, u32[]{:S(2)}) collective-permute-start(bf16[64,768]{1,0:T(8,128)(2,1)S(1)} %project.7.refs_0_), channel_id=1, source_target_pairs={{0,64},{32,96},{64,128},{96,160},{128,192},{160,224},{192,0},{224,... | collective-permute-start | bytes 294920 | tf_op jit(solution)/shard_map/ppermute | solution.py:448
  48.8 0.3 collective-permute-start.11
  49.1 1.4 %collective-permute-start.13 = (bf16[64,768]{1,0:T(8,128)(2,1)S(1)}, bf16[64,768]{1,0:T(8,128)(2,1)S(1)}, u32[]{:S(2)}, u32[]{:S(2)}) collective-permute-start(bf16[64,768]{1,0:T(8,128)(2,1)S(1)} %collective-permute-done.7.refs_1_), channel_id=1, source_target_pairs={{0,128},{32,160},{64,192},{96,224},{128,0},{160,32},{192,64},{224,... | collective-permute-start | bytes 294920 | tf_op jit(solution)/shard_map/ppermute | solution.py:448
  50.5 2.6 %collective-permute-start.9 = (bf16[64,768]{1,0:T(8,128)(2,1)S(1)}, bf16[64,768]{1,0:T(8,128)(2,1)S(1)}, u32[]{:S(2)}, u32[]{:S(2)}) collective-permute-start(bf16[64,768]{1,0:T(8,128)(2,1)S(1)} %collective-permute-done.7.refs_1_), channel_id=1, source_target_pairs={{0,64},{32,96},{64,128},{96,160},{128,192},{160,224},{192,0},{224,... | collective-permute-start | bytes 294920 | tf_op jit(solution)/shard_map/ppermute | solution.py:448
  53.1 3.9 %filter_tables.1 = (bf16[16,256,256]{2,1,0:T(8,128)(2,1)S(1)}, bf16[256,1152]{1,0:T(8,128)(2,1)S(1)}, f32[2,256]{1,0:T(2,128)S(1)}, f32[768,3]{1,0:T(8,128)S(1)}) custom-call(f32[16,16]{1,0:T(8,128)S(1)} %copy-done.2, f32[16,16]{1,0:T(8,128)S(1)} %sqrt_multiply_fusion.gain_ref, f32[3,3,256]{2,1,0:T(4,128)S(1)} %copy-done.7), custom_call_target="tpu_custom_call" | custom-call | flops 402653184 | bytes 5242880 | tf_op jit(solution)/shard_map/filter_tables/pallas_call | solution.py:140
  57.1 12.6 %mixer.1 = (bf16[256,256]{1,0:T(8,128)(2,1)}, bf16[768,256]{1,0:T(8,128)(2,1)S(1)}, bf16[1,2,256,256]{3,2,1,0:T(8,128)(2,1)S(1)}, bf16[1,2,256,256]{3,2,1,0:T(8,128)(2,1)S(1)}) custom-call(bf16[64,768]{1,0:T(8,128)(2,1)S(1)} %project.7.refs_0_, bf16[64,768]{1,0:T(8,128)(2,1)S(1)} %collective-permute-done.7.refs_1_, ...), custom_call_target="tpu_custom_call" | custom-call | flops 3221225472 | bytes 8388608 | tf_op jit(solution)/shard_map/mixer/pallas_call | solution.py:361
  69.8 3.1 %back_project.3 = (bf16[2,2,256,256]{3,2,1,0:T(8,128)(2,1)S(1)}, bf16[2,2,256,256]{3,2,1,0:T(8,128)(2,1)S(1)}) custom-call(s32[2]{0:T(128)S(1)} %copy-done.6, bf16[768,256]{1,0:T(8,128)(2,1)S(1)} %get-tuple-element.85.grad_ref, bf16[3,2,8,2,256,256]{5,4,3,2,1,0:T(8,128)(2,1)} %bitcast.77), custom_call_target="tpu_custom_call" | custom-call | flops 805306368 | bytes 4194304 | tf_op jit(solution)/shard_map/back_project/pallas_call | solution.py:409
  73.0 0.6 collective-permute-start.15
  73.7 2.0 %collective-permute-start.17 = (bf16[256,256]{1,0:T(8,128)(2,1)S(1)}, bf16[256,256]{1,0:T(8,128)(2,1)S(1)}, u32[]{:S(2)}, u32[]{:S(2)}) collective-permute-start(bf16[256,256]{1,0:T(8,128)(2,1)S(1)} %get-tuple-element.110), channel_id=1, source_target_pairs={{0,2},{1,3},{2,4},{3,5},{4,6},{5,7},{6,8},{7,9},{8,10},{9,11},{10,... | collective-permute-start | bytes 393224 | tf_op jit(solution)/shard_map/ppermute | solution.py:461
  75.7 3.1 %back_project.4 = (bf16[2,2,256,256]{3,2,1,0:T(8,128)(2,1)S(1)}, bf16[2,2,256,256]{3,2,1,0:T(8,128)(2,1)S(1)}) custom-call(s32[2]{0:T(128)S(1)} %copy-done.5, bf16[768,256]{1,0:T(8,128)(2,1)S(1)} %get-tuple-element.85.grad_ref, bf16[3,2,8,2,256,256]{5,4,3,2,1,0:T(8,128)(2,1)} %bitcast.78), custom_call_target="tpu_custom_call" | custom-call | flops 805306368 | bytes 4194304 | tf_op jit(solution)/shard_map/back_project/pallas_call | solution.py:409
  78.8 0.3 collective-permute-done.16
  79.1 1.5 %collective-permute-done.17 = bf16[256,256]{1,0:T(8,128)(2,1)S(1)} collective-permute-done((bf16[256,256]{1,0:T(8,128)(2,1)S(1)}, bf16[256,256]{1,0:T(8,128)(2,1)S(1)}, u32[]{:S(2)}, u32[]{:S(2)}) %collective-permute-start.17) | collective-permute-done | bytes 131104 | tf_op jit(solution)/shard_map/ppermute | solution.py:461
  80.7 0.3 collective-permute-start.19
  81.0 3.0 %collective-permute-start.20 = (bf16[256,256]{1,0:T(8,128)(2,1)S(1)}, bf16[256,256]{1,0:T(8,128)(2,1)S(1)}, u32[]{:S(2)}, u32[]{:S(2)}) collective-permute-start(bf16[256,256]{1,0:T(8,128)(2,1)S(1)} %get-tuple-element.108), channel_id=1, source_target_pairs={{0,14},{1,15},{2,0},{3,1},{4,2},{5,3},{6,4},{7,5},{8,6},{9,7},{10,... | collective-permute-start | bytes 393224 | tf_op jit(solution)/shard_map/ppermute | solution.py:461
  84.2 2.0 %collective-permute-start.21 = (bf16[256,256]{1,0:T(8,128)(2,1)S(1)}, bf16[256,256]{1,0:T(8,128)(2,1)S(1)}, u32[]{:S(2)}, u32[]{:S(2)}) collective-permute-start(bf16[256,256]{1,0:T(8,128)(2,1)S(1)} %get-tuple-element.106), channel_id=1, source_target_pairs={{0,2},{1,3},{2,4},{3,5},{4,6},{5,7},{6,8},{7,9},{8,10},{9,11},{10,... | collective-permute-start | bytes 393224 | tf_op jit(solution)/shard_map/ppermute | solution.py:461
  86.3 3.7 %back_project.5 = (bf16[3,2,256,256]{3,2,1,0:T(8,128)(2,1)S(1)}, bf16[3,2,256,256]{3,2,1,0:T(8,128)(2,1)S(1)}) custom-call(s32[3]{0:T(128)S(1)} %copy-done.4, bf16[768,256]{1,0:T(8,128)(2,1)S(1)} %get-tuple-element.85.grad_ref, bf16[3,2,8,2,256,256]{5,4,3,2,1,0:T(8,128)(2,1)} %bitcast.79), custom_call_target="tpu_custom_call" | custom-call | flops 1207959552 | bytes 6291456 | tf_op jit(solution)/shard_map/back_project/pallas_call | solution.py:409
  90.0 0.5 collective-permute-done.21
  90.6 0.2 fusion.9
  90.8 0.7 collective-permute-start.24
  91.5 2.7 %collective-permute-start.26 = (bf16[256,256]{1,0:T(8,128)(2,1)S(1)}, bf16[256,256]{1,0:T(8,128)(2,1)S(1)}, u32[]{:S(2)}, u32[]{:S(2)}) collective-permute-start(bf16[256,256]{1,0:T(8,128)(2,1)S(1)} %get-tuple-element.105), channel_id=1, source_target_pairs={{0,14},{1,15},{2,0},{3,1},{4,2},{5,3},{6,4},{7,5},{8,6},{9,7},{10,... | collective-permute-start | bytes 393224 | tf_op jit(solution)/shard_map/ppermute | solution.py:461
  94.2 3.2 %collective-permute-start.30 = (bf16[256,256]{1,0:T(8,128)(2,1)S(1)}, bf16[256,256]{1,0:T(8,128)(2,1)S(1)}, u32[]{:S(2)}, u32[]{:S(2)}) collective-permute-start(bf16[256,256]{1,0:T(8,128)(2,1)S(1)} %get-tuple-element.103), channel_id=1, source_target_pairs={{0,14},{1,15},{2,0},{3,1},{4,2},{5,3},{6,4},{7,5},{8,6},{9,7},{10,... | collective-permute-start | bytes 393224 | tf_op jit(solution)/shard_map/ppermute | solution.py:461
  97.4 0.6 collective-permute-done.24
  98.0 2.7 %collective-permute-done.28 = bf16[256,256]{1,0:T(8,128)(2,1)S(1)} collective-permute-done((bf16[256,256]{1,0:T(8,128)(2,1)S(1)}, bf16[256,256]{1,0:T(8,128)(2,1)S(1)}, u32[]{:S(2)}, u32[]{:S(2)}) %collective-permute-start.28) | collective-permute-done | bytes 131104 | tf_op jit(solution)/shard_map/ppermute | solution.py:461
  101.0 3.2 %collective-permute-start.31 = (bf16[256,256]{1,0:T(8,128)(2,1)S(1)}, bf16[256,256]{1,0:T(8,128)(2,1)S(1)}, u32[]{:S(2)}, u32[]{:S(2)}) collective-permute-start(bf16[256,256]{1,0:T(8,128)(2,1)S(1)} %get-tuple-element.99), channel_id=1, source_target_pairs={{0,14},{1,15},{2,0},{3,1},{4,2},{5,3},{6,4},{7,5},{8,6},{9,7},{10,... | collective-permute-start | bytes 393224 | tf_op jit(solution)/shard_map/ppermute | solution.py:461
  104.2 3.2 %collective-permute-start.27 = (bf16[256,256]{1,0:T(8,128)(2,1)S(1)}, bf16[256,256]{1,0:T(8,128)(2,1)S(1)}, u32[]{:S(2)}, u32[]{:S(2)}) collective-permute-start(bf16[256,256]{1,0:T(8,128)(2,1)S(1)} %get-tuple-element.101), channel_id=1, source_target_pairs={{0,14},{1,15},{2,0},{3,1},{4,2},{5,3},{6,4},{7,5},{8,6},{9,7},{10,... | collective-permute-start | bytes 393224 | tf_op jit(solution)/shard_map/ppermute | solution.py:461
  107.5 0.4 collective-permute-done.29
  107.9 0.3 collective-permute-start.32
  108.3 2.1 %collective-permute-done.25 = bf16[256,256]{1,0:T(8,128)(2,1)S(1)} collective-permute-done((bf16[256,256]{1,0:T(8,128)(2,1)S(1)}, bf16[256,256]{1,0:T(8,128)(2,1)S(1)}, u32[]{:S(2)}, u32[]{:S(2)}) %collective-permute-start.25) | collective-permute-done | bytes 131104 | tf_op jit(solution)/shard_map/ppermute | solution.py:461
  110.4 2.6 %collective-permute-done.32 = bf16[256,256]{1,0:T(8,128)(2,1)S(1)} collective-permute-done((bf16[256,256]{1,0:T(8,128)(2,1)S(1)}, bf16[256,256]{1,0:T(8,128)(2,1)S(1)}, u32[]{:S(2)}, u32[]{:S(2)}) %collective-permute-start.32) | collective-permute-done | bytes 131104 | tf_op jit(solution)/shard_map/ppermute | solution.py:511
  113.1 0.8 copy.12
  (60 shorter events, 1.4 us)
Async XLA Ops:
  0.6 1.0 copy-start
  2.3 20.3 %all-to-all-start = ((bf16[8,64,256]{2,1,0:T(8,128)(2,1)}), bf16[8,64,256]{2,1,0:T(8,128)(2,1)S(1)}, u32[]{:S(2)}, u32[]{:S(2)}) async-start(bf16[8,64,256]{2,1,0:T(8,128)(2,1)} %broadcast_in_dim.2), calls=%async_computation | async-start | bytes 524288 | tf_op jit(solution)/shard_map/all_to_all | solution.py:427
  10.8 0.9 copy-start.1
  11.7 0.7 copy-start.3
  12.5 11.7 %collective-permute-start.2 = (bf16[272,256]{1,0:T(8,128)(2,1)S(1)}, bf16[272,256]{1,0:T(8,128)(2,1)S(1)}, u32[]{:S(2)}, u32[]{:S(2)}) collective-permute-start(bf16[272,256]{1,0:T(8,128)(2,1)S(1)} %payload.1), channel_id=1, source_target_pairs={{0,32},{32,0},{64,96},{96,64},{128,160},{160,128},{192,224},{224,1... | collective-permute-start | bytes 417800 | tf_op jit(solution)/shard_map/ppermute | solution.py:453
  22.6 8.7 %collective-permute-start.1 = (bf16[8,64,256]{2,1,0:T(8,128)(2,1)S(1)}, bf16[8,64,256]{2,1,0:T(8,128)(2,1)S(1)}, u32[]{:S(2)}, u32[]{:S(2)}) collective-permute-start(bf16[8,64,256]{2,1,0:T(8,128)(2,1)S(1)} %all-to-all-done.refs_0_), channel_id=1, source_target_pairs={{0,1},{1,0},{2,3},{3,2},{4,5},{5,4},{6,7},{7,6},{8,9},{9,8},{10,11... | collective-permute-start | bytes 786440 | tf_op jit(solution)/shard_map/ppermute | solution.py:431
  22.7 11.7 %collective-permute-start = (bf16[8,64,256]{2,1,0:T(8,128)(2,1)S(1)}, bf16[8,64,256]{2,1,0:T(8,128)(2,1)S(1)}, u32[]{:S(2)}, u32[]{:S(2)}) collective-permute-start(bf16[8,64,256]{2,1,0:T(8,128)(2,1)S(1)} %all-to-all-done.refs_0_), channel_id=1, source_target_pairs={{0,16},{1,17},{2,18},{3,19},{4,20},{5,21},{6,22},{7,23},{8,24},{9,... | collective-permute-start | bytes 786440 | tf_op jit(solution)/shard_map/ppermute | solution.py:430
  24.2 11.4 %collective-permute-start.4 = (bf16[2,272,256]{2,1,0:T(8,128)(2,1)S(1)}, bf16[2,272,256]{2,1,0:T(8,128)(2,1)S(1)}, u32[]{:S(2)}, u32[]{:S(2)}) collective-permute-start(bf16[2,272,256]{2,1,0:T(8,128)(2,1)S(1)} %pad_maximum_fusion.refs_8_), channel_id=1, source_target_pairs={{0,64},{32,96},{64,128},{96,160},{128,192},{160,224},{192,0},{224,... | collective-permute-start | bytes 835592 | tf_op jit(solution)/shard_map/ppermute | solution.py:457
  24.5 15.8 %collective-permute-start.5 = (bf16[2,272,256]{2,1,0:T(8,128)(2,1)S(1)}, bf16[2,272,256]{2,1,0:T(8,128)(2,1)S(1)}, u32[]{:S(2)}, u32[]{:S(2)}) collective-permute-start(bf16[2,272,256]{2,1,0:T(8,128)(2,1)S(1)} %pad_maximum_fusion.refs_8_), channel_id=1, source_target_pairs={{0,192},{32,224},{64,0},{96,32},{128,64},{160,96},{192,128},{224,1... | collective-permute-start | bytes 835592 | tf_op jit(solution)/shard_map/ppermute | solution.py:457
  26.3 14.0 %collective-permute-start.6 = (bf16[2,272,256]{2,1,0:T(8,128)(2,1)S(1)}, bf16[2,272,256]{2,1,0:T(8,128)(2,1)S(1)}, u32[]{:S(2)}, u32[]{:S(2)}) collective-permute-start(bf16[2,272,256]{2,1,0:T(8,128)(2,1)S(1)} %pad_maximum_fusion.refs_8_), channel_id=1, source_target_pairs={{0,128},{32,160},{64,192},{96,224},{128,0},{160,32},{192,64},{224,... | collective-permute-start | bytes 835592 | tf_op jit(solution)/shard_map/ppermute | solution.py:457
  34.4 6.0 %collective-permute-start.3 = (bf16[8,64,256]{2,1,0:T(8,128)(2,1)S(1)}, bf16[8,64,256]{2,1,0:T(8,128)(2,1)S(1)}, u32[]{:S(2)}, u32[]{:S(2)}) collective-permute-start(bf16[8,64,256]{2,1,0:T(8,128)(2,1)S(1)} %collective-permute-done.refs_0_), channel_id=1, source_target_pairs={{0,1},{1,0},{2,3},{3,2},{4,5},{5,4},{6,7},{7,6},{8,9},{9,8},{10,11... | collective-permute-start | bytes 786440 | tf_op jit(solution)/shard_map/ppermute | solution.py:437
  34.5 18.6 %copy-start.2 = (f32[16,16]{1,0:T(8,128)S(1)}, f32[16,16]{1,0:T(8,128)}, u32[]{:S(2)}) copy-start(f32[16,16]{1,0:T(8,128)} %rate_ref) | copy-start | bytes 3076
  34.5 18.6 %copy-start.8 = (f32[16,16]{1,0:T(8,128)S(1)}, f32[16,16]{1,0:T(8,128)}, u32[]{:S(2)}) copy-start(f32[16,16]{1,0:T(8,128)} %param.15) | copy-start | bytes 3076
  34.5 18.6 %copy-start.7 = (f32[3,3,256]{2,1,0:T(4,128)S(1)}, f32[3,3,256]{2,1,0:T(4,128)}, u32[]{:S(2)}) copy-start(f32[3,3,256]{2,1,0:T(4,128)} %tap_ref.1) | copy-start | bytes 27652
  41.4 7.4 %collective-permute-start.7 = (bf16[64,768]{1,0:T(8,128)(2,1)S(1)}, bf16[64,768]{1,0:T(8,128)(2,1)S(1)}, u32[]{:S(2)}, u32[]{:S(2)}) collective-permute-start(bf16[64,768]{1,0:T(8,128)(2,1)S(1)} %project.7.refs_0_), channel_id=1, source_target_pairs={{0,32},{32,0},{64,96},{96,64},{128,160},{160,128},{192,224},{224,1... | collective-permute-start | bytes 294920 | tf_op jit(solution)/shard_map/ppermute | solution.py:445
  44.2 6.2 %collective-permute-start.10 = (bf16[64,768]{1,0:T(8,128)(2,1)S(1)}, bf16[64,768]{1,0:T(8,128)(2,1)S(1)}, u32[]{:S(2)}, u32[]{:S(2)}) collective-permute-start(bf16[64,768]{1,0:T(8,128)(2,1)S(1)} %project.7.refs_0_), channel_id=1, source_target_pairs={{0,192},{32,224},{64,0},{96,32},{128,64},{160,96},{192,128},{224,1... | collective-permute-start | bytes 294920 | tf_op jit(solution)/shard_map/ppermute | solution.py:448
  44.2 12.8 %collective-permute-start.12 = (bf16[64,768]{1,0:T(8,128)(2,1)S(1)}, bf16[64,768]{1,0:T(8,128)(2,1)S(1)}, u32[]{:S(2)}, u32[]{:S(2)}) collective-permute-start(bf16[64,768]{1,0:T(8,128)(2,1)S(1)} %project.7.refs_0_), channel_id=1, source_target_pairs={{0,128},{32,160},{64,192},{96,224},{128,0},{160,32},{192,64},{224,... | collective-permute-start | bytes 294920 | tf_op jit(solution)/shard_map/ppermute | solution.py:448
  47.1 9.9 %collective-permute-start.8 = (bf16[64,768]{1,0:T(8,128)(2,1)S(1)}, bf16[64,768]{1,0:T(8,128)(2,1)S(1)}, u32[]{:S(2)}, u32[]{:S(2)}) collective-permute-start(bf16[64,768]{1,0:T(8,128)(2,1)S(1)} %project.7.refs_0_), channel_id=1, source_target_pairs={{0,64},{32,96},{64,128},{96,160},{128,192},{160,224},{192,0},{224,... | collective-permute-start | bytes 294920 | tf_op jit(solution)/shard_map/ppermute | solution.py:448
  48.8 8.2 %collective-permute-start.11 = (bf16[64,768]{1,0:T(8,128)(2,1)S(1)}, bf16[64,768]{1,0:T(8,128)(2,1)S(1)}, u32[]{:S(2)}, u32[]{:S(2)}) collective-permute-start(bf16[64,768]{1,0:T(8,128)(2,1)S(1)} %collective-permute-done.7.refs_1_), channel_id=1, source_target_pairs={{0,192},{32,224},{64,0},{96,32},{128,64},{160,96},{192,128},{224,1... | collective-permute-start | bytes 294920 | tf_op jit(solution)/shard_map/ppermute | solution.py:448
  49.1 7.9 %collective-permute-start.13 = (bf16[64,768]{1,0:T(8,128)(2,1)S(1)}, bf16[64,768]{1,0:T(8,128)(2,1)S(1)}, u32[]{:S(2)}, u32[]{:S(2)}) collective-permute-start(bf16[64,768]{1,0:T(8,128)(2,1)S(1)} %collective-permute-done.7.refs_1_), channel_id=1, source_target_pairs={{0,128},{32,160},{64,192},{96,224},{128,0},{160,32},{192,64},{224,... | collective-permute-start | bytes 294920 | tf_op jit(solution)/shard_map/ppermute | solution.py:448
  50.5 6.6 %collective-permute-start.9 = (bf16[64,768]{1,0:T(8,128)(2,1)S(1)}, bf16[64,768]{1,0:T(8,128)(2,1)S(1)}, u32[]{:S(2)}, u32[]{:S(2)}) collective-permute-start(bf16[64,768]{1,0:T(8,128)(2,1)S(1)} %collective-permute-done.7.refs_1_), channel_id=1, source_target_pairs={{0,64},{32,96},{64,128},{96,160},{128,192},{160,224},{192,0},{224,... | collective-permute-start | bytes 294920 | tf_op jit(solution)/shard_map/ppermute | solution.py:448
  57.1 12.7 %copy-start.6 = (s32[2]{0:T(128)S(1)}, s32[2]{0:T(128)}, u32[]{:S(2)}) copy-start(s32[2]{0:T(128)} %constant.20.clone.step_ref) | copy-start | bytes 28
  69.7 3.3 %collective-permute-start.14 = (bf16[1,2,256,256]{3,2,1,0:T(8,128)(2,1)S(1)}, bf16[1,2,256,256]{3,2,1,0:T(8,128)(2,1)S(1)}, u32[]{:S(2)}, u32[]{:S(2)}) collective-permute-start(bf16[1,2,256,256]{3,2,1,0:T(8,128)(2,1)S(1)} %get-tuple-element.70), channel_id=1, source_target_pairs={{0,1},{1,0},{2,3},{3,2},{4,5},{5,4},{6,7},{7,6},{8,9},{9,8},{10,11... | collective-permute-start | bytes 786440 | tf_op jit(solution)/shard_map/ppermute | solution.py:468
  69.8 5.9 %copy-start.5 = (s32[2]{0:T(128)S(1)}, s32[2]{0:T(128)}, u32[]{:S(2)}) copy-start(s32[2]{0:T(128)} %constant.21.clone.step_ref) | copy-start | bytes 28
  73.0 7.7 %collective-permute-start.15 = (bf16[2,2,256,256]{3,2,1,0:T(8,128)(2,1)S(1)}, bf16[2,2,256,256]{3,2,1,0:T(8,128)(2,1)S(1)}, u32[]{:S(2)}, u32[]{:S(2)}) collective-permute-start(bf16[2,2,256,256]{3,2,1,0:T(8,128)(2,1)S(1)} %get-tuple-element.76), channel_id=1, source_target_pairs={{0,1},{1,0},{2,3},{3,2},{4,5},{5,4},{6,7},{7,6},{8,9},{9,8},{10,11... | collective-permute-start | bytes 1572872 | tf_op jit(solution)/shard_map/ppermute | solution.py:468
  73.6 5.5 %collective-permute-start.16 = (bf16[256,256]{1,0:T(8,128)(2,1)S(1)}, bf16[256,256]{1,0:T(8,128)(2,1)S(1)}, u32[]{:S(2)}, u32[]{:S(2)}) collective-permute-start(bf16[256,256]{1,0:T(8,128)(2,1)S(1)} %get-tuple-element.111), channel_id=1, source_target_pairs={{0,14},{1,15},{2,0},{3,1},{4,2},{5,3},{6,4},{7,5},{8,6},{9,7},{10,... | collective-permute-start | bytes 393224 | tf_op jit(solution)/shard_map/ppermute | solution.py:461
  73.7 12.6 %copy-start.4 = (s32[3]{0:T(128)S(1)}, s32[3]{0:T(128)}, u32[]{:S(2)}) copy-start(s32[3]{0:T(128)} %constant.22.clone.step_ref) | copy-start | bytes 40
  73.7 6.9 %collective-permute-start.17 = (bf16[256,256]{1,0:T(8,128)(2,1)S(1)}, bf16[256,256]{1,0:T(8,128)(2,1)S(1)}, u32[]{:S(2)}, u32[]{:S(2)}) collective-permute-start(bf16[256,256]{1,0:T(8,128)(2,1)S(1)} %get-tuple-element.110), channel_id=1, source_target_pairs={{0,2},{1,3},{2,4},{3,5},{4,6},{5,7},{6,8},{7,9},{8,10},{9,11},{10,... | collective-permute-start | bytes 393224 | tf_op jit(solution)/shard_map/ppermute | solution.py:461
  80.7 9.3 %collective-permute-start.19 = (bf16[256,256]{1,0:T(8,128)(2,1)S(1)}, bf16[256,256]{1,0:T(8,128)(2,1)S(1)}, u32[]{:S(2)}, u32[]{:S(2)}) collective-permute-start(bf16[256,256]{1,0:T(8,128)(2,1)S(1)} %get-tuple-element.109), channel_id=1, source_target_pairs={{0,2},{1,3},{2,4},{3,5},{4,6},{5,7},{6,8},{7,9},{8,10},{9,11},{10,... | collective-permute-start | bytes 393224 | tf_op jit(solution)/shard_map/ppermute | solution.py:461
  81.0 9.0 %collective-permute-start.20 = (bf16[256,256]{1,0:T(8,128)(2,1)S(1)}, bf16[256,256]{1,0:T(8,128)(2,1)S(1)}, u32[]{:S(2)}, u32[]{:S(2)}) collective-permute-start(bf16[256,256]{1,0:T(8,128)(2,1)S(1)} %get-tuple-element.108), channel_id=1, source_target_pairs={{0,14},{1,15},{2,0},{3,1},{4,2},{5,3},{6,4},{7,5},{8,6},{9,7},{10,... | collective-permute-start | bytes 393224 | tf_op jit(solution)/shard_map/ppermute | solution.py:461
  84.1 5.9 %collective-permute-start.18 = (bf16[256,256]{1,0:T(8,128)(2,1)S(1)}, bf16[256,256]{1,0:T(8,128)(2,1)S(1)}, u32[]{:S(2)}, u32[]{:S(2)}) collective-permute-start(bf16[256,256]{1,0:T(8,128)(2,1)S(1)} %get-tuple-element.107), channel_id=1, source_target_pairs={{0,14},{1,15},{2,0},{3,1},{4,2},{5,3},{6,4},{7,5},{8,6},{9,7},{10,... | collective-permute-start | bytes 393224 | tf_op jit(solution)/shard_map/ppermute | solution.py:461
  84.2 6.3 %collective-permute-start.21 = (bf16[256,256]{1,0:T(8,128)(2,1)S(1)}, bf16[256,256]{1,0:T(8,128)(2,1)S(1)}, u32[]{:S(2)}, u32[]{:S(2)}) collective-permute-start(bf16[256,256]{1,0:T(8,128)(2,1)S(1)} %get-tuple-element.106), channel_id=1, source_target_pairs={{0,2},{1,3},{2,4},{3,5},{4,6},{5,7},{6,8},{7,9},{8,10},{9,11},{10,... | collective-permute-start | bytes 393224 | tf_op jit(solution)/shard_map/ppermute | solution.py:461
  86.2 4.4 %collective-permute-start.23 = (bf16[2,2,256,256]{3,2,1,0:T(8,128)(2,1)S(1)}, bf16[2,2,256,256]{3,2,1,0:T(8,128)(2,1)S(1)}, u32[]{:S(2)}, u32[]{:S(2)}) collective-permute-start(bf16[2,2,256,256]{3,2,1,0:T(8,128)(2,1)S(1)} %get-tuple-element.92), channel_id=1, source_target_pairs={{0,1},{1,0},{2,3},{3,2},{4,5},{5,4},{6,7},{7,6},{8,9},{9,8},{10,11... | collective-permute-start | bytes 1572872 | tf_op jit(solution)/shard_map/ppermute | solution.py:468
  90.5 10.2 %collective-permute-start.22 = (bf16[3,2,256,256]{3,2,1,0:T(8,128)(2,1)S(1)}, bf16[3,2,256,256]{3,2,1,0:T(8,128)(2,1)S(1)}, u32[]{:S(2)}, u32[]{:S(2)}) collective-permute-start(bf16[3,2,256,256]{3,2,1,0:T(8,128)(2,1)S(1)} %get-tuple-element.89), channel_id=1, source_target_pairs={{0,1},{1,0},{2,3},{3,2},{4,5},{5,4},{6,7},{7,6},{8,9},{9,8},{10,11... | collective-permute-start | bytes 2359304 | tf_op jit(solution)/shard_map/ppermute | solution.py:468
  90.8 7.1 %collective-permute-start.24 = (bf16[256,256]{1,0:T(8,128)(2,1)S(1)}, bf16[256,256]{1,0:T(8,128)(2,1)S(1)}, u32[]{:S(2)}, u32[]{:S(2)}) collective-permute-start(bf16[256,256]{1,0:T(8,128)(2,1)S(1)} %get-tuple-element.102), channel_id=1, source_target_pairs={{0,2},{1,3},{2,4},{3,5},{4,6},{5,7},{6,8},{7,9},{8,10},{9,11},{10,... | collective-permute-start | bytes 393224 | tf_op jit(solution)/shard_map/ppermute | solution.py:461
  91.5 6.5 %collective-permute-start.26 = (bf16[256,256]{1,0:T(8,128)(2,1)S(1)}, bf16[256,256]{1,0:T(8,128)(2,1)S(1)}, u32[]{:S(2)}, u32[]{:S(2)}) collective-permute-start(bf16[256,256]{1,0:T(8,128)(2,1)S(1)} %get-tuple-element.105), channel_id=1, source_target_pairs={{0,14},{1,15},{2,0},{3,1},{4,2},{5,3},{6,4},{7,5},{8,6},{9,7},{10,... | collective-permute-start | bytes 393224 | tf_op jit(solution)/shard_map/ppermute | solution.py:461
  94.2 6.5 %collective-permute-start.28 = (bf16[256,256]{1,0:T(8,128)(2,1)S(1)}, bf16[256,256]{1,0:T(8,128)(2,1)S(1)}, u32[]{:S(2)}, u32[]{:S(2)}) collective-permute-start(bf16[256,256]{1,0:T(8,128)(2,1)S(1)} %get-tuple-element.104), channel_id=1, source_target_pairs={{0,2},{1,3},{2,4},{3,5},{4,6},{5,7},{6,8},{7,9},{8,10},{9,11},{10,... | collective-permute-start | bytes 393224 | tf_op jit(solution)/shard_map/ppermute | solution.py:461
  94.2 6.5 %collective-permute-start.30 = (bf16[256,256]{1,0:T(8,128)(2,1)S(1)}, bf16[256,256]{1,0:T(8,128)(2,1)S(1)}, u32[]{:S(2)}, u32[]{:S(2)}) collective-permute-start(bf16[256,256]{1,0:T(8,128)(2,1)S(1)} %get-tuple-element.103), channel_id=1, source_target_pairs={{0,14},{1,15},{2,0},{3,1},{4,2},{5,3},{6,4},{7,5},{8,6},{9,7},{10,... | collective-permute-start | bytes 393224 | tf_op jit(solution)/shard_map/ppermute | solution.py:461
  100.9 6.9 %collective-permute-start.29 = (bf16[256,256]{1,0:T(8,128)(2,1)S(1)}, bf16[256,256]{1,0:T(8,128)(2,1)S(1)}, u32[]{:S(2)}, u32[]{:S(2)}) collective-permute-start(bf16[256,256]{1,0:T(8,128)(2,1)S(1)} %get-tuple-element.100), channel_id=1, source_target_pairs={{0,2},{1,3},{2,4},{3,5},{4,6},{5,7},{6,8},{7,9},{8,10},{9,11},{10,... | collective-permute-start | bytes 393224 | tf_op jit(solution)/shard_map/ppermute | solution.py:461
  101.0 6.8 %collective-permute-start.31 = (bf16[256,256]{1,0:T(8,128)(2,1)S(1)}, bf16[256,256]{1,0:T(8,128)(2,1)S(1)}, u32[]{:S(2)}, u32[]{:S(2)}) collective-permute-start(bf16[256,256]{1,0:T(8,128)(2,1)S(1)} %get-tuple-element.99), channel_id=1, source_target_pairs={{0,14},{1,15},{2,0},{3,1},{4,2},{5,3},{6,4},{7,5},{8,6},{9,7},{10,... | collective-permute-start | bytes 393224 | tf_op jit(solution)/shard_map/ppermute | solution.py:461
  104.2 6.2 %collective-permute-start.25 = (bf16[256,256]{1,0:T(8,128)(2,1)S(1)}, bf16[256,256]{1,0:T(8,128)(2,1)S(1)}, u32[]{:S(2)}, u32[]{:S(2)}) collective-permute-start(bf16[256,256]{1,0:T(8,128)(2,1)S(1)} %get-tuple-element.98), channel_id=1, source_target_pairs={{0,2},{1,3},{2,4},{3,5},{4,6},{5,7},{6,8},{7,9},{8,10},{9,11},{10,... | collective-permute-start | bytes 393224 | tf_op jit(solution)/shard_map/ppermute | solution.py:461
  104.2 6.2 %collective-permute-start.27 = (bf16[256,256]{1,0:T(8,128)(2,1)S(1)}, bf16[256,256]{1,0:T(8,128)(2,1)S(1)}, u32[]{:S(2)}, u32[]{:S(2)}) collective-permute-start(bf16[256,256]{1,0:T(8,128)(2,1)S(1)} %get-tuple-element.101), channel_id=1, source_target_pairs={{0,14},{1,15},{2,0},{3,1},{4,2},{5,3},{6,4},{7,5},{8,6},{9,7},{10,... | collective-permute-start | bytes 393224 | tf_op jit(solution)/shard_map/ppermute | solution.py:461
  107.9 5.1 %collective-permute-start.32 = (bf16[256,256]{1,0:T(8,128)(2,1)S(1)}, bf16[256,256]{1,0:T(8,128)(2,1)S(1)}, u32[]{:S(2)}, u32[]{:S(2)}) collective-permute-start(bf16[256,256]{1,0:T(8,128)(2,1)S(1)} %fusion.5), channel_id=1, source_target_pairs={{0,16},{1,17},{2,18},{3,19},{4,20},{5,21},{6,22},{7,23},{8,24},{9,... | collective-permute-start | bytes 393224 | tf_op jit(solution)/shard_map/ppermute | solution.py:511

commit v6 on v5

--- a/solution.py
+++ b/solution.py
@@ -31,6 +31,8 @@
 
 CORE_SWAP = [(i, i ^ 1) for i in range(N_CHAN)]
 X_SWAP = [(i, i ^ 16) for i in range(N_CHAN)]
+FAR_STEPS = (4, 3, 5)
+NEAR_STEPS = (2, 6, 1, 7, 0)
 X_HALF_SWAP = [(i, i ^ 1) for i in range(N_CTX)]
 Y_STEPS = (1, -1, 2)
 Z_GROUPS = [[x * 16 + z * 2 + c for z in range(N_Z)] for x in range(2) for c in range(2)]
@@ -221,16 +223,19 @@
     own = lax.axis_index("ctx")
     table_refs, refs = refs[:N_CTX], refs[N_CTX:]
     sources, refs = refs[:7], refs[7:]
-    row_ref, tap_ref, out_ref, grad_proj_ref, own_ref, other_ref = refs[:6]
-    raw_ref, tapped_ref, id_ref, grad_ref, side_ref, fwd_ref, weight_ref, sems = refs[6:]
+    row_ref, tap_ref, out_ref, grad_proj_ref, own_ref, other_ref, ahead_ref = refs[:7]
+    raw_ref, tapped_ref, id_ref, grad_ref, side_ref, fwd_ref, weight_ref, sems = refs[7:]
     copies = []
     for n in range(N_CTX):
         target = grad_ref.at[source_of(own, n)]
         copies.append(pltpu.make_async_copy(sources[n // 2].at[n % 2], target, sems.at[n]))
     copies.append(pltpu.make_async_copy(sources[4], side_ref, sems.at[N_CTX]))
     copies.append(pltpu.make_async_copy(sources[5], fwd_ref, sems.at[N_CTX + 1]))
-    far_z = (place_of("z") + N_Z // 2) & (N_Z - 1)
-    copies.append(pltpu.make_async_copy(sources[6].at[:, :, far_z], weight_ref.at[0], sems.at[N_CTX + 2]))
+    for n, step in enumerate(FAR_STEPS + NEAR_STEPS):
+        z = (place_of("z") + step) & (N_Z - 1)
+        far = n < len(FAR_STEPS)
+        target = weight_ref.at[n] if far else ahead_ref.at[n - len(FAR_STEPS)]
+        copies.append(pltpu.make_async_copy(sources[6].at[:, :, z], target, sems.at[N_CTX + 2 + n]))
     for copy in copies:
         copy.start()
     table = jnp.concatenate([ref[...].astype(F32) for ref in table_refs], axis=0).T.astype(BF16)
@@ -351,8 +356,14 @@
         for tap in (1, 2):
             total += tap_ref[rows, tap : tap + 1] * grads[:, tap : tap + BLOCK]
         grad_proj_ref[rows, :] = total.astype(BF16)
-    copies[N_CTX + 2].wait()
-    back_step(0, weight_ref, grad_proj_ref, own_ref, other_ref)
+    for copy in copies[N_CTX + 2 :]:
+        copy.wait()
+
+    def far_step(n, carried):
+        back_step(n, weight_ref, grad_proj_ref, own_ref, other_ref)
+        return carried
+
+    lax.fori_loop(0, len(FAR_STEPS), far_step, 0)
 
 
 def mix(pieces, grads, tables, weight):
@@ -363,11 +374,12 @@
         out_shape=(
             jax.ShapeDtypeStruct((BLOCK, BLOCK), BF16),
             jax.ShapeDtypeStruct((3 * BLOCK, BLOCK), BF16),
-            jax.ShapeDtypeStruct((1, 2, BLOCK, BLOCK), BF16),
-            jax.ShapeDtypeStruct((1, 2, BLOCK, BLOCK), BF16),
+            jax.ShapeDtypeStruct((len(FAR_STEPS), 2, BLOCK, BLOCK), BF16),
+            jax.ShapeDtypeStruct((len(FAR_STEPS), 2, BLOCK, BLOCK), BF16),
+            jax.ShapeDtypeStruct((len(NEAR_STEPS), 3, 2, 2, BLOCK, BLOCK), BF16),
         ),
         in_specs=[vmem] * N_CTX + [pl.BlockSpec(memory_space=pl.ANY)] * 7 + [vmem] * 2,
-        out_specs=(vmem,) * 4,
+        out_specs=(vmem,) * 5,
         scratch_shapes=[
             pltpu.VMEM((3 * BLOCK, 2 * BLOCK), F32),
             pltpu.VMEM((3 * BLOCK, 3 * VOCAB), BF16),
@@ -375,52 +387,38 @@
             pltpu.VMEM((N_CTX, BLOCK + EXTRA, BLOCK), BF16),
             pltpu.VMEM((BLOCK, SIDE), BF16),
             pltpu.VMEM((GROUPS, BLOCK, BLOCK), BF16),
-            pltpu.VMEM((1, 3, 2, 2, BLOCK, BLOCK), BF16),
-            pltpu.SemaphoreType.DMA((N_CTX + 3,)),
+            pltpu.VMEM((len(FAR_STEPS), 3, 2, 2, BLOCK, BLOCK), BF16),
+            pltpu.SemaphoreType.DMA((N_CTX + 2 + N_Z,)),
         ],
-        compiler_params=pltpu.CompilerParams(vmem_limit_bytes=47 << 20),
+        compiler_params=pltpu.CompilerParams(vmem_limit_bytes=36 << 20),
         cost_estimate=pl.CostEstimate(flops=3 << 30, bytes_accessed=8 << 20, transcendentals=1 << 16),
         name="mixer",
     )(*pieces, *grads, side, fwd, weight, row, taps)
 
 
-def back_kernel(step_ref, grad_ref, weight_ref, own_ref, other_ref, held_ref, sems):
-    count = own_ref.shape[0]
-
-    def copy(n):
-        z = (place_of("z") + step_ref[n]) & (N_Z - 1)
-        return pltpu.make_async_copy(weight_ref.at[:, :, z], held_ref.at[n], sems.at[n])
-
-    for n in range(count):
-        copy(n).start()
-
+def back_kernel(grad_ref, held_ref, own_ref, other_ref):
     def one_step(n, carried):
-        copy(n).wait()
         back_step(n, held_ref, grad_ref, own_ref, other_ref)
         return carried
 
-    lax.fori_loop(0, count, one_step, 0)
-
-
-def back_project(grad_proj, weight, steps):
+    lax.fori_loop(0, own_ref.shape[0], one_step, 0)
+
+
+def back_project(grad_proj, held):
     vmem = pl.BlockSpec(memory_space=pltpu.VMEM)
-    count = len(steps)
+    count = held.shape[0]
     part = jax.ShapeDtypeStruct((count, 2, BLOCK, BLOCK), BF16)
     return pl.pallas_call(
         back_kernel,
         out_shape=(part, part),
-        in_specs=[pl.BlockSpec(memory_space=pltpu.SMEM), vmem, pl.BlockSpec(memory_space=pltpu.HBM)],
-        out_specs=(vmem, vmem),
-        scratch_shapes=[
-            pltpu.VMEM((count, 3, 2, 2, BLOCK, BLOCK), BF16),
-            pltpu.SemaphoreType.DMA((count,)),
-        ],
-        compiler_params=pltpu.CompilerParams(vmem_limit_bytes=50 << 20),
+        in_specs=[vmem] * 2,
+        out_specs=(vmem,) * 2,
+        compiler_params=pltpu.CompilerParams(vmem_limit_bytes=4 << 20),
         cost_estimate=pl.CostEstimate(
             flops=2 * 256 * 768 * 1024 * count, bytes_accessed=count << 21, transcendentals=0
         ),
         name="back_project",
-    )(jnp.asarray(steps, jnp.int32), grad_proj, weight)
+    )(grad_proj, held)
 
 
 def project_features(rows, weight, pair):
@@ -461,54 +459,26 @@
     return lax.ppermute(value.astype(BF16), "chan", z_shift(by))
 
 
-def reduce_chan(far_parts, grad_proj, weight):
+def reduce_chan(own, other, grad_proj, held):
     terms = {}
-
-    def swap(parts):
-        return parts[0], lax.ppermute(parts[1], "chan", CORE_SWAP)
 
     def add_terms(steps, own, swapped):
         for n, step in enumerate(steps):
-            for half in range(2):
-                terms[step, half] = own[n, half].astype(F32) + swapped[n, half].astype(F32)
-
-    def arrive(values, tied):
-        values, tied = lax.optimization_barrier((values, tied))
-        return values, tied
-
-    def send(values):
-        return {(half, by): moved(value, by) for (half, by), value in values.items()}
-
-    own, swapped = swap(far_parts)
-    near = back_project(grad_proj, weight, (3, 5))
-    (swapped, near) = lax.optimization_barrier((swapped, near))
-    add_terms((4,), own, swapped)
-    ways = {1: (1, -1), 0: (-1, 1)}
-    chain = send({(half, ways[half][0]): terms[4, half] for half in (1, 0)})
-    grad_proj, near = lax.optimization_barrier((grad_proj, near))
-    near_own, near_swapped = swap(near)
-    middle = back_project(grad_proj, weight, (2, 6))
-    arrived, middle = arrive(chain, middle)
-    add_terms((3, 5), near_own, near_swapped)
-    middle_own, middle_swapped = swap(middle)
-    chain = {}
-    for half in (1, 0):
-        long, short = ways[half]
-        chain[half, long] = terms[(3 * long) % 8, half] + arrived[half, long].astype(F32)
-        chain[half, short] = terms[(3 * short) % 8, half]
-    chain = send(chain)
-    grad_proj, middle_own = lax.optimization_barrier((grad_proj, middle_own))
-    last = back_project(grad_proj, weight, (1, 7, 0))
-    arrived, last = arrive(chain, last)
-    add_terms((2, 6), middle_own, middle_swapped)
-    last_own, last_swapped = swap(last)
-    chain = send({(half, by): value.astype(F32) + terms[(2 * by) % 8, half] for (half, by), value in arrived.items()})
-    add_terms((1, 7, 0), last_own, last_swapped)
-    chain = send({(half, by): value.astype(F32) + terms[by % 8, half] for (half, by), value in chain.items()})
-    far_half, near_half = (
-        terms[0, half] + chain[half, 1].astype(F32) + chain[half, -1].astype(F32) for half in (1, 0)
-    )
-    total = near_half + lax.ppermute(far_half.astype(BF16), "chan", X_SWAP).astype(F32)
+            terms[step] = own[n].astype(F32) + swapped[n].astype(F32)
+
+    swapped = lax.ppermute(other, "chan", CORE_SWAP)
+    near_own, near_other = back_project(grad_proj, held)
+    swapped, near_own, near_other = lax.optimization_barrier((swapped, near_own, near_other))
+    add_terms(FAR_STEPS, own, swapped)
+    add_terms(NEAR_STEPS, near_own, lax.ppermute(near_other, "chan", CORE_SWAP))
+    ahead, behind = moved(terms[4][0], 1).astype(F32), moved(terms[4][1], -1).astype(F32)
+    ahead = jnp.stack([terms[3][0] + ahead, terms[3][1]])
+    behind = jnp.stack([terms[5][0], terms[5][1] + behind])
+    for near, other in ((2, 6), (1, 7)):
+        ahead = terms[near] + moved(ahead, 1).astype(F32)
+        behind = terms[other] + moved(behind, -1).astype(F32)
+    total = terms[0] + moved(ahead, 1).astype(F32) + moved(behind, -1).astype(F32)
+    total = total[0] + lax.ppermute(total[1].astype(BF16), "chan", X_SWAP).astype(F32)
     return total.astype(BF16)
 
 
@@ -521,8 +491,8 @@
     pieces = gather_ctx(part)
     gains = modal_residues * jnp.sqrt(-jnp.expm1(-2.0 * modal_rates))
     tables = make_tables(modal_rates, gains, feat_taps)
-    output, grad_proj, *far_parts = mix(pieces, grads, tables, weight)
-    return (output, reduce_chan(far_parts, grad_proj, weight).T)
+    output, grad_proj, own, other, held = mix(pieces, grads, tables, weight)
+    return (output, reduce_chan(own, other, grad_proj, held).T)
 
 
 def solution(mesh):

time: 115 us -> 119 us (1.035)
  waiting for transfers between devices: 22.5 us -> 44 us
  starting transfers between devices: 49.8 us -> 38.8 us
  Pallas kernels: 35.6 us -> 29.8 us
    ppermute x14 -> x8, waiting for transfers between devices: 8.11 us -> 27.7 us  [moved(): return lax.ppermute(value.astype(BF16), 'chan', z_shift(by))]
    ppermute x14 -> x8, starting transfers between devices: 20.6 us -> 9.18 us  [moved(): return lax.ppermute(value.astype(BF16), 'chan', z_shift(by))]
    pallas_call x3 -> x1, Pallas kernels: 10 us -> 2.86 us  [back_project(): pl.pallas_call(back_kernel, out_shape=(part, part), in_specs=[vmem] * 2,...]
    ppermute x5 -> x3, waiting for transfers between devices: 2.58 us -> 4.76 us  [the longest x1 4.76 us: reduce_chan(): lax.ppermute(total[1].astype(BF16), 'chan', X_SWAP).astype(F32)]
    pallas_call x1, Pallas kernels: 12.6 us -> 13.9 us  [mix(): pl.pallas_call(mixer_kernel, out_shape=(jax.ShapeDtypeStruct((BLOCK, BLOC...]
    ppermute x3, starting transfers between devices: 3.34 us -> 4.56 us  [gather_pairs(): return [pair] + [lax.ppermute(pair, 'ctx', y_shift(by)) for by in Y_STEPS]]
    unnamed x19 -> x13, local copies, waits for them, and re-layouts: 3.32 us -> 3.3 us
  transfers between devices with their start and end apart: 34 -> 26, of which waited for: 10 -> 9; matrix products, arithmetic and copies ran while one was open for 0% -> 0% of each run, Pallas kernels for 19% -> 12%
where the time goes in v6:
time: 119 us; the launch traced here: 118 us
  waiting for transfers between devices  44 us (37%)
  starting transfers between devices  38.8 us (33%)
  Pallas kernels  29.8 us (25%)
  local copies, waits for them, and re-layouts  4.08 us (3%)
    ppermute x8, waiting for transfers between devices, moved(): return lax.ppermute(value.astype(BF16), 'chan', z_shift(by))  27.7 us
    pallas_call x1, Pallas kernels, mix(): pl.pallas_call(mixer_kernel, out_shape=(jax.ShapeDtypeStruct((BLOCK, BLOC...  13.9 us
    ppermute x8, starting transfers between devices, moved(): return lax.ppermute(value.astype(BF16), 'chan', z_shift(by))  9.18 us
    pallas_call x4, Pallas kernels, project(): pl.pallas_call(functools.partial(project_kernel, part, sums is None, read...  8.97 us
    all_to_all x1, starting transfers between devices, project_features(): lax.all_to_all(jnp.broadcast_to(rows[None], (N_Z,) + rows.shape), 'chan',...  8.47 us
    ppermute x6, starting transfers between devices, gather_ctx(): found += [lax.ppermute(piece, 'ctx', y_shift(by)) for by in Y_STEPS]  8.06 us
    all_to_all x1, waiting for transfers between devices, project_features(): lax.all_to_all(jnp.broadcast_to(rows[None], (N_Z,) + rows.shape), 'chan',...  7.08 us
    ppermute x1, waiting for transfers between devices, reduce_chan(): lax.ppermute(total[1].astype(BF16), 'chan', X_SWAP).astype(F32)  4.76 us
  transfers between devices with their start and end apart: 26, of which 9 were waited for; matrix products, arithmetic and copies ran while one was open for 0% of the time, Pallas kernels for 12%

profile of v6, /device:TPU:24, one launch (start us, length us, event | category | flops | bytes accessed | tf_op | source)
XLA Modules:
  0.0 118.5 jit_solution(16916683273400313706)
XLA Ops:
  0.6 0.9 copy-done
  1.6 0.7 broadcast_in_dim.2
  2.3 8.5 %all-to-all-start = ((bf16[8,64,256]{2,1,0:T(8,128)(2,1)}), bf16[8,64,256]{2,1,0:T(8,128)(2,1)S(1)}, u32[]{:S(2)}, u32[]{:S(2)}) async-start(bf16[8,64,256]{2,1,0:T(8,128)(2,1)} %broadcast_in_dim.2), calls=%async_computation | async-start | bytes 524288 | tf_op jit(solution)/shard_map/all_to_all | solution.py:425
  10.8 0.9 copy-done.1
  11.7 0.7 copy-done.3
  12.4 0.1 payload.1
  12.5 3.1 %collective-permute-start.2 = (bf16[272,256]{1,0:T(8,128)(2,1)S(1)}, bf16[272,256]{1,0:T(8,128)(2,1)S(1)}, u32[]{:S(2)}, u32[]{:S(2)}) collective-permute-start(bf16[272,256]{1,0:T(8,128)(2,1)S(1)} %payload.1), channel_id=1, source_target_pairs={{0,32},{32,0},{64,96},{96,64},{128,160},{160,128},{192,224},{224,1... | collective-permute-start | bytes 417800 | tf_op jit(solution)/shard_map/ppermute | solution.py:451
  15.6 7.1 %all-to-all-done.refs_0_ = bf16[8,64,256]{2,1,0:T(8,128)(2,1)S(1)} async-done(((bf16[8,64,256]{2,1,0:T(8,128)(2,1)}), bf16[8,64,256]{2,1,0:T(8,128)(2,1)S(1)}, u32[]{:S(2)}, u32[]{:S(2)}) %all-to-all-start) | async-done | bytes 262176 | tf_op jit(solution)/shard_map/all_to_all | solution.py:425
  22.7 1.5 %collective-permute-start = (bf16[8,64,256]{2,1,0:T(8,128)(2,1)S(1)}, bf16[8,64,256]{2,1,0:T(8,128)(2,1)S(1)}, u32[]{:S(2)}, u32[]{:S(2)}) collective-permute-start(bf16[8,64,256]{2,1,0:T(8,128)(2,1)S(1)} %all-to-all-done.refs_0_), channel_id=1, source_target_pairs={{0,16},{1,17},{2,18},{3,19},{4,20},{5,21},{6,22},{7,23},{8,24},{9,... | collective-permute-start | bytes 786440 | tf_op jit(solution)/shard_map/ppermute | solution.py:428
  24.2 1.3 %collective-permute-start.6 = (bf16[2,272,256]{2,1,0:T(8,128)(2,1)S(1)}, bf16[2,272,256]{2,1,0:T(8,128)(2,1)S(1)}, u32[]{:S(2)}, u32[]{:S(2)}) collective-permute-start(bf16[2,272,256]{2,1,0:T(8,128)(2,1)S(1)} %pad_maximum_fusion.refs_8_), channel_id=1, source_target_pairs={{0,128},{32,160},{64,192},{96,224},{128,0},{160,32},{192,64},{224,... | collective-permute-start | bytes 835592 | tf_op jit(solution)/shard_map/ppermute | solution.py:455
  25.5 3.2 %collective-permute-start.4 = (bf16[2,272,256]{2,1,0:T(8,128)(2,1)S(1)}, bf16[2,272,256]{2,1,0:T(8,128)(2,1)S(1)}, u32[]{:S(2)}, u32[]{:S(2)}) collective-permute-start(bf16[2,272,256]{2,1,0:T(8,128)(2,1)S(1)} %pad_maximum_fusion.refs_8_), channel_id=1, source_target_pairs={{0,64},{32,96},{64,128},{96,160},{128,192},{160,224},{192,0},{224,... | collective-permute-start | bytes 835592 | tf_op jit(solution)/shard_map/ppermute | solution.py:455
  28.7 3.8 %project.4 = (f32[64,768]{1,0:T(8,128)S(1)}, bf16[3,8,256,256]{3,2,1,0:T(8,128)(2,1)S(1)}, bf16[3,8,256,256]{3,2,1,0:T(8,128)(2,1)S(1)}) custom-call(bf16[8,64,256]{2,1,0:T(8,128)(2,1)S(1)} %all-to-all-done.refs_0_, bf16[3,2,8,2,256,256]{5,4,3,2,1,0:T(8,128)(2,1)} %bitcast.68), custom_call_target="tpu_custom_call" | custom-call | flops 201326592 | bytes 9437184 | tf_op jit(solution)/shard_map/project/pallas_call | solution.py:192
  32.5 3.0 %project.5.refs_2_ = f32[64,768]{1,0:T(8,128)S(1)} custom-call(bf16[8,64,256]{2,1,0:T(8,128)(2,1)S(1)} %collective-permute-done.1.refs_0_, bf16[3,2,8,2,256,256]{5,4,3,2,1,0:T(8,128)(2,1)} %bitcast.69, f32[64,768]{1,0:T(8,128)S(1)} %get-tuple-element.32.refs_2_), custom_call_target="tpu_custom_call" | custom-call | flops 201326592 | bytes 3145728 | tf_op jit(solution)/shard_map/project/pallas_call | solution.py:192
  35.6 0.1 collective-permute-start.3
  35.7 1.1 project.6.refs_2_
  36.8 3.8 %collective-permute-done.5.refs_10_ = bf16[2,272,256]{2,1,0:T(8,128)(2,1)S(1)} collective-permute-done((bf16[2,272,256]{2,1,0:T(8,128)(2,1)S(1)}, bf16[2,272,256]{2,1,0:T(8,128)(2,1)S(1)}, u32[]{:S(2)}, u32[]{:S(2)}) %collective-permute-start.5) | collective-permute-done | bytes 278560 | tf_op jit(solution)/shard_map/ppermute | solution.py:455
  40.6 1.1 project.7.refs_0_
  41.7 2.8 %collective-permute-start.7 = (bf16[64,768]{1,0:T(8,128)(2,1)S(1)}, bf16[64,768]{1,0:T(8,128)(2,1)S(1)}, u32[]{:S(2)}, u32[]{:S(2)}) collective-permute-start(bf16[64,768]{1,0:T(8,128)(2,1)S(1)} %project.7.refs_0_), channel_id=1, source_target_pairs={{0,32},{32,0},{64,96},{96,64},{128,160},{160,128},{192,224},{224,1... | collective-permute-start | bytes 294920 | tf_op jit(solution)/shard_map/ppermute | solution.py:443
  44.5 1.4 %collective-permute-start.12 = (bf16[64,768]{1,0:T(8,128)(2,1)S(1)}, bf16[64,768]{1,0:T(8,128)(2,1)S(1)}, u32[]{:S(2)}, u32[]{:S(2)}) collective-permute-start(bf16[64,768]{1,0:T(8,128)(2,1)S(1)} %project.7.refs_0_), channel_id=1, source_target_pairs={{0,128},{32,160},{64,192},{96,224},{128,0},{160,32},{192,64},{224,... | collective-permute-start | bytes 294920 | tf_op jit(solution)/shard_map/ppermute | solution.py:446
  45.9 0.1 collective-permute-start.10
  45.9 3.1 %collective-permute-start.8 = (bf16[64,768]{1,0:T(8,128)(2,1)S(1)}, bf16[64,768]{1,0:T(8,128)(2,1)S(1)}, u32[]{:S(2)}, u32[]{:S(2)}) collective-permute-start(bf16[64,768]{1,0:T(8,128)(2,1)S(1)} %project.7.refs_0_), channel_id=1, source_target_pairs={{0,64},{32,96},{64,128},{96,160},{128,192},{160,224},{192,0},{224,... | collective-permute-start | bytes 294920 | tf_op jit(solution)/shard_map/ppermute | solution.py:446
  49.1 1.0 collective-permute-start.13
  50.0 0.7 collective-permute-start.11
  50.8 0.7 collective-permute-done.12.refs_6_
  51.5 1.8 %collective-permute-start.9 = (bf16[64,768]{1,0:T(8,128)(2,1)S(1)}, bf16[64,768]{1,0:T(8,128)(2,1)S(1)}, u32[]{:S(2)}, u32[]{:S(2)}) collective-permute-start(bf16[64,768]{1,0:T(8,128)(2,1)S(1)} %collective-permute-done.7.refs_1_), channel_id=1, source_target_pairs={{0,64},{32,96},{64,128},{96,160},{128,192},{160,224},{192,0},{224,... | collective-permute-start | bytes 294920 | tf_op jit(solution)/shard_map/ppermute | solution.py:446
  53.3 3.9 %filter_tables.1 = (bf16[16,256,256]{2,1,0:T(8,128)(2,1)S(1)}, bf16[256,1152]{1,0:T(8,128)(2,1)S(1)}, f32[2,256]{1,0:T(2,128)S(1)}, f32[768,3]{1,0:T(8,128)S(1)}) custom-call(f32[16,16]{1,0:T(8,128)S(1)} %copy-done.2, f32[16,16]{1,0:T(8,128)S(1)} %sqrt_multiply_fusion.gain_ref, f32[3,3,256]{2,1,0:T(4,128)S(1)} %copy-done.4), custom_call_target="tpu_custom_call" | custom-call | flops 402653184 | bytes 5242880 | tf_op jit(solution)/shard_map/filter_tables/pallas_call | solution.py:142
  57.3 13.9 %mixer.1 = (bf16[256,256]{1,0:T(8,128)(2,1)}, bf16[768,256]{1,0:T(8,128)(2,1)S(1)}, bf16[3,2,256,256]{3,2,1,0:T(8,128)(2,1)S(1)}, bf16[3,2,256,256]{3,2,1,0:T(8,...) custom-call(bf16[64,768]{1,0:T(8,128)(2,1)S(1)} %project.7.refs_0_, bf16[64,768]{1,0:T(8,128)(2,1)S(1)} %collective-permute-done.7.refs_1_, ...), custom_call_target="tpu_custom_call" | custom-call | flops 3221225472 | bytes 8388608 | tf_op jit(solution)/shard_map/mixer/pallas_call | solution.py:372
  71.2 0.1 collective-permute-start.14
  71.3 2.9 %back_project.1 = (bf16[5,2,256,256]{3,2,1,0:T(8,128)(2,1)S(1)}, bf16[5,2,256,256]{3,2,1,0:T(8,128)(2,1)S(1)}) custom-call(bf16[768,256]{1,0:T(8,128)(2,1)S(1)} %get-tuple-element.52.grad_ref, bf16[5,3,2,2,256,256]{5,4,3,2,1,0:T(8,128)(2,1)S(1)} %get-tuple-element.53.held_ref), custom_call_target="tpu_custom_call" | custom-call | flops 2013265920 | bytes 10485760 | tf_op jit(solution)/shard_map/back_project/pallas_call | solution.py:411
  74.2 0.6 collective-permute-start.15
  74.8 0.2 convert_add_fusion.1
  75.0 0.6 collective-permute-start.16
  75.6 2.7 %collective-permute-start.20 = (bf16[256,256]{1,0:T(8,128)(2,1)S(1)}, bf16[256,256]{1,0:T(8,128)(2,1)S(1)}, u32[]{:S(2)}, u32[]{:S(2)}) collective-permute-start(bf16[256,256]{1,0:T(8,128)(2,1)S(1)} %get-tuple-element.68), channel_id=1, source_target_pairs={{0,14},{1,15},{2,0},{3,1},{4,2},{5,3},{6,4},{7,5},{8,6},{9,7},{10,... | collective-permute-start | bytes 393224 | tf_op jit(solution)/shard_map/ppermute | solution.py:459
  78.3 3.3 %collective-permute-done.16 = bf16[256,256]{1,0:T(8,128)(2,1)S(1)} collective-permute-done((bf16[256,256]{1,0:T(8,128)(2,1)S(1)}, bf16[256,256]{1,0:T(8,128)(2,1)S(1)}, u32[]{:S(2)}, u32[]{:S(2)}) %collective-permute-start.16) | collective-permute-done | bytes 131104 | tf_op jit(solution)/shard_map/ppermute | solution.py:459
  81.9 3.3 %collective-permute-start.21 = (bf16[2,256,256]{2,1,0:T(8,128)(2,1)S(1)}, bf16[2,256,256]{2,1,0:T(8,128)(2,1)S(1)}, u32[]{:S(2)}, u32[]{:S(2)}) collective-permute-start(bf16[2,256,256]{2,1,0:T(8,128)(2,1)S(1)} %pad_maximum_fusion.2), channel_id=1, source_target_pairs={{0,14},{1,15},{2,0},{3,1},{4,2},{5,3},{6,4},{7,5},{8,6},{9,7},{10,... | collective-permute-start | bytes 786440 | tf_op jit(solution)/shard_map/ppermute | solution.py:459
  85.2 5.2 %collective-permute-done.17 = bf16[2,256,256]{2,1,0:T(8,128)(2,1)S(1)} collective-permute-done((bf16[2,256,256]{2,1,0:T(8,128)(2,1)S(1)}, bf16[2,256,256]{2,1,0:T(8,128)(2,1)S(1)}, u32[]{:S(2)}, u32[]{:S(2)}) %collective-permute-start.17) | collective-permute-done | bytes 262176 | tf_op jit(solution)/shard_map/ppermute | solution.py:459
  90.4 0.1 fusion.2
  90.6 7.6 %collective-permute-done.18 = bf16[2,256,256]{2,1,0:T(8,128)(2,1)S(1)} collective-permute-done((bf16[2,256,256]{2,1,0:T(8,128)(2,1)S(1)}, bf16[2,256,256]{2,1,0:T(8,128)(2,1)S(1)}, u32[]{:S(2)}, u32[]{:S(2)}) %collective-permute-start.18) | collective-permute-done | bytes 262176 | tf_op jit(solution)/shard_map/ppermute | solution.py:459
  98.3 0.2 fusion.3
  98.6 2.0 %collective-permute-start.19 = (bf16[2,256,256]{2,1,0:T(8,128)(2,1)S(1)}, bf16[2,256,256]{2,1,0:T(8,128)(2,1)S(1)}, u32[]{:S(2)}, u32[]{:S(2)}) collective-permute-start(bf16[2,256,256]{2,1,0:T(8,128)(2,1)S(1)} %get-tuple-element.62), channel_id=1, source_target_pairs={{0,2},{1,3},{2,4},{3,5},{4,6},{5,7},{6,8},{7,9},{8,10},{9,11},{10,... | collective-permute-start | bytes 786440 | tf_op jit(solution)/shard_map/ppermute | solution.py:459
  100.6 5.3 %collective-permute-done.22 = bf16[2,256,256]{2,1,0:T(8,128)(2,1)S(1)} collective-permute-done((bf16[2,256,256]{2,1,0:T(8,128)(2,1)S(1)}, bf16[2,256,256]{2,1,0:T(8,128)(2,1)S(1)}, u32[]{:S(2)}, u32[]{:S(2)}) %collective-permute-start.22) | collective-permute-done | bytes 262176 | tf_op jit(solution)/shard_map/ppermute | solution.py:459
  105.9 0.1 fusion.1
  106.0 0.3 collective-permute-start.23
  106.3 6.1 %collective-permute-done.23 = bf16[2,256,256]{2,1,0:T(8,128)(2,1)S(1)} collective-permute-done((bf16[2,256,256]{2,1,0:T(8,128)(2,1)S(1)}, bf16[2,256,256]{2,1,0:T(8,128)(2,1)S(1)}, u32[]{:S(2)}, u32[]{:S(2)}) %collective-permute-start.23) | collective-permute-done | bytes 262176 | tf_op jit(solution)/shard_map/ppermute | solution.py:459
  112.5 0.1 fusion.4
  112.6 0.3 collective-permute-start.24
  112.9 4.8 %collective-permute-done.24 = bf16[256,256]{1,0:T(8,128)(2,1)S(1)} collective-permute-done((bf16[256,256]{1,0:T(8,128)(2,1)S(1)}, bf16[256,256]{1,0:T(8,128)(2,1)S(1)}, u32[]{:S(2)}, u32[]{:S(2)}) %collective-permute-start.24) | collective-permute-done | bytes 131104 | tf_op jit(solution)/shard_map/ppermute | solution.py:481
  117.7 0.8 copy.9
  (43 shorter events, 0.6 us)
Async XLA Ops:
  0.6 1.0 copy-start
  2.3 20.3 %all-to-all-start = ((bf16[8,64,256]{2,1,0:T(8,128)(2,1)}), bf16[8,64,256]{2,1,0:T(8,128)(2,1)S(1)}, u32[]{:S(2)}, u32[]{:S(2)}) async-start(bf16[8,64,256]{2,1,0:T(8,128)(2,1)} %broadcast_in_dim.2), calls=%async_computation | async-start | bytes 524288 | tf_op jit(solution)/shard_map/all_to_all | solution.py:425
  10.8 0.9 copy-start.1
  11.7 0.7 copy-start.3
  12.5 11.7 %collective-permute-start.2 = (bf16[272,256]{1,0:T(8,128)(2,1)S(1)}, bf16[272,256]{1,0:T(8,128)(2,1)S(1)}, u32[]{:S(2)}, u32[]{:S(2)}) collective-permute-start(bf16[272,256]{1,0:T(8,128)(2,1)S(1)} %payload.1), channel_id=1, source_target_pairs={{0,32},{32,0},{64,96},{96,64},{128,160},{160,128},{192,224},{224,1... | collective-permute-start | bytes 417800 | tf_op jit(solution)/shard_map/ppermute | solution.py:451
  22.6 9.9 %collective-permute-start.1 = (bf16[8,64,256]{2,1,0:T(8,128)(2,1)S(1)}, bf16[8,64,256]{2,1,0:T(8,128)(2,1)S(1)}, u32[]{:S(2)}, u32[]{:S(2)}) collective-permute-start(bf16[8,64,256]{2,1,0:T(8,128)(2,1)S(1)} %all-to-all-done.refs_0_), channel_id=1, source_target_pairs={{0,1},{1,0},{2,3},{3,2},{4,5},{5,4},{6,7},{7,6},{8,9},{9,8},{10,11... | collective-permute-start | bytes 786440 | tf_op jit(solution)/shard_map/ppermute | solution.py:429
  22.7 12.9 %collective-permute-start = (bf16[8,64,256]{2,1,0:T(8,128)(2,1)S(1)}, bf16[8,64,256]{2,1,0:T(8,128)(2,1)S(1)}, u32[]{:S(2)}, u32[]{:S(2)}) collective-permute-start(bf16[8,64,256]{2,1,0:T(8,128)(2,1)S(1)} %all-to-all-done.refs_0_), channel_id=1, source_target_pairs={{0,16},{1,17},{2,18},{3,19},{4,20},{5,21},{6,22},{7,23},{8,24},{9,... | collective-permute-start | bytes 786440 | tf_op jit(solution)/shard_map/ppermute | solution.py:428
  24.2 12.6 %collective-permute-start.6 = (bf16[2,272,256]{2,1,0:T(8,128)(2,1)S(1)}, bf16[2,272,256]{2,1,0:T(8,128)(2,1)S(1)}, u32[]{:S(2)}, u32[]{:S(2)}) collective-permute-start(bf16[2,272,256]{2,1,0:T(8,128)(2,1)S(1)} %pad_maximum_fusion.refs_8_), channel_id=1, source_target_pairs={{0,128},{32,160},{64,192},{96,224},{128,0},{160,32},{192,64},{224,... | collective-permute-start | bytes 835592 | tf_op jit(solution)/shard_map/ppermute | solution.py:455
  25.5 15.0 %collective-permute-start.5 = (bf16[2,272,256]{2,1,0:T(8,128)(2,1)S(1)}, bf16[2,272,256]{2,1,0:T(8,128)(2,1)S(1)}, u32[]{:S(2)}, u32[]{:S(2)}) collective-permute-start(bf16[2,272,256]{2,1,0:T(8,128)(2,1)S(1)} %pad_maximum_fusion.refs_8_), channel_id=1, source_target_pairs={{0,192},{32,224},{64,0},{96,32},{128,64},{160,96},{192,128},{224,1... | collective-permute-start | bytes 835592 | tf_op jit(solution)/shard_map/ppermute | solution.py:455
  25.5 15.0 %collective-permute-start.4 = (bf16[2,272,256]{2,1,0:T(8,128)(2,1)S(1)}, bf16[2,272,256]{2,1,0:T(8,128)(2,1)S(1)}, u32[]{:S(2)}, u32[]{:S(2)}) collective-permute-start(bf16[2,272,256]{2,1,0:T(8,128)(2,1)S(1)} %pad_maximum_fusion.refs_8_), channel_id=1, source_target_pairs={{0,64},{32,96},{64,128},{96,160},{128,192},{160,224},{192,0},{224,... | collective-permute-start | bytes 835592 | tf_op jit(solution)/shard_map/ppermute | solution.py:455
  35.6 5.0 %collective-permute-start.3 = (bf16[8,64,256]{2,1,0:T(8,128)(2,1)S(1)}, bf16[8,64,256]{2,1,0:T(8,128)(2,1)S(1)}, u32[]{:S(2)}, u32[]{:S(2)}) collective-permute-start(bf16[8,64,256]{2,1,0:T(8,128)(2,1)S(1)} %collective-permute-done.refs_0_), channel_id=1, source_target_pairs={{0,1},{1,0},{2,3},{3,2},{4,5},{5,4},{6,7},{7,6},{8,9},{9,8},{10,11... | collective-permute-start | bytes 786440 | tf_op jit(solution)/shard_map/ppermute | solution.py:435
  40.5 12.8 %copy-start.2 = (f32[16,16]{1,0:T(8,128)S(1)}, f32[16,16]{1,0:T(8,128)}, u32[]{:S(2)}) copy-start(f32[16,16]{1,0:T(8,128)} %rate_ref) | copy-start | bytes 3076
  40.5 12.8 %copy-start.5 = (f32[16,16]{1,0:T(8,128)S(1)}, f32[16,16]{1,0:T(8,128)}, u32[]{:S(2)}) copy-start(f32[16,16]{1,0:T(8,128)} %param.12) | copy-start | bytes 3076
  40.6 12.8 %copy-start.4 = (f32[3,3,256]{2,1,0:T(4,128)S(1)}, f32[3,3,256]{2,1,0:T(4,128)}, u32[]{:S(2)}) copy-start(f32[3,3,256]{2,1,0:T(4,128)} %tap_ref.1) | copy-start | bytes 27652
  41.7 7.4 %collective-permute-start.7 = (bf16[64,768]{1,0:T(8,128)(2,1)S(1)}, bf16[64,768]{1,0:T(8,128)(2,1)S(1)}, u32[]{:S(2)}, u32[]{:S(2)}) collective-permute-start(bf16[64,768]{1,0:T(8,128)(2,1)S(1)} %project.7.refs_0_), channel_id=1, source_target_pairs={{0,32},{32,0},{64,96},{96,64},{128,160},{160,128},{192,224},{224,1... | collective-permute-start | bytes 294920 | tf_op jit(solution)/shard_map/ppermute | solution.py:443
  44.5 7.0 %collective-permute-start.12 = (bf16[64,768]{1,0:T(8,128)(2,1)S(1)}, bf16[64,768]{1,0:T(8,128)(2,1)S(1)}, u32[]{:S(2)}, u32[]{:S(2)}) collective-permute-start(bf16[64,768]{1,0:T(8,128)(2,1)S(1)} %project.7.refs_0_), channel_id=1, source_target_pairs={{0,128},{32,160},{64,192},{96,224},{128,0},{160,32},{192,64},{224,... | collective-permute-start | bytes 294920 | tf_op jit(solution)/shard_map/ppermute | solution.py:446
  45.9 11.4 %collective-permute-start.10 = (bf16[64,768]{1,0:T(8,128)(2,1)S(1)}, bf16[64,768]{1,0:T(8,128)(2,1)S(1)}, u32[]{:S(2)}, u32[]{:S(2)}) collective-permute-start(bf16[64,768]{1,0:T(8,128)(2,1)S(1)} %project.7.refs_0_), channel_id=1, source_target_pairs={{0,192},{32,224},{64,0},{96,32},{128,64},{160,96},{192,128},{224,1... | collective-permute-start | bytes 294920 | tf_op jit(solution)/shard_map/ppermute | solution.py:446
  45.9 11.3 %collective-permute-start.8 = (bf16[64,768]{1,0:T(8,128)(2,1)S(1)}, bf16[64,768]{1,0:T(8,128)(2,1)S(1)}, u32[]{:S(2)}, u32[]{:S(2)}) collective-permute-start(bf16[64,768]{1,0:T(8,128)(2,1)S(1)} %project.7.refs_0_), channel_id=1, source_target_pairs={{0,64},{32,96},{64,128},{96,160},{128,192},{160,224},{192,0},{224,... | collective-permute-start | bytes 294920 | tf_op jit(solution)/shard_map/ppermute | solution.py:446
  49.1 8.2 %collective-permute-start.13 = (bf16[64,768]{1,0:T(8,128)(2,1)S(1)}, bf16[64,768]{1,0:T(8,128)(2,1)S(1)}, u32[]{:S(2)}, u32[]{:S(2)}) collective-permute-start(bf16[64,768]{1,0:T(8,128)(2,1)S(1)} %collective-permute-done.7.refs_1_), channel_id=1, source_target_pairs={{0,128},{32,160},{64,192},{96,224},{128,0},{160,32},{192,64},{224,... | collective-permute-start | bytes 294920 | tf_op jit(solution)/shard_map/ppermute | solution.py:446
  50.0 7.2 %collective-permute-start.11 = (bf16[64,768]{1,0:T(8,128)(2,1)S(1)}, bf16[64,768]{1,0:T(8,128)(2,1)S(1)}, u32[]{:S(2)}, u32[]{:S(2)}) collective-permute-start(bf16[64,768]{1,0:T(8,128)(2,1)S(1)} %collective-permute-done.7.refs_1_), channel_id=1, source_target_pairs={{0,192},{32,224},{64,0},{96,32},{128,64},{160,96},{192,128},{224,1... | collective-permute-start | bytes 294920 | tf_op jit(solution)/shard_map/ppermute | solution.py:446
  51.5 5.8 %collective-permute-start.9 = (bf16[64,768]{1,0:T(8,128)(2,1)S(1)}, bf16[64,768]{1,0:T(8,128)(2,1)S(1)}, u32[]{:S(2)}, u32[]{:S(2)}) collective-permute-start(bf16[64,768]{1,0:T(8,128)(2,1)S(1)} %collective-permute-done.7.refs_1_), channel_id=1, source_target_pairs={{0,64},{32,96},{64,128},{96,160},{128,192},{160,224},{192,0},{224,... | collective-permute-start | bytes 294920 | tf_op jit(solution)/shard_map/ppermute | solution.py:446
  71.2 3.0 %collective-permute-start.14 = (bf16[3,2,256,256]{3,2,1,0:T(8,128)(2,1)S(1)}, bf16[3,2,256,256]{3,2,1,0:T(8,128)(2,1)S(1)}, u32[]{:S(2)}, u32[]{:S(2)}) collective-permute-start(bf16[3,2,256,256]{3,2,1,0:T(8,128)(2,1)S(1)} %get-tuple-element.51), channel_id=1, source_target_pairs={{0,1},{1,0},{2,3},{3,2},{4,5},{5,4},{6,7},{7,6},{8,9},{9,8},{10,11... | collective-permute-start | bytes 2359304 | tf_op jit(solution)/shard_map/ppermute | solution.py:469
  74.2 16.2 %collective-permute-start.15 = (bf16[5,2,256,256]{3,2,1,0:T(8,128)(2,1)S(1)}, bf16[5,2,256,256]{3,2,1,0:T(8,128)(2,1)S(1)}, u32[]{:S(2)}, u32[]{:S(2)}) collective-permute-start(bf16[5,2,256,256]{3,2,1,0:T(8,128)(2,1)S(1)} %get-tuple-element.57), channel_id=1, source_target_pairs={{0,1},{1,0},{2,3},{3,2},{4,5},{5,4},{6,7},{7,6},{8,9},{9,8},{10,11... | collective-permute-start | bytes 3932168 | tf_op jit(solution)/shard_map/ppermute | solution.py:473
  75.0 6.7 %collective-permute-start.16 = (bf16[256,256]{1,0:T(8,128)(2,1)S(1)}, bf16[256,256]{1,0:T(8,128)(2,1)S(1)}, u32[]{:S(2)}, u32[]{:S(2)}) collective-permute-start(bf16[256,256]{1,0:T(8,128)(2,1)S(1)} %get-tuple-element.67), channel_id=1, source_target_pairs={{0,2},{1,3},{2,4},{3,5},{4,6},{5,7},{6,8},{7,9},{8,10},{9,11},{10,... | collective-permute-start | bytes 393224 | tf_op jit(solution)/shard_map/ppermute | solution.py:459
  75.6 6.2 %collective-permute-start.20 = (bf16[256,256]{1,0:T(8,128)(2,1)S(1)}, bf16[256,256]{1,0:T(8,128)(2,1)S(1)}, u32[]{:S(2)}, u32[]{:S(2)}) collective-permute-start(bf16[256,256]{1,0:T(8,128)(2,1)S(1)} %get-tuple-element.68), channel_id=1, source_target_pairs={{0,14},{1,15},{2,0},{3,1},{4,2},{5,3},{6,4},{7,5},{8,6},{9,7},{10,... | collective-permute-start | bytes 393224 | tf_op jit(solution)/shard_map/ppermute | solution.py:459
  81.8 8.7 %collective-permute-start.17 = (bf16[2,256,256]{2,1,0:T(8,128)(2,1)S(1)}, bf16[2,256,256]{2,1,0:T(8,128)(2,1)S(1)}, u32[]{:S(2)}, u32[]{:S(2)}) collective-permute-start(bf16[2,256,256]{2,1,0:T(8,128)(2,1)S(1)} %pad_maximum_fusion.1), channel_id=1, source_target_pairs={{0,2},{1,3},{2,4},{3,5},{4,6},{5,7},{6,8},{7,9},{8,10},{9,11},{10,... | collective-permute-start | bytes 786440 | tf_op jit(solution)/shard_map/ppermute | solution.py:459
  81.9 8.7 %collective-permute-start.21 = (bf16[2,256,256]{2,1,0:T(8,128)(2,1)S(1)}, bf16[2,256,256]{2,1,0:T(8,128)(2,1)S(1)}, u32[]{:S(2)}, u32[]{:S(2)}) collective-permute-start(bf16[2,256,256]{2,1,0:T(8,128)(2,1)S(1)} %pad_maximum_fusion.2), channel_id=1, source_target_pairs={{0,14},{1,15},{2,0},{3,1},{4,2},{5,3},{6,4},{7,5},{8,6},{9,7},{10,... | collective-permute-start | bytes 786440 | tf_op jit(solution)/shard_map/ppermute | solution.py:459
  90.5 7.7 %collective-permute-start.18 = (bf16[2,256,256]{2,1,0:T(8,128)(2,1)S(1)}, bf16[2,256,256]{2,1,0:T(8,128)(2,1)S(1)}, u32[]{:S(2)}, u32[]{:S(2)}) collective-permute-start(bf16[2,256,256]{2,1,0:T(8,128)(2,1)S(1)} %fusion.2), channel_id=1, source_target_pairs={{0,2},{1,3},{2,4},{3,5},{4,6},{5,7},{6,8},{7,9},{8,10},{9,11},{10,... | collective-permute-start | bytes 786440 | tf_op jit(solution)/shard_map/ppermute | solution.py:459
  98.5 7.4 %collective-permute-start.22 = (bf16[2,256,256]{2,1,0:T(8,128)(2,1)S(1)}, bf16[2,256,256]{2,1,0:T(8,128)(2,1)S(1)}, u32[]{:S(2)}, u32[]{:S(2)}) collective-permute-start(bf16[2,256,256]{2,1,0:T(8,128)(2,1)S(1)} %get-tuple-element.63), channel_id=1, source_target_pairs={{0,14},{1,15},{2,0},{3,1},{4,2},{5,3},{6,4},{7,5},{8,6},{9,7},{10,... | collective-permute-start | bytes 786440 | tf_op jit(solution)/shard_map/ppermute | solution.py:459
  98.6 7.8 %collective-permute-start.19 = (bf16[2,256,256]{2,1,0:T(8,128)(2,1)S(1)}, bf16[2,256,256]{2,1,0:T(8,128)(2,1)S(1)}, u32[]{:S(2)}, u32[]{:S(2)}) collective-permute-start(bf16[2,256,256]{2,1,0:T(8,128)(2,1)S(1)} %get-tuple-element.62), channel_id=1, source_target_pairs={{0,2},{1,3},{2,4},{3,5},{4,6},{5,7},{6,8},{7,9},{8,10},{9,11},{10,... | collective-permute-start | bytes 786440 | tf_op jit(solution)/shard_map/ppermute | solution.py:459
  106.0 6.4 %collective-permute-start.23 = (bf16[2,256,256]{2,1,0:T(8,128)(2,1)S(1)}, bf16[2,256,256]{2,1,0:T(8,128)(2,1)S(1)}, u32[]{:S(2)}, u32[]{:S(2)}) collective-permute-start(bf16[2,256,256]{2,1,0:T(8,128)(2,1)S(1)} %fusion.1), channel_id=1, source_target_pairs={{0,14},{1,15},{2,0},{3,1},{4,2},{5,3},{6,4},{7,5},{8,6},{9,7},{10,... | collective-permute-start | bytes 786440 | tf_op jit(solution)/shard_map/ppermute | solution.py:459
  112.6 5.1 %collective-permute-start.24 = (bf16[256,256]{1,0:T(8,128)(2,1)S(1)}, bf16[256,256]{1,0:T(8,128)(2,1)S(1)}, u32[]{:S(2)}, u32[]{:S(2)}) collective-permute-start(bf16[256,256]{1,0:T(8,128)(2,1)S(1)} %fusion.16), channel_id=1, source_target_pairs={{0,16},{1,17},{2,18},{3,19},{4,20},{5,21},{6,22},{7,23},{8,24},{9,... | collective-permute-start | bytes 393224 | tf_op jit(solution)/shard_map/ppermute | solution.py:481

commit v7 on v6

--- a/solution.py
+++ b/solution.py
@@ -460,26 +460,84 @@
 
 
 def reduce_chan(own, other, grad_proj, held):
-    terms = {}
-
-    def add_terms(steps, own, swapped):
+    half = BLOCK // 2
+    wide = lambda value: value.astype(F32)
+    parts, found = {}, {}
+
+    def add_parts(steps, own, swapped):
         for n, step in enumerate(steps):
-            terms[step] = own[n].astype(F32) + swapped[n].astype(F32)
+            parts[step] = (own[n], swapped[n])
+
+    def lower(step, x):
+        return sum(wide(part[x, :half]) for part in parts[step])
+
+    def upper(step, rows=slice(0, half)):
+        mine = sum(wide(part[0, half + rows.start : half + rows.stop]) for part in parts[step])
+        return mine + wide(found[step][rows])
+
+    def swap_upper(steps):
+        sent = [sum(wide(part[1, half:]) for part in parts[step]).astype(BF16) for step in steps]
+        return lax.ppermute(jnp.concatenate(sent, axis=0) if len(sent) > 1 else sent[0], "chan", X_SWAP)
+
+    def keep_upper(steps, value):
+        for n, step in enumerate(steps):
+            found[step] = value[n * half : (n + 1) * half]
+
+    def hop(ahead, behind):
+        join = lambda rows: jnp.concatenate([row.astype(BF16) for row in rows], axis=0)
+        return moved(join(ahead), 1), moved(join(behind), -1)
 
     swapped = lax.ppermute(other, "chan", CORE_SWAP)
     near_own, near_other = back_project(grad_proj, held)
     swapped, near_own, near_other = lax.optimization_barrier((swapped, near_own, near_other))
-    add_terms(FAR_STEPS, own, swapped)
-    add_terms(NEAR_STEPS, near_own, lax.ppermute(near_other, "chan", CORE_SWAP))
-    ahead, behind = moved(terms[4][0], 1).astype(F32), moved(terms[4][1], -1).astype(F32)
-    ahead = jnp.stack([terms[3][0] + ahead, terms[3][1]])
-    behind = jnp.stack([terms[5][0], terms[5][1] + behind])
-    for near, other in ((2, 6), (1, 7)):
-        ahead = terms[near] + moved(ahead, 1).astype(F32)
-        behind = terms[other] + moved(behind, -1).astype(F32)
-    total = terms[0] + moved(ahead, 1).astype(F32) + moved(behind, -1).astype(F32)
-    total = total[0] + lax.ppermute(total[1].astype(BF16), "chan", X_SWAP).astype(F32)
-    return total.astype(BF16)
+    add_parts(FAR_STEPS, own, swapped)
+    near_swapped = lax.ppermute(near_other, "chan", CORE_SWAP)
+    first, last = slice(0, half // 2), slice(half // 2, half)
+    ahead, behind = hop([lower(4, 0)], [lower(4, 1)])
+    keep_upper((4,), swap_upper((4,)))
+    swap_far = swap_upper((3, 5))
+    ahead, behind = hop(
+        [lower(3, 0) + wide(ahead), lower(3, 1), upper(4, first)],
+        [lower(5, 0), lower(5, 1) + wide(behind), upper(4, last)],
+    )
+    swap_far, ahead, behind = lax.optimization_barrier((swap_far, ahead, behind))
+    keep_upper((3, 5), swap_far)
+    add_parts(NEAR_STEPS, near_own, near_swapped)
+    swap_middle = swap_upper((2, 6))
+    swap_near = swap_upper((1, 7, 0))
+    ahead, behind = hop(
+        [
+            lower(2, 0) + wide(ahead[:half]),
+            lower(2, 1) + wide(ahead[half:BLOCK]),
+            upper(3, first) + wide(ahead[BLOCK:]),
+            upper(3, last),
+        ],
+        [
+            lower(6, 0) + wide(behind[:half]),
+            lower(6, 1) + wide(behind[half:BLOCK]),
+            upper(5, first),
+            upper(5, last) + wide(behind[BLOCK:]),
+        ],
+    )
+    swap_middle, ahead, behind = lax.optimization_barrier((swap_middle, ahead, behind))
+    keep_upper((2, 6), swap_middle)
+
+    def onward(step, rows):
+        return [
+            lower(step, 0) + wide(rows[:half]),
+            lower(step, 1) + wide(rows[half:BLOCK]),
+            upper((step + (1 if step < 4 else -1)) % N_Z) + wide(rows[BLOCK:]),
+        ]
+
+    ahead, behind = hop(onward(1, ahead), onward(7, behind))
+    swap_near, ahead, behind = lax.optimization_barrier((swap_near, ahead, behind))
+    keep_upper((1, 7, 0), swap_near)
+    final = hop([upper(1) + wide(ahead[BLOCK:])], [upper(7) + wide(behind[BLOCK:])])
+    mine, sent = (
+        lower(0, x) + wide(ahead[x * half : (x + 1) * half]) + wide(behind[x * half : (x + 1) * half]) for x in range(2)
+    )
+    mine = mine + wide(lax.ppermute(sent.astype(BF16), "chan", X_SWAP))
+    return jnp.concatenate([mine, upper(0) + wide(final[0]) + wide(final[1])], axis=0).astype(BF16)
 
 
 def body(token_ids, embed_table, in_weight, feat_taps, modal_rates, modal_residues, out_grad):

time: 119 us -> 117 us (0.983)
  waiting for transfers between devices: 44 us -> 29 us
  starting transfers between devices: 38.8 us -> 51.1 us
    ppermute x8 -> x10, waiting for transfers between devices: 27.7 us -> 16.4 us  [moved(): return lax.ppermute(value.astype(BF16), 'chan', z_shift(by))]
    ppermute x8 -> x10, starting transfers between devices: 9.18 us -> 15.7 us  [moved(): return lax.ppermute(value.astype(BF16), 'chan', z_shift(by))]
    ppermute x2 -> x6, starting transfers between devices: 0.88 us -> 6.72 us  [the longest x4 4.4 us: swap_upper(): lax.ppermute(jnp.concatenate(sent, axis=0) if len(sent) > 1 else sent[0],...]
    ppermute x2 -> x6, waiting for transfers between devices: 4.76 us -> 1.01 us  [the longest x4 1 us: swap_upper(): lax.ppermute(jnp.concatenate(sent, axis=0) if len(sent) > 1 else sent[0],...]
  transfers between devices with their start and end apart: 26 -> 32, of which waited for: 9 -> 11; matrix products, arithmetic and copies ran while one was open for 0% -> 1% of each run, Pallas kernels for 12% -> 13%
where the time goes in v7:
time: 117 us; the launch traced here: 116 us
  starting transfers between devices  51.1 us (44%)
  Pallas kernels  29.8 us (25%)
  waiting for transfers between devices  29 us (25%)
  local copies, waits for them, and re-layouts  4.3 us (4%)
    ppermute x10, waiting for transfers between devices, moved(): return lax.ppermute(value.astype(BF16), 'chan', z_shift(by))  16.4 us
    ppermute x10, starting transfers between devices, moved(): return lax.ppermute(value.astype(BF16), 'chan', z_shift(by))  15.7 us
    pallas_call x1, Pallas kernels, mix(): pl.pallas_call(mixer_kernel, out_shape=(jax.ShapeDtypeStruct((BLOCK, BLOC...  13.9 us
    pallas_call x4, Pallas kernels, project(): pl.pallas_call(functools.partial(project_kernel, part, sums is None, read...  8.97 us
    all_to_all x1, starting transfers between devices, project_features(): lax.all_to_all(jnp.broadcast_to(rows[None], (N_Z,) + rows.shape), 'chan',...  8.47 us
    ppermute x6, starting transfers between devices, gather_ctx(): found += [lax.ppermute(piece, 'ctx', y_shift(by)) for by in Y_STEPS]  8.07 us
    all_to_all x1, waiting for transfers between devices, project_features(): lax.all_to_all(jnp.broadcast_to(rows[None], (N_Z,) + rows.shape), 'chan',...  7.08 us
    ppermute x3, starting transfers between devices, gather_pairs(): return [pair] + [lax.ppermute(pair, 'ctx', y_shift(by)) for by in Y_STEPS]  4.56 us
  transfers between devices with their start and end apart: 32, of which 11 were waited for; matrix products, arithmetic and copies ran while one was open for 1% of the time, Pallas kernels for 13%

profile of v7, /device:TPU:24, one launch (start us, length us, event | category | flops | bytes accessed | tf_op | source)
XLA Modules:
  0.0 116.2 jit_solution(6982513551279011549)
XLA Ops:
  0.6 0.9 copy-done
  1.6 0.7 broadcast_in_dim.2
  2.3 8.5 %all-to-all-start = ((bf16[8,64,256]{2,1,0:T(8,128)(2,1)}), bf16[8,64,256]{2,1,0:T(8,128)(2,1)S(1)}, u32[]{:S(2)}, u32[]{:S(2)}) async-start(bf16[8,64,256]{2,1,0:T(8,128)(2,1)} %broadcast_in_dim.2), calls=%async_computation | async-start | bytes 524288 | tf_op jit(solution)/shard_map/all_to_all | solution.py:425
  10.8 0.9 copy-done.1
  11.7 0.7 copy-done.3
  12.5 3.1 %collective-permute-start.2 = (bf16[272,256]{1,0:T(8,128)(2,1)S(1)}, bf16[272,256]{1,0:T(8,128)(2,1)S(1)}, u32[]{:S(2)}, u32[]{:S(2)}) collective-permute-start(bf16[272,256]{1,0:T(8,128)(2,1)S(1)} %payload.1), channel_id=1, source_target_pairs={{0,32},{32,0},{64,96},{96,64},{128,160},{160,128},{192,224},{224,1... | collective-permute-start | bytes 417800 | tf_op jit(solution)/shard_map/ppermute | solution.py:451
  15.6 7.1 %all-to-all-done.refs_0_ = bf16[8,64,256]{2,1,0:T(8,128)(2,1)S(1)} async-done(((bf16[8,64,256]{2,1,0:T(8,128)(2,1)}), bf16[8,64,256]{2,1,0:T(8,128)(2,1)S(1)}, u32[]{:S(2)}, u32[]{:S(2)}) %all-to-all-start) | async-done | bytes 262176 | tf_op jit(solution)/shard_map/all_to_all | solution.py:425
  22.6 1.5 %collective-permute-start = (bf16[8,64,256]{2,1,0:T(8,128)(2,1)S(1)}, bf16[8,64,256]{2,1,0:T(8,128)(2,1)S(1)}, u32[]{:S(2)}, u32[]{:S(2)}) collective-permute-start(bf16[8,64,256]{2,1,0:T(8,128)(2,1)S(1)} %all-to-all-done.refs_0_), channel_id=1, source_target_pairs={{0,16},{1,17},{2,18},{3,19},{4,20},{5,21},{6,22},{7,23},{8,24},{9,... | collective-permute-start | bytes 786440 | tf_op jit(solution)/shard_map/ppermute | solution.py:428
  24.2 1.3 %collective-permute-start.6 = (bf16[2,272,256]{2,1,0:T(8,128)(2,1)S(1)}, bf16[2,272,256]{2,1,0:T(8,128)(2,1)S(1)}, u32[]{:S(2)}, u32[]{:S(2)}) collective-permute-start(bf16[2,272,256]{2,1,0:T(8,128)(2,1)S(1)} %pad_maximum_fusion.refs_8_), channel_id=1, source_target_pairs={{0,128},{32,160},{64,192},{96,224},{128,0},{160,32},{192,64},{224,... | collective-permute-start | bytes 835592 | tf_op jit(solution)/shard_map/ppermute | solution.py:455
  25.5 3.2 %collective-permute-start.4 = (bf16[2,272,256]{2,1,0:T(8,128)(2,1)S(1)}, bf16[2,272,256]{2,1,0:T(8,128)(2,1)S(1)}, u32[]{:S(2)}, u32[]{:S(2)}) collective-permute-start(bf16[2,272,256]{2,1,0:T(8,128)(2,1)S(1)} %pad_maximum_fusion.refs_8_), channel_id=1, source_target_pairs={{0,64},{32,96},{64,128},{96,160},{128,192},{160,224},{192,0},{224,... | collective-permute-start | bytes 835592 | tf_op jit(solution)/shard_map/ppermute | solution.py:455
  28.7 3.8 %project.4 = (f32[64,768]{1,0:T(8,128)S(1)}, bf16[3,8,256,256]{3,2,1,0:T(8,128)(2,1)S(1)}, bf16[3,8,256,256]{3,2,1,0:T(8,128)(2,1)S(1)}) custom-call(bf16[8,64,256]{2,1,0:T(8,128)(2,1)S(1)} %all-to-all-done.refs_0_, bf16[3,2,8,2,256,256]{5,4,3,2,1,0:T(8,128)(2,1)} %bitcast.180), custom_call_target="tpu_custom_call" | custom-call | flops 201326592 | bytes 9437184 | tf_op jit(solution)/shard_map/project/pallas_call | solution.py:192
  32.5 3.0 %project.5.refs_2_ = f32[64,768]{1,0:T(8,128)S(1)} custom-call(bf16[8,64,256]{2,1,0:T(8,128)(2,1)S(1)} %collective-permute-done.1.refs_0_, bf16[3,2,8,2,256,256]{5,4,3,2,1,0:T(8,128)(2,1)} %bitcast.181, f32[64,768]{1,0:T(8,128)S(1)} %get-tuple-element.41.refs_2_), custom_call_target="tpu_custom_call" | custom-call | flops 201326592 | bytes 3145728 | tf_op jit(solution)/shard_map/project/pallas_call | solution.py:192
  35.7 1.1 project.6.refs_2_
  36.8 3.7 %collective-permute-done.5.refs_10_ = bf16[2,272,256]{2,1,0:T(8,128)(2,1)S(1)} collective-permute-done((bf16[2,272,256]{2,1,0:T(8,128)(2,1)S(1)}, bf16[2,272,256]{2,1,0:T(8,128)(2,1)S(1)}, u32[]{:S(2)}, u32[]{:S(2)}) %collective-permute-start.5) | collective-permute-done | bytes 278560 | tf_op jit(solution)/shard_map/ppermute | solution.py:455
  40.5 1.1 project.7.refs_0_
  41.6 2.8 %collective-permute-start.7 = (bf16[64,768]{1,0:T(8,128)(2,1)S(1)}, bf16[64,768]{1,0:T(8,128)(2,1)S(1)}, u32[]{:S(2)}, u32[]{:S(2)}) collective-permute-start(bf16[64,768]{1,0:T(8,128)(2,1)S(1)} %project.7.refs_0_), channel_id=1, source_target_pairs={{0,32},{32,0},{64,96},{96,64},{128,160},{160,128},{192,224},{224,1... | collective-permute-start | bytes 294920 | tf_op jit(solution)/shard_map/ppermute | solution.py:443
  44.4 1.4 %collective-permute-start.12 = (bf16[64,768]{1,0:T(8,128)(2,1)S(1)}, bf16[64,768]{1,0:T(8,128)(2,1)S(1)}, u32[]{:S(2)}, u32[]{:S(2)}) collective-permute-start(bf16[64,768]{1,0:T(8,128)(2,1)S(1)} %project.7.refs_0_), channel_id=1, source_target_pairs={{0,128},{32,160},{64,192},{96,224},{128,0},{160,32},{192,64},{224,... | collective-permute-start | bytes 294920 | tf_op jit(solution)/shard_map/ppermute | solution.py:446
  45.9 3.2 %collective-permute-start.8 = (bf16[64,768]{1,0:T(8,128)(2,1)S(1)}, bf16[64,768]{1,0:T(8,128)(2,1)S(1)}, u32[]{:S(2)}, u32[]{:S(2)}) collective-permute-start(bf16[64,768]{1,0:T(8,128)(2,1)S(1)} %project.7.refs_0_), channel_id=1, source_target_pairs={{0,64},{32,96},{64,128},{96,160},{128,192},{160,224},{192,0},{224,... | collective-permute-start | bytes 294920 | tf_op jit(solution)/shard_map/ppermute | solution.py:446
  49.1 0.9 collective-permute-start.13
  50.0 0.7 collective-permute-start.11
  50.7 0.7 collective-permute-done.12.refs_6_
  51.5 1.8 %collective-permute-start.9 = (bf16[64,768]{1,0:T(8,128)(2,1)S(1)}, bf16[64,768]{1,0:T(8,128)(2,1)S(1)}, u32[]{:S(2)}, u32[]{:S(2)}) collective-permute-start(bf16[64,768]{1,0:T(8,128)(2,1)S(1)} %collective-permute-done.7.refs_1_), channel_id=1, source_target_pairs={{0,64},{32,96},{64,128},{96,160},{128,192},{160,224},{192,0},{224,... | collective-permute-start | bytes 294920 | tf_op jit(solution)/shard_map/ppermute | solution.py:446
  53.3 3.9 %filter_tables.1 = (bf16[16,256,256]{2,1,0:T(8,128)(2,1)S(1)}, bf16[256,1152]{1,0:T(8,128)(2,1)S(1)}, f32[2,256]{1,0:T(2,128)S(1)}, f32[768,3]{1,0:T(8,128)S(1)}) custom-call(f32[16,16]{1,0:T(8,128)S(1)} %copy-done.2, f32[16,16]{1,0:T(8,128)S(1)} %sqrt_multiply_fusion.gain_ref, f32[3,3,256]{2,1,0:T(4,128)S(1)} %copy-done.4), custom_call_target="tpu_custom_call" | custom-call | flops 402653184 | bytes 5242880 | tf_op jit(solution)/shard_map/filter_tables/pallas_call | solution.py:142
  57.3 13.9 %mixer.1 = (bf16[256,256]{1,0:T(8,128)(2,1)}, bf16[768,256]{1,0:T(8,128)(2,1)S(1)}, bf16[3,2,256,256]{3,2,1,0:T(8,128)(2,1)S(1)}, bf16[3,2,256,256]{3,2,1,0:T(8,...) custom-call(bf16[64,768]{1,0:T(8,128)(2,1)S(1)} %project.7.refs_0_, bf16[64,768]{1,0:T(8,128)(2,1)S(1)} %collective-permute-done.7.refs_1_, ...), custom_call_target="tpu_custom_call" | custom-call | flops 3221225472 | bytes 8388608 | tf_op jit(solution)/shard_map/mixer/pallas_call | solution.py:372
  71.3 2.9 %back_project.1 = (bf16[5,2,256,256]{3,2,1,0:T(8,128)(2,1)S(1)}, bf16[5,2,256,256]{3,2,1,0:T(8,128)(2,1)S(1)}) custom-call(bf16[768,256]{1,0:T(8,128)(2,1)S(1)} %get-tuple-element.61.grad_ref, bf16[5,3,2,2,256,256]{5,4,3,2,1,0:T(8,128)(2,1)S(1)} %get-tuple-element.62.held_ref), custom_call_target="tpu_custom_call" | custom-call | flops 2013265920 | bytes 10485760 | tf_op jit(solution)/shard_map/back_project/pallas_call | solution.py:411
  74.3 0.3 collective-permute-start.20
  74.7 1.9 %collective-permute-start.18 = (bf16[256,256]{1,0:T(8,128)(2,1)S(1)}, bf16[256,256]{1,0:T(8,128)(2,1)S(1)}, u32[]{:S(2)}, u32[]{:S(2)}) collective-permute-start(bf16[256,256]{1,0:T(8,128)(2,1)S(1)} %pad_maximum_fusion.9), channel_id=1, source_target_pairs={{0,16},{1,17},{2,18},{3,19},{4,20},{5,21},{6,22},{7,23},{8,24},{9,... | collective-permute-start | bytes 393224 | tf_op jit(solution)/shard_map/ppermute | solution.py:480
  76.6 2.0 %collective-permute-start.19 = (bf16[128,256]{1,0:T(8,128)(2,1)S(1)}, bf16[128,256]{1,0:T(8,128)(2,1)S(1)}, u32[]{:S(2)}, u32[]{:S(2)}) collective-permute-start(bf16[128,256]{1,0:T(8,128)(2,1)S(1)} %get-tuple-element.116), channel_id=1, source_target_pairs={{0,2},{1,3},{2,4},{3,5},{4,6},{5,7},{6,8},{7,9},{8,10},{9,11},{10,... | collective-permute-start | bytes 196616 | tf_op jit(solution)/shard_map/ppermute | solution.py:459
  78.7 0.6 collective-permute-done.20
  79.3 2.8 %collective-permute-done.19 = bf16[128,256]{1,0:T(8,128)(2,1)S(1)} collective-permute-done((bf16[128,256]{1,0:T(8,128)(2,1)S(1)}, bf16[128,256]{1,0:T(8,128)(2,1)S(1)}, u32[]{:S(2)}, u32[]{:S(2)}) %collective-permute-start.19) | collective-permute-done | bytes 65568 | tf_op jit(solution)/shard_map/ppermute | solution.py:459
  82.2 0.9 collective-permute-start.21
  83.1 2.5 %collective-permute-start.23 = (bf16[320,256]{1,0:T(8,128)(2,1)S(1)}, bf16[320,256]{1,0:T(8,128)(2,1)S(1)}, u32[]{:S(2)}, u32[]{:S(2)}) collective-permute-start(bf16[320,256]{1,0:T(8,128)(2,1)S(1)} %pad_maximum_fusion.7), channel_id=1, source_target_pairs={{0,14},{1,15},{2,0},{3,1},{4,2},{5,3},{6,4},{7,5},{8,6},{9,7},{10,... | collective-permute-start | bytes 491528 | tf_op jit(solution)/shard_map/ppermute | solution.py:459
  85.7 3.1 %collective-permute-done.21 = bf16[320,256]{1,0:T(8,128)(2,1)S(1)} collective-permute-done((bf16[320,256]{1,0:T(8,128)(2,1)S(1)}, bf16[320,256]{1,0:T(8,128)(2,1)S(1)}, u32[]{:S(2)}, u32[]{:S(2)}) %collective-permute-start.21) | collective-permute-done | bytes 163872 | tf_op jit(solution)/shard_map/ppermute | solution.py:459
  88.9 0.1 fusion.17
  89.1 0.5 collective-permute-start.17
  89.6 0.3 collective-permute-start.24
  89.9 3.3 %collective-permute-start.25 = (bf16[384,256]{1,0:T(8,128)(2,1)S(1)}, bf16[384,256]{1,0:T(8,128)(2,1)S(1)}, u32[]{:S(2)}, u32[]{:S(2)}) collective-permute-start(bf16[384,256]{1,0:T(8,128)(2,1)S(1)} %pad_maximum_fusion.3), channel_id=1, source_target_pairs={{0,14},{1,15},{2,0},{3,1},{4,2},{5,3},{6,4},{7,5},{8,6},{9,7},{10,... | collective-permute-start | bytes 589832 | tf_op jit(solution)/shard_map/ppermute | solution.py:459
  93.3 1.7 %collective-permute-start.16 = (bf16[384,256]{1,0:T(8,128)(2,1)S(1)}, bf16[384,256]{1,0:T(8,128)(2,1)S(1)}, u32[]{:S(2)}, u32[]{:S(2)}) collective-permute-start(bf16[384,256]{1,0:T(8,128)(2,1)S(1)} %pad_maximum_fusion.1), channel_id=1, source_target_pairs={{0,16},{1,17},{2,18},{3,19},{4,20},{5,21},{6,22},{7,23},{8,24},{9,... | collective-permute-start | bytes 589832 | tf_op jit(solution)/shard_map/ppermute | solution.py:480
  95.0 0.3 collective-permute-done.17
  95.3 1.4 %collective-permute-done.24 = bf16[384,256]{1,0:T(8,128)(2,1)S(1)} collective-permute-done((bf16[384,256]{1,0:T(8,128)(2,1)S(1)}, bf16[384,256]{1,0:T(8,128)(2,1)S(1)}, u32[]{:S(2)}, u32[]{:S(2)}) %collective-permute-start.24) | collective-permute-done | bytes 196640 | tf_op jit(solution)/shard_map/ppermute | solution.py:459
  96.9 3.4 %collective-permute-start.27 = (bf16[384,256]{1,0:T(8,128)(2,1)S(1)}, bf16[384,256]{1,0:T(8,128)(2,1)S(1)}, u32[]{:S(2)}, u32[]{:S(2)}) collective-permute-start(bf16[384,256]{1,0:T(8,128)(2,1)S(1)} %pad_maximum_fusion.5), channel_id=1, source_target_pairs={{0,14},{1,15},{2,0},{3,1},{4,2},{5,3},{6,4},{7,5},{8,6},{9,7},{10,... | collective-permute-start | bytes 589832 | tf_op jit(solution)/shard_map/ppermute | solution.py:459
  100.5 3.1 %collective-permute-done.27 = bf16[384,256]{1,0:T(8,128)(2,1)S(1)} collective-permute-done((bf16[384,256]{1,0:T(8,128)(2,1)S(1)}, bf16[384,256]{1,0:T(8,128)(2,1)S(1)}, u32[]{:S(2)}, u32[]{:S(2)}) %collective-permute-start.27) | collective-permute-done | bytes 196640 | tf_op jit(solution)/shard_map/ppermute | solution.py:459
  103.5 3.9 %collective-permute-done.26 = bf16[384,256]{1,0:T(8,128)(2,1)S(1)} collective-permute-done((bf16[384,256]{1,0:T(8,128)(2,1)S(1)}, bf16[384,256]{1,0:T(8,128)(2,1)S(1)}, u32[]{:S(2)}, u32[]{:S(2)}) %collective-permute-start.26) | collective-permute-done | bytes 196640 | tf_op jit(solution)/shard_map/ppermute | solution.py:459
  107.4 0.1 fusion.8
  107.5 2.3 %collective-permute-start.28 = (bf16[128,256]{1,0:T(8,128)(2,1)S(1)}, bf16[128,256]{1,0:T(8,128)(2,1)S(1)}, u32[]{:S(2)}, u32[]{:S(2)}) collective-permute-start(bf16[128,256]{1,0:T(8,128)(2,1)S(1)} %get-tuple-element.119), channel_id=1, source_target_pairs={{0,16},{1,17},{2,18},{3,19},{4,20},{5,21},{6,22},{7,23},{8,24},{9,... | collective-permute-start | bytes 196616 | tf_op jit(solution)/shard_map/ppermute | solution.py:539
  109.8 3.2 %collective-permute-start.30 = (bf16[128,256]{1,0:T(8,128)(2,1)S(1)}, bf16[128,256]{1,0:T(8,128)(2,1)S(1)}, u32[]{:S(2)}, u32[]{:S(2)}) collective-permute-start(bf16[128,256]{1,0:T(8,128)(2,1)S(1)} %get-tuple-element.121), channel_id=1, source_target_pairs={{0,14},{1,15},{2,0},{3,1},{4,2},{5,3},{6,4},{7,5},{8,6},{9,7},{10,... | collective-permute-start | bytes 196616 | tf_op jit(solution)/shard_map/ppermute | solution.py:459
  113.1 2.2 %collective-permute-done.29 = bf16[128,256]{1,0:T(8,128)(2,1)S(1)} collective-permute-done((bf16[128,256]{1,0:T(8,128)(2,1)S(1)}, bf16[128,256]{1,0:T(8,128)(2,1)S(1)}, u32[]{:S(2)}, u32[]{:S(2)}) %collective-permute-start.29) | collective-permute-done | bytes 65568 | tf_op jit(solution)/shard_map/ppermute | solution.py:459
  115.4 0.8 copy.9
  (70 shorter events, 1.6 us)
Async XLA Ops:
  0.6 1.0 copy-start
  2.3 20.3 %all-to-all-start = ((bf16[8,64,256]{2,1,0:T(8,128)(2,1)}), bf16[8,64,256]{2,1,0:T(8,128)(2,1)S(1)}, u32[]{:S(2)}, u32[]{:S(2)}) async-start(bf16[8,64,256]{2,1,0:T(8,128)(2,1)} %broadcast_in_dim.2), calls=%async_computation | async-start | bytes 524288 | tf_op jit(solution)/shard_map/all_to_all | solution.py:425
  10.8 0.9 copy-start.1
  11.7 0.7 copy-start.3
  12.5 11.7 %collective-permute-start.2 = (bf16[272,256]{1,0:T(8,128)(2,1)S(1)}, bf16[272,256]{1,0:T(8,128)(2,1)S(1)}, u32[]{:S(2)}, u32[]{:S(2)}) collective-permute-start(bf16[272,256]{1,0:T(8,128)(2,1)S(1)} %payload.1), channel_id=1, source_target_pairs={{0,32},{32,0},{64,96},{96,64},{128,160},{160,128},{192,224},{224,1... | collective-permute-start | bytes 417800 | tf_op jit(solution)/shard_map/ppermute | solution.py:451
  22.6 9.9 %collective-permute-start.1 = (bf16[8,64,256]{2,1,0:T(8,128)(2,1)S(1)}, bf16[8,64,256]{2,1,0:T(8,128)(2,1)S(1)}, u32[]{:S(2)}, u32[]{:S(2)}) collective-permute-start(bf16[8,64,256]{2,1,0:T(8,128)(2,1)S(1)} %all-to-all-done.refs_0_), channel_id=1, source_target_pairs={{0,1},{1,0},{2,3},{3,2},{4,5},{5,4},{6,7},{7,6},{8,9},{9,8},{10,11... | collective-permute-start | bytes 786440 | tf_op jit(solution)/shard_map/ppermute | solution.py:429
  22.6 12.9 %collective-permute-start = (bf16[8,64,256]{2,1,0:T(8,128)(2,1)S(1)}, bf16[8,64,256]{2,1,0:T(8,128)(2,1)S(1)}, u32[]{:S(2)}, u32[]{:S(2)}) collective-permute-start(bf16[8,64,256]{2,1,0:T(8,128)(2,1)S(1)} %all-to-all-done.refs_0_), channel_id=1, source_target_pairs={{0,16},{1,17},{2,18},{3,19},{4,20},{5,21},{6,22},{7,23},{8,24},{9,... | collective-permute-start | bytes 786440 | tf_op jit(solution)/shard_map/ppermute | solution.py:428
  24.2 12.6 %collective-permute-start.6 = (bf16[2,272,256]{2,1,0:T(8,128)(2,1)S(1)}, bf16[2,272,256]{2,1,0:T(8,128)(2,1)S(1)}, u32[]{:S(2)}, u32[]{:S(2)}) collective-permute-start(bf16[2,272,256]{2,1,0:T(8,128)(2,1)S(1)} %pad_maximum_fusion.refs_8_), channel_id=1, source_target_pairs={{0,128},{32,160},{64,192},{96,224},{128,0},{160,32},{192,64},{224,... | collective-permute-start | bytes 835592 | tf_op jit(solution)/shard_map/ppermute | solution.py:455
  25.5 15.0 %collective-permute-start.5 = (bf16[2,272,256]{2,1,0:T(8,128)(2,1)S(1)}, bf16[2,272,256]{2,1,0:T(8,128)(2,1)S(1)}, u32[]{:S(2)}, u32[]{:S(2)}) collective-permute-start(bf16[2,272,256]{2,1,0:T(8,128)(2,1)S(1)} %pad_maximum_fusion.refs_8_), channel_id=1, source_target_pairs={{0,192},{32,224},{64,0},{96,32},{128,64},{160,96},{192,128},{224,1... | collective-permute-start | bytes 835592 | tf_op jit(solution)/shard_map/ppermute | solution.py:455
  25.5 15.0 %collective-permute-start.4 = (bf16[2,272,256]{2,1,0:T(8,128)(2,1)S(1)}, bf16[2,272,256]{2,1,0:T(8,128)(2,1)S(1)}, u32[]{:S(2)}, u32[]{:S(2)}) collective-permute-start(bf16[2,272,256]{2,1,0:T(8,128)(2,1)S(1)} %pad_maximum_fusion.refs_8_), channel_id=1, source_target_pairs={{0,64},{32,96},{64,128},{96,160},{128,192},{160,224},{192,0},{224,... | collective-permute-start | bytes 835592 | tf_op jit(solution)/shard_map/ppermute | solution.py:455
  35.6 5.0 %collective-permute-start.3 = (bf16[8,64,256]{2,1,0:T(8,128)(2,1)S(1)}, bf16[8,64,256]{2,1,0:T(8,128)(2,1)S(1)}, u32[]{:S(2)}, u32[]{:S(2)}) collective-permute-start(bf16[8,64,256]{2,1,0:T(8,128)(2,1)S(1)} %collective-permute-done.refs_0_), channel_id=1, source_target_pairs={{0,1},{1,0},{2,3},{3,2},{4,5},{5,4},{6,7},{7,6},{8,9},{9,8},{10,11... | collective-permute-start | bytes 786440 | tf_op jit(solution)/shard_map/ppermute | solution.py:435
  36.8 16.5 %copy-start.2 = (f32[16,16]{1,0:T(8,128)S(1)}, f32[16,16]{1,0:T(8,128)}, u32[]{:S(2)}) copy-start(f32[16,16]{1,0:T(8,128)} %rate_ref) | copy-start | bytes 3076
  36.8 16.5 %copy-start.5 = (f32[16,16]{1,0:T(8,128)S(1)}, f32[16,16]{1,0:T(8,128)}, u32[]{:S(2)}) copy-start(f32[16,16]{1,0:T(8,128)} %param.12) | copy-start | bytes 3076
  36.8 16.5 %copy-start.4 = (f32[3,3,256]{2,1,0:T(4,128)S(1)}, f32[3,3,256]{2,1,0:T(4,128)}, u32[]{:S(2)}) copy-start(f32[3,3,256]{2,1,0:T(4,128)} %tap_ref.1) | copy-start | bytes 27652
  41.6 7.4 %collective-permute-start.7 = (bf16[64,768]{1,0:T(8,128)(2,1)S(1)}, bf16[64,768]{1,0:T(8,128)(2,1)S(1)}, u32[]{:S(2)}, u32[]{:S(2)}) collective-permute-start(bf16[64,768]{1,0:T(8,128)(2,1)S(1)} %project.7.refs_0_), channel_id=1, source_target_pairs={{0,32},{32,0},{64,96},{96,64},{128,160},{160,128},{192,224},{224,1... | collective-permute-start | bytes 294920 | tf_op jit(solution)/shard_map/ppermute | solution.py:443
  44.4 7.0 %collective-permute-start.12 = (bf16[64,768]{1,0:T(8,128)(2,1)S(1)}, bf16[64,768]{1,0:T(8,128)(2,1)S(1)}, u32[]{:S(2)}, u32[]{:S(2)}) collective-permute-start(bf16[64,768]{1,0:T(8,128)(2,1)S(1)} %project.7.refs_0_), channel_id=1, source_target_pairs={{0,128},{32,160},{64,192},{96,224},{128,0},{160,32},{192,64},{224,... | collective-permute-start | bytes 294920 | tf_op jit(solution)/shard_map/ppermute | solution.py:446
  45.8 11.4 %collective-permute-start.10 = (bf16[64,768]{1,0:T(8,128)(2,1)S(1)}, bf16[64,768]{1,0:T(8,128)(2,1)S(1)}, u32[]{:S(2)}, u32[]{:S(2)}) collective-permute-start(bf16[64,768]{1,0:T(8,128)(2,1)S(1)} %project.7.refs_0_), channel_id=1, source_target_pairs={{0,192},{32,224},{64,0},{96,32},{128,64},{160,96},{192,128},{224,1... | collective-permute-start | bytes 294920 | tf_op jit(solution)/shard_map/ppermute | solution.py:446
  45.9 11.3 %collective-permute-start.8 = (bf16[64,768]{1,0:T(8,128)(2,1)S(1)}, bf16[64,768]{1,0:T(8,128)(2,1)S(1)}, u32[]{:S(2)}, u32[]{:S(2)}) collective-permute-start(bf16[64,768]{1,0:T(8,128)(2,1)S(1)} %project.7.refs_0_), channel_id=1, source_target_pairs={{0,64},{32,96},{64,128},{96,160},{128,192},{160,224},{192,0},{224,... | collective-permute-start | bytes 294920 | tf_op jit(solution)/shard_map/ppermute | solution.py:446
  49.1 8.2 %collective-permute-start.13 = (bf16[64,768]{1,0:T(8,128)(2,1)S(1)}, bf16[64,768]{1,0:T(8,128)(2,1)S(1)}, u32[]{:S(2)}, u32[]{:S(2)}) collective-permute-start(bf16[64,768]{1,0:T(8,128)(2,1)S(1)} %collective-permute-done.7.refs_1_), channel_id=1, source_target_pairs={{0,128},{32,160},{64,192},{96,224},{128,0},{160,32},{192,64},{224,... | collective-permute-start | bytes 294920 | tf_op jit(solution)/shard_map/ppermute | solution.py:446
  50.0 7.2 %collective-permute-start.11 = (bf16[64,768]{1,0:T(8,128)(2,1)S(1)}, bf16[64,768]{1,0:T(8,128)(2,1)S(1)}, u32[]{:S(2)}, u32[]{:S(2)}) collective-permute-start(bf16[64,768]{1,0:T(8,128)(2,1)S(1)} %collective-permute-done.7.refs_1_), channel_id=1, source_target_pairs={{0,192},{32,224},{64,0},{96,32},{128,64},{160,96},{192,128},{224,1... | collective-permute-start | bytes 294920 | tf_op jit(solution)/shard_map/ppermute | solution.py:446
  51.5 5.8 %collective-permute-start.9 = (bf16[64,768]{1,0:T(8,128)(2,1)S(1)}, bf16[64,768]{1,0:T(8,128)(2,1)S(1)}, u32[]{:S(2)}, u32[]{:S(2)}) collective-permute-start(bf16[64,768]{1,0:T(8,128)(2,1)S(1)} %collective-permute-done.7.refs_1_), channel_id=1, source_target_pairs={{0,64},{32,96},{64,128},{96,160},{128,192},{160,224},{192,0},{224,... | collective-permute-start | bytes 294920 | tf_op jit(solution)/shard_map/ppermute | solution.py:446
  71.2 3.0 %collective-permute-start.14 = (bf16[3,2,256,256]{3,2,1,0:T(8,128)(2,1)S(1)}, bf16[3,2,256,256]{3,2,1,0:T(8,128)(2,1)S(1)}, u32[]{:S(2)}, u32[]{:S(2)}) collective-permute-start(bf16[3,2,256,256]{3,2,1,0:T(8,128)(2,1)S(1)} %get-tuple-element.60), channel_id=1, source_target_pairs={{0,1},{1,0},{2,3},{3,2},{4,5},{5,4},{6,7},{7,6},{8,9},{9,8},{10,11... | collective-permute-start | bytes 2359304 | tf_op jit(solution)/shard_map/ppermute | solution.py:490
  74.3 5.0 %collective-permute-start.20 = (bf16[128,256]{1,0:T(8,128)(2,1)S(1)}, bf16[128,256]{1,0:T(8,128)(2,1)S(1)}, u32[]{:S(2)}, u32[]{:S(2)}) collective-permute-start(bf16[128,256]{1,0:T(8,128)(2,1)S(1)} %get-tuple-element.115), channel_id=1, source_target_pairs={{0,16},{1,17},{2,18},{3,19},{4,20},{5,21},{6,22},{7,23},{8,24},{9,... | collective-permute-start | bytes 196616 | tf_op jit(solution)/shard_map/ppermute | solution.py:480
  74.7 11.0 %collective-permute-start.18 = (bf16[256,256]{1,0:T(8,128)(2,1)S(1)}, bf16[256,256]{1,0:T(8,128)(2,1)S(1)}, u32[]{:S(2)}, u32[]{:S(2)}) collective-permute-start(bf16[256,256]{1,0:T(8,128)(2,1)S(1)} %pad_maximum_fusion.9), channel_id=1, source_target_pairs={{0,16},{1,17},{2,18},{3,19},{4,20},{5,21},{6,22},{7,23},{8,24},{9,... | collective-permute-start | bytes 393224 | tf_op jit(solution)/shard_map/ppermute | solution.py:480
  76.6 6.4 %collective-permute-start.22 = (bf16[128,256]{1,0:T(8,128)(2,1)S(1)}, bf16[128,256]{1,0:T(8,128)(2,1)S(1)}, u32[]{:S(2)}, u32[]{:S(2)}) collective-permute-start(bf16[128,256]{1,0:T(8,128)(2,1)S(1)} %get-tuple-element.114), channel_id=1, source_target_pairs={{0,14},{1,15},{2,0},{3,1},{4,2},{5,3},{6,4},{7,5},{8,6},{9,7},{10,... | collective-permute-start | bytes 196616 | tf_op jit(solution)/shard_map/ppermute | solution.py:459
  76.6 5.5 %collective-permute-start.19 = (bf16[128,256]{1,0:T(8,128)(2,1)S(1)}, bf16[128,256]{1,0:T(8,128)(2,1)S(1)}, u32[]{:S(2)}, u32[]{:S(2)}) collective-permute-start(bf16[128,256]{1,0:T(8,128)(2,1)S(1)} %get-tuple-element.116), channel_id=1, source_target_pairs={{0,2},{1,3},{2,4},{3,5},{4,6},{5,7},{6,8},{7,9},{8,10},{9,11},{10,... | collective-permute-start | bytes 196616 | tf_op jit(solution)/shard_map/ppermute | solution.py:459
  78.7 10.2 %collective-permute-start.15 = (bf16[5,2,256,256]{3,2,1,0:T(8,128)(2,1)S(1)}, bf16[5,2,256,256]{3,2,1,0:T(8,128)(2,1)S(1)}, u32[]{:S(2)}, u32[]{:S(2)}) collective-permute-start(bf16[5,2,256,256]{3,2,1,0:T(8,128)(2,1)S(1)} %get-tuple-element.66), channel_id=1, source_target_pairs={{0,1},{1,0},{2,3},{3,2},{4,5},{5,4},{6,7},{7,6},{8,9},{9,8},{10,11... | collective-permute-start | bytes 3932168 | tf_op jit(solution)/shard_map/ppermute | solution.py:494
  82.2 6.6 %collective-permute-start.21 = (bf16[320,256]{1,0:T(8,128)(2,1)S(1)}, bf16[320,256]{1,0:T(8,128)(2,1)S(1)}, u32[]{:S(2)}, u32[]{:S(2)}) collective-permute-start(bf16[320,256]{1,0:T(8,128)(2,1)S(1)} %pad_maximum_fusion.6), channel_id=1, source_target_pairs={{0,2},{1,3},{2,4},{3,5},{4,6},{5,7},{6,8},{7,9},{8,10},{9,11},{10,... | collective-permute-start | bytes 491528 | tf_op jit(solution)/shard_map/ppermute | solution.py:459
  83.1 5.7 %collective-permute-start.23 = (bf16[320,256]{1,0:T(8,128)(2,1)S(1)}, bf16[320,256]{1,0:T(8,128)(2,1)S(1)}, u32[]{:S(2)}, u32[]{:S(2)}) collective-permute-start(bf16[320,256]{1,0:T(8,128)(2,1)S(1)} %pad_maximum_fusion.7), channel_id=1, source_target_pairs={{0,14},{1,15},{2,0},{3,1},{4,2},{5,3},{6,4},{7,5},{8,6},{9,7},{10,... | collective-permute-start | bytes 491528 | tf_op jit(solution)/shard_map/ppermute | solution.py:459
  89.1 6.2 %collective-permute-start.17 = (bf16[256,256]{1,0:T(8,128)(2,1)S(1)}, bf16[256,256]{1,0:T(8,128)(2,1)S(1)}, u32[]{:S(2)}, u32[]{:S(2)}) collective-permute-start(bf16[256,256]{1,0:T(8,128)(2,1)S(1)} %pad_maximum_fusion.8), channel_id=1, source_target_pairs={{0,16},{1,17},{2,18},{3,19},{4,20},{5,21},{6,22},{7,23},{8,24},{9,... | collective-permute-start | bytes 393224 | tf_op jit(solution)/shard_map/ppermute | solution.py:480
  89.6 7.1 %collective-permute-start.24 = (bf16[384,256]{1,0:T(8,128)(2,1)S(1)}, bf16[384,256]{1,0:T(8,128)(2,1)S(1)}, u32[]{:S(2)}, u32[]{:S(2)}) collective-permute-start(bf16[384,256]{1,0:T(8,128)(2,1)S(1)} %pad_maximum_fusion.2), channel_id=1, source_target_pairs={{0,2},{1,3},{2,4},{3,5},{4,6},{5,7},{6,8},{7,9},{8,10},{9,11},{10,... | collective-permute-start | bytes 589832 | tf_op jit(solution)/shard_map/ppermute | solution.py:459
  89.9 6.8 %collective-permute-start.25 = (bf16[384,256]{1,0:T(8,128)(2,1)S(1)}, bf16[384,256]{1,0:T(8,128)(2,1)S(1)}, u32[]{:S(2)}, u32[]{:S(2)}) collective-permute-start(bf16[384,256]{1,0:T(8,128)(2,1)S(1)} %pad_maximum_fusion.3), channel_id=1, source_target_pairs={{0,14},{1,15},{2,0},{3,1},{4,2},{5,3},{6,4},{7,5},{8,6},{9,7},{10,... | collective-permute-start | bytes 589832 | tf_op jit(solution)/shard_map/ppermute | solution.py:459
  93.3 7.2 %collective-permute-start.16 = (bf16[384,256]{1,0:T(8,128)(2,1)S(1)}, bf16[384,256]{1,0:T(8,128)(2,1)S(1)}, u32[]{:S(2)}, u32[]{:S(2)}) collective-permute-start(bf16[384,256]{1,0:T(8,128)(2,1)S(1)} %pad_maximum_fusion.1), channel_id=1, source_target_pairs={{0,16},{1,17},{2,18},{3,19},{4,20},{5,21},{6,22},{7,23},{8,24},{9,... | collective-permute-start | bytes 589832 | tf_op jit(solution)/shard_map/ppermute | solution.py:480
  96.9 6.6 %collective-permute-start.27 = (bf16[384,256]{1,0:T(8,128)(2,1)S(1)}, bf16[384,256]{1,0:T(8,128)(2,1)S(1)}, u32[]{:S(2)}, u32[]{:S(2)}) collective-permute-start(bf16[384,256]{1,0:T(8,128)(2,1)S(1)} %pad_maximum_fusion.5), channel_id=1, source_target_pairs={{0,14},{1,15},{2,0},{3,1},{4,2},{5,3},{6,4},{7,5},{8,6},{9,7},{10,... | collective-permute-start | bytes 589832 | tf_op jit(solution)/shard_map/ppermute | solution.py:459
  100.4 7.1 %collective-permute-start.26 = (bf16[384,256]{1,0:T(8,128)(2,1)S(1)}, bf16[384,256]{1,0:T(8,128)(2,1)S(1)}, u32[]{:S(2)}, u32[]{:S(2)}) collective-permute-start(bf16[384,256]{1,0:T(8,128)(2,1)S(1)} %pad_maximum_fusion.4), channel_id=1, source_target_pairs={{0,2},{1,3},{2,4},{3,5},{4,6},{5,7},{6,8},{7,9},{8,10},{9,11},{10,... | collective-permute-start | bytes 589832 | tf_op jit(solution)/shard_map/ppermute | solution.py:459
  107.5 5.6 %collective-permute-start.28 = (bf16[128,256]{1,0:T(8,128)(2,1)S(1)}, bf16[128,256]{1,0:T(8,128)(2,1)S(1)}, u32[]{:S(2)}, u32[]{:S(2)}) collective-permute-start(bf16[128,256]{1,0:T(8,128)(2,1)S(1)} %get-tuple-element.119), channel_id=1, source_target_pairs={{0,16},{1,17},{2,18},{3,19},{4,20},{5,21},{6,22},{7,23},{8,24},{9,... | collective-permute-start | bytes 196616 | tf_op jit(solution)/shard_map/ppermute | solution.py:539
  109.8 5.5 %collective-permute-start.29 = (bf16[128,256]{1,0:T(8,128)(2,1)S(1)}, bf16[128,256]{1,0:T(8,128)(2,1)S(1)}, u32[]{:S(2)}, u32[]{:S(2)}) collective-permute-start(bf16[128,256]{1,0:T(8,128)(2,1)S(1)} %get-tuple-element.120), channel_id=1, source_target_pairs={{0,2},{1,3},{2,4},{3,5},{4,6},{5,7},{6,8},{7,9},{8,10},{9,11},{10,... | collective-permute-start | bytes 196616 | tf_op jit(solution)/shard_map/ppermute | solution.py:459
  109.8 5.5 %collective-permute-start.30 = (bf16[128,256]{1,0:T(8,128)(2,1)S(1)}, bf16[128,256]{1,0:T(8,128)(2,1)S(1)}, u32[]{:S(2)}, u32[]{:S(2)}) collective-permute-start(bf16[128,256]{1,0:T(8,128)(2,1)S(1)} %get-tuple-element.121), channel_id=1, source_target_pairs={{0,14},{1,15},{2,0},{3,1},{4,2},{5,3},{6,4},{7,5},{8,6},{9,7},{10,... | collective-permute-start | bytes 196616 | tf_op jit(solution)/shard_map/ppermute | solution.py:459

commit v8 on v5

--- a/solution.py
+++ b/solution.py
@@ -31,6 +31,7 @@
 
 CORE_SWAP = [(i, i ^ 1) for i in range(N_CHAN)]
 X_SWAP = [(i, i ^ 16) for i in range(N_CHAN)]
+NEAR_STEPS = (3, 5, 2, 6, 1, 7, 0)
 X_HALF_SWAP = [(i, i ^ 1) for i in range(N_CTX)]
 Y_STEPS = (1, -1, 2)
 Z_GROUPS = [[x * 16 + z * 2 + c for z in range(N_Z)] for x in range(2) for c in range(2)]
@@ -193,7 +194,7 @@
         in_specs=[vmem, vmem if ready else pl.BlockSpec(memory_space=pltpu.HBM)] + [vmem] * len(earlier),
         out_specs=(vmem,) * (1 + len(ahead)),
         scratch_shapes=[] if ready else scratch,
-        compiler_params=pltpu.CompilerParams(vmem_limit_bytes=(4 if ready else 46) << 20),
+        compiler_params=pltpu.CompilerParams(vmem_limit_bytes=(4 if ready else 44) << 20),
         cost_estimate=pl.CostEstimate(
             flops=2 * 64 * 768 * 2048, bytes_accessed=(1 + len(ahead)) * (3 << 20), transcendentals=0
         ),
@@ -201,15 +202,15 @@
     )(rows, weight, *earlier)
 
 
-def back_step(n, held_ref, grad_ref, own_ref, other_ref):
+def back_step(n, at, held_ref, grad_ref, own_ref, other_ref):
     for core in (1, 0):
         target = other_ref if core else own_ref
         c = place_of("core") ^ core
         for shift in range(2):
             x = place_of("x") ^ shift
-            total = nn(held_ref[n, 0, x, c], grad_ref[0:BLOCK])
-            total += nn(held_ref[n, 1, x, c], grad_ref[BLOCK : 2 * BLOCK])
-            total += nn(held_ref[n, 2, x, c], grad_ref[2 * BLOCK :])
+            total = nn(held_ref[at, 0, x, c], grad_ref[0:BLOCK])
+            total += nn(held_ref[at, 1, x, c], grad_ref[BLOCK : 2 * BLOCK])
+            total += nn(held_ref[at, 2, x, c], grad_ref[2 * BLOCK :])
             target[n, shift] = total.astype(BF16)
 
 
@@ -221,8 +222,8 @@
     own = lax.axis_index("ctx")
     table_refs, refs = refs[:N_CTX], refs[N_CTX:]
     sources, refs = refs[:7], refs[7:]
-    row_ref, tap_ref, out_ref, grad_proj_ref, own_ref, other_ref = refs[:6]
-    raw_ref, tapped_ref, id_ref, grad_ref, side_ref, fwd_ref, weight_ref, sems = refs[6:]
+    row_ref, tap_ref, out_ref, grad_proj_ref, own_ref, other_ref, ahead_ref = refs[:7]
+    raw_ref, tapped_ref, id_ref, grad_ref, side_ref, fwd_ref, weight_ref, sems = refs[7:]
     copies = []
     for n in range(N_CTX):
         target = grad_ref.at[source_of(own, n)]
@@ -231,7 +232,10 @@
     copies.append(pltpu.make_async_copy(sources[5], fwd_ref, sems.at[N_CTX + 1]))
     far_z = (place_of("z") + N_Z // 2) & (N_Z - 1)
     copies.append(pltpu.make_async_copy(sources[6].at[:, :, far_z], weight_ref.at[0], sems.at[N_CTX + 2]))
-    for copy in copies:
+    for n, step in enumerate(NEAR_STEPS):
+        z = (place_of("z") + step) & (N_Z - 1)
+        copies.append(pltpu.make_async_copy(sources[6].at[:, :, z], ahead_ref.at[n], sems.at[N_CTX + 3 + n]))
+    for copy in copies[: N_CTX + 2]:
         copy.start()
     table = jnp.concatenate([ref[...].astype(F32) for ref in table_refs], axis=0).T.astype(BF16)
     table = jnp.concatenate([ref[...].astype(F32) for ref in table_refs], axis=0).T
@@ -248,6 +252,8 @@
         ids = grad_ref[block, BLOCK : BLOCK + EXTRA, :].astype(F32)
         ids = (ids[0:1] * 256.0 + ids[1:2]).astype(jnp.int32)
         id_ref[:, HALO + block * BLOCK : HALO + (block + 1) * BLOCK] = ids
+    for copy in copies[N_CTX + 2 :]:
+        copy.start()
     copies[N_CTX].wait()
 
     tile_rows = [(lax.broadcasted_iota(jnp.int32, (16, BLOCK), 0) + 16 * n).astype(F32).astype(BF16) for n in range(SHARE // 16)]
@@ -351,8 +357,9 @@
         for tap in (1, 2):
             total += tap_ref[rows, tap : tap + 1] * grads[:, tap : tap + BLOCK]
         grad_proj_ref[rows, :] = total.astype(BF16)
-    copies[N_CTX + 2].wait()
-    back_step(0, weight_ref, grad_proj_ref, own_ref, other_ref)
+    for copy in copies[N_CTX + 2 :]:
+        copy.wait()
+    back_step(0, 0, weight_ref, grad_proj_ref, own_ref, other_ref)
 
 
 def mix(pieces, grads, tables, weight):
@@ -365,9 +372,10 @@
             jax.ShapeDtypeStruct((3 * BLOCK, BLOCK), BF16),
             jax.ShapeDtypeStruct((1, 2, BLOCK, BLOCK), BF16),
             jax.ShapeDtypeStruct((1, 2, BLOCK, BLOCK), BF16),
+            jax.ShapeDtypeStruct((len(NEAR_STEPS), 3, 2, 2, BLOCK, BLOCK), BF16),
         ),
         in_specs=[vmem] * N_CTX + [pl.BlockSpec(memory_space=pl.ANY)] * 7 + [vmem] * 2,
-        out_specs=(vmem,) * 4,
+        out_specs=(vmem,) * 5,
         scratch_shapes=[
             pltpu.VMEM((3 * BLOCK, 2 * BLOCK), F32),
             pltpu.VMEM((3 * BLOCK, 3 * VOCAB), BF16),
@@ -376,51 +384,36 @@
             pltpu.VMEM((BLOCK, SIDE), BF16),
             pltpu.VMEM((GROUPS, BLOCK, BLOCK), BF16),
             pltpu.VMEM((1, 3, 2, 2, BLOCK, BLOCK), BF16),
-            pltpu.SemaphoreType.DMA((N_CTX + 3,)),
+            pltpu.SemaphoreType.DMA((N_CTX + 3 + len(NEAR_STEPS),)),
         ],
-        compiler_params=pltpu.CompilerParams(vmem_limit_bytes=47 << 20),
+        compiler_params=pltpu.CompilerParams(vmem_limit_bytes=30 << 20),
         cost_estimate=pl.CostEstimate(flops=3 << 30, bytes_accessed=8 << 20, transcendentals=1 << 16),
         name="mixer",
     )(*pieces, *grads, side, fwd, weight, row, taps)
 
 
-def back_kernel(step_ref, grad_ref, weight_ref, own_ref, other_ref, held_ref, sems):
-    count = own_ref.shape[0]
-
-    def copy(n):
-        z = (place_of("z") + step_ref[n]) & (N_Z - 1)
-        return pltpu.make_async_copy(weight_ref.at[:, :, z], held_ref.at[n], sems.at[n])
-
-    for n in range(count):
-        copy(n).start()
-
+def back_kernel(begin, grad_ref, held_ref, own_ref, other_ref):
     def one_step(n, carried):
-        copy(n).wait()
-        back_step(n, held_ref, grad_ref, own_ref, other_ref)
+        back_step(n, begin + n, held_ref, grad_ref, own_ref, other_ref)
         return carried
 
-    lax.fori_loop(0, count, one_step, 0)
-
-
-def back_project(grad_proj, weight, steps):
+    lax.fori_loop(0, own_ref.shape[0], one_step, 0)
+
+
+def back_project(grad_proj, held, begin, count):
     vmem = pl.BlockSpec(memory_space=pltpu.VMEM)
-    count = len(steps)
     part = jax.ShapeDtypeStruct((count, 2, BLOCK, BLOCK), BF16)
     return pl.pallas_call(
-        back_kernel,
+        functools.partial(back_kernel, begin),
         out_shape=(part, part),
-        in_specs=[pl.BlockSpec(memory_space=pltpu.SMEM), vmem, pl.BlockSpec(memory_space=pltpu.HBM)],
-        out_specs=(vmem, vmem),
-        scratch_shapes=[
-            pltpu.VMEM((count, 3, 2, 2, BLOCK, BLOCK), BF16),
-            pltpu.SemaphoreType.DMA((count,)),
-        ],
-        compiler_params=pltpu.CompilerParams(vmem_limit_bytes=50 << 20),
+        in_specs=[vmem] * 2,
+        out_specs=(vmem,) * 2,
+        compiler_params=pltpu.CompilerParams(vmem_limit_bytes=4 << 20),
         cost_estimate=pl.CostEstimate(
             flops=2 * 256 * 768 * 1024 * count, bytes_accessed=count << 21, transcendentals=0
         ),
         name="back_project",
-    )(jnp.asarray(steps, jnp.int32), grad_proj, weight)
+    )(grad_proj, held)
 
 
 def project_features(rows, weight, pair):
@@ -431,8 +424,8 @@
     across = lax.ppermute(held, "chan", CORE_SWAP)
     held, pair = lax.optimization_barrier((held, pair))
     grads = gather_pairs(pair)
-    sums, weight_beside, weight_both = project(0, held, weight, ahead=(1, 3))
-    (sums,) = project(2, across, weight, sums)
+    sums, weight_across, weight_beside, weight_both = project(0, held, weight, ahead=(2, 1, 3))
+    (sums,) = project(2, across, weight_across, sums, ready=True)
     beside, sums = lax.optimization_barrier((beside, sums))
     both = lax.ppermute(beside, "chan", CORE_SWAP)
     (sums,) = project(1, beside, weight_beside, sums, ready=True)
@@ -461,7 +454,7 @@
     return lax.ppermute(value.astype(BF16), "chan", z_shift(by))
 
 
-def reduce_chan(far_parts, grad_proj, weight):
+def reduce_chan(far_parts, grad_proj, held):
     terms = {}
 
     def swap(parts):
@@ -480,14 +473,14 @@
         return {(half, by): moved(value, by) for (half, by), value in values.items()}
 
     own, swapped = swap(far_parts)
-    near = back_project(grad_proj, weight, (3, 5))
+    near = back_project(grad_proj, held, 0, 2)
     (swapped, near) = lax.optimization_barrier((swapped, near))
     add_terms((4,), own, swapped)
     ways = {1: (1, -1), 0: (-1, 1)}
     chain = send({(half, ways[half][0]): terms[4, half] for half in (1, 0)})
     grad_proj, near = lax.optimization_barrier((grad_proj, near))
     near_own, near_swapped = swap(near)
-    middle = back_project(grad_proj, weight, (2, 6))
+    middle = back_project(grad_proj, held, 2, 2)
     arrived, middle = arrive(chain, middle)
     add_terms((3, 5), near_own, near_swapped)
     middle_own, middle_swapped = swap(middle)
@@ -498,7 +491,7 @@
         chain[half, short] = terms[(3 * short) % 8, half]
     chain = send(chain)
     grad_proj, middle_own = lax.optimization_barrier((grad_proj, middle_own))
-    last = back_project(grad_proj, weight, (1, 7, 0))
+    last = back_project(grad_proj, held, 4, 3)
     arrived, last = arrive(chain, last)
     add_terms((2, 6), middle_own, middle_swapped)
     last_own, last_swapped = swap(last)
@@ -521,8 +514,8 @@
     pieces = gather_ctx(part)
     gains = modal_residues * jnp.sqrt(-jnp.expm1(-2.0 * modal_rates))
     tables = make_tables(modal_rates, gains, feat_taps)
-    output, grad_proj, *far_parts = mix(pieces, grads, tables, weight)
-    return (output, reduce_chan(far_parts, grad_proj, weight).T)
+    output, grad_proj, own, other, held = mix(pieces, grads, tables, weight)
+    return (output, reduce_chan((own, other), grad_proj, held).T)
 
 
 def solution(mesh):

time: 115 us -> 117 us (1.017)
  waiting for transfers between devices: 22.5 us -> 30.1 us
  Pallas kernels: 35.6 us -> 28.7 us
  starting transfers between devices: 49.8 us -> 51.8 us
    pallas_call x3, Pallas kernels: 10 us -> 4 us  [back_project(): pl.pallas_call(functools.partial(back_kernel, begin), out_shape=(part, pa...]
    ppermute x14, waiting for transfers between devices: 8.11 us -> 13.4 us  [moved(): return lax.ppermute(value.astype(BF16), 'chan', z_shift(by))]
    ppermute x14, starting transfers between devices: 20.6 us -> 22.6 us  [moved(): return lax.ppermute(value.astype(BF16), 'chan', z_shift(by))]
    ppermute x3, starting transfers between devices: 3.34 us -> 4.56 us  [gather_pairs(): return [pair] + [lax.ppermute(pair, 'ctx', y_shift(by)) for by in Y_STEPS]]
    unnamed x19 -> x13, local copies, waits for them, and re-layouts: 3.32 us -> 3.3 us
  transfers between devices with their start and end apart: 34 -> 34, of which waited for: 10 -> 12; matrix products, arithmetic and copies ran while one was open for 0% -> 0% of each run, Pallas kernels for 19% -> 13%
where the time goes in v8:
time: 117 us; the launch traced here: 116 us
  starting transfers between devices  51.8 us (44%)
  waiting for transfers between devices  30.1 us (26%)
  Pallas kernels  28.7 us (25%)
  local copies, waits for them, and re-layouts  4.02 us (3%)
    ppermute x14, starting transfers between devices, moved(): return lax.ppermute(value.astype(BF16), 'chan', z_shift(by))  22.6 us
    ppermute x14, waiting for transfers between devices, moved(): return lax.ppermute(value.astype(BF16), 'chan', z_shift(by))  13.4 us
    pallas_call x1, Pallas kernels, mix(): pl.pallas_call(mixer_kernel, out_shape=(jax.ShapeDtypeStruct((BLOCK, BLOC...  12.7 us
    all_to_all x1, starting transfers between devices, project_features(): lax.all_to_all(jnp.broadcast_to(rows[None], (N_Z,) + rows.shape), 'chan',...  8.47 us
    ppermute x6, starting transfers between devices, gather_ctx(): found += [lax.ppermute(piece, 'ctx', y_shift(by)) for by in Y_STEPS]  8.07 us
    pallas_call x4, Pallas kernels, project(): pl.pallas_call(functools.partial(project_kernel, part, sums is None, read...  7.96 us
    all_to_all x1, waiting for transfers between devices, project_features(): lax.all_to_all(jnp.broadcast_to(rows[None], (N_Z,) + rows.shape), 'chan',...  7.08 us
    ppermute x3, waiting for transfers between devices, gather_pairs(): return [pair] + [lax.ppermute(pair, 'ctx', y_shift(by)) for by in Y_STEPS]  4.75 us
  transfers between devices with their start and end apart: 34, of which 12 were waited for; matrix products, arithmetic and copies ran while one was open for 0% of the time, Pallas kernels for 13%

profile of v8, /device:TPU:24, one launch (start us, length us, event | category | flops | bytes accessed | tf_op | source)
XLA Modules:
  0.0 116.4 jit_solution(7584041395661439485)
XLA Ops:
  0.6 0.9 copy-done
  1.6 0.7 broadcast_in_dim.2
  2.3 8.5 %all-to-all-start = ((bf16[8,64,256]{2,1,0:T(8,128)(2,1)}), bf16[8,64,256]{2,1,0:T(8,128)(2,1)S(1)}, u32[]{:S(2)}, u32[]{:S(2)}) async-start(bf16[8,64,256]{2,1,0:T(8,128)(2,1)} %broadcast_in_dim.2), calls=%async_computation | async-start | bytes 524288 | tf_op jit(solution)/shard_map/all_to_all | solution.py:420
  10.8 0.9 copy-done.1
  11.7 0.7 copy-done.3
  12.5 3.1 %collective-permute-start.2 = (bf16[272,256]{1,0:T(8,128)(2,1)S(1)}, bf16[272,256]{1,0:T(8,128)(2,1)S(1)}, u32[]{:S(2)}, u32[]{:S(2)}) collective-permute-start(bf16[272,256]{1,0:T(8,128)(2,1)S(1)} %payload.1), channel_id=1, source_target_pairs={{0,32},{32,0},{64,96},{96,64},{128,160},{160,128},{192,224},{224,1... | collective-permute-start | bytes 417800 | tf_op jit(solution)/shard_map/ppermute | solution.py:446
  15.6 7.1 %all-to-all-done.refs_0_ = bf16[8,64,256]{2,1,0:T(8,128)(2,1)S(1)} async-done(((bf16[8,64,256]{2,1,0:T(8,128)(2,1)}), bf16[8,64,256]{2,1,0:T(8,128)(2,1)S(1)}, u32[]{:S(2)}, u32[]{:S(2)}) %all-to-all-start) | async-done | bytes 262176 | tf_op jit(solution)/shard_map/all_to_all | solution.py:420
  22.6 1.5 %collective-permute-start = (bf16[8,64,256]{2,1,0:T(8,128)(2,1)S(1)}, bf16[8,64,256]{2,1,0:T(8,128)(2,1)S(1)}, u32[]{:S(2)}, u32[]{:S(2)}) collective-permute-start(bf16[8,64,256]{2,1,0:T(8,128)(2,1)S(1)} %all-to-all-done.refs_0_), channel_id=1, source_target_pairs={{0,16},{1,17},{2,18},{3,19},{4,20},{5,21},{6,22},{7,23},{8,24},{9,... | collective-permute-start | bytes 786440 | tf_op jit(solution)/shard_map/ppermute | solution.py:423
  24.2 1.3 %collective-permute-start.6 = (bf16[2,272,256]{2,1,0:T(8,128)(2,1)S(1)}, bf16[2,272,256]{2,1,0:T(8,128)(2,1)S(1)}, u32[]{:S(2)}, u32[]{:S(2)}) collective-permute-start(bf16[2,272,256]{2,1,0:T(8,128)(2,1)S(1)} %pad_maximum_fusion.refs_8_), channel_id=1, source_target_pairs={{0,128},{32,160},{64,192},{96,224},{128,0},{160,32},{192,64},{224,... | collective-permute-start | bytes 835592 | tf_op jit(solution)/shard_map/ppermute | solution.py:450
  25.5 3.2 %collective-permute-start.4 = (bf16[2,272,256]{2,1,0:T(8,128)(2,1)S(1)}, bf16[2,272,256]{2,1,0:T(8,128)(2,1)S(1)}, u32[]{:S(2)}, u32[]{:S(2)}) collective-permute-start(bf16[2,272,256]{2,1,0:T(8,128)(2,1)S(1)} %pad_maximum_fusion.refs_8_), channel_id=1, source_target_pairs={{0,64},{32,96},{64,128},{96,160},{128,192},{160,224},{192,0},{224,... | collective-permute-start | bytes 835592 | tf_op jit(solution)/shard_map/ppermute | solution.py:450
  28.7 4.7 %project.4 = (f32[64,768]{1,0:T(8,128)S(1)}, bf16[3,8,256,256]{3,2,1,0:T(8,128)(2,1)S(1)}, bf16[3,8,256,256]{3,2,1,0:T(8,128)(2,1)S(1)}, bf16[3,8,256,256]{3,2,1,0:T(8,128)(2,1)S(1)}) custom-call(bf16[8,64,256]{2,1,0:T(8,128)(2,1)S(1)} %all-to-all-done.refs_0_, bf16[3,2,8,2,256,256]{5,4,3,2,1,0:T(8,128)(2,1)} %bitcast.74), custom_call_target="tpu_custom_call" | custom-call | flops 201326592 | bytes 12582912 | tf_op jit(solution)/shard_map/project/pallas_call | solution.py:191
  33.4 1.1 project.5.refs_2_
  34.7 1.1 project.6.refs_2_
  35.8 4.7 %collective-permute-done.5.refs_10_ = bf16[2,272,256]{2,1,0:T(8,128)(2,1)S(1)} collective-permute-done((bf16[2,272,256]{2,1,0:T(8,128)(2,1)S(1)}, bf16[2,272,256]{2,1,0:T(8,128)(2,1)S(1)}, u32[]{:S(2)}, u32[]{:S(2)}) %collective-permute-start.5) | collective-permute-done | bytes 278560 | tf_op jit(solution)/shard_map/ppermute | solution.py:450
  40.5 1.1 project.7.refs_0_
  41.6 2.8 %collective-permute-start.7 = (bf16[64,768]{1,0:T(8,128)(2,1)S(1)}, bf16[64,768]{1,0:T(8,128)(2,1)S(1)}, u32[]{:S(2)}, u32[]{:S(2)}) collective-permute-start(bf16[64,768]{1,0:T(8,128)(2,1)S(1)} %project.7.refs_0_), channel_id=1, source_target_pairs={{0,32},{32,0},{64,96},{96,64},{128,160},{160,128},{192,224},{224,1... | collective-permute-start | bytes 294920 | tf_op jit(solution)/shard_map/ppermute | solution.py:438
  44.4 1.4 %collective-permute-start.12 = (bf16[64,768]{1,0:T(8,128)(2,1)S(1)}, bf16[64,768]{1,0:T(8,128)(2,1)S(1)}, u32[]{:S(2)}, u32[]{:S(2)}) collective-permute-start(bf16[64,768]{1,0:T(8,128)(2,1)S(1)} %project.7.refs_0_), channel_id=1, source_target_pairs={{0,128},{32,160},{64,192},{96,224},{128,0},{160,32},{192,64},{224,... | collective-permute-start | bytes 294920 | tf_op jit(solution)/shard_map/ppermute | solution.py:441
  45.9 3.2 %collective-permute-start.8 = (bf16[64,768]{1,0:T(8,128)(2,1)S(1)}, bf16[64,768]{1,0:T(8,128)(2,1)S(1)}, u32[]{:S(2)}, u32[]{:S(2)}) collective-permute-start(bf16[64,768]{1,0:T(8,128)(2,1)S(1)} %project.7.refs_0_), channel_id=1, source_target_pairs={{0,64},{32,96},{64,128},{96,160},{128,192},{160,224},{192,0},{224,... | collective-permute-start | bytes 294920 | tf_op jit(solution)/shard_map/ppermute | solution.py:441
  49.1 0.9 collective-permute-start.13
  50.0 0.7 collective-permute-start.11
  50.7 0.7 collective-permute-done.12.refs_6_
  51.5 1.8 %collective-permute-start.9 = (bf16[64,768]{1,0:T(8,128)(2,1)S(1)}, bf16[64,768]{1,0:T(8,128)(2,1)S(1)}, u32[]{:S(2)}, u32[]{:S(2)}) collective-permute-start(bf16[64,768]{1,0:T(8,128)(2,1)S(1)} %collective-permute-done.7.refs_1_), channel_id=1, source_target_pairs={{0,64},{32,96},{64,128},{96,160},{128,192},{160,224},{192,0},{224,... | collective-permute-start | bytes 294920 | tf_op jit(solution)/shard_map/ppermute | solution.py:441
  53.3 3.9 %filter_tables.1 = (bf16[16,256,256]{2,1,0:T(8,128)(2,1)S(1)}, bf16[256,1152]{1,0:T(8,128)(2,1)S(1)}, f32[2,256]{1,0:T(2,128)S(1)}, f32[768,3]{1,0:T(8,128)S(1)}) custom-call(f32[16,16]{1,0:T(8,128)S(1)} %copy-done.2, f32[16,16]{1,0:T(8,128)S(1)} %sqrt_multiply_fusion.gain_ref, f32[3,3,256]{2,1,0:T(4,128)S(1)} %copy-done.4), custom_call_target="tpu_custom_call" | custom-call | flops 402653184 | bytes 5242880 | tf_op jit(solution)/shard_map/filter_tables/pallas_call | solution.py:141
  57.3 12.7 %mixer.1 = (bf16[256,256]{1,0:T(8,128)(2,1)}, bf16[768,256]{1,0:T(8,128)(2,1)S(1)}, bf16[1,2,256,256]{3,2,1,0:T(8,128)(2,1)S(1)}, bf16[1,2,256,256]{3,2,1,0:T(8,...) custom-call(bf16[64,768]{1,0:T(8,128)(2,1)S(1)} %project.7.refs_0_, bf16[64,768]{1,0:T(8,128)(2,1)S(1)} %collective-permute-done.7.refs_1_, ...), custom_call_target="tpu_custom_call" | custom-call | flops 3221225472 | bytes 8388608 | tf_op jit(solution)/shard_map/mixer/pallas_call | solution.py:368
  70.1 1.1 back_project.3
  71.2 0.4 collective-permute-done.14
  71.9 0.6 collective-permute-start.17
  72.5 2.7 %collective-permute-start.16 = (bf16[256,256]{1,0:T(8,128)(2,1)S(1)}, bf16[256,256]{1,0:T(8,128)(2,1)S(1)}, u32[]{:S(2)}, u32[]{:S(2)}) collective-permute-start(bf16[256,256]{1,0:T(8,128)(2,1)S(1)} %get-tuple-element.115), channel_id=1, source_target_pairs={{0,14},{1,15},{2,0},{3,1},{4,2},{5,3},{6,4},{7,5},{8,6},{9,7},{10,... | collective-permute-start | bytes 393224 | tf_op jit(solution)/shard_map/ppermute | solution.py:454
  75.2 1.1 back_project.4
  76.3 2.5 %collective-permute-done.17 = bf16[256,256]{1,0:T(8,128)(2,1)S(1)} collective-permute-done((bf16[256,256]{1,0:T(8,128)(2,1)S(1)}, bf16[256,256]{1,0:T(8,128)(2,1)S(1)}, u32[]{:S(2)}, u32[]{:S(2)}) %collective-permute-start.17) | collective-permute-done | bytes 131104 | tf_op jit(solution)/shard_map/ppermute | solution.py:454
  78.9 3.0 %collective-permute-start.20 = (bf16[256,256]{1,0:T(8,128)(2,1)S(1)}, bf16[256,256]{1,0:T(8,128)(2,1)S(1)}, u32[]{:S(2)}, u32[]{:S(2)}) collective-permute-start(bf16[256,256]{1,0:T(8,128)(2,1)S(1)} %get-tuple-element.112), channel_id=1, source_target_pairs={{0,14},{1,15},{2,0},{3,1},{4,2},{5,3},{6,4},{7,5},{8,6},{9,7},{10,... | collective-permute-start | bytes 393224 | tf_op jit(solution)/shard_map/ppermute | solution.py:454
  82.2 3.3 %collective-permute-start.18 = (bf16[256,256]{1,0:T(8,128)(2,1)S(1)}, bf16[256,256]{1,0:T(8,128)(2,1)S(1)}, u32[]{:S(2)}, u32[]{:S(2)}) collective-permute-start(bf16[256,256]{1,0:T(8,128)(2,1)S(1)} %get-tuple-element.111), channel_id=1, source_target_pairs={{0,14},{1,15},{2,0},{3,1},{4,2},{5,3},{6,4},{7,5},{8,6},{9,7},{10,... | collective-permute-start | bytes 393224 | tf_op jit(solution)/shard_map/ppermute | solution.py:454
  85.5 1.7 %back_project.5 = (bf16[3,2,256,256]{3,2,1,0:T(8,128)(2,1)S(1)}, bf16[3,2,256,256]{3,2,1,0:T(8,128)(2,1)S(1)}) custom-call(bf16[768,256]{1,0:T(8,128)(2,1)S(1)} %get-tuple-element.89.grad_ref, bf16[7,3,2,2,256,256]{5,4,3,2,1,0:T(8,128)(2,1)S(1)} %get-tuple-element.74.held_ref), custom_call_target="tpu_custom_call" | custom-call | flops 1207959552 | bytes 6291456 | tf_op jit(solution)/shard_map/back_project/pallas_call | solution.py:406
  87.2 1.7 %collective-permute-done.19 = bf16[256,256]{1,0:T(8,128)(2,1)S(1)} collective-permute-done((bf16[256,256]{1,0:T(8,128)(2,1)S(1)}, bf16[256,256]{1,0:T(8,128)(2,1)S(1)}, u32[]{:S(2)}, u32[]{:S(2)}) %collective-permute-start.19) | collective-permute-done | bytes 131104 | tf_op jit(solution)/shard_map/ppermute | solution.py:454
  88.9 1.4 %collective-permute-done.21 = bf16[256,256]{1,0:T(8,128)(2,1)S(1)} collective-permute-done((bf16[256,256]{1,0:T(8,128)(2,1)S(1)}, bf16[256,256]{1,0:T(8,128)(2,1)S(1)}, u32[]{:S(2)}, u32[]{:S(2)}) %collective-permute-start.21) | collective-permute-done | bytes 131104 | tf_op jit(solution)/shard_map/ppermute | solution.py:454
  90.3 0.2 fusion.9
  90.6 3.2 %collective-permute-start.30 = (bf16[256,256]{1,0:T(8,128)(2,1)S(1)}, bf16[256,256]{1,0:T(8,128)(2,1)S(1)}, u32[]{:S(2)}, u32[]{:S(2)}) collective-permute-start(bf16[256,256]{1,0:T(8,128)(2,1)S(1)} %get-tuple-element.107), channel_id=1, source_target_pairs={{0,14},{1,15},{2,0},{3,1},{4,2},{5,3},{6,4},{7,5},{8,6},{9,7},{10,... | collective-permute-start | bytes 393224 | tf_op jit(solution)/shard_map/ppermute | solution.py:454
  93.8 3.2 %collective-permute-start.26 = (bf16[256,256]{1,0:T(8,128)(2,1)S(1)}, bf16[256,256]{1,0:T(8,128)(2,1)S(1)}, u32[]{:S(2)}, u32[]{:S(2)}) collective-permute-start(bf16[256,256]{1,0:T(8,128)(2,1)S(1)} %get-tuple-element.109), channel_id=1, source_target_pairs={{0,14},{1,15},{2,0},{3,1},{4,2},{5,3},{6,4},{7,5},{8,6},{9,7},{10,... | collective-permute-start | bytes 393224 | tf_op jit(solution)/shard_map/ppermute | solution.py:454
  97.1 0.7 collective-permute-done.24
  97.8 2.7 %collective-permute-done.28 = bf16[256,256]{1,0:T(8,128)(2,1)S(1)} collective-permute-done((bf16[256,256]{1,0:T(8,128)(2,1)S(1)}, bf16[256,256]{1,0:T(8,128)(2,1)S(1)}, u32[]{:S(2)}, u32[]{:S(2)}) %collective-permute-start.28) | collective-permute-done | bytes 131104 | tf_op jit(solution)/shard_map/ppermute | solution.py:454
  100.5 0.2 fusion.8
  100.7 3.0 %collective-permute-start.31 = (bf16[256,256]{1,0:T(8,128)(2,1)S(1)}, bf16[256,256]{1,0:T(8,128)(2,1)S(1)}, u32[]{:S(2)}, u32[]{:S(2)}) collective-permute-start(bf16[256,256]{1,0:T(8,128)(2,1)S(1)} %get-tuple-element.103), channel_id=1, source_target_pairs={{0,14},{1,15},{2,0},{3,1},{4,2},{5,3},{6,4},{7,5},{8,6},{9,7},{10,... | collective-permute-start | bytes 393224 | tf_op jit(solution)/shard_map/ppermute | solution.py:454
  103.8 3.3 %collective-permute-start.27 = (bf16[256,256]{1,0:T(8,128)(2,1)S(1)}, bf16[256,256]{1,0:T(8,128)(2,1)S(1)}, u32[]{:S(2)}, u32[]{:S(2)}) collective-permute-start(bf16[256,256]{1,0:T(8,128)(2,1)S(1)} %get-tuple-element.105), channel_id=1, source_target_pairs={{0,14},{1,15},{2,0},{3,1},{4,2},{5,3},{6,4},{7,5},{8,6},{9,7},{10,... | collective-permute-start | bytes 393224 | tf_op jit(solution)/shard_map/ppermute | solution.py:454
  107.1 3.3 %collective-permute-done.29 = bf16[256,256]{1,0:T(8,128)(2,1)S(1)} collective-permute-done((bf16[256,256]{1,0:T(8,128)(2,1)S(1)}, bf16[256,256]{1,0:T(8,128)(2,1)S(1)}, u32[]{:S(2)}, u32[]{:S(2)}) %collective-permute-start.29) | collective-permute-done | bytes 131104 | tf_op jit(solution)/shard_map/ppermute | solution.py:454
  110.5 0.3 collective-permute-start.32
  110.8 1.0 collective-permute-done.25
  111.8 3.7 %collective-permute-done.32 = bf16[256,256]{1,0:T(8,128)(2,1)S(1)} collective-permute-done((bf16[256,256]{1,0:T(8,128)(2,1)S(1)}, bf16[256,256]{1,0:T(8,128)(2,1)S(1)}, u32[]{:S(2)}, u32[]{:S(2)}) %collective-permute-start.32) | collective-permute-done | bytes 131104 | tf_op jit(solution)/shard_map/ppermute | solution.py:504
  115.6 0.8 copy.9
  (54 shorter events, 1.3 us)
Async XLA Ops:
  0.6 1.0 copy-start
  2.3 20.3 %all-to-all-start = ((bf16[8,64,256]{2,1,0:T(8,128)(2,1)}), bf16[8,64,256]{2,1,0:T(8,128)(2,1)S(1)}, u32[]{:S(2)}, u32[]{:S(2)}) async-start(bf16[8,64,256]{2,1,0:T(8,128)(2,1)} %broadcast_in_dim.2), calls=%async_computation | async-start | bytes 524288 | tf_op jit(solution)/shard_map/all_to_all | solution.py:420
  10.8 0.9 copy-start.1
  11.7 0.7 copy-start.3
  12.5 11.7 %collective-permute-start.2 = (bf16[272,256]{1,0:T(8,128)(2,1)S(1)}, bf16[272,256]{1,0:T(8,128)(2,1)S(1)}, u32[]{:S(2)}, u32[]{:S(2)}) collective-permute-start(bf16[272,256]{1,0:T(8,128)(2,1)S(1)} %payload.1), channel_id=1, source_target_pairs={{0,32},{32,0},{64,96},{96,64},{128,160},{160,128},{192,224},{224,1... | collective-permute-start | bytes 417800 | tf_op jit(solution)/shard_map/ppermute | solution.py:446
  22.6 10.8 %collective-permute-start.1 = (bf16[8,64,256]{2,1,0:T(8,128)(2,1)S(1)}, bf16[8,64,256]{2,1,0:T(8,128)(2,1)S(1)}, u32[]{:S(2)}, u32[]{:S(2)}) collective-permute-start(bf16[8,64,256]{2,1,0:T(8,128)(2,1)S(1)} %all-to-all-done.refs_0_), channel_id=1, source_target_pairs={{0,1},{1,0},{2,3},{3,2},{4,5},{5,4},{6,7},{7,6},{8,9},{9,8},{10,11... | collective-permute-start | bytes 786440 | tf_op jit(solution)/shard_map/ppermute | solution.py:424
  22.6 11.9 %collective-permute-start = (bf16[8,64,256]{2,1,0:T(8,128)(2,1)S(1)}, bf16[8,64,256]{2,1,0:T(8,128)(2,1)S(1)}, u32[]{:S(2)}, u32[]{:S(2)}) collective-permute-start(bf16[8,64,256]{2,1,0:T(8,128)(2,1)S(1)} %all-to-all-done.refs_0_), channel_id=1, source_target_pairs={{0,16},{1,17},{2,18},{3,19},{4,20},{5,21},{6,22},{7,23},{8,24},{9,... | collective-permute-start | bytes 786440 | tf_op jit(solution)/shard_map/ppermute | solution.py:423
  24.2 11.6 %collective-permute-start.6 = (bf16[2,272,256]{2,1,0:T(8,128)(2,1)S(1)}, bf16[2,272,256]{2,1,0:T(8,128)(2,1)S(1)}, u32[]{:S(2)}, u32[]{:S(2)}) collective-permute-start(bf16[2,272,256]{2,1,0:T(8,128)(2,1)S(1)} %pad_maximum_fusion.refs_8_), channel_id=1, source_target_pairs={{0,128},{32,160},{64,192},{96,224},{128,0},{160,32},{192,64},{224,... | collective-permute-start | bytes 835592 | tf_op jit(solution)/shard_map/ppermute | solution.py:450
  25.5 15.0 %collective-permute-start.5 = (bf16[2,272,256]{2,1,0:T(8,128)(2,1)S(1)}, bf16[2,272,256]{2,1,0:T(8,128)(2,1)S(1)}, u32[]{:S(2)}, u32[]{:S(2)}) collective-permute-start(bf16[2,272,256]{2,1,0:T(8,128)(2,1)S(1)} %pad_maximum_fusion.refs_8_), channel_id=1, source_target_pairs={{0,192},{32,224},{64,0},{96,32},{128,64},{160,96},{192,128},{224,1... | collective-permute-start | bytes 835592 | tf_op jit(solution)/shard_map/ppermute | solution.py:450
  25.5 15.0 %collective-permute-start.4 = (bf16[2,272,256]{2,1,0:T(8,128)(2,1)S(1)}, bf16[2,272,256]{2,1,0:T(8,128)(2,1)S(1)}, u32[]{:S(2)}, u32[]{:S(2)}) collective-permute-start(bf16[2,272,256]{2,1,0:T(8,128)(2,1)S(1)} %pad_maximum_fusion.refs_8_), channel_id=1, source_target_pairs={{0,64},{32,96},{64,128},{96,160},{128,192},{160,224},{192,0},{224,... | collective-permute-start | bytes 835592 | tf_op jit(solution)/shard_map/ppermute | solution.py:450
  34.5 6.0 %collective-permute-start.3 = (bf16[8,64,256]{2,1,0:T(8,128)(2,1)S(1)}, bf16[8,64,256]{2,1,0:T(8,128)(2,1)S(1)}, u32[]{:S(2)}, u32[]{:S(2)}) collective-permute-start(bf16[8,64,256]{2,1,0:T(8,128)(2,1)S(1)} %collective-permute-done.refs_0_), channel_id=1, source_target_pairs={{0,1},{1,0},{2,3},{3,2},{4,5},{5,4},{6,7},{7,6},{8,9},{9,8},{10,11... | collective-permute-start | bytes 786440 | tf_op jit(solution)/shard_map/ppermute | solution.py:430
  34.6 18.6 %copy-start.2 = (f32[16,16]{1,0:T(8,128)S(1)}, f32[16,16]{1,0:T(8,128)}, u32[]{:S(2)}) copy-start(f32[16,16]{1,0:T(8,128)} %rate_ref) | copy-start | bytes 3076
  34.7 18.6 %copy-start.5 = (f32[16,16]{1,0:T(8,128)S(1)}, f32[16,16]{1,0:T(8,128)}, u32[]{:S(2)}) copy-start(f32[16,16]{1,0:T(8,128)} %param.12) | copy-start | bytes 3076
  34.7 18.6 %copy-start.4 = (f32[3,3,256]{2,1,0:T(4,128)S(1)}, f32[3,3,256]{2,1,0:T(4,128)}, u32[]{:S(2)}) copy-start(f32[3,3,256]{2,1,0:T(4,128)} %tap_ref.1) | copy-start | bytes 27652
  41.6 7.4 %collective-permute-start.7 = (bf16[64,768]{1,0:T(8,128)(2,1)S(1)}, bf16[64,768]{1,0:T(8,128)(2,1)S(1)}, u32[]{:S(2)}, u32[]{:S(2)}) collective-permute-start(bf16[64,768]{1,0:T(8,128)(2,1)S(1)} %project.7.refs_0_), channel_id=1, source_target_pairs={{0,32},{32,0},{64,96},{96,64},{128,160},{160,128},{192,224},{224,1... | collective-permute-start | bytes 294920 | tf_op jit(solution)/shard_map/ppermute | solution.py:438
  44.4 7.0 %collective-permute-start.12 = (bf16[64,768]{1,0:T(8,128)(2,1)S(1)}, bf16[64,768]{1,0:T(8,128)(2,1)S(1)}, u32[]{:S(2)}, u32[]{:S(2)}) collective-permute-start(bf16[64,768]{1,0:T(8,128)(2,1)S(1)} %project.7.refs_0_), channel_id=1, source_target_pairs={{0,128},{32,160},{64,192},{96,224},{128,0},{160,32},{192,64},{224,... | collective-permute-start | bytes 294920 | tf_op jit(solution)/shard_map/ppermute | solution.py:441
  45.8 11.4 %collective-permute-start.10 = (bf16[64,768]{1,0:T(8,128)(2,1)S(1)}, bf16[64,768]{1,0:T(8,128)(2,1)S(1)}, u32[]{:S(2)}, u32[]{:S(2)}) collective-permute-start(bf16[64,768]{1,0:T(8,128)(2,1)S(1)} %project.7.refs_0_), channel_id=1, source_target_pairs={{0,192},{32,224},{64,0},{96,32},{128,64},{160,96},{192,128},{224,1... | collective-permute-start | bytes 294920 | tf_op jit(solution)/shard_map/ppermute | solution.py:441
  45.9 11.3 %collective-permute-start.8 = (bf16[64,768]{1,0:T(8,128)(2,1)S(1)}, bf16[64,768]{1,0:T(8,128)(2,1)S(1)}, u32[]{:S(2)}, u32[]{:S(2)}) collective-permute-start(bf16[64,768]{1,0:T(8,128)(2,1)S(1)} %project.7.refs_0_), channel_id=1, source_target_pairs={{0,64},{32,96},{64,128},{96,160},{128,192},{160,224},{192,0},{224,... | collective-permute-start | bytes 294920 | tf_op jit(solution)/shard_map/ppermute | solution.py:441
  49.1 8.2 %collective-permute-start.13 = (bf16[64,768]{1,0:T(8,128)(2,1)S(1)}, bf16[64,768]{1,0:T(8,128)(2,1)S(1)}, u32[]{:S(2)}, u32[]{:S(2)}) collective-permute-start(bf16[64,768]{1,0:T(8,128)(2,1)S(1)} %collective-permute-done.7.refs_1_), channel_id=1, source_target_pairs={{0,128},{32,160},{64,192},{96,224},{128,0},{160,32},{192,64},{224,... | collective-permute-start | bytes 294920 | tf_op jit(solution)/shard_map/ppermute | solution.py:441
  50.0 7.2 %collective-permute-start.11 = (bf16[64,768]{1,0:T(8,128)(2,1)S(1)}, bf16[64,768]{1,0:T(8,128)(2,1)S(1)}, u32[]{:S(2)}, u32[]{:S(2)}) collective-permute-start(bf16[64,768]{1,0:T(8,128)(2,1)S(1)} %collective-permute-done.7.refs_1_), channel_id=1, source_target_pairs={{0,192},{32,224},{64,0},{96,32},{128,64},{160,96},{192,128},{224,1... | collective-permute-start | bytes 294920 | tf_op jit(solution)/shard_map/ppermute | solution.py:441
  51.5 5.8 %collective-permute-start.9 = (bf16[64,768]{1,0:T(8,128)(2,1)S(1)}, bf16[64,768]{1,0:T(8,128)(2,1)S(1)}, u32[]{:S(2)}, u32[]{:S(2)}) collective-permute-start(bf16[64,768]{1,0:T(8,128)(2,1)S(1)} %collective-permute-done.7.refs_1_), channel_id=1, source_target_pairs={{0,64},{32,96},{64,128},{96,160},{128,192},{160,224},{192,0},{224,... | collective-permute-start | bytes 294920 | tf_op jit(solution)/shard_map/ppermute | solution.py:441
  70.0 1.6 %collective-permute-start.14 = (bf16[1,2,256,256]{3,2,1,0:T(8,128)(2,1)S(1)}, bf16[1,2,256,256]{3,2,1,0:T(8,128)(2,1)S(1)}, u32[]{:S(2)}, u32[]{:S(2)}) collective-permute-start(bf16[1,2,256,256]{3,2,1,0:T(8,128)(2,1)S(1)} %get-tuple-element.73), channel_id=1, source_target_pairs={{0,1},{1,0},{2,3},{3,2},{4,5},{5,4},{6,7},{7,6},{8,9},{9,8},{10,11... | collective-permute-start | bytes 786440 | tf_op jit(solution)/shard_map/ppermute | solution.py:461
  71.6 7.3 %collective-permute-start.15 = (bf16[2,2,256,256]{3,2,1,0:T(8,128)(2,1)S(1)}, bf16[2,2,256,256]{3,2,1,0:T(8,128)(2,1)S(1)}, u32[]{:S(2)}, u32[]{:S(2)}) collective-permute-start(bf16[2,2,256,256]{3,2,1,0:T(8,128)(2,1)S(1)} %get-tuple-element.80), channel_id=1, source_target_pairs={{0,1},{1,0},{2,3},{3,2},{4,5},{5,4},{6,7},{7,6},{8,9},{9,8},{10,11... | collective-permute-start | bytes 1572872 | tf_op jit(solution)/shard_map/ppermute | solution.py:461
  71.9 7.0 %collective-permute-start.17 = (bf16[256,256]{1,0:T(8,128)(2,1)S(1)}, bf16[256,256]{1,0:T(8,128)(2,1)S(1)}, u32[]{:S(2)}, u32[]{:S(2)}) collective-permute-start(bf16[256,256]{1,0:T(8,128)(2,1)S(1)} %get-tuple-element.114), channel_id=1, source_target_pairs={{0,2},{1,3},{2,4},{3,5},{4,6},{5,7},{6,8},{7,9},{8,10},{9,11},{10,... | collective-permute-start | bytes 393224 | tf_op jit(solution)/shard_map/ppermute | solution.py:454
  72.5 6.3 %collective-permute-start.16 = (bf16[256,256]{1,0:T(8,128)(2,1)S(1)}, bf16[256,256]{1,0:T(8,128)(2,1)S(1)}, u32[]{:S(2)}, u32[]{:S(2)}) collective-permute-start(bf16[256,256]{1,0:T(8,128)(2,1)S(1)} %get-tuple-element.115), channel_id=1, source_target_pairs={{0,14},{1,15},{2,0},{3,1},{4,2},{5,3},{6,4},{7,5},{8,6},{9,7},{10,... | collective-permute-start | bytes 393224 | tf_op jit(solution)/shard_map/ppermute | solution.py:454
  78.9 8.3 %collective-permute-start.20 = (bf16[256,256]{1,0:T(8,128)(2,1)S(1)}, bf16[256,256]{1,0:T(8,128)(2,1)S(1)}, u32[]{:S(2)}, u32[]{:S(2)}) collective-permute-start(bf16[256,256]{1,0:T(8,128)(2,1)S(1)} %get-tuple-element.112), channel_id=1, source_target_pairs={{0,14},{1,15},{2,0},{3,1},{4,2},{5,3},{6,4},{7,5},{8,6},{9,7},{10,... | collective-permute-start | bytes 393224 | tf_op jit(solution)/shard_map/ppermute | solution.py:454
  82.0 6.9 %collective-permute-start.19 = (bf16[256,256]{1,0:T(8,128)(2,1)S(1)}, bf16[256,256]{1,0:T(8,128)(2,1)S(1)}, u32[]{:S(2)}, u32[]{:S(2)}) collective-permute-start(bf16[256,256]{1,0:T(8,128)(2,1)S(1)} %get-tuple-element.113), channel_id=1, source_target_pairs={{0,2},{1,3},{2,4},{3,5},{4,6},{5,7},{6,8},{7,9},{8,10},{9,11},{10,... | collective-permute-start | bytes 393224 | tf_op jit(solution)/shard_map/ppermute | solution.py:454
  82.1 8.2 %collective-permute-start.21 = (bf16[256,256]{1,0:T(8,128)(2,1)S(1)}, bf16[256,256]{1,0:T(8,128)(2,1)S(1)}, u32[]{:S(2)}, u32[]{:S(2)}) collective-permute-start(bf16[256,256]{1,0:T(8,128)(2,1)S(1)} %get-tuple-element.110), channel_id=1, source_target_pairs={{0,2},{1,3},{2,4},{3,5},{4,6},{5,7},{6,8},{7,9},{8,10},{9,11},{10,... | collective-permute-start | bytes 393224 | tf_op jit(solution)/shard_map/ppermute | solution.py:454
  82.2 8.1 %collective-permute-start.18 = (bf16[256,256]{1,0:T(8,128)(2,1)S(1)}, bf16[256,256]{1,0:T(8,128)(2,1)S(1)}, u32[]{:S(2)}, u32[]{:S(2)}) collective-permute-start(bf16[256,256]{1,0:T(8,128)(2,1)S(1)} %get-tuple-element.111), channel_id=1, source_target_pairs={{0,14},{1,15},{2,0},{3,1},{4,2},{5,3},{6,4},{7,5},{8,6},{9,7},{10,... | collective-permute-start | bytes 393224 | tf_op jit(solution)/shard_map/ppermute | solution.py:454
  85.5 4.8 %collective-permute-start.23 = (bf16[2,2,256,256]{3,2,1,0:T(8,128)(2,1)S(1)}, bf16[2,2,256,256]{3,2,1,0:T(8,128)(2,1)S(1)}, u32[]{:S(2)}, u32[]{:S(2)}) collective-permute-start(bf16[2,2,256,256]{3,2,1,0:T(8,128)(2,1)S(1)} %get-tuple-element.96), channel_id=1, source_target_pairs={{0,1},{1,0},{2,3},{3,2},{4,5},{5,4},{6,7},{7,6},{8,9},{9,8},{10,11... | collective-permute-start | bytes 1572872 | tf_op jit(solution)/shard_map/ppermute | solution.py:461
  90.3 10.2 %collective-permute-start.22 = (bf16[3,2,256,256]{3,2,1,0:T(8,128)(2,1)S(1)}, bf16[3,2,256,256]{3,2,1,0:T(8,128)(2,1)S(1)}, u32[]{:S(2)}, u32[]{:S(2)}) collective-permute-start(bf16[3,2,256,256]{3,2,1,0:T(8,128)(2,1)S(1)} %get-tuple-element.93), channel_id=1, source_target_pairs={{0,1},{1,0},{2,3},{3,2},{4,5},{5,4},{6,7},{7,6},{8,9},{9,8},{10,11... | collective-permute-start | bytes 2359304 | tf_op jit(solution)/shard_map/ppermute | solution.py:461
  90.5 7.3 %collective-permute-start.24 = (bf16[256,256]{1,0:T(8,128)(2,1)S(1)}, bf16[256,256]{1,0:T(8,128)(2,1)S(1)}, u32[]{:S(2)}, u32[]{:S(2)}) collective-permute-start(bf16[256,256]{1,0:T(8,128)(2,1)S(1)} %get-tuple-element.106), channel_id=1, source_target_pairs={{0,2},{1,3},{2,4},{3,5},{4,6},{5,7},{6,8},{7,9},{8,10},{9,11},{10,... | collective-permute-start | bytes 393224 | tf_op jit(solution)/shard_map/ppermute | solution.py:454
  90.6 7.2 %collective-permute-start.30 = (bf16[256,256]{1,0:T(8,128)(2,1)S(1)}, bf16[256,256]{1,0:T(8,128)(2,1)S(1)}, u32[]{:S(2)}, u32[]{:S(2)}) collective-permute-start(bf16[256,256]{1,0:T(8,128)(2,1)S(1)} %get-tuple-element.107), channel_id=1, source_target_pairs={{0,14},{1,15},{2,0},{3,1},{4,2},{5,3},{6,4},{7,5},{8,6},{9,7},{10,... | collective-permute-start | bytes 393224 | tf_op jit(solution)/shard_map/ppermute | solution.py:454
  93.8 6.7 %collective-permute-start.28 = (bf16[256,256]{1,0:T(8,128)(2,1)S(1)}, bf16[256,256]{1,0:T(8,128)(2,1)S(1)}, u32[]{:S(2)}, u32[]{:S(2)}) collective-permute-start(bf16[256,256]{1,0:T(8,128)(2,1)S(1)} %get-tuple-element.108), channel_id=1, source_target_pairs={{0,2},{1,3},{2,4},{3,5},{4,6},{5,7},{6,8},{7,9},{8,10},{9,11},{10,... | collective-permute-start | bytes 393224 | tf_op jit(solution)/shard_map/ppermute | solution.py:454
  93.8 6.7 %collective-permute-start.26 = (bf16[256,256]{1,0:T(8,128)(2,1)S(1)}, bf16[256,256]{1,0:T(8,128)(2,1)S(1)}, u32[]{:S(2)}, u32[]{:S(2)}) collective-permute-start(bf16[256,256]{1,0:T(8,128)(2,1)S(1)} %get-tuple-element.109), channel_id=1, source_target_pairs={{0,14},{1,15},{2,0},{3,1},{4,2},{5,3},{6,4},{7,5},{8,6},{9,7},{10,... | collective-permute-start | bytes 393224 | tf_op jit(solution)/shard_map/ppermute | solution.py:454
  100.7 6.3 %collective-permute-start.31 = (bf16[256,256]{1,0:T(8,128)(2,1)S(1)}, bf16[256,256]{1,0:T(8,128)(2,1)S(1)}, u32[]{:S(2)}, u32[]{:S(2)}) collective-permute-start(bf16[256,256]{1,0:T(8,128)(2,1)S(1)} %get-tuple-element.103), channel_id=1, source_target_pairs={{0,14},{1,15},{2,0},{3,1},{4,2},{5,3},{6,4},{7,5},{8,6},{9,7},{10,... | collective-permute-start | bytes 393224 | tf_op jit(solution)/shard_map/ppermute | solution.py:454
  103.8 6.6 %collective-permute-start.29 = (bf16[256,256]{1,0:T(8,128)(2,1)S(1)}, bf16[256,256]{1,0:T(8,128)(2,1)S(1)}, u32[]{:S(2)}, u32[]{:S(2)}) collective-permute-start(bf16[256,256]{1,0:T(8,128)(2,1)S(1)} %get-tuple-element.104), channel_id=1, source_target_pairs={{0,2},{1,3},{2,4},{3,5},{4,6},{5,7},{6,8},{7,9},{8,10},{9,11},{10,... | collective-permute-start | bytes 393224 | tf_op jit(solution)/shard_map/ppermute | solution.py:454
  103.8 8.0 %collective-permute-start.25 = (bf16[256,256]{1,0:T(8,128)(2,1)S(1)}, bf16[256,256]{1,0:T(8,128)(2,1)S(1)}, u32[]{:S(2)}, u32[]{:S(2)}) collective-permute-start(bf16[256,256]{1,0:T(8,128)(2,1)S(1)} %get-tuple-element.102), channel_id=1, source_target_pairs={{0,2},{1,3},{2,4},{3,5},{4,6},{5,7},{6,8},{7,9},{8,10},{9,11},{10,... | collective-permute-start | bytes 393224 | tf_op jit(solution)/shard_map/ppermute | solution.py:454
  103.8 8.0 %collective-permute-start.27 = (bf16[256,256]{1,0:T(8,128)(2,1)S(1)}, bf16[256,256]{1,0:T(8,128)(2,1)S(1)}, u32[]{:S(2)}, u32[]{:S(2)}) collective-permute-start(bf16[256,256]{1,0:T(8,128)(2,1)S(1)} %get-tuple-element.105), channel_id=1, source_target_pairs={{0,14},{1,15},{2,0},{3,1},{4,2},{5,3},{6,4},{7,5},{8,6},{9,7},{10,... | collective-permute-start | bytes 393224 | tf_op jit(solution)/shard_map/ppermute | solution.py:454
  110.5 5.1 %collective-permute-start.32 = (bf16[256,256]{1,0:T(8,128)(2,1)S(1)}, bf16[256,256]{1,0:T(8,128)(2,1)S(1)}, u32[]{:S(2)}, u32[]{:S(2)}) collective-permute-start(bf16[256,256]{1,0:T(8,128)(2,1)S(1)} %fusion.5), channel_id=1, source_target_pairs={{0,16},{1,17},{2,18},{3,19},{4,20},{5,21},{6,22},{7,23},{8,24},{9,... | collective-permute-start | bytes 393224 | tf_op jit(solution)/shard_map/ppermute | solution.py:504

commit v9 on v8

--- a/solution.py
+++ b/solution.py
@@ -435,11 +435,10 @@
 
 
 def gather_ctx(value):
+    shift = lambda piece, by: lax.ppermute(piece, "ctx", y_shift(by))
     across = lax.ppermute(value, "ctx", X_HALF_SWAP)
-    found = [value, across]
-    for piece in (value, across):
-        found += [lax.ppermute(piece, "ctx", y_shift(by)) for by in Y_STEPS]
-    return [found[n] for n in (0, 1, 2, 5, 3, 6, 4, 7)]
+    above = shift(value, -1)
+    return [value, across, shift(value, 1), shift(across, 1), above, shift(across, -1), shift(above, -1), shift(across, 2)]
 
 
 def pair_ctx(value):
@@ -447,7 +446,9 @@
 
 
 def gather_pairs(pair):
-    return [pair] + [lax.ppermute(pair, "ctx", y_shift(by)) for by in Y_STEPS]
+    below, above = (lax.ppermute(pair, "ctx", y_shift(by)) for by in (1, -1))
+    far = [lax.ppermute(below[0], "ctx", y_shift(1)), lax.ppermute(above[1], "ctx", y_shift(-1))]
+    return [pair, below, above, jnp.stack(far)]
 
 
 def moved(value, by):

time: 117 us -> 119 us (1.017)
  starting transfers between devices: 51.8 us -> 56.3 us
  waiting for transfers between devices: 30.1 us -> 27.1 us
    ppermute x9 -> x10, starting transfers between devices: 12.6 us -> 16.3 us  [the longest x6 9.17 us: gather_ctx(): shift = lambda piece, by: lax.ppermute(piece, 'ctx', y_shift(by))]
    ppermute x9 -> x10, waiting for transfers between devices: 5.49 us -> 3.13 us  [the longest x1 2.39 us: gather_pairs(): lax.ppermute(above[1], 'ctx', y_shift(-1))]
  transfers between devices with their start and end apart: 34 -> 35, of which waited for: 12 -> 13; matrix products, arithmetic and copies ran while one was open for 0% -> 0% of each run, Pallas kernels for 13% -> 13%
where the time goes in v9:
time: 119 us; the launch traced here: 118 us
  starting transfers between devices  56.3 us (47%)
  Pallas kernels  28.7 us (24%)
  waiting for transfers between devices  27.1 us (23%)
  local copies, waits for them, and re-layouts  4.04 us (3%)
    ppermute x14, starting transfers between devices, moved(): return lax.ppermute(value.astype(BF16), 'chan', z_shift(by))  22.6 us
    pallas_call x1, Pallas kernels, mix(): pl.pallas_call(mixer_kernel, out_shape=(jax.ShapeDtypeStruct((BLOCK, BLOC...  12.7 us
    ppermute x14, waiting for transfers between devices, moved(): return lax.ppermute(value.astype(BF16), 'chan', z_shift(by))  12.6 us
    ppermute x6, starting transfers between devices, gather_ctx(): shift = lambda piece, by: lax.ppermute(piece, 'ctx', y_shift(by))  9.17 us
    all_to_all x1, starting transfers between devices, project_features(): lax.all_to_all(jnp.broadcast_to(rows[None], (N_Z,) + rows.shape), 'chan',...  8.47 us
    pallas_call x4, Pallas kernels, project(): pl.pallas_call(functools.partial(project_kernel, part, sums is None, read...  7.95 us
    all_to_all x1, waiting for transfers between devices, project_features(): lax.all_to_all(jnp.broadcast_to(rows[None], (N_Z,) + rows.shape), 'chan',...  7.08 us
    pallas_call x3, Pallas kernels, back_project(): pl.pallas_call(functools.partial(back_kernel, begin), out_shape=(part, pa...  4 us
  transfers between devices with their start and end apart: 35, of which 13 were waited for; matrix products, arithmetic and copies ran while one was open for 0% of the time, Pallas kernels for 13%

profile of v9, /device:TPU:24, one launch (start us, length us, event | category | flops | bytes accessed | tf_op | source)
XLA Modules:
  0.0 117.9 jit_solution(13066047697802516645)
XLA Ops:
  0.6 0.9 copy-done
  1.6 0.7 broadcast_in_dim.2
  2.3 8.5 %all-to-all-start = ((bf16[8,64,256]{2,1,0:T(8,128)(2,1)}), bf16[8,64,256]{2,1,0:T(8,128)(2,1)S(1)}, u32[]{:S(2)}, u32[]{:S(2)}) async-start(bf16[8,64,256]{2,1,0:T(8,128)(2,1)} %broadcast_in_dim.2), calls=%async_computation | async-start | bytes 524288 | tf_op jit(solution)/shard_map/all_to_all | solution.py:420
  10.8 0.9 copy-done.1
  11.7 0.7 copy-done.3
  12.5 3.1 %collective-permute-start.2 = (bf16[272,256]{1,0:T(8,128)(2,1)S(1)}, bf16[272,256]{1,0:T(8,128)(2,1)S(1)}, u32[]{:S(2)}, u32[]{:S(2)}) collective-permute-start(bf16[272,256]{1,0:T(8,128)(2,1)S(1)} %payload.1), channel_id=1, source_target_pairs={{0,32},{32,0},{64,96},{96,64},{128,160},{160,128},{192,224},{224,1... | collective-permute-start | bytes 417800 | tf_op jit(solution)/shard_map/ppermute | solution.py:445
  15.6 7.1 %all-to-all-done.refs_0_ = bf16[8,64,256]{2,1,0:T(8,128)(2,1)S(1)} async-done(((bf16[8,64,256]{2,1,0:T(8,128)(2,1)}), bf16[8,64,256]{2,1,0:T(8,128)(2,1)S(1)}, u32[]{:S(2)}, u32[]{:S(2)}) %all-to-all-start) | async-done | bytes 262176 | tf_op jit(solution)/shard_map/all_to_all | solution.py:420
  22.7 0.8 collective-permute-start.5
  23.5 1.5 %collective-permute-start = (bf16[8,64,256]{2,1,0:T(8,128)(2,1)S(1)}, bf16[8,64,256]{2,1,0:T(8,128)(2,1)S(1)}, u32[]{:S(2)}, u32[]{:S(2)}) collective-permute-start(bf16[8,64,256]{2,1,0:T(8,128)(2,1)S(1)} %all-to-all-done.refs_0_), channel_id=1, source_target_pairs={{0,16},{1,17},{2,18},{3,19},{4,20},{5,21},{6,22},{7,23},{8,24},{9,... | collective-permute-start | bytes 786440 | tf_op jit(solution)/shard_map/ppermute | solution.py:423
  25.0 2.5 %collective-permute-start.4 = (bf16[2,272,256]{2,1,0:T(8,128)(2,1)S(1)}, bf16[2,272,256]{2,1,0:T(8,128)(2,1)S(1)}, u32[]{:S(2)}, u32[]{:S(2)}) collective-permute-start(bf16[2,272,256]{2,1,0:T(8,128)(2,1)S(1)} %pad_maximum_fusion.refs_8_), channel_id=1, source_target_pairs={{0,64},{32,96},{64,128},{96,160},{128,192},{160,224},{192,0},{224,... | collective-permute-start | bytes 835592 | tf_op jit(solution)/shard_map/ppermute | solution.py:449
  27.5 4.7 %project.4 = (f32[64,768]{1,0:T(8,128)S(1)}, bf16[3,8,256,256]{3,2,1,0:T(8,128)(2,1)S(1)}, bf16[3,8,256,256]{3,2,1,0:T(8,128)(2,1)S(1)}, bf16[3,8,256,256]{3,2,1,0:T(8,128)(2,1)S(1)}) custom-call(bf16[8,64,256]{2,1,0:T(8,128)(2,1)S(1)} %all-to-all-done.refs_0_, bf16[3,2,8,2,256,256]{5,4,3,2,1,0:T(8,128)(2,1)} %bitcast.80), custom_call_target="tpu_custom_call" | custom-call | flops 201326592 | bytes 12582912 | tf_op jit(solution)/shard_map/project/pallas_call | solution.py:191
  32.2 1.1 project.5.refs_2_
  33.6 3.8 %collective-permute-start.6 = (bf16[272,256]{1,0:T(8,128)(2,1)S(1)}, bf16[272,256]{1,0:T(8,128)(2,1)S(1)}, u32[]{:S(2)}, u32[]{:S(2)}) collective-permute-start(bf16[272,256]{1,0:T(8,128)(2,1)S(1)} %slice_bitcast_fusion.1), channel_id=1, source_target_pairs={{0,64},{32,96},{64,128},{96,160},{128,192},{160,224},{192,0},{224,... | collective-permute-start | bytes 417800 | tf_op jit(solution)/shard_map/ppermute | solution.py:450
  37.3 1.1 project.6.refs_2_
  38.4 2.4 %collective-permute-done.7 = bf16[272,256]{1,0:T(8,128)(2,1)S(1)} collective-permute-done((bf16[272,256]{1,0:T(8,128)(2,1)S(1)}, bf16[272,256]{1,0:T(8,128)(2,1)S(1)}, u32[]{:S(2)}, u32[]{:S(2)}) %collective-permute-start.7) | collective-permute-done | bytes 139296 | tf_op jit(solution)/shard_map/ppermute | solution.py:450
  40.8 1.1 project.7.refs_0_
  41.9 2.8 %collective-permute-start.8 = (bf16[64,768]{1,0:T(8,128)(2,1)S(1)}, bf16[64,768]{1,0:T(8,128)(2,1)S(1)}, u32[]{:S(2)}, u32[]{:S(2)}) collective-permute-start(bf16[64,768]{1,0:T(8,128)(2,1)S(1)} %project.7.refs_0_), channel_id=1, source_target_pairs={{0,32},{32,0},{64,96},{96,64},{128,160},{160,128},{192,224},{224,1... | collective-permute-start | bytes 294920 | tf_op jit(solution)/shard_map/ppermute | solution.py:439
  44.8 3.2 %collective-permute-start.9 = (bf16[64,768]{1,0:T(8,128)(2,1)S(1)}, bf16[64,768]{1,0:T(8,128)(2,1)S(1)}, u32[]{:S(2)}, u32[]{:S(2)}) collective-permute-start(bf16[64,768]{1,0:T(8,128)(2,1)S(1)} %project.7.refs_0_), channel_id=1, source_target_pairs={{0,64},{32,96},{64,128},{96,160},{128,192},{160,224},{192,0},{224,... | collective-permute-start | bytes 294920 | tf_op jit(solution)/shard_map/ppermute | solution.py:438
  48.1 1.6 %collective-permute-start.14 = (bf16[64,768]{1,0:T(8,128)(2,1)S(1)}, bf16[64,768]{1,0:T(8,128)(2,1)S(1)}, u32[]{:S(2)}, u32[]{:S(2)}) collective-permute-start(bf16[64,768]{1,0:T(8,128)(2,1)S(1)} %collective-permute-done.8.refs_1_), channel_id=1, source_target_pairs={{0,128},{32,160},{64,192},{96,224},{128,0},{160,32},{192,64},{224,... | collective-permute-start | bytes 294920 | tf_op jit(solution)/shard_map/ppermute | solution.py:438
  49.7 2.3 %collective-permute-start.12 = (bf16[64,768]{1,0:T(8,128)(2,1)S(1)}, bf16[64,768]{1,0:T(8,128)(2,1)S(1)}, u32[]{:S(2)}, u32[]{:S(2)}) collective-permute-start(bf16[64,768]{1,0:T(8,128)(2,1)S(1)} %collective-permute-done.8.refs_1_), channel_id=1, source_target_pairs={{0,192},{32,224},{64,0},{96,32},{128,64},{160,96},{192,128},{224,1... | collective-permute-start | bytes 294920 | tf_op jit(solution)/shard_map/ppermute | solution.py:438
  52.0 0.9 collective-permute-start.10
  52.9 1.1 collective-permute-start.13
  54.1 3.9 %filter_tables.1 = (bf16[16,256,256]{2,1,0:T(8,128)(2,1)S(1)}, bf16[256,1152]{1,0:T(8,128)(2,1)S(1)}, f32[2,256]{1,0:T(2,128)S(1)}, f32[768,3]{1,0:T(8,128)S(1)}) custom-call(f32[16,16]{1,0:T(8,128)S(1)} %copy-done.2, f32[16,16]{1,0:T(8,128)S(1)} %sqrt_multiply_fusion.gain_ref, f32[3,3,256]{2,1,0:T(4,128)S(1)} %copy-done.4), custom_call_target="tpu_custom_call" | custom-call | flops 402653184 | bytes 5242880 | tf_op jit(solution)/shard_map/filter_tables/pallas_call | solution.py:141
  58.1 0.7 collective-permute-done.13.refs_6_
  58.8 12.7 %mixer.1 = (bf16[256,256]{1,0:T(8,128)(2,1)}, bf16[768,256]{1,0:T(8,128)(2,1)S(1)}, bf16[1,2,256,256]{3,2,1,0:T(8,128)(2,1)S(1)}, bf16[1,2,256,256]{3,2,1,0:T(8,...) custom-call(bf16[64,768]{1,0:T(8,128)(2,1)S(1)} %project.7.refs_0_, bf16[64,768]{1,0:T(8,128)(2,1)S(1)} %collective-permute-done.8.refs_1_, ...), custom_call_target="tpu_custom_call" | custom-call | flops 3221225472 | bytes 8388608 | tf_op jit(solution)/shard_map/mixer/pallas_call | solution.py:368
  71.6 1.1 back_project.3
  72.7 0.4 collective-permute-done.15
  73.4 0.6 collective-permute-start.18
  74.0 2.7 %collective-permute-start.17 = (bf16[256,256]{1,0:T(8,128)(2,1)S(1)}, bf16[256,256]{1,0:T(8,128)(2,1)S(1)}, u32[]{:S(2)}, u32[]{:S(2)}) collective-permute-start(bf16[256,256]{1,0:T(8,128)(2,1)S(1)} %get-tuple-element.115), channel_id=1, source_target_pairs={{0,14},{1,15},{2,0},{3,1},{4,2},{5,3},{6,4},{7,5},{8,6},{9,7},{10,... | collective-permute-start | bytes 393224 | tf_op jit(solution)/shard_map/ppermute | solution.py:455
  76.7 1.1 back_project.4
  77.9 2.5 %collective-permute-done.18 = bf16[256,256]{1,0:T(8,128)(2,1)S(1)} collective-permute-done((bf16[256,256]{1,0:T(8,128)(2,1)S(1)}, bf16[256,256]{1,0:T(8,128)(2,1)S(1)}, u32[]{:S(2)}, u32[]{:S(2)}) %collective-permute-start.18) | collective-permute-done | bytes 131104 | tf_op jit(solution)/shard_map/ppermute | solution.py:455
  80.5 3.0 %collective-permute-start.21 = (bf16[256,256]{1,0:T(8,128)(2,1)S(1)}, bf16[256,256]{1,0:T(8,128)(2,1)S(1)}, u32[]{:S(2)}, u32[]{:S(2)}) collective-permute-start(bf16[256,256]{1,0:T(8,128)(2,1)S(1)} %get-tuple-element.112), channel_id=1, source_target_pairs={{0,14},{1,15},{2,0},{3,1},{4,2},{5,3},{6,4},{7,5},{8,6},{9,7},{10,... | collective-permute-start | bytes 393224 | tf_op jit(solution)/shard_map/ppermute | solution.py:455
  83.7 3.3 %collective-permute-start.19 = (bf16[256,256]{1,0:T(8,128)(2,1)S(1)}, bf16[256,256]{1,0:T(8,128)(2,1)S(1)}, u32[]{:S(2)}, u32[]{:S(2)}) collective-permute-start(bf16[256,256]{1,0:T(8,128)(2,1)S(1)} %get-tuple-element.111), channel_id=1, source_target_pairs={{0,14},{1,15},{2,0},{3,1},{4,2},{5,3},{6,4},{7,5},{8,6},{9,7},{10,... | collective-permute-start | bytes 393224 | tf_op jit(solution)/shard_map/ppermute | solution.py:455
  87.0 1.7 %back_project.5 = (bf16[3,2,256,256]{3,2,1,0:T(8,128)(2,1)S(1)}, bf16[3,2,256,256]{3,2,1,0:T(8,128)(2,1)S(1)}) custom-call(bf16[768,256]{1,0:T(8,128)(2,1)S(1)} %get-tuple-element.89.grad_ref, bf16[7,3,2,2,256,256]{5,4,3,2,1,0:T(8,128)(2,1)S(1)} %get-tuple-element.74.held_ref), custom_call_target="tpu_custom_call" | custom-call | flops 1207959552 | bytes 6291456 | tf_op jit(solution)/shard_map/back_project/pallas_call | solution.py:406
  88.7 1.7 %collective-permute-done.20 = bf16[256,256]{1,0:T(8,128)(2,1)S(1)} collective-permute-done((bf16[256,256]{1,0:T(8,128)(2,1)S(1)}, bf16[256,256]{1,0:T(8,128)(2,1)S(1)}, u32[]{:S(2)}, u32[]{:S(2)}) %collective-permute-start.20) | collective-permute-done | bytes 131104 | tf_op jit(solution)/shard_map/ppermute | solution.py:455
  90.4 1.4 %collective-permute-done.22 = bf16[256,256]{1,0:T(8,128)(2,1)S(1)} collective-permute-done((bf16[256,256]{1,0:T(8,128)(2,1)S(1)}, bf16[256,256]{1,0:T(8,128)(2,1)S(1)}, u32[]{:S(2)}, u32[]{:S(2)}) %collective-permute-start.22) | collective-permute-done | bytes 131104 | tf_op jit(solution)/shard_map/ppermute | solution.py:455
  91.8 0.2 fusion.9
  92.1 3.2 %collective-permute-start.31 = (bf16[256,256]{1,0:T(8,128)(2,1)S(1)}, bf16[256,256]{1,0:T(8,128)(2,1)S(1)}, u32[]{:S(2)}, u32[]{:S(2)}) collective-permute-start(bf16[256,256]{1,0:T(8,128)(2,1)S(1)} %get-tuple-element.107), channel_id=1, source_target_pairs={{0,14},{1,15},{2,0},{3,1},{4,2},{5,3},{6,4},{7,5},{8,6},{9,7},{10,... | collective-permute-start | bytes 393224 | tf_op jit(solution)/shard_map/ppermute | solution.py:455
  95.3 3.2 %collective-permute-start.27 = (bf16[256,256]{1,0:T(8,128)(2,1)S(1)}, bf16[256,256]{1,0:T(8,128)(2,1)S(1)}, u32[]{:S(2)}, u32[]{:S(2)}) collective-permute-start(bf16[256,256]{1,0:T(8,128)(2,1)S(1)} %get-tuple-element.109), channel_id=1, source_target_pairs={{0,14},{1,15},{2,0},{3,1},{4,2},{5,3},{6,4},{7,5},{8,6},{9,7},{10,... | collective-permute-start | bytes 393224 | tf_op jit(solution)/shard_map/ppermute | solution.py:455
  98.6 0.7 collective-permute-done.25
  99.3 2.7 %collective-permute-done.29 = bf16[256,256]{1,0:T(8,128)(2,1)S(1)} collective-permute-done((bf16[256,256]{1,0:T(8,128)(2,1)S(1)}, bf16[256,256]{1,0:T(8,128)(2,1)S(1)}, u32[]{:S(2)}, u32[]{:S(2)}) %collective-permute-start.29) | collective-permute-done | bytes 131104 | tf_op jit(solution)/shard_map/ppermute | solution.py:455
  102.0 0.2 fusion.8
  102.3 3.0 %collective-permute-start.32 = (bf16[256,256]{1,0:T(8,128)(2,1)S(1)}, bf16[256,256]{1,0:T(8,128)(2,1)S(1)}, u32[]{:S(2)}, u32[]{:S(2)}) collective-permute-start(bf16[256,256]{1,0:T(8,128)(2,1)S(1)} %get-tuple-element.103), channel_id=1, source_target_pairs={{0,14},{1,15},{2,0},{3,1},{4,2},{5,3},{6,4},{7,5},{8,6},{9,7},{10,... | collective-permute-start | bytes 393224 | tf_op jit(solution)/shard_map/ppermute | solution.py:455
  105.3 3.3 %collective-permute-start.28 = (bf16[256,256]{1,0:T(8,128)(2,1)S(1)}, bf16[256,256]{1,0:T(8,128)(2,1)S(1)}, u32[]{:S(2)}, u32[]{:S(2)}) collective-permute-start(bf16[256,256]{1,0:T(8,128)(2,1)S(1)} %get-tuple-element.105), channel_id=1, source_target_pairs={{0,14},{1,15},{2,0},{3,1},{4,2},{5,3},{6,4},{7,5},{8,6},{9,7},{10,... | collective-permute-start | bytes 393224 | tf_op jit(solution)/shard_map/ppermute | solution.py:455
  108.6 3.3 %collective-permute-done.30 = bf16[256,256]{1,0:T(8,128)(2,1)S(1)} collective-permute-done((bf16[256,256]{1,0:T(8,128)(2,1)S(1)}, bf16[256,256]{1,0:T(8,128)(2,1)S(1)}, u32[]{:S(2)}, u32[]{:S(2)}) %collective-permute-start.30) | collective-permute-done | bytes 131104 | tf_op jit(solution)/shard_map/ppermute | solution.py:455
  112.0 1.1 collective-permute-start.33
  113.3 3.7 %collective-permute-done.33 = bf16[256,256]{1,0:T(8,128)(2,1)S(1)} collective-permute-done((bf16[256,256]{1,0:T(8,128)(2,1)S(1)}, bf16[256,256]{1,0:T(8,128)(2,1)S(1)}, u32[]{:S(2)}, u32[]{:S(2)}) %collective-permute-start.33) | collective-permute-done | bytes 131104 | tf_op jit(solution)/shard_map/ppermute | solution.py:505
  117.2 0.8 copy.9
  (59 shorter events, 1.7 us)
Async XLA Ops:
  0.6 1.0 copy-start
  2.3 20.3 %all-to-all-start = ((bf16[8,64,256]{2,1,0:T(8,128)(2,1)}), bf16[8,64,256]{2,1,0:T(8,128)(2,1)S(1)}, u32[]{:S(2)}, u32[]{:S(2)}) async-start(bf16[8,64,256]{2,1,0:T(8,128)(2,1)} %broadcast_in_dim.2), calls=%async_computation | async-start | bytes 524288 | tf_op jit(solution)/shard_map/all_to_all | solution.py:420
  10.8 0.9 copy-start.1
  11.7 0.7 copy-start.3
  12.5 10.2 %collective-permute-start.2 = (bf16[272,256]{1,0:T(8,128)(2,1)S(1)}, bf16[272,256]{1,0:T(8,128)(2,1)S(1)}, u32[]{:S(2)}, u32[]{:S(2)}) collective-permute-start(bf16[272,256]{1,0:T(8,128)(2,1)S(1)} %payload.1), channel_id=1, source_target_pairs={{0,32},{32,0},{64,96},{96,64},{128,160},{160,128},{192,224},{224,1... | collective-permute-start | bytes 417800 | tf_op jit(solution)/shard_map/ppermute | solution.py:445
  22.7 9.5 %collective-permute-start.1 = (bf16[8,64,256]{2,1,0:T(8,128)(2,1)S(1)}, bf16[8,64,256]{2,1,0:T(8,128)(2,1)S(1)}, u32[]{:S(2)}, u32[]{:S(2)}) collective-permute-start(bf16[8,64,256]{2,1,0:T(8,128)(2,1)S(1)} %all-to-all-done.refs_0_), channel_id=1, source_target_pairs={{0,1},{1,0},{2,3},{3,2},{4,5},{5,4},{6,7},{7,6},{8,9},{9,8},{10,11... | collective-permute-start | bytes 786440 | tf_op jit(solution)/shard_map/ppermute | solution.py:424
  22.7 10.7 %collective-permute-start.5 = (bf16[2,272,256]{2,1,0:T(8,128)(2,1)S(1)}, bf16[2,272,256]{2,1,0:T(8,128)(2,1)S(1)}, u32[]{:S(2)}, u32[]{:S(2)}) collective-permute-start(bf16[2,272,256]{2,1,0:T(8,128)(2,1)S(1)} %pad_maximum_fusion.refs_8_), channel_id=1, source_target_pairs={{0,192},{32,224},{64,0},{96,32},{128,64},{160,96},{192,128},{224,1... | collective-permute-start | bytes 835592 | tf_op jit(solution)/shard_map/ppermute | solution.py:449
  23.5 9.8 %collective-permute-start = (bf16[8,64,256]{2,1,0:T(8,128)(2,1)S(1)}, bf16[8,64,256]{2,1,0:T(8,128)(2,1)S(1)}, u32[]{:S(2)}, u32[]{:S(2)}) collective-permute-start(bf16[8,64,256]{2,1,0:T(8,128)(2,1)S(1)} %all-to-all-done.refs_0_), channel_id=1, source_target_pairs={{0,16},{1,17},{2,18},{3,19},{4,20},{5,21},{6,22},{7,23},{8,24},{9,... | collective-permute-start | bytes 786440 | tf_op jit(solution)/shard_map/ppermute | solution.py:423
  25.0 8.5 %collective-permute-start.4 = (bf16[2,272,256]{2,1,0:T(8,128)(2,1)S(1)}, bf16[2,272,256]{2,1,0:T(8,128)(2,1)S(1)}, u32[]{:S(2)}, u32[]{:S(2)}) collective-permute-start(bf16[2,272,256]{2,1,0:T(8,128)(2,1)S(1)} %pad_maximum_fusion.refs_8_), channel_id=1, source_target_pairs={{0,64},{32,96},{64,128},{96,160},{128,192},{160,224},{192,0},{224,... | collective-permute-start | bytes 835592 | tf_op jit(solution)/shard_map/ppermute | solution.py:449
  33.3 7.5 %collective-permute-start.3 = (bf16[8,64,256]{2,1,0:T(8,128)(2,1)S(1)}, bf16[8,64,256]{2,1,0:T(8,128)(2,1)S(1)}, u32[]{:S(2)}, u32[]{:S(2)}) collective-permute-start(bf16[8,64,256]{2,1,0:T(8,128)(2,1)S(1)} %collective-permute-done.refs_0_), channel_id=1, source_target_pairs={{0,1},{1,0},{2,3},{3,2},{4,5},{5,4},{6,7},{7,6},{8,9},{9,8},{10,11... | collective-permute-start | bytes 786440 | tf_op jit(solution)/shard_map/ppermute | solution.py:430
  33.4 7.4 %collective-permute-start.7 = (bf16[272,256]{1,0:T(8,128)(2,1)S(1)}, bf16[272,256]{1,0:T(8,128)(2,1)S(1)}, u32[]{:S(2)}, u32[]{:S(2)}) collective-permute-start(bf16[272,256]{1,0:T(8,128)(2,1)S(1)} %slice_bitcast_fusion), channel_id=1, source_target_pairs={{0,192},{32,224},{64,0},{96,32},{128,64},{160,96},{192,128},{224,1... | collective-permute-start | bytes 417800 | tf_op jit(solution)/shard_map/ppermute | solution.py:450
  33.6 7.2 %collective-permute-start.6 = (bf16[272,256]{1,0:T(8,128)(2,1)S(1)}, bf16[272,256]{1,0:T(8,128)(2,1)S(1)}, u32[]{:S(2)}, u32[]{:S(2)}) collective-permute-start(bf16[272,256]{1,0:T(8,128)(2,1)S(1)} %slice_bitcast_fusion.1), channel_id=1, source_target_pairs={{0,64},{32,96},{64,128},{96,160},{128,192},{160,224},{192,0},{224,... | collective-permute-start | bytes 417800 | tf_op jit(solution)/shard_map/ppermute | solution.py:450
  37.3 16.8 %copy-start.2 = (f32[16,16]{1,0:T(8,128)S(1)}, f32[16,16]{1,0:T(8,128)}, u32[]{:S(2)}) copy-start(f32[16,16]{1,0:T(8,128)} %rate_ref) | copy-start | bytes 3076
  37.3 16.8 %copy-start.5 = (f32[16,16]{1,0:T(8,128)S(1)}, f32[16,16]{1,0:T(8,128)}, u32[]{:S(2)}) copy-start(f32[16,16]{1,0:T(8,128)} %param.12) | copy-start | bytes 3076
  37.3 16.8 %copy-start.4 = (f32[3,3,256]{2,1,0:T(4,128)S(1)}, f32[3,3,256]{2,1,0:T(4,128)}, u32[]{:S(2)}) copy-start(f32[3,3,256]{2,1,0:T(4,128)} %tap_ref.1) | copy-start | bytes 27652
  41.9 6.2 %collective-permute-start.8 = (bf16[64,768]{1,0:T(8,128)(2,1)S(1)}, bf16[64,768]{1,0:T(8,128)(2,1)S(1)}, u32[]{:S(2)}, u32[]{:S(2)}) collective-permute-start(bf16[64,768]{1,0:T(8,128)(2,1)S(1)} %project.7.refs_0_), channel_id=1, source_target_pairs={{0,32},{32,0},{64,96},{96,64},{128,160},{160,128},{192,224},{224,1... | collective-permute-start | bytes 294920 | tf_op jit(solution)/shard_map/ppermute | solution.py:439
  44.8 8.2 %collective-permute-start.11 = (bf16[64,768]{1,0:T(8,128)(2,1)S(1)}, bf16[64,768]{1,0:T(8,128)(2,1)S(1)}, u32[]{:S(2)}, u32[]{:S(2)}) collective-permute-start(bf16[64,768]{1,0:T(8,128)(2,1)S(1)} %project.7.refs_0_), channel_id=1, source_target_pairs={{0,192},{32,224},{64,0},{96,32},{128,64},{160,96},{192,128},{224,1... | collective-permute-start | bytes 294920 | tf_op jit(solution)/shard_map/ppermute | solution.py:438
  44.8 13.3 %collective-permute-start.9 = (bf16[64,768]{1,0:T(8,128)(2,1)S(1)}, bf16[64,768]{1,0:T(8,128)(2,1)S(1)}, u32[]{:S(2)}, u32[]{:S(2)}) collective-permute-start(bf16[64,768]{1,0:T(8,128)(2,1)S(1)} %project.7.refs_0_), channel_id=1, source_target_pairs={{0,64},{32,96},{64,128},{96,160},{128,192},{160,224},{192,0},{224,... | collective-permute-start | bytes 294920 | tf_op jit(solution)/shard_map/ppermute | solution.py:438
  48.1 10.6 %collective-permute-start.14 = (bf16[64,768]{1,0:T(8,128)(2,1)S(1)}, bf16[64,768]{1,0:T(8,128)(2,1)S(1)}, u32[]{:S(2)}, u32[]{:S(2)}) collective-permute-start(bf16[64,768]{1,0:T(8,128)(2,1)S(1)} %collective-permute-done.8.refs_1_), channel_id=1, source_target_pairs={{0,128},{32,160},{64,192},{96,224},{128,0},{160,32},{192,64},{224,... | collective-permute-start | bytes 294920 | tf_op jit(solution)/shard_map/ppermute | solution.py:438
  49.7 9.1 %collective-permute-start.12 = (bf16[64,768]{1,0:T(8,128)(2,1)S(1)}, bf16[64,768]{1,0:T(8,128)(2,1)S(1)}, u32[]{:S(2)}, u32[]{:S(2)}) collective-permute-start(bf16[64,768]{1,0:T(8,128)(2,1)S(1)} %collective-permute-done.8.refs_1_), channel_id=1, source_target_pairs={{0,192},{32,224},{64,0},{96,32},{128,64},{160,96},{192,128},{224,1... | collective-permute-start | bytes 294920 | tf_op jit(solution)/shard_map/ppermute | solution.py:438
  52.0 6.7 %collective-permute-start.10 = (bf16[64,768]{1,0:T(8,128)(2,1)S(1)}, bf16[64,768]{1,0:T(8,128)(2,1)S(1)}, u32[]{:S(2)}, u32[]{:S(2)}) collective-permute-start(bf16[64,768]{1,0:T(8,128)(2,1)S(1)} %collective-permute-done.8.refs_1_), channel_id=1, source_target_pairs={{0,64},{32,96},{64,128},{96,160},{128,192},{160,224},{192,0},{224,... | collective-permute-start | bytes 294920 | tf_op jit(solution)/shard_map/ppermute | solution.py:438
  52.9 5.8 %collective-permute-start.13 = (bf16[64,768]{1,0:T(8,128)(2,1)S(1)}, bf16[64,768]{1,0:T(8,128)(2,1)S(1)}, u32[]{:S(2)}, u32[]{:S(2)}) collective-permute-start(bf16[64,768]{1,0:T(8,128)(2,1)S(1)} %collective-permute-done.11.refs_4_), channel_id=1, source_target_pairs={{0,192},{32,224},{64,0},{96,32},{128,64},{160,96},{192,128},{224,1... | collective-permute-start | bytes 294920 | tf_op jit(solution)/shard_map/ppermute | solution.py:438
  71.5 1.6 %collective-permute-start.15 = (bf16[1,2,256,256]{3,2,1,0:T(8,128)(2,1)S(1)}, bf16[1,2,256,256]{3,2,1,0:T(8,128)(2,1)S(1)}, u32[]{:S(2)}, u32[]{:S(2)}) collective-permute-start(bf16[1,2,256,256]{3,2,1,0:T(8,128)(2,1)S(1)} %get-tuple-element.73), channel_id=1, source_target_pairs={{0,1},{1,0},{2,3},{3,2},{4,5},{5,4},{6,7},{7,6},{8,9},{9,8},{10,11... | collective-permute-start | bytes 786440 | tf_op jit(solution)/shard_map/ppermute | solution.py:462
  73.1 7.3 %collective-permute-start.16 = (bf16[2,2,256,256]{3,2,1,0:T(8,128)(2,1)S(1)}, bf16[2,2,256,256]{3,2,1,0:T(8,128)(2,1)S(1)}, u32[]{:S(2)}, u32[]{:S(2)}) collective-permute-start(bf16[2,2,256,256]{3,2,1,0:T(8,128)(2,1)S(1)} %get-tuple-element.80), channel_id=1, source_target_pairs={{0,1},{1,0},{2,3},{3,2},{4,5},{5,4},{6,7},{7,6},{8,9},{9,8},{10,11... | collective-permute-start | bytes 1572872 | tf_op jit(solution)/shard_map/ppermute | solution.py:462
  73.4 7.0 %collective-permute-start.18 = (bf16[256,256]{1,0:T(8,128)(2,1)S(1)}, bf16[256,256]{1,0:T(8,128)(2,1)S(1)}, u32[]{:S(2)}, u32[]{:S(2)}) collective-permute-start(bf16[256,256]{1,0:T(8,128)(2,1)S(1)} %get-tuple-element.114), channel_id=1, source_target_pairs={{0,2},{1,3},{2,4},{3,5},{4,6},{5,7},{6,8},{7,9},{8,10},{9,11},{10,... | collective-permute-start | bytes 393224 | tf_op jit(solution)/shard_map/ppermute | solution.py:455
  74.0 6.3 %collective-permute-start.17 = (bf16[256,256]{1,0:T(8,128)(2,1)S(1)}, bf16[256,256]{1,0:T(8,128)(2,1)S(1)}, u32[]{:S(2)}, u32[]{:S(2)}) collective-permute-start(bf16[256,256]{1,0:T(8,128)(2,1)S(1)} %get-tuple-element.115), channel_id=1, source_target_pairs={{0,14},{1,15},{2,0},{3,1},{4,2},{5,3},{6,4},{7,5},{8,6},{9,7},{10,... | collective-permute-start | bytes 393224 | tf_op jit(solution)/shard_map/ppermute | solution.py:455
  80.5 8.3 %collective-permute-start.21 = (bf16[256,256]{1,0:T(8,128)(2,1)S(1)}, bf16[256,256]{1,0:T(8,128)(2,1)S(1)}, u32[]{:S(2)}, u32[]{:S(2)}) collective-permute-start(bf16[256,256]{1,0:T(8,128)(2,1)S(1)} %get-tuple-element.112), channel_id=1, source_target_pairs={{0,14},{1,15},{2,0},{3,1},{4,2},{5,3},{6,4},{7,5},{8,6},{9,7},{10,... | collective-permute-start | bytes 393224 | tf_op jit(solution)/shard_map/ppermute | solution.py:455
  83.5 6.9 %collective-permute-start.20 = (bf16[256,256]{1,0:T(8,128)(2,1)S(1)}, bf16[256,256]{1,0:T(8,128)(2,1)S(1)}, u32[]{:S(2)}, u32[]{:S(2)}) collective-permute-start(bf16[256,256]{1,0:T(8,128)(2,1)S(1)} %get-tuple-element.113), channel_id=1, source_target_pairs={{0,2},{1,3},{2,4},{3,5},{4,6},{5,7},{6,8},{7,9},{8,10},{9,11},{10,... | collective-permute-start | bytes 393224 | tf_op jit(solution)/shard_map/ppermute | solution.py:455
  83.6 8.2 %collective-permute-start.22 = (bf16[256,256]{1,0:T(8,128)(2,1)S(1)}, bf16[256,256]{1,0:T(8,128)(2,1)S(1)}, u32[]{:S(2)}, u32[]{:S(2)}) collective-permute-start(bf16[256,256]{1,0:T(8,128)(2,1)S(1)} %get-tuple-element.110), channel_id=1, source_target_pairs={{0,2},{1,3},{2,4},{3,5},{4,6},{5,7},{6,8},{7,9},{8,10},{9,11},{10,... | collective-permute-start | bytes 393224 | tf_op jit(solution)/shard_map/ppermute | solution.py:455
  83.7 8.1 %collective-permute-start.19 = (bf16[256,256]{1,0:T(8,128)(2,1)S(1)}, bf16[256,256]{1,0:T(8,128)(2,1)S(1)}, u32[]{:S(2)}, u32[]{:S(2)}) collective-permute-start(bf16[256,256]{1,0:T(8,128)(2,1)S(1)} %get-tuple-element.111), channel_id=1, source_target_pairs={{0,14},{1,15},{2,0},{3,1},{4,2},{5,3},{6,4},{7,5},{8,6},{9,7},{10,... | collective-permute-start | bytes 393224 | tf_op jit(solution)/shard_map/ppermute | solution.py:455
  87.0 4.8 %collective-permute-start.24 = (bf16[2,2,256,256]{3,2,1,0:T(8,128)(2,1)S(1)}, bf16[2,2,256,256]{3,2,1,0:T(8,128)(2,1)S(1)}, u32[]{:S(2)}, u32[]{:S(2)}) collective-permute-start(bf16[2,2,256,256]{3,2,1,0:T(8,128)(2,1)S(1)} %get-tuple-element.96), channel_id=1, source_target_pairs={{0,1},{1,0},{2,3},{3,2},{4,5},{5,4},{6,7},{7,6},{8,9},{9,8},{10,11... | collective-permute-start | bytes 1572872 | tf_op jit(solution)/shard_map/ppermute | solution.py:462
  91.8 10.2 %collective-permute-start.23 = (bf16[3,2,256,256]{3,2,1,0:T(8,128)(2,1)S(1)}, bf16[3,2,256,256]{3,2,1,0:T(8,128)(2,1)S(1)}, u32[]{:S(2)}, u32[]{:S(2)}) collective-permute-start(bf16[3,2,256,256]{3,2,1,0:T(8,128)(2,1)S(1)} %get-tuple-element.93), channel_id=1, source_target_pairs={{0,1},{1,0},{2,3},{3,2},{4,5},{5,4},{6,7},{7,6},{8,9},{9,8},{10,11... | collective-permute-start | bytes 2359304 | tf_op jit(solution)/shard_map/ppermute | solution.py:462
  92.0 7.3 %collective-permute-start.25 = (bf16[256,256]{1,0:T(8,128)(2,1)S(1)}, bf16[256,256]{1,0:T(8,128)(2,1)S(1)}, u32[]{:S(2)}, u32[]{:S(2)}) collective-permute-start(bf16[256,256]{1,0:T(8,128)(2,1)S(1)} %get-tuple-element.106), channel_id=1, source_target_pairs={{0,2},{1,3},{2,4},{3,5},{4,6},{5,7},{6,8},{7,9},{8,10},{9,11},{10,... | collective-permute-start | bytes 393224 | tf_op jit(solution)/shard_map/ppermute | solution.py:455
  92.1 7.2 %collective-permute-start.31 = (bf16[256,256]{1,0:T(8,128)(2,1)S(1)}, bf16[256,256]{1,0:T(8,128)(2,1)S(1)}, u32[]{:S(2)}, u32[]{:S(2)}) collective-permute-start(bf16[256,256]{1,0:T(8,128)(2,1)S(1)} %get-tuple-element.107), channel_id=1, source_target_pairs={{0,14},{1,15},{2,0},{3,1},{4,2},{5,3},{6,4},{7,5},{8,6},{9,7},{10,... | collective-permute-start | bytes 393224 | tf_op jit(solution)/shard_map/ppermute | solution.py:455
  95.3 6.7 %collective-permute-start.29 = (bf16[256,256]{1,0:T(8,128)(2,1)S(1)}, bf16[256,256]{1,0:T(8,128)(2,1)S(1)}, u32[]{:S(2)}, u32[]{:S(2)}) collective-permute-start(bf16[256,256]{1,0:T(8,128)(2,1)S(1)} %get-tuple-element.108), channel_id=1, source_target_pairs={{0,2},{1,3},{2,4},{3,5},{4,6},{5,7},{6,8},{7,9},{8,10},{9,11},{10,... | collective-permute-start | bytes 393224 | tf_op jit(solution)/shard_map/ppermute | solution.py:455
  95.3 6.7 %collective-permute-start.27 = (bf16[256,256]{1,0:T(8,128)(2,1)S(1)}, bf16[256,256]{1,0:T(8,128)(2,1)S(1)}, u32[]{:S(2)}, u32[]{:S(2)}) collective-permute-start(bf16[256,256]{1,0:T(8,128)(2,1)S(1)} %get-tuple-element.109), channel_id=1, source_target_pairs={{0,14},{1,15},{2,0},{3,1},{4,2},{5,3},{6,4},{7,5},{8,6},{9,7},{10,... | collective-permute-start | bytes 393224 | tf_op jit(solution)/shard_map/ppermute | solution.py:455
  102.3 6.3 %collective-permute-start.32 = (bf16[256,256]{1,0:T(8,128)(2,1)S(1)}, bf16[256,256]{1,0:T(8,128)(2,1)S(1)}, u32[]{:S(2)}, u32[]{:S(2)}) collective-permute-start(bf16[256,256]{1,0:T(8,128)(2,1)S(1)} %get-tuple-element.103), channel_id=1, source_target_pairs={{0,14},{1,15},{2,0},{3,1},{4,2},{5,3},{6,4},{7,5},{8,6},{9,7},{10,... | collective-permute-start | bytes 393224 | tf_op jit(solution)/shard_map/ppermute | solution.py:455
  105.3 6.6 %collective-permute-start.30 = (bf16[256,256]{1,0:T(8,128)(2,1)S(1)}, bf16[256,256]{1,0:T(8,128)(2,1)S(1)}, u32[]{:S(2)}, u32[]{:S(2)}) collective-permute-start(bf16[256,256]{1,0:T(8,128)(2,1)S(1)} %get-tuple-element.104), channel_id=1, source_target_pairs={{0,2},{1,3},{2,4},{3,5},{4,6},{5,7},{6,8},{7,9},{8,10},{9,11},{10,... | collective-permute-start | bytes 393224 | tf_op jit(solution)/shard_map/ppermute | solution.py:455
  105.3 8.0 %collective-permute-start.26 = (bf16[256,256]{1,0:T(8,128)(2,1)S(1)}, bf16[256,256]{1,0:T(8,128)(2,1)S(1)}, u32[]{:S(2)}, u32[]{:S(2)}) collective-permute-start(bf16[256,256]{1,0:T(8,128)(2,1)S(1)} %get-tuple-element.102), channel_id=1, source_target_pairs={{0,2},{1,3},{2,4},{3,5},{4,6},{5,7},{6,8},{7,9},{8,10},{9,11},{10,... | collective-permute-start | bytes 393224 | tf_op jit(solution)/shard_map/ppermute | solution.py:455
  105.3 8.0 %collective-permute-start.28 = (bf16[256,256]{1,0:T(8,128)(2,1)S(1)}, bf16[256,256]{1,0:T(8,128)(2,1)S(1)}, u32[]{:S(2)}, u32[]{:S(2)}) collective-permute-start(bf16[256,256]{1,0:T(8,128)(2,1)S(1)} %get-tuple-element.105), channel_id=1, source_target_pairs={{0,14},{1,15},{2,0},{3,1},{4,2},{5,3},{6,4},{7,5},{8,6},{9,7},{10,... | collective-permute-start | bytes 393224 | tf_op jit(solution)/shard_map/ppermute | solution.py:455
  112.0 5.1 %collective-permute-start.33 = (bf16[256,256]{1,0:T(8,128)(2,1)S(1)}, bf16[256,256]{1,0:T(8,128)(2,1)S(1)}, u32[]{:S(2)}, u32[]{:S(2)}) collective-permute-start(bf16[256,256]{1,0:T(8,128)(2,1)S(1)} %fusion.5), channel_id=1, source_target_pairs={{0,16},{1,17},{2,18},{3,19},{4,20},{5,21},{6,22},{7,23},{8,24},{9,... | collective-permute-start | bytes 393224 | tf_op jit(solution)/shard_map/ppermute | solution.py:505
